TPU v7x, 256 devices: a whole 4x4x8 slice. The times are simulated.
256 devices in a mesh: row: 64 (over y, z, core), col: 4 (over x).
Axes of the slice: x: 4, y: 4, z: 8, core: 2. Of those that a mesh axis runs over, the one named last changes fastest.
Arguments:
- trailing: float32 [65536, 4096], P('row', 'col'), may hold values from -6 to 6
- panel_y: float32 [65536, 256], P(('row', 'col')), may hold values from -0.1875 to 0.1875
- panel_t: float32 [16384, 256], P('row'), may hold values from 0.5 to 1.5
- tree_v: float32 [3, 16384, 256], P(None, 'row'), may hold values from -0.375 to 0.375, as said below
- tree_t: float32 [3, 16384, 256], P(None, 'row'), may hold values from 0.5 to 1.5, as said below
Outputs:
- updated: float32 [65536, 4096], P('row', 'col')
Inputs may be any that keep to these rules, and one draw needn't show every extreme that they name: For each level l, the blocks of 256 rows that tree_v[l] holds for two tile rows that differ only in bit l are equal. For each level l, the blocks of 256 rows that tree_t[l] holds for two tile rows that differ only in bit l are equal.
All inputs are finite; a program needn't handle non-finite values.
Results may differ from a plain program's by a relative error of at most 0.0001.
Values sent between devices are 32-bit elements; how exact they have to be, the bound alone decides.
No kernel may reach another device: no remote copies, remote signals or barrier semaphores. Data moves between devices by JAX's collectives and lax.ppermute only.
A program may use at most 64 MiB of HBM per device.

v0:
```python
import functools
import math

import jax
import jax.numpy as jnp
from jax import lax
from jax.experimental import pallas as pl
from jax.experimental.pallas import tpu as pltpu
from jax.sharding import PartitionSpec as P


WIDTHS = (128, 128, 256, 256, 256)
F32 = jnp.float32
BF16 = jnp.bfloat16
VMEM = pl.BlockSpec(memory_space=pltpu.VMEM)
SMEM = pl.BlockSpec(memory_space=pltpu.SMEM)
HBM = pl.BlockSpec(memory_space=pltpu.HBM)
ANY = pl.BlockSpec(memory_space=pl.ANY)


def split(values):
    high = values.astype(BF16)
    return high, (values - high.astype(F32)).astype(BF16)


def dot3(left, right):
    mul = functools.partial(jnp.dot, preferred_element_type=F32)
    return mul(left[0], right[0]) + (mul(left[0], right[1]) + mul(left[1], right[0]))


def grids(shape):
    return lax.broadcasted_iota(jnp.int32, shape, 0), lax.broadcasted_iota(jnp.int32, shape, 1)


def unit_lower(values, first_row):
    rows, cols = grids(values.shape)
    rows = rows + first_row
    return jnp.where(rows > cols, values, jnp.where(rows == cols, F32(1.0), F32(0.0)))


def triangle_factor(values):
    rows, cols = grids(values.shape)
    scale = 2.0 / math.sqrt(values.shape[-1])
    return jnp.where(rows == cols, values, jnp.where(cols > rows, (values - 1.0) * scale, F32(0.0)))


def upper_part(values):
    rows, cols = grids(values.shape)
    return jnp.where(cols >= rows, values, F32(0.0))


def mix_level(leads, tree_v, tree_t, high, low):
    width = tree_v.shape[0]
    vees = upper_part(tree_v)
    tees = split(triangle_factor(tree_t).T)

    @pl.when(leads)
    def _():
        high[:, :width], low[:, :width] = tees
        high[:, width:], low[:, width:] = split(dot3(tees, split(vees.T)))

    @pl.when(jnp.logical_not(leads))
    def _():
        both = split(dot3(split(vees), tees))
        high[:, width:], low[:, width:] = both
        high[:, :width], low[:, :width] = split(dot3(both, split(vees.T)))


def start_all(pairs, sems):
    copies = [pltpu.make_async_copy(a, b, sems.at[i]) for i, (a, b) in enumerate(pairs)]
    for copy in copies:
        copy.start()
    return copies


def prepare_kernel(place, panel_t, tree_v, tree_t, trailing, th, tl, high, low, block, tri, vee, tee, sems):
    piece = trailing.at[:, : block.shape[1]]
    copies = start_all(((panel_t, tri), (tree_v.at[0], vee), (tree_t.at[0], tee), (piece, block)), sems)
    copies[0].wait()
    th[...], tl[...] = split(triangle_factor(tri[...]).T)
    copies[1].wait()
    copies[2].wait()
    mix_level(place[0] & 1 == 0, vee[...], tee[...], high, low)
    copies[3].wait()


def mixes_kernel(place, tree_v, tree_t, trailing, after, *args):
    del after
    levels = tree_v.shape[0]
    mixes, block, (vee, tee, sems) = args[:-4], args[-4], args[-3:]
    pairs = []
    for level in range(1, levels):
        pairs += [(tree_v.at[level], vee.at[level - 1]), (tree_t.at[level], tee.at[level - 1])]
    pairs.append((trailing.at[:, trailing.shape[1] - block.shape[1] :], block))
    copies = start_all(pairs, sems)
    for level in range(1, levels):
        copies[2 * level - 2].wait()
        copies[2 * level - 1].wait()
        mix_level((place[0] >> level) & 1 == 0, vee[level - 1], tee[level - 1], *mixes[2 * level - 2 : 2 * level])
    copies[-1].wait()


def opposite_rows(col, size, count):
    return pl.multiple_of(lax.rem(col + count // 2, count) * size, size)


def keep(rows, start, yh, yl, fh, fl):
    here = pl.ds(start, rows.shape[0])
    rows = unit_lower(rows, start)
    flipped = split(rows.T)
    yh[here, :], yl[here, :] = split(rows)
    fh[:, here], fl[:, here] = flipped
    return flipped


def early_kernel(place, own, left_a, left_b, right_a, right_b, block, partial, yh, yl, fh, fl):
    col = place[1]
    size = own.shape[0]
    count = block.shape[0] // size
    width = partial.shape[1]
    total = None
    for shift, parts in ((0, (own,)), (count - 1, (left_a, left_b)), (1, (right_a, right_b))):
        start = pl.multiple_of(lax.rem(col + shift, count) * size, size)
        rows = parts[0][...] if len(parts) == 1 else jnp.concatenate([p[...] for p in parts], axis=0)
        flipped = keep(rows, start, yh, yl, fh, fl)
        term = dot3(flipped, split(block[pl.ds(start, size), :width]))
        total = term if total is None else total + term
    partial[...] = total


def first_kernel(place, partial, opp_a, opp_b, block, th, tl, *args):
    top, proj, gh, gl, yh, yl, fh, fl = args[4:]
    size = 2 * opp_a.shape[0]
    width = partial.shape[1]
    start = opposite_rows(place[1], size, block.shape[0] // size)
    rows = jnp.concatenate([opp_a[...], opp_b[...]], axis=0)
    flipped = keep(rows, start, yh, yl, fh, fl)
    gain = split(dot3((yh[:size, :], yl[:size, :]), (th[...], tl[...])))
    value = partial[...] + dot3(flipped, split(block[pl.ds(start, size), :width]))
    top[...] = block[:size, :width] - dot3(gain, split(value))
    proj[...] = value
    gh[...], gl[...] = gain


def next_kernel(span, block, fh, fl, gh, gl, top, proj):
    values = block[:, span]
    value = dot3((fh[...], fl[...]), split(values))
    top[...] = values[: top.shape[0]] - dot3((gh[...], gl[...]), split(value))
    proj[...] = value


def rest_kernel(block, yh, yl, th, tl, *args):
    projs, out = args[:-1], args[-1]
    first = 0
    for proj in projs:
        span = slice(first, first + proj.shape[1])
        weight = dot3((th[...], tl[...]), split(proj[...]))
        out[:, span] = block[:, span] - dot3((yh[...], yl[...]), split(weight))
        first += proj.shape[1]


def mixed(mine, theirs, high, low):
    width = mine.shape[0]
    one = dot3((high[:, :width], low[:, :width]), split(mine[...]))
    two = dot3((high[:, width:], low[:, width:]), split(theirs[...]))
    return mine[...] - (one + two)


def level_kernel(mine, theirs, high, low, out):
    out[...] = mixed(mine, theirs, high, low)


def final_kernel(mine, theirs, high, low, whole, out):
    out[...] = mixed(mine, theirs, high, low)


def shaped(shape, dtype=F32):
    return jax.ShapeDtypeStruct(shape, dtype)


EARLY = 2


def call(kernel, **options):
    mib = options.pop("mib")
    flops, moved = options.pop("cost")
    return pl.pallas_call(
        kernel,
        compiler_params=pltpu.CompilerParams(vmem_limit_bytes=mib << 20),
        cost_estimate=pl.CostEstimate(flops=flops, bytes_accessed=moved, transcendentals=0),
        **options,
    )


def fixed(values):
    return pltpu.with_memory_space_constraint(values, pltpu.HBM)


def whole(shape):
    return pl.BlockSpec(shape, lambda i: (0, 0))


def update(trailing, panel_y, panel_t, tree_v, tree_t):
    size, width = panel_y.shape
    rows, columns = trailing.shape
    levels = tree_v.shape[0]
    half = size // 2
    count = lax.axis_size("col")
    place = jnp.stack([lax.axis_index("row"), lax.axis_index("col")]).astype(jnp.int32)
    onward = [(c, (c + 1) % count) for c in range(count)]
    backward = [(c, (c - 1) % count) for c in range(count)]

    own_a, own_b = panel_y[:half], panel_y[half:]
    left_a = lax.ppermute(own_a, "col", onward)
    right_b = lax.ppermute(own_b, "col", backward)
    left_b = lax.ppermute(own_b, "col", onward)
    right_a = lax.ppermute(own_a, "col", backward)
    opp_a = lax.ppermute(left_a, "col", onward)
    opp_b = lax.ppermute(right_b, "col", backward)

    square = shaped((width, width), BF16)
    mix = shaped((width, 2 * width), BF16)
    tall = shaped((rows, width), BF16)
    wide = shaped((width, rows), BF16)
    ahead = sum(WIDTHS[:EARLY])
    cube = 2 * 3 * width**3
    trailing = fixed(trailing)
    panel_t, tree_v, tree_t = fixed(panel_t), fixed(tree_v), fixed(tree_t)
    th, tl, high0, low0, block = call(
        prepare_kernel,
        out_shape=[square, square, mix, mix, shaped((rows, ahead))],
        in_specs=[SMEM] + [HBM] * 4,
        out_specs=[VMEM] * 5,
        scratch_shapes=[pltpu.VMEM((width, width), F32)] * 3 + [pltpu.SemaphoreType.DMA((4,))],
        mib=12,
        cost=(3 * cube, 2 << 20),
    )(place, panel_t, tree_v, tree_t, trailing)

    w = WIDTHS[0]
    partial, yh, yl, fh, fl = call(
        early_kernel,
        out_shape=[shaped((width, w)), tall, tall, wide, wide],
        in_specs=[SMEM] + [VMEM] * 6,
        out_specs=[VMEM] * 5,
        mib=12,
        cost=(2 * cube, 4 << 20),
    )(place, panel_y, left_a, left_b, right_a, right_b, block)

    top, proj, gh, gl, yh, yl, fh, fl = call(
        first_kernel,
        out_shape=[shaped((width, w))] * 2 + [square] * 2 + [tall, tall, wide, wide],
        in_specs=[SMEM] + [VMEM] * 10,
        out_specs=[VMEM] * 8,
        mib=12,
        input_output_aliases={7: 4, 8: 5, 9: 6, 10: 7},
        cost=(2 * cube, 2 << 20),
    )(place, partial, opp_a, opp_b, block, th, tl, yh, yl, fh, fl)
    tops, projs = [top], [proj]

    spans, first = [], 0
    for w in WIDTHS:
        spans.append(slice(first, first + w))
        first += w
    mixes = [(high0, low0)]
    out = None

    def exchange(level, k):
        route = [(r, r ^ (1 << level)) for r in range(lax.axis_size("row"))]
        theirs = lax.ppermute(tops[k], "row", route)
        high, low = mixes[level]
        w = WIDTHS[k]
        estimate = (2 * cube * w // width, 1 << 20)
        if level < levels - 1:
            tops[k] = call(
                level_kernel, out_shape=shaped((width, w)), in_specs=[VMEM] * 4, out_specs=VMEM, mib=8, cost=estimate
            )(tops[k], theirs, high, low)
            return out
        spot = spans[k].start // w
        return call(
            final_kernel,
            grid=(1,),
            out_shape=shaped((rows, columns)),
            in_specs=[whole((width, w)), whole((width, w)), whole((width, 2 * width)), whole((width, 2 * width)), ANY],
            out_specs=pl.BlockSpec((width, w), lambda i: (0, spot)),
            input_output_aliases={4: 0},
            mib=8,
            cost=estimate,
        )(tops[k], theirs, high, low, out)

    exchange(0, 0)
    *later, block_late = call(
        mixes_kernel,
        out_shape=[mix] * (2 * levels - 2) + [shaped((rows, columns - ahead))],
        in_specs=[SMEM] + [HBM] * 3 + [ANY],
        out_specs=[VMEM] * (2 * levels - 1),
        scratch_shapes=[pltpu.VMEM((levels - 1, width, width), F32)] * 2
        + [pltpu.SemaphoreType.DMA((2 * levels - 1,))],
        mib=16,
        cost=(2 * (levels - 1) * cube, 4 << 20),
    )(place, tree_v, tree_t, trailing, tops[0])
    mixes += [(later[2 * i], later[2 * i + 1]) for i in range(levels - 1)]

    for k in range(1, len(WIDTHS)):
        source, offset = (block, 0) if k < EARLY else (block_late, ahead)
        span = slice(spans[k].start - offset, spans[k].stop - offset)
        top, proj = call(
            functools.partial(next_kernel, span),
            out_shape=[shaped((width, WIDTHS[k]))] * 2,
            in_specs=[VMEM] * 5,
            out_specs=[VMEM] * 2,
            mib=16,
            cost=(5 * cube * WIDTHS[k] // width, 2 << 20),
        )(source, fh, fl, gh, gl)
        tops.append(top)
        projs.append(proj)
        exchange(0, k)

    out = call(
        rest_kernel,
        grid=(rows // size - 1,),
        out_shape=shaped((rows, columns)),
        in_specs=[
            pl.BlockSpec((size, columns), lambda i: (i + 1, 0)),
            pl.BlockSpec((size, width), lambda i: (i + 1, 0)),
            pl.BlockSpec((size, width), lambda i: (i + 1, 0)),
            whole((width, width)),
            whole((width, width)),
        ]
        + [whole((width, w)) for w in WIDTHS],
        out_specs=pl.BlockSpec((size, columns), lambda i: (i + 1, 0)),
        mib=20,
        cost=(20 * cube, 8 << 20),
    )(trailing, yh, yl, th, tl, *projs)

    for level in range(1, levels):
        for k in range(len(WIDTHS)):
            out = exchange(level, k)
    return out


def solution(mesh):
    placed = (
        P("row", "col"),
        P(("row", "col"), None),
        P("row", None),
        P(None, "row", None),
        P(None, "row", None),
    )
    return jax.shard_map(update, mesh=mesh, in_specs=placed, out_specs=P("row", "col"), check_vma=False)
```

profile of v0, /device:TPU:8, one launch (start us, length us, event | category | flops | bytes accessed | tf_op | source)
XLA Modules:
  0.0 96.1 jit_solution(5741365855056427838)
XLA Ops:
  0.0 1.0 %fusion = (f32[128,256]{1,0:T(8,128)S(1)}, f32[128,256]{1,0:T(8,128)S(1)}) fusion(f32[256,256]{1,0:T(8,128)} %own.1), kind=kLoop, calls=%fused_computation.1 | loop fusion | bytes 524288 | tf_op jit(solution)/shard_map/slice | solution.py:213
  1.0 2.8 %collective-permute-start.3 = (f32[128,256]{1,0:T(8,128)S(1)}, f32[128,256]{1,0:T(8,128)S(1)}, u32[]{:S(2)}, u32[]{:S(2)}) collective-permute-start(f32[128,256]{1,0:T(8,128)S(1)} %get-tuple-element.67), channel_id=1, source_target_pairs={{0,3},{1,0},{2,1},{3,2},{4,7},{5,4},{6,5},{7,6},{8,11},{9,8},{10,9... | collective-permute-start | bytes 393224 | tf_op jit(solution)/shard_map/ppermute | solution.py:215
  4.6 2.5 %collective-permute-start.2 = (f32[128,256]{1,0:T(8,128)S(1)}, f32[128,256]{1,0:T(8,128)S(1)}, u32[]{:S(2)}, u32[]{:S(2)}) collective-permute-start(f32[128,256]{1,0:T(8,128)S(1)} %get-tuple-element.68), channel_id=1, source_target_pairs={{0,3},{1,0},{2,1},{3,2},{4,7},{5,4},{6,5},{7,6},{8,11},{9,8},{10,9... | collective-permute-start | bytes 393224 | tf_op jit(solution)/shard_map/ppermute | solution.py:217
  7.1 3.3 %collective-permute-start.5 = (f32[128,256]{1,0:T(8,128)S(1)}, f32[128,256]{1,0:T(8,128)S(1)}, u32[]{:S(2)}, u32[]{:S(2)}) collective-permute-start(f32[128,256]{1,0:T(8,128)S(1)} %collective-permute-done.3.right_b), channel_id=1, source_target_pairs={{0,3},{1,0},{2,1},{3,2},{4,7},{5,4},{6,5},{7,6},{8,11},{9,8},{10,9... | collective-permute-start | bytes 393224 | tf_op jit(solution)/shard_map/ppermute | solution.py:219
  10.4 1.0 %collective-permute-done.left_a = f32[128,256]{1,0:T(8,128)S(1)} collective-permute-done((f32[128,256]{1,0:T(8,128)S(1)}, f32[128,256]{1,0:T(8,128)S(1)}, u32[]{:S(2)}, u32[]{:S(2)}) %collective-permute-start) | collective-permute-done | bytes 131104 | tf_op jit(solution)/shard_map/ppermute | solution.py:214
  11.5 2.2 %shard_map.55 = (bf16[256,256]{1,0:T(8,128)(2,1)S(1)}, bf16[256,256]{1,0:T(8,128)(2,1)S(1)}, bf16[256,512]{1,0:T(8,128)(2,1)S(1)}, bf16[256,512]{1,0:T(8,128)(2,1)S(1)}, f32[1024,256]{1,0:T(8,128)S(1)}) custom-call(s32[2]{0:T(128)S(1)} %pad_add_fusion.place, f32[256,256]{1,0:T(8,128)} %panel_t.1, f32[3,256,256]{2,1,0:T(8,128)} %tree_v.3, ...), custom_call_target="tpu_custom_call" | custom-call | flops 301989888 | bytes 2097152 | tf_op jit(solution)/shard_map/pallas_call | solution.py:229
  13.8 1.2 %shard_map.56 = (f32[256,128]{1,0:T(8,128)S(1)}, bf16[1024,256]{1,0:T(8,128)(2,1)S(1)}, bf16[1024,256]{1,0:T(8,128)(2,1)S(1)}, bf16[256,1024]{1,0:T(8,128)(2,1)S(1)}, bf16[256,1024]{1,0:T(8,128)(2,1)S(1)}) custom-call(s32[2]{0:T(128)S(1)} %pad_add_fusion.place, f32[256,256]{1,0:T(8,128)S(1)} %copy-done, f32[128,256]{1,0:T(8,128)S(1)} %collective-permute-done.left_a, ...), custom_call_target="tpu_custom_call" | custom-call | flops 201326592 | bytes 4194304 | tf_op jit(solution)/shard_map/pallas_call | solution.py:240
  15.0 2.6 %collective-permute-done.4.opp_a = f32[128,256]{1,0:T(8,128)S(1)} collective-permute-done((f32[128,256]{1,0:T(8,128)S(1)}, f32[128,256]{1,0:T(8,128)S(1)}, u32[]{:S(2)}, u32[]{:S(2)}) %collective-permute-start.4) | collective-permute-done | bytes 131104 | tf_op jit(solution)/shard_map/ppermute | solution.py:218
  17.6 1.2 %shard_map.57 = (f32[256,128]{1,0:T(8,128)S(1)}, f32[256,128]{1,0:T(8,128)S(1)}, bf16[256,256]{1,0:T(8,128)(2,1)S(1)}, bf16[256,256]{1,0:T(8,128)(2,1)S(1)}, bf1...) custom-call(s32[2]{0:T(128)S(1)} %pad_add_fusion.place, ...), custom_call_target="tpu_custom_call", output_to_operand_aliasing={{4}: (7, {}), {5}: (8, {}), {6}: (9, {}), {7}: (10, {})} | custom-call | flops 201326592 | bytes 2097152 | tf_op jit(solution)/shard_map/pallas_call | solution.py:249
  19.0 1.3 %collective-permute-done.6.theirs = f32[256,128]{1,0:T(8,128)S(1)} collective-permute-done((f32[256,128]{1,0:T(8,128)S(1)}, f32[256,128]{1,0:T(8,128)S(1)}, u32[]{:S(2)}, u32[]{:S(2)}) %collective-permute-start.6) | collective-permute-done | bytes 131104 | tf_op jit(solution)/shard_map/ppermute | solution.py:269
  20.7 2.8 %shard_map.59 = (bf16[256,512]{1,0:T(8,128)(2,1)S(1)}, bf16[256,512]{1,0:T(8,128)(2,1)S(1)}, bf16[256,512]{1,0:T(8,128)(2,1)S(1)}, bf16[256,512]{1,0:T(8,128)(2,1)S(1)}, f32[1024,768]{1,0:T(8,128)S(1)}) custom-call(s32[2]{0:T(128)S(1)} %pad_add_fusion.place, f32[3,256,256]{2,1,0:T(8,128)} %tree_v.3, f32[3,256,256]{2,1,0:T(8,128)} %tree_t.3, ...), custom_call_target="tpu_custom_call" | custom-call | flops 402653184 | bytes 4194304 | tf_op jit(solution)/shard_map/pallas_call | solution.py:291
  23.5 1.0 %shard_map.66 = (f32[256,256]{1,0:T(8,128)S(1)}, f32[256,256]{1,0:T(8,128)S(1)}) custom-call(f32[1024,768]{1,0:T(8,128)S(1)} %get-tuple-element.47.block, bf16[256,1024]{1,0:T(8,128)(2,1)S(1)} %get-tuple-element.48.fh, bf16[256,1024]{1,0:T(8,128)(2,1)S(1)} %get-tuple-element.49.fl, bf16[256,256]{1,0:T(8,128)(2,1)S(1)} %get-tuple-element.50.gh, ...), custom_call_target="tpu_custom_call" | custom-call | flops 503316480 | bytes 2097152 | tf_op jit(solution)/shard_map/pallas_call | solution.py:306
  24.5 1.0 %shard_map.63 = (f32[256,256]{1,0:T(8,128)S(1)}, f32[256,256]{1,0:T(8,128)S(1)}) custom-call(f32[1024,768]{1,0:T(8,128)S(1)} %get-tuple-element.47.block, bf16[256,1024]{1,0:T(8,128)(2,1)S(1)} %get-tuple-element.48.fh, bf16[256,1024]{1,0:T(8,128)(2,1)S(1)} %get-tuple-element.49.fl, bf16[256,256]{1,0:T(8,128)(2,1)S(1)} %get-tuple-element.50.gh, ...), custom_call_target="tpu_custom_call" | custom-call | flops 503316480 | bytes 2097152 | tf_op jit(solution)/shard_map/pallas_call | solution.py:306
  26.1 1.0 %shard_map.60 = (f32[256,256]{1,0:T(8,128)S(1)}, f32[256,256]{1,0:T(8,128)S(1)}) custom-call(f32[1024,768]{1,0:T(8,128)S(1)} %get-tuple-element.47.block, bf16[256,1024]{1,0:T(8,128)(2,1)S(1)} %get-tuple-element.48.fh, bf16[256,1024]{1,0:T(8,128)(2,1)S(1)} %get-tuple-element.49.fl, bf16[256,256]{1,0:T(8,128)(2,1)S(1)} %get-tuple-element.50.gh, ...), custom_call_target="tpu_custom_call" | custom-call | flops 503316480 | bytes 2097152 | tf_op jit(solution)/shard_map/pallas_call | solution.py:306
  27.9 2.1 %collective-permute-start.14 = (f32[256,256]{1,0:T(8,128)S(1)}, f32[256,256]{1,0:T(8,128)S(1)}, u32[]{:S(2)}, u32[]{:S(2)}) collective-permute-start(f32[256,256]{1,0:T(8,128)S(1)} %shard_map.67.mine), channel_id=1, source_target_pairs={{0,8},{4,12},{8,0},{12,4},{16,24},{20,28},{24,16},{28,20},{32,40},... | collective-permute-start | bytes 786440 | tf_op jit(solution)/shard_map/ppermute | solution.py:269
  30.9 2.1 %collective-permute-start.8 = (f32[256,256]{1,0:T(8,128)S(1)}, f32[256,256]{1,0:T(8,128)S(1)}, u32[]{:S(2)}, u32[]{:S(2)}) collective-permute-start(f32[256,256]{1,0:T(8,128)S(1)} %shard_map.61.mine), channel_id=1, source_target_pairs={{0,8},{4,12},{8,0},{12,4},{16,24},{20,28},{24,16},{28,20},{32,40},... | collective-permute-start | bytes 786440 | tf_op jit(solution)/shard_map/ppermute | solution.py:269
  34.0 1.3 %collective-permute-done.16.theirs = f32[256,128]{1,0:T(8,128)S(1)} collective-permute-done((f32[256,128]{1,0:T(8,128)S(1)}, f32[256,128]{1,0:T(8,128)S(1)}, u32[]{:S(2)}, u32[]{:S(2)}) %collective-permute-start.16) | collective-permute-done | bytes 131104 | tf_op jit(solution)/shard_map/ppermute | solution.py:269
  35.8 2.0 %collective-permute-start.19 = (f32[256,128]{1,0:T(8,128)S(1)}, f32[256,128]{1,0:T(8,128)S(1)}, u32[]{:S(2)}, u32[]{:S(2)}) collective-permute-start(f32[256,128]{1,0:T(8,128)S(1)} %shard_map.58.after.mine), channel_id=1, source_target_pairs={{0,8},{4,12},{8,0},{12,4},{16,24},{20,28},{24,16},{28,20},{32,40},... | collective-permute-start | bytes 393224 | tf_op jit(solution)/shard_map/ppermute | solution.py:269
  38.2 3.6 %collective-permute-start.15 = (f32[256,256]{1,0:T(8,128)S(1)}, f32[256,256]{1,0:T(8,128)S(1)}, u32[]{:S(2)}, u32[]{:S(2)}) collective-permute-start(f32[256,256]{1,0:T(8,128)S(1)} %shard_map.68.mine), channel_id=1, source_target_pairs={{0,16},{4,20},{8,24},{12,28},{16,0},{20,4},{24,8},{28,12},{32,48},... | collective-permute-start | bytes 786440 | tf_op jit(solution)/shard_map/ppermute | solution.py:269
  41.8 6.6 %collective-permute-done.11.theirs = f32[256,256]{1,0:T(8,128)S(1)} collective-permute-done((f32[256,256]{1,0:T(8,128)S(1)}, f32[256,256]{1,0:T(8,128)S(1)}, u32[]{:S(2)}, u32[]{:S(2)}) %collective-permute-start.11) | collective-permute-done | bytes 262176 | tf_op jit(solution)/shard_map/ppermute | solution.py:269
  48.8 3.1 %collective-permute-start.12 = (f32[256,256]{1,0:T(8,128)S(1)}, f32[256,256]{1,0:T(8,128)S(1)}, u32[]{:S(2)}, u32[]{:S(2)}) collective-permute-start(f32[256,256]{1,0:T(8,128)S(1)} %shard_map.65.mine), channel_id=1, source_target_pairs={{0,16},{4,20},{8,24},{12,28},{16,0},{20,4},{24,8},{28,12},{32,48},... | collective-permute-start | bytes 786440 | tf_op jit(solution)/shard_map/ppermute | solution.py:269
  51.9 7.2 %collective-permute-done.8.theirs = f32[256,256]{1,0:T(8,128)S(1)} collective-permute-done((f32[256,256]{1,0:T(8,128)S(1)}, f32[256,256]{1,0:T(8,128)S(1)}, u32[]{:S(2)}, u32[]{:S(2)}) %collective-permute-start.8) | collective-permute-done | bytes 262176 | tf_op jit(solution)/shard_map/ppermute | solution.py:269
  59.7 2.3 %collective-permute-done.17.theirs = f32[256,128]{1,0:T(8,128)S(1)} collective-permute-done((f32[256,128]{1,0:T(8,128)S(1)}, f32[256,128]{1,0:T(8,128)S(1)}, u32[]{:S(2)}, u32[]{:S(2)}) %collective-permute-start.17) | collective-permute-done | bytes 131104 | tf_op jit(solution)/shard_map/ppermute | solution.py:269
  63.0 1.3 %collective-permute-done.19.theirs = f32[256,128]{1,0:T(8,128)S(1)} collective-permute-done((f32[256,128]{1,0:T(8,128)S(1)}, f32[256,128]{1,0:T(8,128)S(1)}, u32[]{:S(2)}, u32[]{:S(2)}) %collective-permute-start.19) | collective-permute-done | bytes 131104 | tf_op jit(solution)/shard_map/ppermute | solution.py:269
  64.7 1.3 %collective-permute-start.20 = (f32[256,128]{1,0:T(8,128)S(1)}, f32[256,128]{1,0:T(8,128)S(1)}, u32[]{:S(2)}, u32[]{:S(2)}) collective-permute-start(f32[256,128]{1,0:T(8,128)S(1)} %shard_map.72.mine), channel_id=1, source_target_pairs={{0,16},{4,20},{8,24},{12,28},{16,0},{20,4},{24,8},{28,12},{32,48},... | collective-permute-start | bytes 393224 | tf_op jit(solution)/shard_map/ppermute | solution.py:269
  66.0 7.6 %shard_map.73.whole = f32[1024,1024]{1,0:T(8,128)} custom-call(f32[1024,1024]{1,0:T(8,128)} %block.1, bf16[1024,256]{1,0:T(8,128)(2,1)S(1)} %get-tuple-element.60.yh, bf16[1024,256]{1,0:T(8,128)(2,1)S(1)} %get-tuple-element.61.yl, bf16[256,256]{1,0:T(8,128)(2,1)S(1)} %get-tuple-element.38.th, bf16[256,256]{1,0:T(8,128)(2,1)S(1)} %get-tuple-element.39.tl, ...), custom_call_target="tpu_custom_call" | custom-call | flops 2013265920 | bytes 8388608 | tf_op jit(solution)/shard_map/pallas_call | solution.py:318
  73.6 17.2 %collective-permute-done.20.theirs = f32[256,128]{1,0:T(8,128)S(1)} collective-permute-done((f32[256,128]{1,0:T(8,128)S(1)}, f32[256,128]{1,0:T(8,128)S(1)}, u32[]{:S(2)}, u32[]{:S(2)}) %collective-permute-start.20) | collective-permute-done | bytes 131104 | tf_op jit(solution)/shard_map/ppermute | solution.py:269
  90.8 1.0 %shard_map.74.whole = f32[1024,1024]{1,0:T(8,128)} custom-call(f32[256,128]{1,0:T(8,128)S(1)} %shard_map.72.mine, f32[256,128]{1,0:T(8,128)S(1)} %collective-permute-done.20.theirs, bf16[256,512]{1,0:T(8,128)(2,1)S(1)} %get-tuple-element.55.high, bf16[256,512]{1,0:T(8,128)(2,1)S(1)} %get-tuple-element.56.low, ...), custom_call_target="tpu_custom_call", output_to_operand_aliasing={{}: (4, {})} | custom-call | flops 100663296 | bytes 1048576 | tf_op jit(solution)/shard_map/pallas_call | solution.py:279
  91.8 1.0 %shard_map.75.whole = f32[1024,1024]{1,0:T(8,128)} custom-call(f32[256,128]{1,0:T(8,128)S(1)} %shard_map.71.mine, f32[256,128]{1,0:T(8,128)S(1)} %collective-permute-done.18.theirs, bf16[256,512]{1,0:T(8,128)(2,1)S(1)} %get-tuple-element.55.high, bf16[256,512]{1,0:T(8,128)(2,1)S(1)} %get-tuple-element.56.low, ...), custom_call_target="tpu_custom_call", output_to_operand_aliasing={{}: (4, {})} | custom-call | flops 100663296 | bytes 1048576 | tf_op jit(solution)/shard_map/pallas_call | solution.py:279
  92.8 1.1 %shard_map.76.whole = f32[1024,1024]{1,0:T(8,128)} custom-call(f32[256,256]{1,0:T(8,128)S(1)} %shard_map.68.mine, f32[256,256]{1,0:T(8,128)S(1)} %collective-permute-done.15.theirs, bf16[256,512]{1,0:T(8,128)(2,1)S(1)} %get-tuple-element.55.high, bf16[256,512]{1,0:T(8,128)(2,1)S(1)} %get-tuple-element.56.low, ...), custom_call_target="tpu_custom_call", output_to_operand_aliasing={{}: (4, {})} | custom-call | flops 201326592 | bytes 1048576 | tf_op jit(solution)/shard_map/pallas_call | solution.py:279
  93.9 1.1 %shard_map.77.whole = f32[1024,1024]{1,0:T(8,128)} custom-call(f32[256,256]{1,0:T(8,128)S(1)} %shard_map.65.mine, f32[256,256]{1,0:T(8,128)S(1)} %collective-permute-done.12.theirs, bf16[256,512]{1,0:T(8,128)(2,1)S(1)} %get-tuple-element.55.high, bf16[256,512]{1,0:T(8,128)(2,1)S(1)} %get-tuple-element.56.low, ...), custom_call_target="tpu_custom_call", output_to_operand_aliasing={{}: (4, {})} | custom-call | flops 201326592 | bytes 1048576 | tf_op jit(solution)/shard_map/pallas_call | solution.py:279
  95.0 1.1 %shard_map.78 = f32[1024,1024]{1,0:T(8,128)} custom-call(f32[256,256]{1,0:T(8,128)S(1)} %shard_map.62.mine, f32[256,256]{1,0:T(8,128)S(1)} %collective-permute-done.9.theirs, bf16[256,512]{1,0:T(8,128)(2,1)S(1)} %get-tuple-element.55.high, bf16[256,512]{1,0:T(8,128)(2,1)S(1)} %get-tuple-element.56.low, ...), custom_call_target="tpu_custom_call", output_to_operand_aliasing={{}: (4, {})} | custom-call | flops 201326592 | bytes 1048576 | tf_op jit(solution)/shard_map/pallas_call | solution.py:279
  (38 shorter events, 7.6 us)
Async XLA Ops:
  0.0 13.8 %copy-start = (f32[256,256]{1,0:T(8,128)S(1)}, f32[256,256]{1,0:T(8,128)}, u32[]{:S(2)}) copy-start(f32[256,256]{1,0:T(8,128)} %own.1) | copy-start | bytes 786436
  1.0 6.1 %collective-permute-start.3 = (f32[128,256]{1,0:T(8,128)S(1)}, f32[128,256]{1,0:T(8,128)S(1)}, u32[]{:S(2)}, u32[]{:S(2)}) collective-permute-start(f32[128,256]{1,0:T(8,128)S(1)} %get-tuple-element.67), channel_id=1, source_target_pairs={{0,3},{1,0},{2,1},{3,2},{4,7},{5,4},{6,5},{7,6},{8,11},{9,8},{10,9... | collective-permute-start | bytes 393224 | tf_op jit(solution)/shard_map/ppermute | solution.py:215
  3.9 7.6 %collective-permute-start = (f32[128,256]{1,0:T(8,128)S(1)}, f32[128,256]{1,0:T(8,128)S(1)}, u32[]{:S(2)}, u32[]{:S(2)}) collective-permute-start(f32[128,256]{1,0:T(8,128)S(1)} %get-tuple-element.68), channel_id=1, source_target_pairs={{0,1},{1,2},{2,3},{3,0},{4,5},{5,6},{6,7},{7,4},{8,9},{9,10},{10,1... | collective-permute-start | bytes 393224 | tf_op jit(solution)/shard_map/ppermute | solution.py:214
  3.9 9.9 %collective-permute-start.1 = (f32[128,256]{1,0:T(8,128)S(1)}, f32[128,256]{1,0:T(8,128)S(1)}, u32[]{:S(2)}, u32[]{:S(2)}) collective-permute-start(f32[128,256]{1,0:T(8,128)S(1)} %get-tuple-element.67), channel_id=1, source_target_pairs={{0,1},{1,2},{2,3},{3,0},{4,5},{5,6},{6,7},{7,4},{8,9},{9,10},{10,1... | collective-permute-start | bytes 393224 | tf_op jit(solution)/shard_map/ppermute | solution.py:216
  4.6 9.1 %collective-permute-start.2 = (f32[128,256]{1,0:T(8,128)S(1)}, f32[128,256]{1,0:T(8,128)S(1)}, u32[]{:S(2)}, u32[]{:S(2)}) collective-permute-start(f32[128,256]{1,0:T(8,128)S(1)} %get-tuple-element.68), channel_id=1, source_target_pairs={{0,3},{1,0},{2,1},{3,2},{4,7},{5,4},{6,5},{7,6},{8,11},{9,8},{10,9... | collective-permute-start | bytes 393224 | tf_op jit(solution)/shard_map/ppermute | solution.py:217
  7.1 7.8 %collective-permute-start.5 = (f32[128,256]{1,0:T(8,128)S(1)}, f32[128,256]{1,0:T(8,128)S(1)}, u32[]{:S(2)}, u32[]{:S(2)}) collective-permute-start(f32[128,256]{1,0:T(8,128)S(1)} %collective-permute-done.3.right_b), channel_id=1, source_target_pairs={{0,3},{1,0},{2,1},{3,2},{4,7},{5,4},{6,5},{7,6},{8,11},{9,8},{10,9... | collective-permute-start | bytes 393224 | tf_op jit(solution)/shard_map/ppermute | solution.py:219
  11.4 6.2 %collective-permute-start.4 = (f32[128,256]{1,0:T(8,128)S(1)}, f32[128,256]{1,0:T(8,128)S(1)}, u32[]{:S(2)}, u32[]{:S(2)}) collective-permute-start(f32[128,256]{1,0:T(8,128)S(1)} %collective-permute-done.left_a), channel_id=1, source_target_pairs={{0,1},{1,2},{2,3},{3,0},{4,5},{5,6},{6,7},{7,4},{8,9},{9,10},{10,1... | collective-permute-start | bytes 393224 | tf_op jit(solution)/shard_map/ppermute | solution.py:218
  18.9 1.4 %collective-permute-start.6 = (f32[256,128]{1,0:T(8,128)S(1)}, f32[256,128]{1,0:T(8,128)S(1)}, u32[]{:S(2)}, u32[]{:S(2)}) collective-permute-start(f32[256,128]{1,0:T(8,128)S(1)} %get-tuple-element.44.mine), channel_id=1, source_target_pairs={{0,4},{4,0},{8,12},{12,8},{16,20},{20,16},{24,28},{28,24},{32,36},... | collective-permute-start | bytes 393224 | tf_op jit(solution)/shard_map/ppermute | solution.py:269
  25.5 2.0 %collective-permute-start.13 = (f32[256,256]{1,0:T(8,128)S(1)}, f32[256,256]{1,0:T(8,128)S(1)}, u32[]{:S(2)}, u32[]{:S(2)}) collective-permute-start(f32[256,256]{1,0:T(8,128)S(1)} %get-tuple-element.58.mine), channel_id=1, source_target_pairs={{0,4},{4,0},{8,12},{12,8},{16,20},{20,16},{24,28},{28,24},{32,36},... | collective-permute-start | bytes 786440 | tf_op jit(solution)/shard_map/ppermute | solution.py:269
  25.7 4.3 %collective-permute-start.10 = (f32[256,256]{1,0:T(8,128)S(1)}, f32[256,256]{1,0:T(8,128)S(1)}, u32[]{:S(2)}, u32[]{:S(2)}) collective-permute-start(f32[256,256]{1,0:T(8,128)S(1)} %get-tuple-element.57.mine), channel_id=1, source_target_pairs={{0,4},{4,0},{8,12},{12,8},{16,20},{20,16},{24,28},{28,24},{32,36},... | collective-permute-start | bytes 786440 | tf_op jit(solution)/shard_map/ppermute | solution.py:269
  27.1 3.4 %collective-permute-start.7 = (f32[256,256]{1,0:T(8,128)S(1)}, f32[256,256]{1,0:T(8,128)S(1)}, u32[]{:S(2)}, u32[]{:S(2)}) collective-permute-start(f32[256,256]{1,0:T(8,128)S(1)} %get-tuple-element.52.mine), channel_id=1, source_target_pairs={{0,4},{4,0},{8,12},{12,8},{16,20},{20,16},{24,28},{28,24},{32,36},... | collective-permute-start | bytes 786440 | tf_op jit(solution)/shard_map/ppermute | solution.py:269
  27.9 9.9 %collective-permute-start.14 = (f32[256,256]{1,0:T(8,128)S(1)}, f32[256,256]{1,0:T(8,128)S(1)}, u32[]{:S(2)}, u32[]{:S(2)}) collective-permute-start(f32[256,256]{1,0:T(8,128)S(1)} %shard_map.67.mine), channel_id=1, source_target_pairs={{0,8},{4,12},{8,0},{12,4},{16,24},{20,28},{24,16},{28,20},{32,40},... | collective-permute-start | bytes 786440 | tf_op jit(solution)/shard_map/ppermute | solution.py:269
  30.4 18.0 %collective-permute-start.11 = (f32[256,256]{1,0:T(8,128)S(1)}, f32[256,256]{1,0:T(8,128)S(1)}, u32[]{:S(2)}, u32[]{:S(2)}) collective-permute-start(f32[256,256]{1,0:T(8,128)S(1)} %shard_map.64.mine), channel_id=1, source_target_pairs={{0,8},{4,12},{8,0},{12,4},{16,24},{20,28},{24,16},{28,20},{32,40},... | collective-permute-start | bytes 786440 | tf_op jit(solution)/shard_map/ppermute | solution.py:269
  30.9 28.2 %collective-permute-start.8 = (f32[256,256]{1,0:T(8,128)S(1)}, f32[256,256]{1,0:T(8,128)S(1)}, u32[]{:S(2)}, u32[]{:S(2)}) collective-permute-start(f32[256,256]{1,0:T(8,128)S(1)} %shard_map.61.mine), channel_id=1, source_target_pairs={{0,8},{4,12},{8,0},{12,4},{16,24},{20,28},{24,16},{28,20},{32,40},... | collective-permute-start | bytes 786440 | tf_op jit(solution)/shard_map/ppermute | solution.py:269
  33.9 1.4 %collective-permute-start.16 = (f32[256,128]{1,0:T(8,128)S(1)}, f32[256,128]{1,0:T(8,128)S(1)}, u32[]{:S(2)}, u32[]{:S(2)}) collective-permute-start(f32[256,128]{1,0:T(8,128)S(1)} %get-tuple-element.59.mine), channel_id=1, source_target_pairs={{0,4},{4,0},{8,12},{12,8},{16,20},{20,16},{24,28},{28,24},{32,36},... | collective-permute-start | bytes 393224 | tf_op jit(solution)/shard_map/ppermute | solution.py:269
  35.7 26.3 %collective-permute-start.17 = (f32[256,128]{1,0:T(8,128)S(1)}, f32[256,128]{1,0:T(8,128)S(1)}, u32[]{:S(2)}, u32[]{:S(2)}) collective-permute-start(f32[256,128]{1,0:T(8,128)S(1)} %shard_map.70.mine), channel_id=1, source_target_pairs={{0,8},{4,12},{8,0},{12,4},{16,24},{20,28},{24,16},{28,20},{32,40},... | collective-permute-start | bytes 393224 | tf_op jit(solution)/shard_map/ppermute | solution.py:269
  35.8 28.5 %collective-permute-start.19 = (f32[256,128]{1,0:T(8,128)S(1)}, f32[256,128]{1,0:T(8,128)S(1)}, u32[]{:S(2)}, u32[]{:S(2)}) collective-permute-start(f32[256,128]{1,0:T(8,128)S(1)} %shard_map.58.after.mine), channel_id=1, source_target_pairs={{0,8},{4,12},{8,0},{12,4},{16,24},{20,28},{24,16},{28,20},{32,40},... | collective-permute-start | bytes 393224 | tf_op jit(solution)/shard_map/ppermute | solution.py:269
  38.2 54.6 %collective-permute-start.15 = (f32[256,256]{1,0:T(8,128)S(1)}, f32[256,256]{1,0:T(8,128)S(1)}, u32[]{:S(2)}, u32[]{:S(2)}) collective-permute-start(f32[256,256]{1,0:T(8,128)S(1)} %shard_map.68.mine), channel_id=1, source_target_pairs={{0,16},{4,20},{8,24},{12,28},{16,0},{20,4},{24,8},{28,12},{32,48},... | collective-permute-start | bytes 786440 | tf_op jit(solution)/shard_map/ppermute | solution.py:269
  48.8 45.1 %collective-permute-start.12 = (f32[256,256]{1,0:T(8,128)S(1)}, f32[256,256]{1,0:T(8,128)S(1)}, u32[]{:S(2)}, u32[]{:S(2)}) collective-permute-start(f32[256,256]{1,0:T(8,128)S(1)} %shard_map.65.mine), channel_id=1, source_target_pairs={{0,16},{4,20},{8,24},{12,28},{16,0},{20,4},{24,8},{28,12},{32,48},... | collective-permute-start | bytes 786440 | tf_op jit(solution)/shard_map/ppermute | solution.py:269
  59.6 35.5 %collective-permute-start.9 = (f32[256,256]{1,0:T(8,128)S(1)}, f32[256,256]{1,0:T(8,128)S(1)}, u32[]{:S(2)}, u32[]{:S(2)}) collective-permute-start(f32[256,256]{1,0:T(8,128)S(1)} %shard_map.62.mine), channel_id=1, source_target_pairs={{0,16},{4,20},{8,24},{12,28},{16,0},{20,4},{24,8},{28,12},{32,48},... | collective-permute-start | bytes 786440 | tf_op jit(solution)/shard_map/ppermute | solution.py:269
  62.3 29.5 %collective-permute-start.18 = (f32[256,128]{1,0:T(8,128)S(1)}, f32[256,128]{1,0:T(8,128)S(1)}, u32[]{:S(2)}, u32[]{:S(2)}) collective-permute-start(f32[256,128]{1,0:T(8,128)S(1)} %shard_map.71.mine), channel_id=1, source_target_pairs={{0,16},{4,20},{8,24},{12,28},{16,0},{20,4},{24,8},{28,12},{32,48},... | collective-permute-start | bytes 393224 | tf_op jit(solution)/shard_map/ppermute | solution.py:269
  64.7 26.1 %collective-permute-start.20 = (f32[256,128]{1,0:T(8,128)S(1)}, f32[256,128]{1,0:T(8,128)S(1)}, u32[]{:S(2)}, u32[]{:S(2)}) collective-permute-start(f32[256,128]{1,0:T(8,128)S(1)} %shard_map.72.mine), channel_id=1, source_target_pairs={{0,16},{4,20},{8,24},{12,28},{16,0},{20,4},{24,8},{28,12},{32,48},... | collective-permute-start | bytes 393224 | tf_op jit(solution)/shard_map/ppermute | solution.py:269
where the time goes:
time: 96.9 us; the launch traced here: 96.1 us
  waiting for transfers between devices  41 us (42%)
  Pallas kernels  28 us (29%)
  starting transfers between devices  25.8 us (27%)
  local copies, waits for them, and re-layouts  1.03 us (1%)
    ppermute x15, waiting for transfers between devices, exchange(): theirs = lax.ppermute(tops[k], 'row', route)  37.4 us
    ppermute x15, starting transfers between devices, exchange(): theirs = lax.ppermute(tops[k], 'row', route)  16.4 us
    pallas_call x1, Pallas kernels, update(): call(rest_kernel, grid=(rows // size - 1,), out_shape=shaped((rows, colum...  7.58 us
    pallas_call x5, Pallas kernels, exchange(): call(final_kernel, grid=(1,), out_shape=shaped((rows, columns)), in_specs...  5.32 us
    pallas_call x4, Pallas kernels, update(): call(functools.partial(next_kernel, span), out_shape=[shaped((width, WIDT...  3.88 us
    pallas_call x10, Pallas kernels, exchange(): call(level_kernel, out_shape=shaped((width, w)), in_specs=[VMEM] * 4, out...  3.76 us
    ppermute x1, starting transfers between devices, update(): opp_b = lax.ppermute(right_b, 'col', backward)  3.29 us
    ppermute x1, starting transfers between devices, update(): right_b = lax.ppermute(own_b, 'col', backward)  2.84 us
  transfers between devices with their start and end apart: 21, of which 9 were waited for; matrix products, arithmetic and copies ran while one was open for 0% of the time, Pallas kernels for 21%

commit v1 on v0

v1 whole, which is shorter than its diff:
```python
import functools
import math

import jax
import jax.numpy as jnp
from jax import lax
from jax.experimental import pallas as pl
from jax.experimental.pallas import tpu as pltpu
from jax.sharding import PartitionSpec as P


UNITS = ((128, 128), (128, 128), (256,), (256,))
F32 = jnp.float32
BF16 = jnp.bfloat16
VMEM = pl.BlockSpec(memory_space=pltpu.VMEM)
SMEM = pl.BlockSpec(memory_space=pltpu.SMEM)
HBM = pl.BlockSpec(memory_space=pltpu.HBM)
ANY = pl.BlockSpec(memory_space=pl.ANY)


def split(values):
    high = values.astype(BF16)
    return high, (values - high.astype(F32)).astype(BF16)


def dot3(left, right):
    mul = functools.partial(jnp.dot, preferred_element_type=F32)
    return mul(left[0], right[0]) + (mul(left[0], right[1]) + mul(left[1], right[0]))


def grids(shape):
    return lax.broadcasted_iota(jnp.int32, shape, 0), lax.broadcasted_iota(jnp.int32, shape, 1)


def unit_lower(values, first_row):
    rows, cols = grids(values.shape)
    rows = rows + first_row
    return jnp.where(rows > cols, values, jnp.where(rows == cols, F32(1.0), F32(0.0)))


def triangle_factor(values):
    rows, cols = grids(values.shape)
    scale = 2.0 / math.sqrt(values.shape[-1])
    return jnp.where(rows == cols, values, jnp.where(cols > rows, (values - 1.0) * scale, F32(0.0)))


def upper_part(values):
    rows, cols = grids(values.shape)
    return jnp.where(cols >= rows, values, F32(0.0))


def mix_level(leads, tree_v, tree_t, high, low):
    width = tree_v.shape[0]
    vees = upper_part(tree_v)
    tees = split(triangle_factor(tree_t).T)

    @pl.when(leads)
    def _():
        high[:, :width], low[:, :width] = tees
        high[:, width:], low[:, width:] = split(dot3(tees, split(vees.T)))

    @pl.when(jnp.logical_not(leads))
    def _():
        both = split(dot3(split(vees), tees))
        high[:, width:], low[:, width:] = both
        high[:, :width], low[:, :width] = split(dot3(both, split(vees.T)))


def start_all(pairs, sems):
    copies = [pltpu.make_async_copy(a, b, sems.at[i]) for i, (a, b) in enumerate(pairs)]
    for copy in copies:
        copy.start()
    return copies


def prepare_kernel(place, panel_t, tree_v, tree_t, trailing, th, tl, *args):
    mixes, (block, tri, vee, tee, sems) = args[:-5], args[-5:]
    ahead = len(mixes) // 2
    pairs = [(panel_t, tri)]
    for level in range(ahead):
        pairs += [(tree_v.at[level], vee.at[level]), (tree_t.at[level], tee.at[level])]
    copies = start_all(pairs + [(trailing, block)], sems)
    copies[0].wait()
    th[...], tl[...] = split(triangle_factor(tri[...]).T)
    for level in range(ahead):
        copies[2 * level + 1].wait()
        copies[2 * level + 2].wait()
        mix_level((place[0] >> level) & 1 == 0, vee[level], tee[level], *mixes[2 * level : 2 * level + 2])
    copies[-1].wait()


def mixes_kernel(level, place, tree_v, tree_t, after, high, low, vee, tee, sems):
    del after
    for copy in start_all(((tree_v.at[level], vee), (tree_t.at[level], tee)), sems):
        copy.wait()
    mix_level((place[0] >> level) & 1 == 0, vee[...], tee[...], high, low)


def opposite_rows(col, size, count):
    return pl.multiple_of(lax.rem(col + count // 2, count) * size, size)


def both_ways(rows, start):
    rows = unit_lower(rows, start)
    return split(rows), split(rows.T)


def early_kernel(place, own, left_a, left_b, right_a, right_b, block, partial, yh, yl, fh, fl):
    col = place[1]
    size = own.shape[0]
    count = block.shape[0] // size
    width = partial.shape[1]
    total = None
    for shift, parts in ((0, (own,)), (count - 1, (left_a, left_b)), (1, (right_a, right_b))):
        start = pl.multiple_of(lax.rem(col + shift, count) * size, size)
        rows = parts[0][...] if len(parts) == 1 else jnp.concatenate([p[...] for p in parts], axis=0)
        here = pl.ds(start, size)
        straight, flipped = both_ways(rows, start)
        yh[here, :], yl[here, :] = straight
        fh[:, here], fl[:, here] = flipped
        term = dot3(flipped, split(block[pl.ds(start, size), :width]))
        total = term if total is None else total + term
    partial[...] = total


def store_parts(value, parts):
    first = 0
    for part in parts:
        part[...] = value[:, first : first + part.shape[1]]
        first += part.shape[1]


def first_kernel(place, partial, opp_a, opp_b, block, th, tl, yh, yl, top, proj, gh, gl, oh, ol, ph, plow):
    size = 2 * opp_a.shape[0]
    width = partial.shape[1]
    start = opposite_rows(place[1], size, block.shape[0] // size)
    rows = jnp.concatenate([opp_a[...], opp_b[...]], axis=0)
    straight, flipped = both_ways(rows, start)
    upper = [jnp.where(start == 0, new, old[:size, :]) for new, old in zip(straight, (yh, yl))]
    gain = split(dot3(upper, (th[...], tl[...])))
    value = partial[...] + dot3(flipped, split(block[pl.ds(start, size), :width]))
    top[...] = block[:size, :width] - dot3(gain, split(value))
    proj[...] = value
    gh[...], gl[...] = gain
    oh[...], ol[...] = straight
    ph[...], plow[...] = flipped


def assemble_kernel(place, yh_in, yl_in, fh_in, fl_in, oh, ol, ph, plow, yh, yl, fh, fl):
    size = oh.shape[0]
    here = pl.ds(opposite_rows(place[1], size, yh.shape[0] // size), size)
    for out, old, new in ((yh, yh_in, oh), (yl, yl_in, ol)):
        out[...] = old[...]
        out[here, :] = new[...]
    for out, old, new in ((fh, fh_in, ph), (fl, fl_in, plow)):
        out[...] = old[...]
        out[:, here] = new[...]


def next_kernel(span, block, fh, fl, gh, gl, top, proj):
    values = block[:, span]
    value = dot3((fh[...], fl[...]), split(values))
    top[...] = values[: top.shape[0]] - dot3((gh[...], gl[...]), split(value))
    proj[...] = value


def rest_kernel(first, block, yh, yl, th, tl, *args):
    projs, (out, slots, sems) = args[: -3 - (first > 0)], args[-3:]
    count, size, width = slots.shape
    weights = [split(dot3((th[...], tl[...]), split(proj[...]))) for proj in projs]
    copies = []
    for i in range(count):
        here = slice((i + 1) * size, (i + 2) * size)
        at = 0
        for weight in weights:
            wide = weight[0].shape[1]
            values = block[here, first + at : first + at + wide]
            slots[i, :, at : at + wide] = values - dot3((yh[here, :], yl[here, :]), weight)
            at += wide
        target = out.at[pl.ds((i + 1) * size, size), pl.ds(first, width)]
        copies.append(pltpu.make_async_copy(slots.at[i], target, sems.at[i]))
        copies[-1].start()
    for copy in copies:
        copy.wait()


def mixed(mine, theirs, high, low):
    width = mine.shape[0]
    one = dot3((high[:, :width], low[:, :width]), split(mine[...]))
    two = dot3((high[:, width:], low[:, width:]), split(theirs[...]))
    return mine[...] - (one + two)


def level_kernel(mine, theirs, high, low, *parts):
    store_parts(mixed(mine, theirs, high, low), parts)


def final_kernel(first, mine, theirs, high, low, whole, out, slot, sem):
    del whole
    slot[...] = mixed(mine, theirs, high, low)
    copy = pltpu.make_async_copy(slot, out.at[pl.ds(0, slot.shape[0]), pl.ds(first, slot.shape[1])], sem)
    copy.start()
    copy.wait()


def shaped(shape, dtype=F32):
    return jax.ShapeDtypeStruct(shape, dtype)


def layout():
    units, chunks, first = [], [], 0
    for unit in UNITS:
        units.append((first, sum(unit)))
        for w in unit:
            chunks.append((first, w))
            first += w
    return units, chunks


def call(kernel, **options):
    mib = options.pop("mib")
    flops, moved = options.pop("cost")
    return pl.pallas_call(
        kernel,
        compiler_params=pltpu.CompilerParams(vmem_limit_bytes=mib << 20),
        cost_estimate=pl.CostEstimate(flops=flops, bytes_accessed=moved, transcendentals=0),
        **options,
    )


def fixed(values):
    return pltpu.with_memory_space_constraint(values, pltpu.HBM)


def update(trailing, panel_y, panel_t, tree_v, tree_t):
    size, width = panel_y.shape
    rows, columns = trailing.shape
    levels = tree_v.shape[0]
    half = size // 2
    count = lax.axis_size("col")
    place = jnp.stack([lax.axis_index("row"), lax.axis_index("col")]).astype(jnp.int32)
    onward = [(c, (c + 1) % count) for c in range(count)]
    backward = [(c, (c - 1) % count) for c in range(count)]

    own_a, own_b = panel_y[:half], panel_y[half:]
    left_a = lax.ppermute(own_a, "col", onward)
    right_b = lax.ppermute(own_b, "col", backward)
    left_b = lax.ppermute(own_b, "col", onward)
    right_a = lax.ppermute(own_a, "col", backward)
    opp_a = lax.ppermute(left_a, "col", onward)
    opp_b = lax.ppermute(right_b, "col", backward)

    square = shaped((width, width), BF16)
    mix = shaped((width, 2 * width), BF16)
    tall = shaped((rows, width), BF16)
    wide = shaped((width, rows), BF16)
    cube = 2 * 3 * width**3
    trailing = fixed(trailing)
    panel_t, tree_v, tree_t = fixed(panel_t), fixed(tree_v), fixed(tree_t)
    units, chunks = layout()
    ahead = levels - 1
    th, tl, *mixes, block = call(
        prepare_kernel,
        out_shape=[square, square] + [mix] * (2 * ahead) + [shaped((rows, columns))],
        in_specs=[SMEM] + [HBM] * 4,
        out_specs=[VMEM] * (3 + 2 * ahead),
        scratch_shapes=[pltpu.VMEM((width, width), F32)]
        + [pltpu.VMEM((ahead, width, width), F32)] * 2
        + [pltpu.SemaphoreType.DMA((2 * ahead + 2,))],
        mib=16,
        cost=(5 * cube, 5 << 20),
    )(place, panel_t, tree_v, tree_t, trailing)

    w = units[0][1]
    partial, yh, yl, fh, fl = call(
        early_kernel,
        out_shape=[shaped((width, w)), tall, tall, wide, wide],
        in_specs=[SMEM] + [VMEM] * 6,
        out_specs=[VMEM] * 5,
        mib=16,
        cost=(2 * cube, 4 << 20),
    )(place, panel_y, left_a, left_b, right_a, right_b, block)

    top, proj, gh, gl, *opposite = call(
        first_kernel,
        out_shape=[shaped((width, w))] * 2 + [square] * 6,
        in_specs=[SMEM] + [VMEM] * 8,
        out_specs=[VMEM] * 8,
        mib=16,
        cost=(2 * cube, 2 << 20),
    )(place, partial, opp_a, opp_b, block, th, tl, yh, yl)

    yh, yl, fh, fl = call(
        assemble_kernel,
        out_shape=[tall, tall, wide, wide],
        in_specs=[SMEM] + [VMEM] * 8,
        out_specs=[VMEM] * 4,
        mib=16,
        cost=(0, 4 << 20),
    )(place, yh, yl, fh, fl, *opposite)

    def swap(level, values):
        route = [(r, r ^ (1 << level)) for r in range(lax.axis_size("row"))]
        return lax.ppermute(values, "row", route)

    def combine(level, values, widths):
        w = values.shape[1]
        return call(
            level_kernel,
            out_shape=[shaped((width, w)) for w in widths],
            in_specs=[VMEM] * 4,
            out_specs=[VMEM] * len(widths),
            mib=8,
            cost=(2 * cube * w // width, 1 << 20),
        )(values, swap(level, values), *mixes[2 * level : 2 * level + 2])

    tops, projs = [], []
    for u, (first, w) in enumerate(units):
        if u:
            top, proj = call(
                functools.partial(next_kernel, slice(first, first + w)),
                out_shape=[shaped((width, w))] * 2,
                in_specs=[VMEM] * 5,
                out_specs=[VMEM] * 2,
                mib=16,
                cost=(5 * cube * w // width, 2 << 20),
            )(block, fh, fl, gh, gl)
        projs.append(proj)
        tops += combine(0, top, UNITS[u])

    for level in range(1, levels - 1):
        tops = [combine(level, top, (top.shape[1],))[0] for top in tops]

    level = levels - 1
    mixes += call(
        functools.partial(mixes_kernel, level),
        out_shape=[mix] * 2,
        in_specs=[SMEM] + [HBM] * 2 + [ANY],
        out_specs=[VMEM] * 2,
        scratch_shapes=[pltpu.VMEM((width, width), F32)] * 2 + [pltpu.SemaphoreType.DMA((2,))],
        mib=8,
        cost=(2 * cube, 1 << 20),
    )(place, tree_v, tree_t, projs[-1])

    out = ()
    parts = rows // size - 1
    for group in ((0, 1), (2, 3)):
        first = units[group[0]][0]
        w = sum(units[u][1] for u in group)
        out = (
            call(
                functools.partial(rest_kernel, first),
                out_shape=shaped((rows, columns)),
                in_specs=[VMEM] * (5 + len(group)) + [HBM] * len(out),
                out_specs=HBM,
                scratch_shapes=[pltpu.VMEM((parts, size, w), F32), pltpu.SemaphoreType.DMA((parts,))],
                input_output_aliases={5 + len(group): 0} if out else {},
                mib=16,
                cost=(10 * cube, 4 << 20),
            )(block, yh, yl, th, tl, *[projs[u] for u in group], *out),
        )
    out = out[0]

    for k, (first, w) in enumerate(chunks):
        out = call(
            functools.partial(final_kernel, first),
            out_shape=shaped((rows, columns)),
            in_specs=[VMEM] * 4 + [HBM],
            out_specs=HBM,
            scratch_shapes=[pltpu.VMEM((width, w), F32), pltpu.SemaphoreType.DMA],
            input_output_aliases={4: 0},
            mib=8,
            cost=(2 * cube * w // width, 1 << 20),
        )(tops[k], swap(level, tops[k]), *mixes[2 * level :], out)
    return out


def solution(mesh):
    placed = (
        P("row", "col"),
        P(("row", "col"), None),
        P("row", None),
        P(None, "row", None),
        P(None, "row", None),
    )
    return jax.shard_map(
        update, mesh=mesh, in_specs=placed, out_specs=P("row", "col"), check_vma=False
    )
```

time: 96.9 us -> 94.6 us (0.976)
  starting transfers between devices: 25.8 us -> 29.7 us
  waiting for transfers between devices: 41 us -> 37.3 us
  Pallas kernels: 28 us -> 25.9 us
    ppermute x15 -> x16, starting transfers between devices: 16.4 us -> 19.9 us  [swap(): return lax.ppermute(values, 'row', route)]
    ppermute x1, waiting for transfers between devices: 2.63 us -> 0.01 us  [update(): opp_a = lax.ppermute(left_a, 'col', onward)]
    pallas_call x23 -> x25, Pallas kernels: 26.8 us -> 24.7 us  [the longest x6 6.35 us: update(): call(functools.partial(final_kernel, first), out_shape=shaped((rows, colu...]
    ppermute x1, starting transfers between devices: 0.01 us -> 1.57 us  [update(): left_a = lax.ppermute(own_a, 'col', onward)]
    ppermute x1, starting transfers between devices: 3.29 us -> 1.95 us  [update(): opp_b = lax.ppermute(right_b, 'col', backward)]
    ppermute x1, starting transfers between devices: 0.01 us -> 1.28 us  [update(): opp_a = lax.ppermute(left_a, 'col', onward)]
    ppermute x1, starting transfers between devices: 2.84 us -> 1.75 us  [update(): right_b = lax.ppermute(own_b, 'col', backward)]
    ppermute x15 -> x16, waiting for transfers between devices: 37.4 us -> 37.2 us  [swap(): return lax.ppermute(values, 'row', route)]
  transfers between devices with their start and end apart: 21 -> 22, of which waited for: 9 -> 5; matrix products, arithmetic and copies ran while one was open for 0% -> 0% of each run, Pallas kernels for 21% -> 23%
where the time goes in v1:
time: 94.6 us; the launch traced here: 94.5 us
  waiting for transfers between devices  37.3 us (39%)
  starting transfers between devices  29.7 us (31%)
  Pallas kernels  25.9 us (27%)
  local copies, waits for them, and re-layouts  1.03 us (1%)
    ppermute x16, waiting for transfers between devices, swap(): return lax.ppermute(values, 'row', route)  37.2 us
    ppermute x16, starting transfers between devices, swap(): return lax.ppermute(values, 'row', route)  19.9 us
    pallas_call x6, Pallas kernels, update(): call(functools.partial(final_kernel, first), out_shape=shaped((rows, colu...  6.35 us
    pallas_call x2, Pallas kernels, update(): call(functools.partial(rest_kernel, first), out_shape=shaped((rows, colum...  3.93 us
    pallas_call x10, Pallas kernels, combine(): call(level_kernel, out_shape=[shaped((width, w)) for w in widths], in_spe...  3.77 us
    pallas_call x1, Pallas kernels, update(): call(prepare_kernel, out_shape=[square, square] + [mix] * (2 * ahead) + [...  3.19 us
    pallas_call x3, Pallas kernels, update(): call(functools.partial(next_kernel, slice(first, first + w)), out_shape=[...  3.03 us
    ppermute x1, starting transfers between devices, update(): right_a = lax.ppermute(own_a, 'col', backward)  2.96 us
  transfers between devices with their start and end apart: 22, of which 5 were waited for; matrix products, arithmetic and copies ran while one was open for 0% of the time, Pallas kernels for 23%

profile of v1, /device:TPU:8, one launch (start us, length us, event | category | flops | bytes accessed | tf_op | source)
XLA Modules:
  0.0 94.5 jit_solution(13883298823380738408)
XLA Ops:
  0.0 1.0 %fusion = (f32[128,256]{1,0:T(8,128)S(1)}, f32[128,256]{1,0:T(8,128)S(1)}) fusion(f32[256,256]{1,0:T(8,128)} %own.1), kind=kLoop, calls=%fused_computation.1 | loop fusion | bytes 524288 | tf_op jit(solution)/shard_map/slice | solution.py:245
  1.0 1.6 %collective-permute-start = (f32[128,256]{1,0:T(8,128)S(1)}, f32[128,256]{1,0:T(8,128)S(1)}, u32[]{:S(2)}, u32[]{:S(2)}) collective-permute-start(f32[128,256]{1,0:T(8,128)S(1)} %get-tuple-element.78), channel_id=1, source_target_pairs={{0,1},{1,2},{2,3},{3,0},{4,5},{5,6},{6,7},{7,4},{8,9},{9,10},{10,1... | collective-permute-start | bytes 393224 | tf_op jit(solution)/shard_map/ppermute | solution.py:246
  2.6 1.7 %collective-permute-start.3 = (f32[128,256]{1,0:T(8,128)S(1)}, f32[128,256]{1,0:T(8,128)S(1)}, u32[]{:S(2)}, u32[]{:S(2)}) collective-permute-start(f32[128,256]{1,0:T(8,128)S(1)} %get-tuple-element.77), channel_id=1, source_target_pairs={{0,3},{1,0},{2,1},{3,2},{4,7},{5,4},{6,5},{7,6},{8,11},{9,8},{10,9... | collective-permute-start | bytes 393224 | tf_op jit(solution)/shard_map/ppermute | solution.py:247
  4.6 3.0 %collective-permute-start.2 = (f32[128,256]{1,0:T(8,128)S(1)}, f32[128,256]{1,0:T(8,128)S(1)}, u32[]{:S(2)}, u32[]{:S(2)}) collective-permute-start(f32[128,256]{1,0:T(8,128)S(1)} %get-tuple-element.78), channel_id=1, source_target_pairs={{0,3},{1,0},{2,1},{3,2},{4,7},{5,4},{6,5},{7,6},{8,11},{9,8},{10,9... | collective-permute-start | bytes 393224 | tf_op jit(solution)/shard_map/ppermute | solution.py:249
  7.7 1.3 %collective-permute-start.4 = (f32[128,256]{1,0:T(8,128)S(1)}, f32[128,256]{1,0:T(8,128)S(1)}, u32[]{:S(2)}, u32[]{:S(2)}) collective-permute-start(f32[128,256]{1,0:T(8,128)S(1)} %collective-permute-done.left_a), channel_id=1, source_target_pairs={{0,1},{1,2},{2,3},{3,0},{4,5},{5,6},{6,7},{7,4},{8,9},{9,10},{10,1... | collective-permute-start | bytes 393224 | tf_op jit(solution)/shard_map/ppermute | solution.py:250
  9.0 2.0 %collective-permute-start.5 = (f32[128,256]{1,0:T(8,128)S(1)}, f32[128,256]{1,0:T(8,128)S(1)}, u32[]{:S(2)}, u32[]{:S(2)}) collective-permute-start(f32[128,256]{1,0:T(8,128)S(1)} %collective-permute-done.3.right_b), channel_id=1, source_target_pairs={{0,3},{1,0},{2,1},{3,2},{4,7},{5,4},{6,5},{7,6},{8,11},{9,8},{10,9... | collective-permute-start | bytes 393224 | tf_op jit(solution)/shard_map/ppermute | solution.py:251
  11.0 3.2 %shard_map.55 = (bf16[256,256]{1,0:T(8,128)(2,1)S(1)}, bf16[256,256]{1,0:T(8,128)(2,1)S(1)}, bf16[256,512]{1,0:T(8,128)(2,1)S(1)}, bf16[256,512]{1,0:T(8,128)(2,...) custom-call(s32[2]{0:T(128)S(1)} %pad_add_fusion.place, ...), custom_call_target="tpu_custom_call" | custom-call | flops 503316480 | bytes 5242880 | tf_op jit(solution)/shard_map/pallas_call | solution.py:262
  14.2 1.3 %shard_map.56 = (f32[256,256]{1,0:T(8,128)S(1)}, bf16[1024,256]{1,0:T(8,128)(2,1)S(1)}, bf16[1024,256]{1,0:T(8,128)(2,1)S(1)}, bf16[256,1024]{1,0:T(8,128)(2,1)S(1)}, bf16[256,1024]{1,0:T(8,128)(2,1)S(1)}) custom-call(s32[2]{0:T(128)S(1)} %pad_add_fusion.place, f32[256,256]{1,0:T(8,128)S(1)} %copy-done, f32[128,256]{1,0:T(8,128)S(1)} %collective-permute-done.left_a, ...), custom_call_target="tpu_custom_call" | custom-call | flops 201326592 | bytes 4194304 | tf_op jit(solution)/shard_map/pallas_call | solution.py:275
  15.5 1.4 %shard_map.57 = (f32[256,256]{1,0:T(8,128)S(1)}, f32[256,256]{1,0:T(8,128)S(1)}, bf16[256,256]{1,0:T(8,128)(2,1)S(1)}, bf16[256,256]{1,0:T(8,128)(2,1)S(1)}, bf1...) custom-call(s32[2]{0:T(128)S(1)} %pad_add_fusion.place, ...), custom_call_target="tpu_custom_call" | custom-call | flops 201326592 | bytes 2097152 | tf_op jit(solution)/shard_map/pallas_call | solution.py:284
  16.9 0.7 shard_map.58
  17.6 1.0 %shard_map.63 = (f32[256,256]{1,0:T(8,128)S(1)}, f32[256,256]{1,0:T(8,128)S(1)}) custom-call(f32[1024,1024]{1,0:T(8,128)S(1)} %get-tuple-element.41.block, bf16[256,1024]{1,0:T(8,128)(2,1)S(1)} %get-tuple-element.53.fh, bf16[256,1024]{1,0:T(8,128)(2,1)S(1)} %get-tuple-element.54.fl, bf16[256,256]{1,0:T(8,128)(2,1)S(1)} %get-tuple-element.55.gh, ...), custom_call_target="tpu_custom_call" | custom-call | flops 503316480 | bytes 2097152 | tf_op jit(solution)/shard_map/pallas_call | solution.py:320
  18.7 1.0 %shard_map.59 = (f32[256,256]{1,0:T(8,128)S(1)}, f32[256,256]{1,0:T(8,128)S(1)}) custom-call(f32[1024,1024]{1,0:T(8,128)S(1)} %get-tuple-element.41.block, bf16[256,1024]{1,0:T(8,128)(2,1)S(1)} %get-tuple-element.53.fh, bf16[256,1024]{1,0:T(8,128)(2,1)S(1)} %get-tuple-element.54.fl, bf16[256,256]{1,0:T(8,128)(2,1)S(1)} %get-tuple-element.55.gh, ...), custom_call_target="tpu_custom_call" | custom-call | flops 503316480 | bytes 2097152 | tf_op jit(solution)/shard_map/pallas_call | solution.py:320
  20.4 1.0 %shard_map.66 = (f32[256,256]{1,0:T(8,128)S(1)}, f32[256,256]{1,0:T(8,128)S(1)}) custom-call(f32[1024,1024]{1,0:T(8,128)S(1)} %get-tuple-element.41.block, bf16[256,1024]{1,0:T(8,128)(2,1)S(1)} %get-tuple-element.53.fh, bf16[256,1024]{1,0:T(8,128)(2,1)S(1)} %get-tuple-element.54.fl, bf16[256,256]{1,0:T(8,128)(2,1)S(1)} %get-tuple-element.55.gh, ...), custom_call_target="tpu_custom_call" | custom-call | flops 503316480 | bytes 2097152 | tf_op jit(solution)/shard_map/pallas_call | solution.py:320
  22.5 2.0 %collective-permute-start.10 = (f32[256,256]{1,0:T(8,128)S(1)}, f32[256,256]{1,0:T(8,128)S(1)}, u32[]{:S(2)}, u32[]{:S(2)}) collective-permute-start(f32[256,256]{1,0:T(8,128)S(1)} %shard_map.64.mine), channel_id=1, source_target_pairs={{0,8},{4,12},{8,0},{12,4},{16,24},{20,28},{24,16},{28,20},{32,40},... | collective-permute-start | bytes 786440 | tf_op jit(solution)/shard_map/ppermute | solution.py:304
  25.5 2.0 %collective-permute-start.20 = (f32[256,128]{1,0:T(8,128)S(1)}, f32[256,128]{1,0:T(8,128)S(1)}, u32[]{:S(2)}, u32[]{:S(2)}) collective-permute-start(f32[256,128]{1,0:T(8,128)S(1)} %get-tuple-element.71.mine), channel_id=1, source_target_pairs={{0,8},{4,12},{8,0},{12,4},{16,24},{20,28},{24,16},{28,20},{32,40},... | collective-permute-start | bytes 393224 | tf_op jit(solution)/shard_map/ppermute | solution.py:304
  28.0 2.0 %collective-permute-start.15 = (f32[256,128]{1,0:T(8,128)S(1)}, f32[256,128]{1,0:T(8,128)S(1)}, u32[]{:S(2)}, u32[]{:S(2)}) collective-permute-start(f32[256,128]{1,0:T(8,128)S(1)} %get-tuple-element.68.mine), channel_id=1, source_target_pairs={{0,8},{4,12},{8,0},{12,4},{16,24},{20,28},{24,16},{28,20},{32,40},... | collective-permute-start | bytes 393224 | tf_op jit(solution)/shard_map/ppermute | solution.py:304
  30.1 10.2 %collective-permute-done.20.theirs = f32[256,128]{1,0:T(8,128)S(1)} collective-permute-done((f32[256,128]{1,0:T(8,128)S(1)}, f32[256,128]{1,0:T(8,128)S(1)}, u32[]{:S(2)}, u32[]{:S(2)}) %collective-permute-start.20) | collective-permute-done | bytes 131104 | tf_op jit(solution)/shard_map/ppermute | solution.py:304
  40.2 1.9 %collective-permute-start.13 = (f32[256,128]{1,0:T(8,128)S(1)}, f32[256,128]{1,0:T(8,128)S(1)}, u32[]{:S(2)}, u32[]{:S(2)}) collective-permute-start(f32[256,128]{1,0:T(8,128)S(1)} %get-tuple-element.67.mine), channel_id=1, source_target_pairs={{0,8},{4,12},{8,0},{12,4},{16,24},{20,28},{24,16},{28,20},{32,40},... | collective-permute-start | bytes 393224 | tf_op jit(solution)/shard_map/ppermute | solution.py:304
  42.5 3.4 %collective-permute-start.21 = (f32[256,128]{1,0:T(8,128)S(1)}, f32[256,128]{1,0:T(8,128)S(1)}, u32[]{:S(2)}, u32[]{:S(2)}) collective-permute-start(f32[256,128]{1,0:T(8,128)S(1)} %shard_map.72.mine), channel_id=1, source_target_pairs={{0,16},{4,20},{8,24},{12,28},{16,0},{20,4},{24,8},{28,12},{32,48},... | collective-permute-start | bytes 393224 | tf_op jit(solution)/shard_map/ppermute | solution.py:304
  46.8 3.0 %collective-permute-start.8 = (f32[256,256]{1,0:T(8,128)S(1)}, f32[256,256]{1,0:T(8,128)S(1)}, u32[]{:S(2)}, u32[]{:S(2)}) collective-permute-start(f32[256,256]{1,0:T(8,128)S(1)} %shard_map.61.mine), channel_id=1, source_target_pairs={{0,16},{4,20},{8,24},{12,28},{16,0},{20,4},{24,8},{28,12},{32,48},... | collective-permute-start | bytes 786440 | tf_op jit(solution)/shard_map/ppermute | solution.py:304
  49.8 2.0 %shard_map.73.args_2_ = f32[1024,1024]{1,0:T(8,128)} custom-call(f32[1024,1024]{1,0:T(8,128)S(1)} %get-tuple-element.41.block, bf16[1024,256]{1,0:T(8,128)(2,1)S(1)} %get-tuple-element.72.yh, bf16[1024,256]{1,0:T(8,128)(2,1)S(1)} %get-tuple-element.73.yl, bf16[256,256]{1,0:T(8,128)(2,1)S(1)} %get-tuple-element.47.th, ...), custom_call_target="tpu_custom_call" | custom-call | flops 1006632960 | bytes 4194304 | tf_op jit(solution)/shard_map/pallas_call | solution.py:351
  53.2 2.5 %collective-permute-start.16 = (f32[256,128]{1,0:T(8,128)S(1)}, f32[256,128]{1,0:T(8,128)S(1)}, u32[]{:S(2)}, u32[]{:S(2)}) collective-permute-start(f32[256,128]{1,0:T(8,128)S(1)} %shard_map.69.mine), channel_id=1, source_target_pairs={{0,16},{4,20},{8,24},{12,28},{16,0},{20,4},{24,8},{28,12},{32,48},... | collective-permute-start | bytes 393224 | tf_op jit(solution)/shard_map/ppermute | solution.py:304
  56.6 2.3 %shard_map.62 = (bf16[256,512]{1,0:T(8,128)(2,1)S(1)}, bf16[256,512]{1,0:T(8,128)(2,1)S(1)}) custom-call(s32[2]{0:T(128)S(1)} %pad_add_fusion.place, f32[3,256,256]{2,1,0:T(8,128)} %tree_v.3, f32[3,256,256]{2,1,0:T(8,128)} %tree_t.3, f32[256,256]{1,0:T(8,128)S(1)} %get-tuple-element.62.after.args_1_), custom_call_target="tpu_custom_call" | custom-call | flops 201326592 | bytes 1048576 | tf_op jit(solution)/shard_map/pallas_call | solution.py:335
  59.0 2.0 %shard_map.74.whole = f32[1024,1024]{1,0:T(8,128)} custom-call(f32[1024,1024]{1,0:T(8,128)S(1)} %get-tuple-element.41.block, bf16[1024,256]{1,0:T(8,128)(2,1)S(1)} %get-tuple-element.72.yh, bf16[1024,256]{1,0:T(8,128)(2,1)S(1)} %get-tuple-element.73.yl, bf16[256,256]{1,0:T(8,128)(2,1)S(1)} %get-tuple-element.47.th, ...), custom_call_target="tpu_custom_call", output_to_operand_aliasing={{}: (7, {})} | custom-call | flops 1006632960 | bytes 4194304 | tf_op jit(solution)/shard_map/pallas_call | solution.py:351
  60.9 1.0 %shard_map.75.whole = f32[1024,1024]{1,0:T(8,128)} custom-call(f32[256,128]{1,0:T(8,128)S(1)} %shard_map.72.mine, f32[256,128]{1,0:T(8,128)S(1)} %collective-permute-done.21.theirs, bf16[256,512]{1,0:T(8,128)(2,1)S(1)} %get-tuple-element.63.high, bf16[256,512]{1,0:T(8,128)(2,1)S(1)} %get-tuple-element.64.low, ...), custom_call_target="tpu_custom_call", output_to_operand_aliasing={{}: (4, {})} | custom-call | flops 100663296 | bytes 1048576 | tf_op jit(solution)/shard_map/pallas_call | solution.py:365
  62.0 24.9 %collective-permute-done.19.theirs = f32[256,128]{1,0:T(8,128)S(1)} collective-permute-done((f32[256,128]{1,0:T(8,128)S(1)}, f32[256,128]{1,0:T(8,128)S(1)}, u32[]{:S(2)}, u32[]{:S(2)}) %collective-permute-start.19) | collective-permute-done | bytes 131104 | tf_op jit(solution)/shard_map/ppermute | solution.py:304
  86.9 1.0 %shard_map.76.whole = f32[1024,1024]{1,0:T(8,128)} custom-call(f32[256,128]{1,0:T(8,128)S(1)} %shard_map.71.mine, f32[256,128]{1,0:T(8,128)S(1)} %collective-permute-done.19.theirs, bf16[256,512]{1,0:T(8,128)(2,1)S(1)} %get-tuple-element.63.high, bf16[256,512]{1,0:T(8,128)(2,1)S(1)} %get-tuple-element.64.low, ...), custom_call_target="tpu_custom_call", output_to_operand_aliasing={{}: (4, {})} | custom-call | flops 100663296 | bytes 1048576 | tf_op jit(solution)/shard_map/pallas_call | solution.py:365
  87.9 1.7 %collective-permute-done.16.theirs = f32[256,128]{1,0:T(8,128)S(1)} collective-permute-done((f32[256,128]{1,0:T(8,128)S(1)}, f32[256,128]{1,0:T(8,128)S(1)}, u32[]{:S(2)}, u32[]{:S(2)}) %collective-permute-start.16) | collective-permute-done | bytes 131104 | tf_op jit(solution)/shard_map/ppermute | solution.py:304
  89.6 1.0 %shard_map.77.whole = f32[1024,1024]{1,0:T(8,128)} custom-call(f32[256,128]{1,0:T(8,128)S(1)} %shard_map.69.mine, f32[256,128]{1,0:T(8,128)S(1)} %collective-permute-done.16.theirs, bf16[256,512]{1,0:T(8,128)(2,1)S(1)} %get-tuple-element.63.high, bf16[256,512]{1,0:T(8,128)(2,1)S(1)} %get-tuple-element.64.low, ...), custom_call_target="tpu_custom_call", output_to_operand_aliasing={{}: (4, {})} | custom-call | flops 100663296 | bytes 1048576 | tf_op jit(solution)/shard_map/pallas_call | solution.py:365
  91.0 1.0 %shard_map.78.whole = f32[1024,1024]{1,0:T(8,128)} custom-call(f32[256,128]{1,0:T(8,128)S(1)} %shard_map.68.mine, f32[256,128]{1,0:T(8,128)S(1)} %collective-permute-done.14.theirs, bf16[256,512]{1,0:T(8,128)(2,1)S(1)} %get-tuple-element.63.high, bf16[256,512]{1,0:T(8,128)(2,1)S(1)} %get-tuple-element.64.low, ...), custom_call_target="tpu_custom_call", output_to_operand_aliasing={{}: (4, {})} | custom-call | flops 100663296 | bytes 1048576 | tf_op jit(solution)/shard_map/pallas_call | solution.py:365
  92.1 1.1 %shard_map.79.whole = f32[1024,1024]{1,0:T(8,128)} custom-call(f32[256,256]{1,0:T(8,128)S(1)} %shard_map.65.mine, f32[256,256]{1,0:T(8,128)S(1)} %collective-permute-done.11.theirs, bf16[256,512]{1,0:T(8,128)(2,1)S(1)} %get-tuple-element.63.high, bf16[256,512]{1,0:T(8,128)(2,1)S(1)} %get-tuple-element.64.low, ...), custom_call_target="tpu_custom_call", output_to_operand_aliasing={{}: (4, {})} | custom-call | flops 201326592 | bytes 1048576 | tf_op jit(solution)/shard_map/pallas_call | solution.py:365
  93.2 1.1 %shard_map.80 = f32[1024,1024]{1,0:T(8,128)} custom-call(f32[256,256]{1,0:T(8,128)S(1)} %shard_map.61.mine, f32[256,256]{1,0:T(8,128)S(1)} %collective-permute-done.8.theirs, bf16[256,512]{1,0:T(8,128)(2,1)S(1)} %get-tuple-element.63.high, bf16[256,512]{1,0:T(8,128)(2,1)S(1)} %get-tuple-element.64.low, ...), custom_call_target="tpu_custom_call", output_to_operand_aliasing={{}: (4, {})} | custom-call | flops 201326592 | bytes 1048576 | tf_op jit(solution)/shard_map/pallas_call | solution.py:365
  (42 shorter events, 7.8 us)
Async XLA Ops:
  0.0 14.2 %copy-start = (f32[256,256]{1,0:T(8,128)S(1)}, f32[256,256]{1,0:T(8,128)}, u32[]{:S(2)}) copy-start(f32[256,256]{1,0:T(8,128)} %own.1) | copy-start | bytes 786436
  1.0 6.7 %collective-permute-start = (f32[128,256]{1,0:T(8,128)S(1)}, f32[128,256]{1,0:T(8,128)S(1)}, u32[]{:S(2)}, u32[]{:S(2)}) collective-permute-start(f32[128,256]{1,0:T(8,128)S(1)} %get-tuple-element.78), channel_id=1, source_target_pairs={{0,1},{1,2},{2,3},{3,0},{4,5},{5,6},{6,7},{7,4},{8,9},{9,10},{10,1... | collective-permute-start | bytes 393224 | tf_op jit(solution)/shard_map/ppermute | solution.py:246
  2.6 6.4 %collective-permute-start.3 = (f32[128,256]{1,0:T(8,128)S(1)}, f32[128,256]{1,0:T(8,128)S(1)}, u32[]{:S(2)}, u32[]{:S(2)}) collective-permute-start(f32[128,256]{1,0:T(8,128)S(1)} %get-tuple-element.77), channel_id=1, source_target_pairs={{0,3},{1,0},{2,1},{3,2},{4,7},{5,4},{6,5},{7,6},{8,11},{9,8},{10,9... | collective-permute-start | bytes 393224 | tf_op jit(solution)/shard_map/ppermute | solution.py:247
  4.3 9.9 %collective-permute-start.1 = (f32[128,256]{1,0:T(8,128)S(1)}, f32[128,256]{1,0:T(8,128)S(1)}, u32[]{:S(2)}, u32[]{:S(2)}) collective-permute-start(f32[128,256]{1,0:T(8,128)S(1)} %get-tuple-element.77), channel_id=1, source_target_pairs={{0,1},{1,2},{2,3},{3,0},{4,5},{5,6},{6,7},{7,4},{8,9},{9,10},{10,1... | collective-permute-start | bytes 393224 | tf_op jit(solution)/shard_map/ppermute | solution.py:248
  4.6 9.6 %collective-permute-start.2 = (f32[128,256]{1,0:T(8,128)S(1)}, f32[128,256]{1,0:T(8,128)S(1)}, u32[]{:S(2)}, u32[]{:S(2)}) collective-permute-start(f32[128,256]{1,0:T(8,128)S(1)} %get-tuple-element.78), channel_id=1, source_target_pairs={{0,3},{1,0},{2,1},{3,2},{4,7},{5,4},{6,5},{7,6},{8,11},{9,8},{10,9... | collective-permute-start | bytes 393224 | tf_op jit(solution)/shard_map/ppermute | solution.py:249
  7.7 7.8 %collective-permute-start.4 = (f32[128,256]{1,0:T(8,128)S(1)}, f32[128,256]{1,0:T(8,128)S(1)}, u32[]{:S(2)}, u32[]{:S(2)}) collective-permute-start(f32[128,256]{1,0:T(8,128)S(1)} %collective-permute-done.left_a), channel_id=1, source_target_pairs={{0,1},{1,2},{2,3},{3,0},{4,5},{5,6},{6,7},{7,4},{8,9},{9,10},{10,1... | collective-permute-start | bytes 393224 | tf_op jit(solution)/shard_map/ppermute | solution.py:250
  9.0 6.6 %collective-permute-start.5 = (f32[128,256]{1,0:T(8,128)S(1)}, f32[128,256]{1,0:T(8,128)S(1)}, u32[]{:S(2)}, u32[]{:S(2)}) collective-permute-start(f32[128,256]{1,0:T(8,128)S(1)} %collective-permute-done.3.right_b), channel_id=1, source_target_pairs={{0,3},{1,0},{2,1},{3,2},{4,7},{5,4},{6,5},{7,6},{8,11},{9,8},{10,9... | collective-permute-start | bytes 393224 | tf_op jit(solution)/shard_map/ppermute | solution.py:251
  18.6 3.5 %collective-permute-start.9 = (f32[256,256]{1,0:T(8,128)S(1)}, f32[256,256]{1,0:T(8,128)S(1)}, u32[]{:S(2)}, u32[]{:S(2)}) collective-permute-start(f32[256,256]{1,0:T(8,128)S(1)} %get-tuple-element.65.mine), channel_id=1, source_target_pairs={{0,4},{4,0},{8,12},{12,8},{16,20},{20,16},{24,28},{28,24},{32,36},... | collective-permute-start | bytes 786440 | tf_op jit(solution)/shard_map/ppermute | solution.py:304
  19.8 4.8 %collective-permute-start.6 = (f32[256,256]{1,0:T(8,128)S(1)}, f32[256,256]{1,0:T(8,128)S(1)}, u32[]{:S(2)}, u32[]{:S(2)}) collective-permute-start(f32[256,256]{1,0:T(8,128)S(1)} %get-tuple-element.57.mine), channel_id=1, source_target_pairs={{0,4},{4,0},{8,12},{12,8},{16,20},{20,16},{24,28},{28,24},{32,36},... | collective-permute-start | bytes 786440 | tf_op jit(solution)/shard_map/ppermute | solution.py:304
  20.3 4.8 %collective-permute-start.17 = (f32[256,256]{1,0:T(8,128)S(1)}, f32[256,256]{1,0:T(8,128)S(1)}, u32[]{:S(2)}, u32[]{:S(2)}) collective-permute-start(f32[256,256]{1,0:T(8,128)S(1)} %get-tuple-element.69.mine), channel_id=1, source_target_pairs={{0,4},{4,0},{8,12},{12,8},{16,20},{20,16},{24,28},{28,24},{32,36},... | collective-permute-start | bytes 786440 | tf_op jit(solution)/shard_map/ppermute | solution.py:304
  21.5 6.2 %collective-permute-start.12 = (f32[256,256]{1,0:T(8,128)S(1)}, f32[256,256]{1,0:T(8,128)S(1)}, u32[]{:S(2)}, u32[]{:S(2)}) collective-permute-start(f32[256,256]{1,0:T(8,128)S(1)} %get-tuple-element.66.mine), channel_id=1, source_target_pairs={{0,4},{4,0},{8,12},{12,8},{16,20},{20,16},{24,28},{28,24},{32,36},... | collective-permute-start | bytes 786440 | tf_op jit(solution)/shard_map/ppermute | solution.py:304
  22.5 20.0 %collective-permute-start.10 = (f32[256,256]{1,0:T(8,128)S(1)}, f32[256,256]{1,0:T(8,128)S(1)}, u32[]{:S(2)}, u32[]{:S(2)}) collective-permute-start(f32[256,256]{1,0:T(8,128)S(1)} %shard_map.64.mine), channel_id=1, source_target_pairs={{0,8},{4,12},{8,0},{12,4},{16,24},{20,28},{24,16},{28,20},{32,40},... | collective-permute-start | bytes 786440 | tf_op jit(solution)/shard_map/ppermute | solution.py:304
  25.0 21.3 %collective-permute-start.7 = (f32[256,256]{1,0:T(8,128)S(1)}, f32[256,256]{1,0:T(8,128)S(1)}, u32[]{:S(2)}, u32[]{:S(2)}) collective-permute-start(f32[256,256]{1,0:T(8,128)S(1)} %shard_map.60.mine), channel_id=1, source_target_pairs={{0,8},{4,12},{8,0},{12,4},{16,24},{20,28},{24,16},{28,20},{32,40},... | collective-permute-start | bytes 786440 | tf_op jit(solution)/shard_map/ppermute | solution.py:304
  25.5 14.7 %collective-permute-start.20 = (f32[256,128]{1,0:T(8,128)S(1)}, f32[256,128]{1,0:T(8,128)S(1)}, u32[]{:S(2)}, u32[]{:S(2)}) collective-permute-start(f32[256,128]{1,0:T(8,128)S(1)} %get-tuple-element.71.mine), channel_id=1, source_target_pairs={{0,8},{4,12},{8,0},{12,4},{16,24},{20,28},{24,16},{28,20},{32,40},... | collective-permute-start | bytes 393224 | tf_op jit(solution)/shard_map/ppermute | solution.py:304
  27.5 19.2 %collective-permute-start.18 = (f32[256,128]{1,0:T(8,128)S(1)}, f32[256,128]{1,0:T(8,128)S(1)}, u32[]{:S(2)}, u32[]{:S(2)}) collective-permute-start(f32[256,128]{1,0:T(8,128)S(1)} %get-tuple-element.70.mine), channel_id=1, source_target_pairs={{0,8},{4,12},{8,0},{12,4},{16,24},{20,28},{24,16},{28,20},{32,40},... | collective-permute-start | bytes 393224 | tf_op jit(solution)/shard_map/ppermute | solution.py:304
  28.0 24.1 %collective-permute-start.15 = (f32[256,128]{1,0:T(8,128)S(1)}, f32[256,128]{1,0:T(8,128)S(1)}, u32[]{:S(2)}, u32[]{:S(2)}) collective-permute-start(f32[256,128]{1,0:T(8,128)S(1)} %get-tuple-element.68.mine), channel_id=1, source_target_pairs={{0,8},{4,12},{8,0},{12,4},{16,24},{20,28},{24,16},{28,20},{32,40},... | collective-permute-start | bytes 393224 | tf_op jit(solution)/shard_map/ppermute | solution.py:304
  40.2 12.9 %collective-permute-start.13 = (f32[256,128]{1,0:T(8,128)S(1)}, f32[256,128]{1,0:T(8,128)S(1)}, u32[]{:S(2)}, u32[]{:S(2)}) collective-permute-start(f32[256,128]{1,0:T(8,128)S(1)} %get-tuple-element.67.mine), channel_id=1, source_target_pairs={{0,8},{4,12},{8,0},{12,4},{16,24},{20,28},{24,16},{28,20},{32,40},... | collective-permute-start | bytes 393224 | tf_op jit(solution)/shard_map/ppermute | solution.py:304
  42.5 13.5 %collective-permute-start.21 = (f32[256,128]{1,0:T(8,128)S(1)}, f32[256,128]{1,0:T(8,128)S(1)}, u32[]{:S(2)}, u32[]{:S(2)}) collective-permute-start(f32[256,128]{1,0:T(8,128)S(1)} %shard_map.72.mine), channel_id=1, source_target_pairs={{0,16},{4,20},{8,24},{12,28},{16,0},{20,4},{24,8},{28,12},{32,48},... | collective-permute-start | bytes 393224 | tf_op jit(solution)/shard_map/ppermute | solution.py:304
  46.3 45.8 %collective-permute-start.11 = (f32[256,256]{1,0:T(8,128)S(1)}, f32[256,256]{1,0:T(8,128)S(1)}, u32[]{:S(2)}, u32[]{:S(2)}) collective-permute-start(f32[256,256]{1,0:T(8,128)S(1)} %shard_map.65.mine), channel_id=1, source_target_pairs={{0,16},{4,20},{8,24},{12,28},{16,0},{20,4},{24,8},{28,12},{32,48},... | collective-permute-start | bytes 786440 | tf_op jit(solution)/shard_map/ppermute | solution.py:304
  46.8 46.4 %collective-permute-start.8 = (f32[256,256]{1,0:T(8,128)S(1)}, f32[256,256]{1,0:T(8,128)S(1)}, u32[]{:S(2)}, u32[]{:S(2)}) collective-permute-start(f32[256,256]{1,0:T(8,128)S(1)} %shard_map.61.mine), channel_id=1, source_target_pairs={{0,16},{4,20},{8,24},{12,28},{16,0},{20,4},{24,8},{28,12},{32,48},... | collective-permute-start | bytes 786440 | tf_op jit(solution)/shard_map/ppermute | solution.py:304
  52.1 34.8 %collective-permute-start.19 = (f32[256,128]{1,0:T(8,128)S(1)}, f32[256,128]{1,0:T(8,128)S(1)}, u32[]{:S(2)}, u32[]{:S(2)}) collective-permute-start(f32[256,128]{1,0:T(8,128)S(1)} %shard_map.71.mine), channel_id=1, source_target_pairs={{0,16},{4,20},{8,24},{12,28},{16,0},{20,4},{24,8},{28,12},{32,48},... | collective-permute-start | bytes 393224 | tf_op jit(solution)/shard_map/ppermute | solution.py:304
  53.2 36.5 %collective-permute-start.16 = (f32[256,128]{1,0:T(8,128)S(1)}, f32[256,128]{1,0:T(8,128)S(1)}, u32[]{:S(2)}, u32[]{:S(2)}) collective-permute-start(f32[256,128]{1,0:T(8,128)S(1)} %shard_map.69.mine), channel_id=1, source_target_pairs={{0,16},{4,20},{8,24},{12,28},{16,0},{20,4},{24,8},{28,12},{32,48},... | collective-permute-start | bytes 393224 | tf_op jit(solution)/shard_map/ppermute | solution.py:304
  56.0 35.0 %collective-permute-start.14 = (f32[256,128]{1,0:T(8,128)S(1)}, f32[256,128]{1,0:T(8,128)S(1)}, u32[]{:S(2)}, u32[]{:S(2)}) collective-permute-start(f32[256,128]{1,0:T(8,128)S(1)} %shard_map.68.mine), channel_id=1, source_target_pairs={{0,16},{4,20},{8,24},{12,28},{16,0},{20,4},{24,8},{28,12},{32,48},... | collective-permute-start | bytes 393224 | tf_op jit(solution)/shard_map/ppermute | solution.py:304

commit v2 on v1

--- a/solution.py
+++ b/solution.py
@@ -105,13 +105,13 @@
     return split(rows), split(rows.T)
 
 
-def early_kernel(place, own, left_a, left_b, right_a, right_b, block, partial, yh, yl, fh, fl):
+def early_kernel(place, own, left, right_a, right_b, block, partial, yh, yl, fh, fl):
     col = place[1]
     size = own.shape[0]
     count = block.shape[0] // size
     width = partial.shape[1]
     total = None
-    for shift, parts in ((0, (own,)), (count - 1, (left_a, left_b)), (1, (right_a, right_b))):
+    for shift, parts in ((0, (own,)), (count - 1, (left,)), (1, (right_a, right_b))):
         start = pl.multiple_of(lax.rem(col + shift, count) * size, size)
         rows = parts[0][...] if len(parts) == 1 else jnp.concatenate([p[...] for p in parts], axis=0)
         here = pl.ds(start, size)
@@ -131,7 +131,7 @@
 
 
 def first_kernel(place, partial, opp_a, opp_b, block, th, tl, yh, yl, top, proj, gh, gl, oh, ol, ph, plow):
-    size = 2 * opp_a.shape[0]
+    size = opp_a.shape[0] + opp_b.shape[0]
     width = partial.shape[1]
     start = opposite_rows(place[1], size, block.shape[0] // size)
     rows = jnp.concatenate([opp_a[...], opp_b[...]], axis=0)
@@ -236,19 +236,17 @@
     size, width = panel_y.shape
     rows, columns = trailing.shape
     levels = tree_v.shape[0]
-    half = size // 2
+    cut = size * 7 // 16
     count = lax.axis_size("col")
     place = jnp.stack([lax.axis_index("row"), lax.axis_index("col")]).astype(jnp.int32)
     onward = [(c, (c + 1) % count) for c in range(count)]
     backward = [(c, (c - 1) % count) for c in range(count)]
 
-    own_a, own_b = panel_y[:half], panel_y[half:]
-    left_a = lax.ppermute(own_a, "col", onward)
-    right_b = lax.ppermute(own_b, "col", backward)
-    left_b = lax.ppermute(own_b, "col", onward)
-    right_a = lax.ppermute(own_a, "col", backward)
-    opp_a = lax.ppermute(left_a, "col", onward)
+    left = lax.ppermute(panel_y, "col", onward)
+    right_b = lax.ppermute(panel_y[cut:], "col", backward)
+    right_a = lax.ppermute(panel_y[:cut], "col", backward)
     opp_b = lax.ppermute(right_b, "col", backward)
+    opp_a = lax.ppermute(left[:cut], "col", onward)
 
     square = shaped((width, width), BF16)
     mix = shaped((width, 2 * width), BF16)
@@ -275,11 +273,11 @@
     partial, yh, yl, fh, fl = call(
         early_kernel,
         out_shape=[shaped((width, w)), tall, tall, wide, wide],
-        in_specs=[SMEM] + [VMEM] * 6,
+        in_specs=[SMEM] + [VMEM] * 5,
         out_specs=[VMEM] * 5,
         mib=16,
         cost=(2 * cube, 4 << 20),
-    )(place, panel_y, left_a, left_b, right_a, right_b, block)
+    )(place, panel_y, left, right_a, right_b, block)
 
     top, proj, gh, gl, *opposite = call(
         first_kernel,

time: 94.6 us -> 97 us (1.025)
  waiting for transfers between devices: 37.3 us -> 40.5 us
  starting transfers between devices: 29.7 us -> 28 us
    ppermute x5 -> x4, waiting for transfers between devices: 0.11 us -> 3.3 us  [the longest x1 1.89 us: update(): right_b = lax.ppermute(panel_y[cut:], 'col', backward)]
    ppermute x5 -> x4, starting transfers between devices: 7.83 us -> 4.94 us  [the longest x1 1.82 us: update(): right_b = lax.ppermute(panel_y[cut:], 'col', backward)]
    ppermute x1, starting transfers between devices: 1.95 us -> 3.15 us  [update(): opp_b = lax.ppermute(right_b, 'col', backward)]
  transfers between devices with their start and end apart: 22 -> 21, of which waited for: 5 -> 6; matrix products, arithmetic and copies ran while one was open for 0% -> 2% of each run, Pallas kernels for 23% -> 22%
where the time goes in v2:
time: 97 us; the launch traced here: 96.8 us
  waiting for transfers between devices  40.5 us (42%)
  starting transfers between devices  28 us (29%)
  Pallas kernels  25.9 us (27%)
  local copies, waits for them, and re-layouts  1.87 us (2%)
    ppermute x16, waiting for transfers between devices, swap(): return lax.ppermute(values, 'row', route)  37.2 us
    ppermute x16, starting transfers between devices, swap(): return lax.ppermute(values, 'row', route)  19.9 us
    pallas_call x6, Pallas kernels, update(): call(functools.partial(final_kernel, first), out_shape=shaped((rows, colu...  6.35 us
    pallas_call x2, Pallas kernels, update(): call(functools.partial(rest_kernel, first), out_shape=shaped((rows, colum...  3.92 us
    pallas_call x10, Pallas kernels, combine(): call(level_kernel, out_shape=[shaped((width, w)) for w in widths], in_spe...  3.77 us
    pallas_call x1, Pallas kernels, update(): call(prepare_kernel, out_shape=[square, square] + [mix] * (2 * ahead) + [...  3.19 us
    ppermute x1, starting transfers between devices, update(): opp_b = lax.ppermute(right_b, 'col', backward)  3.15 us
    pallas_call x3, Pallas kernels, update(): call(functools.partial(next_kernel, slice(first, first + w)), out_shape=[...  3.03 us
  transfers between devices with their start and end apart: 21, of which 6 were waited for; matrix products, arithmetic and copies ran while one was open for 2% of the time, Pallas kernels for 22%

profile of v2, /device:TPU:8, one launch (start us, length us, event | category | flops | bytes accessed | tf_op | source)
XLA Modules:
  0.0 96.8 jit_solution(7643035615440826947)
XLA Ops:
  0.0 1.5 %collective-permute-start = (f32[256,256]{1,0:T(8,128)}, f32[256,256]{1,0:T(8,128)S(1)}, u32[]{:S(2)}, u32[]{:S(2)}) collective-permute-start(f32[256,256]{1,0:T(8,128)} %own.1), channel_id=1, source_target_pairs={{0,1},{1,2},{2,3},{3,0},{4,5},{5,6},{6,7},{7,4},{8,9},{9,10},{10,1... | collective-permute-start | bytes 786440 | tf_op jit(solution)/shard_map/ppermute | solution.py:245
  1.5 1.0 slice.10
  2.5 1.8 %collective-permute-start.2 = (f32[144,256]{1,0:T(8,128)S(1)}, f32[144,256]{1,0:T(8,128)S(1)}, u32[]{:S(2)}, u32[]{:S(2)}) collective-permute-start(f32[144,256]{1,0:T(8,128)S(1)} %slice.10), channel_id=1, source_target_pairs={{0,3},{1,0},{2,1},{3,2},{4,7},{5,4},{6,5},{7,6},{8,11},{9,8},{10,9... | collective-permute-start | bytes 442376 | tf_op jit(solution)/shard_map/ppermute | solution.py:246
  5.2 1.5 %collective-permute-start.1 = (f32[112,256]{1,0:T(8,128)S(1)}, f32[112,256]{1,0:T(8,128)S(1)}, u32[]{:S(2)}, u32[]{:S(2)}) collective-permute-start(f32[112,256]{1,0:T(8,128)S(1)} %slice.9), channel_id=1, source_target_pairs={{0,3},{1,0},{2,1},{3,2},{4,7},{5,4},{6,5},{7,6},{8,11},{9,8},{10,9... | collective-permute-start | bytes 344072 | tf_op jit(solution)/shard_map/ppermute | solution.py:247
  6.7 1.9 %collective-permute-done.2.right_b = f32[144,256]{1,0:T(8,128)S(1)} collective-permute-done((f32[144,256]{1,0:T(8,128)S(1)}, f32[144,256]{1,0:T(8,128)S(1)}, u32[]{:S(2)}, u32[]{:S(2)}) %collective-permute-start.2) | collective-permute-done | bytes 147488 | tf_op jit(solution)/shard_map/ppermute | solution.py:246
  8.6 3.2 %collective-permute-start.4 = (f32[144,256]{1,0:T(8,128)S(1)}, f32[144,256]{1,0:T(8,128)S(1)}, u32[]{:S(2)}, u32[]{:S(2)}) collective-permute-start(f32[144,256]{1,0:T(8,128)S(1)} %collective-permute-done.2.right_b), channel_id=1, source_target_pairs={{0,3},{1,0},{2,1},{3,2},{4,7},{5,4},{6,5},{7,6},{8,11},{9,8},{10,9... | collective-permute-start | bytes 442376 | tf_op jit(solution)/shard_map/ppermute | solution.py:248
  12.0 3.2 %shard_map.55 = (bf16[256,256]{1,0:T(8,128)(2,1)S(1)}, bf16[256,256]{1,0:T(8,128)(2,1)S(1)}, bf16[256,512]{1,0:T(8,128)(2,1)S(1)}, bf16[256,512]{1,0:T(8,128)(2,...) custom-call(s32[2]{0:T(128)S(1)} %pad_add_fusion.place, ...), custom_call_target="tpu_custom_call" | custom-call | flops 503316480 | bytes 5242880 | tf_op jit(solution)/shard_map/pallas_call | solution.py:260
  15.2 1.3 %shard_map.56 = (f32[256,256]{1,0:T(8,128)S(1)}, bf16[1024,256]{1,0:T(8,128)(2,1)S(1)}, bf16[1024,256]{1,0:T(8,128)(2,1)S(1)}, bf16[256,1024]{1,0:T(8,128)(2,1)S(1)}, bf16[256,1024]{1,0:T(8,128)(2,1)S(1)}) custom-call(s32[2]{0:T(128)S(1)} %pad_add_fusion.place, f32[256,256]{1,0:T(8,128)S(1)} %copy-done, f32[256,256]{1,0:T(8,128)S(1)} %collective-permute-done.left, ...), custom_call_target="tpu_custom_call" | custom-call | flops 201326592 | bytes 4194304 | tf_op jit(solution)/shard_map/pallas_call | solution.py:273
  16.5 1.4 %collective-permute-done.3.opp_a = f32[112,256]{1,0:T(8,128)S(1)} collective-permute-done((f32[112,256]{1,0:T(8,128)S(1)}, f32[112,256]{1,0:T(8,128)S(1)}, u32[]{:S(2)}, u32[]{:S(2)}) %collective-permute-start.3) | collective-permute-done | bytes 114720 | tf_op jit(solution)/shard_map/ppermute | solution.py:249
  17.9 1.4 %shard_map.57 = (f32[256,256]{1,0:T(8,128)S(1)}, f32[256,256]{1,0:T(8,128)S(1)}, bf16[256,256]{1,0:T(8,128)(2,1)S(1)}, bf16[256,256]{1,0:T(8,128)(2,1)S(1)}, bf1...) custom-call(s32[2]{0:T(128)S(1)} %pad_add_fusion.place, ...), custom_call_target="tpu_custom_call" | custom-call | flops 201326592 | bytes 2097152 | tf_op jit(solution)/shard_map/pallas_call | solution.py:282
  20.0 1.0 %shard_map.63 = (f32[256,256]{1,0:T(8,128)S(1)}, f32[256,256]{1,0:T(8,128)S(1)}) custom-call(f32[1024,1024]{1,0:T(8,128)S(1)} %get-tuple-element.41.block, bf16[256,1024]{1,0:T(8,128)(2,1)S(1)} %get-tuple-element.53.fh, bf16[256,1024]{1,0:T(8,128)(2,1)S(1)} %get-tuple-element.54.fl, bf16[256,256]{1,0:T(8,128)(2,1)S(1)} %get-tuple-element.55.gh, ...), custom_call_target="tpu_custom_call" | custom-call | flops 503316480 | bytes 2097152 | tf_op jit(solution)/shard_map/pallas_call | solution.py:318
  21.1 1.0 %shard_map.59 = (f32[256,256]{1,0:T(8,128)S(1)}, f32[256,256]{1,0:T(8,128)S(1)}) custom-call(f32[1024,1024]{1,0:T(8,128)S(1)} %get-tuple-element.41.block, bf16[256,1024]{1,0:T(8,128)(2,1)S(1)} %get-tuple-element.53.fh, bf16[256,1024]{1,0:T(8,128)(2,1)S(1)} %get-tuple-element.54.fl, bf16[256,256]{1,0:T(8,128)(2,1)S(1)} %get-tuple-element.55.gh, ...), custom_call_target="tpu_custom_call" | custom-call | flops 503316480 | bytes 2097152 | tf_op jit(solution)/shard_map/pallas_call | solution.py:318
  22.8 1.0 %shard_map.66 = (f32[256,256]{1,0:T(8,128)S(1)}, f32[256,256]{1,0:T(8,128)S(1)}) custom-call(f32[1024,1024]{1,0:T(8,128)S(1)} %get-tuple-element.41.block, bf16[256,1024]{1,0:T(8,128)(2,1)S(1)} %get-tuple-element.53.fh, bf16[256,1024]{1,0:T(8,128)(2,1)S(1)} %get-tuple-element.54.fl, bf16[256,256]{1,0:T(8,128)(2,1)S(1)} %get-tuple-element.55.gh, ...), custom_call_target="tpu_custom_call" | custom-call | flops 503316480 | bytes 2097152 | tf_op jit(solution)/shard_map/pallas_call | solution.py:318
  24.7 2.2 %collective-permute-start.9 = (f32[256,256]{1,0:T(8,128)S(1)}, f32[256,256]{1,0:T(8,128)S(1)}, u32[]{:S(2)}, u32[]{:S(2)}) collective-permute-start(f32[256,256]{1,0:T(8,128)S(1)} %shard_map.64.mine), channel_id=1, source_target_pairs={{0,8},{4,12},{8,0},{12,4},{16,24},{20,28},{24,16},{28,20},{32,40},... | collective-permute-start | bytes 786440 | tf_op jit(solution)/shard_map/ppermute | solution.py:302
  27.9 2.0 %collective-permute-start.19 = (f32[256,128]{1,0:T(8,128)S(1)}, f32[256,128]{1,0:T(8,128)S(1)}, u32[]{:S(2)}, u32[]{:S(2)}) collective-permute-start(f32[256,128]{1,0:T(8,128)S(1)} %get-tuple-element.71.mine), channel_id=1, source_target_pairs={{0,8},{4,12},{8,0},{12,4},{16,24},{20,28},{24,16},{28,20},{32,40},... | collective-permute-start | bytes 393224 | tf_op jit(solution)/shard_map/ppermute | solution.py:302
  30.4 2.0 %collective-permute-start.14 = (f32[256,128]{1,0:T(8,128)S(1)}, f32[256,128]{1,0:T(8,128)S(1)}, u32[]{:S(2)}, u32[]{:S(2)}) collective-permute-start(f32[256,128]{1,0:T(8,128)S(1)} %get-tuple-element.68.mine), channel_id=1, source_target_pairs={{0,8},{4,12},{8,0},{12,4},{16,24},{20,28},{24,16},{28,20},{32,40},... | collective-permute-start | bytes 393224 | tf_op jit(solution)/shard_map/ppermute | solution.py:302
  32.4 10.2 %collective-permute-done.19.theirs = f32[256,128]{1,0:T(8,128)S(1)} collective-permute-done((f32[256,128]{1,0:T(8,128)S(1)}, f32[256,128]{1,0:T(8,128)S(1)}, u32[]{:S(2)}, u32[]{:S(2)}) %collective-permute-start.19) | collective-permute-done | bytes 131104 | tf_op jit(solution)/shard_map/ppermute | solution.py:302
  42.6 1.9 %collective-permute-start.12 = (f32[256,128]{1,0:T(8,128)S(1)}, f32[256,128]{1,0:T(8,128)S(1)}, u32[]{:S(2)}, u32[]{:S(2)}) collective-permute-start(f32[256,128]{1,0:T(8,128)S(1)} %get-tuple-element.67.mine), channel_id=1, source_target_pairs={{0,8},{4,12},{8,0},{12,4},{16,24},{20,28},{24,16},{28,20},{32,40},... | collective-permute-start | bytes 393224 | tf_op jit(solution)/shard_map/ppermute | solution.py:302
  44.9 3.4 %collective-permute-start.20 = (f32[256,128]{1,0:T(8,128)S(1)}, f32[256,128]{1,0:T(8,128)S(1)}, u32[]{:S(2)}, u32[]{:S(2)}) collective-permute-start(f32[256,128]{1,0:T(8,128)S(1)} %shard_map.72.mine), channel_id=1, source_target_pairs={{0,16},{4,20},{8,24},{12,28},{16,0},{20,4},{24,8},{28,12},{32,48},... | collective-permute-start | bytes 393224 | tf_op jit(solution)/shard_map/ppermute | solution.py:302
  49.1 3.0 %collective-permute-start.7 = (f32[256,256]{1,0:T(8,128)S(1)}, f32[256,256]{1,0:T(8,128)S(1)}, u32[]{:S(2)}, u32[]{:S(2)}) collective-permute-start(f32[256,256]{1,0:T(8,128)S(1)} %shard_map.61.mine), channel_id=1, source_target_pairs={{0,16},{4,20},{8,24},{12,28},{16,0},{20,4},{24,8},{28,12},{32,48},... | collective-permute-start | bytes 786440 | tf_op jit(solution)/shard_map/ppermute | solution.py:302
  52.1 2.0 %shard_map.73.args_2_ = f32[1024,1024]{1,0:T(8,128)} custom-call(f32[1024,1024]{1,0:T(8,128)S(1)} %get-tuple-element.41.block, bf16[1024,256]{1,0:T(8,128)(2,1)S(1)} %get-tuple-element.72.yh, bf16[1024,256]{1,0:T(8,128)(2,1)S(1)} %get-tuple-element.73.yl, bf16[256,256]{1,0:T(8,128)(2,1)S(1)} %get-tuple-element.47.th, ...), custom_call_target="tpu_custom_call" | custom-call | flops 1006632960 | bytes 4194304 | tf_op jit(solution)/shard_map/pallas_call | solution.py:349
  55.5 2.5 %collective-permute-start.15 = (f32[256,128]{1,0:T(8,128)S(1)}, f32[256,128]{1,0:T(8,128)S(1)}, u32[]{:S(2)}, u32[]{:S(2)}) collective-permute-start(f32[256,128]{1,0:T(8,128)S(1)} %shard_map.69.mine), channel_id=1, source_target_pairs={{0,16},{4,20},{8,24},{12,28},{16,0},{20,4},{24,8},{28,12},{32,48},... | collective-permute-start | bytes 393224 | tf_op jit(solution)/shard_map/ppermute | solution.py:302
  59.0 2.3 %shard_map.62 = (bf16[256,512]{1,0:T(8,128)(2,1)S(1)}, bf16[256,512]{1,0:T(8,128)(2,1)S(1)}) custom-call(s32[2]{0:T(128)S(1)} %pad_add_fusion.place, f32[3,256,256]{2,1,0:T(8,128)} %tree_v.3, f32[3,256,256]{2,1,0:T(8,128)} %tree_t.3, f32[256,256]{1,0:T(8,128)S(1)} %get-tuple-element.62.after.args_1_), custom_call_target="tpu_custom_call" | custom-call | flops 201326592 | bytes 1048576 | tf_op jit(solution)/shard_map/pallas_call | solution.py:333
  61.3 2.0 %shard_map.74.whole = f32[1024,1024]{1,0:T(8,128)} custom-call(f32[1024,1024]{1,0:T(8,128)S(1)} %get-tuple-element.41.block, bf16[1024,256]{1,0:T(8,128)(2,1)S(1)} %get-tuple-element.72.yh, bf16[1024,256]{1,0:T(8,128)(2,1)S(1)} %get-tuple-element.73.yl, bf16[256,256]{1,0:T(8,128)(2,1)S(1)} %get-tuple-element.47.th, ...), custom_call_target="tpu_custom_call", output_to_operand_aliasing={{}: (7, {})} | custom-call | flops 1006632960 | bytes 4194304 | tf_op jit(solution)/shard_map/pallas_call | solution.py:349
  63.3 1.0 %shard_map.75.whole = f32[1024,1024]{1,0:T(8,128)} custom-call(f32[256,128]{1,0:T(8,128)S(1)} %shard_map.72.mine, f32[256,128]{1,0:T(8,128)S(1)} %collective-permute-done.20.theirs, bf16[256,512]{1,0:T(8,128)(2,1)S(1)} %get-tuple-element.63.high, bf16[256,512]{1,0:T(8,128)(2,1)S(1)} %get-tuple-element.64.low, ...), custom_call_target="tpu_custom_call", output_to_operand_aliasing={{}: (4, {})} | custom-call | flops 100663296 | bytes 1048576 | tf_op jit(solution)/shard_map/pallas_call | solution.py:363
  64.3 24.9 %collective-permute-done.18.theirs = f32[256,128]{1,0:T(8,128)S(1)} collective-permute-done((f32[256,128]{1,0:T(8,128)S(1)}, f32[256,128]{1,0:T(8,128)S(1)}, u32[]{:S(2)}, u32[]{:S(2)}) %collective-permute-start.18) | collective-permute-done | bytes 131104 | tf_op jit(solution)/shard_map/ppermute | solution.py:302
  89.3 1.0 %shard_map.76.whole = f32[1024,1024]{1,0:T(8,128)} custom-call(f32[256,128]{1,0:T(8,128)S(1)} %shard_map.71.mine, f32[256,128]{1,0:T(8,128)S(1)} %collective-permute-done.18.theirs, bf16[256,512]{1,0:T(8,128)(2,1)S(1)} %get-tuple-element.63.high, bf16[256,512]{1,0:T(8,128)(2,1)S(1)} %get-tuple-element.64.low, ...), custom_call_target="tpu_custom_call", output_to_operand_aliasing={{}: (4, {})} | custom-call | flops 100663296 | bytes 1048576 | tf_op jit(solution)/shard_map/pallas_call | solution.py:363
  90.3 1.7 %collective-permute-done.15.theirs = f32[256,128]{1,0:T(8,128)S(1)} collective-permute-done((f32[256,128]{1,0:T(8,128)S(1)}, f32[256,128]{1,0:T(8,128)S(1)}, u32[]{:S(2)}, u32[]{:S(2)}) %collective-permute-start.15) | collective-permute-done | bytes 131104 | tf_op jit(solution)/shard_map/ppermute | solution.py:302
  91.9 1.0 %shard_map.77.whole = f32[1024,1024]{1,0:T(8,128)} custom-call(f32[256,128]{1,0:T(8,128)S(1)} %shard_map.69.mine, f32[256,128]{1,0:T(8,128)S(1)} %collective-permute-done.15.theirs, bf16[256,512]{1,0:T(8,128)(2,1)S(1)} %get-tuple-element.63.high, bf16[256,512]{1,0:T(8,128)(2,1)S(1)} %get-tuple-element.64.low, ...), custom_call_target="tpu_custom_call", output_to_operand_aliasing={{}: (4, {})} | custom-call | flops 100663296 | bytes 1048576 | tf_op jit(solution)/shard_map/pallas_call | solution.py:363
  93.3 1.0 %shard_map.78.whole = f32[1024,1024]{1,0:T(8,128)} custom-call(f32[256,128]{1,0:T(8,128)S(1)} %shard_map.68.mine, f32[256,128]{1,0:T(8,128)S(1)} %collective-permute-done.13.theirs, bf16[256,512]{1,0:T(8,128)(2,1)S(1)} %get-tuple-element.63.high, bf16[256,512]{1,0:T(8,128)(2,1)S(1)} %get-tuple-element.64.low, ...), custom_call_target="tpu_custom_call", output_to_operand_aliasing={{}: (4, {})} | custom-call | flops 100663296 | bytes 1048576 | tf_op jit(solution)/shard_map/pallas_call | solution.py:363
  94.4 1.1 %shard_map.79.whole = f32[1024,1024]{1,0:T(8,128)} custom-call(f32[256,256]{1,0:T(8,128)S(1)} %shard_map.65.mine, f32[256,256]{1,0:T(8,128)S(1)} %collective-permute-done.10.theirs, bf16[256,512]{1,0:T(8,128)(2,1)S(1)} %get-tuple-element.63.high, bf16[256,512]{1,0:T(8,128)(2,1)S(1)} %get-tuple-element.64.low, ...), custom_call_target="tpu_custom_call", output_to_operand_aliasing={{}: (4, {})} | custom-call | flops 201326592 | bytes 1048576 | tf_op jit(solution)/shard_map/pallas_call | solution.py:363
  95.5 1.1 %shard_map.80 = f32[1024,1024]{1,0:T(8,128)} custom-call(f32[256,256]{1,0:T(8,128)S(1)} %shard_map.61.mine, f32[256,256]{1,0:T(8,128)S(1)} %collective-permute-done.7.theirs, bf16[256,512]{1,0:T(8,128)(2,1)S(1)} %get-tuple-element.63.high, bf16[256,512]{1,0:T(8,128)(2,1)S(1)} %get-tuple-element.64.low, ...), custom_call_target="tpu_custom_call", output_to_operand_aliasing={{}: (4, {})} | custom-call | flops 201326592 | bytes 1048576 | tf_op jit(solution)/shard_map/pallas_call | solution.py:363
  (42 shorter events, 8.9 us)
Async XLA Ops:
  0.0 15.2 %copy-start = (f32[256,256]{1,0:T(8,128)S(1)}, f32[256,256]{1,0:T(8,128)}, u32[]{:S(2)}) copy-start(f32[256,256]{1,0:T(8,128)} %own.1) | copy-start | bytes 786436
  0.0 11.8 %collective-permute-start = (f32[256,256]{1,0:T(8,128)}, f32[256,256]{1,0:T(8,128)S(1)}, u32[]{:S(2)}, u32[]{:S(2)}) collective-permute-start(f32[256,256]{1,0:T(8,128)} %own.1), channel_id=1, source_target_pairs={{0,1},{1,2},{2,3},{3,0},{4,5},{5,6},{6,7},{7,4},{8,9},{9,10},{10,1... | collective-permute-start | bytes 786440 | tf_op jit(solution)/shard_map/ppermute | solution.py:245
  2.5 6.2 %collective-permute-start.2 = (f32[144,256]{1,0:T(8,128)S(1)}, f32[144,256]{1,0:T(8,128)S(1)}, u32[]{:S(2)}, u32[]{:S(2)}) collective-permute-start(f32[144,256]{1,0:T(8,128)S(1)} %slice.10), channel_id=1, source_target_pairs={{0,3},{1,0},{2,1},{3,2},{4,7},{5,4},{6,5},{7,6},{8,11},{9,8},{10,9... | collective-permute-start | bytes 442376 | tf_op jit(solution)/shard_map/ppermute | solution.py:246
  5.2 10.0 %collective-permute-start.1 = (f32[112,256]{1,0:T(8,128)S(1)}, f32[112,256]{1,0:T(8,128)S(1)}, u32[]{:S(2)}, u32[]{:S(2)}) collective-permute-start(f32[112,256]{1,0:T(8,128)S(1)} %slice.9), channel_id=1, source_target_pairs={{0,3},{1,0},{2,1},{3,2},{4,7},{5,4},{6,5},{7,6},{8,11},{9,8},{10,9... | collective-permute-start | bytes 344072 | tf_op jit(solution)/shard_map/ppermute | solution.py:247
  8.6 7.8 %collective-permute-start.4 = (f32[144,256]{1,0:T(8,128)S(1)}, f32[144,256]{1,0:T(8,128)S(1)}, u32[]{:S(2)}, u32[]{:S(2)}) collective-permute-start(f32[144,256]{1,0:T(8,128)S(1)} %collective-permute-done.2.right_b), channel_id=1, source_target_pairs={{0,3},{1,0},{2,1},{3,2},{4,7},{5,4},{6,5},{7,6},{8,11},{9,8},{10,9... | collective-permute-start | bytes 442376 | tf_op jit(solution)/shard_map/ppermute | solution.py:248
  11.8 6.1 %collective-permute-start.3 = (f32[112,256]{1,0:T(8,128)S(1)}, f32[112,256]{1,0:T(8,128)S(1)}, u32[]{:S(2)}, u32[]{:S(2)}) collective-permute-start(f32[112,256]{1,0:T(8,128)S(1)} %slice.12), channel_id=1, source_target_pairs={{0,1},{1,2},{2,3},{3,0},{4,5},{5,6},{6,7},{7,4},{8,9},{9,10},{10,1... | collective-permute-start | bytes 344072 | tf_op jit(solution)/shard_map/ppermute | solution.py:249
  21.0 3.3 %collective-permute-start.8 = (f32[256,256]{1,0:T(8,128)S(1)}, f32[256,256]{1,0:T(8,128)S(1)}, u32[]{:S(2)}, u32[]{:S(2)}) collective-permute-start(f32[256,256]{1,0:T(8,128)S(1)} %get-tuple-element.65.mine), channel_id=1, source_target_pairs={{0,4},{4,0},{8,12},{12,8},{16,20},{20,16},{24,28},{28,24},{32,36},... | collective-permute-start | bytes 786440 | tf_op jit(solution)/shard_map/ppermute | solution.py:302
  22.1 4.8 %collective-permute-start.5 = (f32[256,256]{1,0:T(8,128)S(1)}, f32[256,256]{1,0:T(8,128)S(1)}, u32[]{:S(2)}, u32[]{:S(2)}) collective-permute-start(f32[256,256]{1,0:T(8,128)S(1)} %get-tuple-element.57.mine), channel_id=1, source_target_pairs={{0,4},{4,0},{8,12},{12,8},{16,20},{20,16},{24,28},{28,24},{32,36},... | collective-permute-start | bytes 786440 | tf_op jit(solution)/shard_map/ppermute | solution.py:302
  22.7 4.8 %collective-permute-start.16 = (f32[256,256]{1,0:T(8,128)S(1)}, f32[256,256]{1,0:T(8,128)S(1)}, u32[]{:S(2)}, u32[]{:S(2)}) collective-permute-start(f32[256,256]{1,0:T(8,128)S(1)} %get-tuple-element.69.mine), channel_id=1, source_target_pairs={{0,4},{4,0},{8,12},{12,8},{16,20},{20,16},{24,28},{28,24},{32,36},... | collective-permute-start | bytes 786440 | tf_op jit(solution)/shard_map/ppermute | solution.py:302
  23.8 6.2 %collective-permute-start.11 = (f32[256,256]{1,0:T(8,128)S(1)}, f32[256,256]{1,0:T(8,128)S(1)}, u32[]{:S(2)}, u32[]{:S(2)}) collective-permute-start(f32[256,256]{1,0:T(8,128)S(1)} %get-tuple-element.66.mine), channel_id=1, source_target_pairs={{0,4},{4,0},{8,12},{12,8},{16,20},{20,16},{24,28},{28,24},{32,36},... | collective-permute-start | bytes 786440 | tf_op jit(solution)/shard_map/ppermute | solution.py:302
  24.7 20.2 %collective-permute-start.9 = (f32[256,256]{1,0:T(8,128)S(1)}, f32[256,256]{1,0:T(8,128)S(1)}, u32[]{:S(2)}, u32[]{:S(2)}) collective-permute-start(f32[256,256]{1,0:T(8,128)S(1)} %shard_map.64.mine), channel_id=1, source_target_pairs={{0,8},{4,12},{8,0},{12,4},{16,24},{20,28},{24,16},{28,20},{32,40},... | collective-permute-start | bytes 786440 | tf_op jit(solution)/shard_map/ppermute | solution.py:302
  27.3 21.3 %collective-permute-start.6 = (f32[256,256]{1,0:T(8,128)S(1)}, f32[256,256]{1,0:T(8,128)S(1)}, u32[]{:S(2)}, u32[]{:S(2)}) collective-permute-start(f32[256,256]{1,0:T(8,128)S(1)} %shard_map.60.mine), channel_id=1, source_target_pairs={{0,8},{4,12},{8,0},{12,4},{16,24},{20,28},{24,16},{28,20},{32,40},... | collective-permute-start | bytes 786440 | tf_op jit(solution)/shard_map/ppermute | solution.py:302
  27.9 14.7 %collective-permute-start.19 = (f32[256,128]{1,0:T(8,128)S(1)}, f32[256,128]{1,0:T(8,128)S(1)}, u32[]{:S(2)}, u32[]{:S(2)}) collective-permute-start(f32[256,128]{1,0:T(8,128)S(1)} %get-tuple-element.71.mine), channel_id=1, source_target_pairs={{0,8},{4,12},{8,0},{12,4},{16,24},{20,28},{24,16},{28,20},{32,40},... | collective-permute-start | bytes 393224 | tf_op jit(solution)/shard_map/ppermute | solution.py:302
  29.9 19.3 %collective-permute-start.17 = (f32[256,128]{1,0:T(8,128)S(1)}, f32[256,128]{1,0:T(8,128)S(1)}, u32[]{:S(2)}, u32[]{:S(2)}) collective-permute-start(f32[256,128]{1,0:T(8,128)S(1)} %get-tuple-element.70.mine), channel_id=1, source_target_pairs={{0,8},{4,12},{8,0},{12,4},{16,24},{20,28},{24,16},{28,20},{32,40},... | collective-permute-start | bytes 393224 | tf_op jit(solution)/shard_map/ppermute | solution.py:302
  30.4 24.1 %collective-permute-start.14 = (f32[256,128]{1,0:T(8,128)S(1)}, f32[256,128]{1,0:T(8,128)S(1)}, u32[]{:S(2)}, u32[]{:S(2)}) collective-permute-start(f32[256,128]{1,0:T(8,128)S(1)} %get-tuple-element.68.mine), channel_id=1, source_target_pairs={{0,8},{4,12},{8,0},{12,4},{16,24},{20,28},{24,16},{28,20},{32,40},... | collective-permute-start | bytes 393224 | tf_op jit(solution)/shard_map/ppermute | solution.py:302
  42.6 12.9 %collective-permute-start.12 = (f32[256,128]{1,0:T(8,128)S(1)}, f32[256,128]{1,0:T(8,128)S(1)}, u32[]{:S(2)}, u32[]{:S(2)}) collective-permute-start(f32[256,128]{1,0:T(8,128)S(1)} %get-tuple-element.67.mine), channel_id=1, source_target_pairs={{0,8},{4,12},{8,0},{12,4},{16,24},{20,28},{24,16},{28,20},{32,40},... | collective-permute-start | bytes 393224 | tf_op jit(solution)/shard_map/ppermute | solution.py:302
  44.9 13.5 %collective-permute-start.20 = (f32[256,128]{1,0:T(8,128)S(1)}, f32[256,128]{1,0:T(8,128)S(1)}, u32[]{:S(2)}, u32[]{:S(2)}) collective-permute-start(f32[256,128]{1,0:T(8,128)S(1)} %shard_map.72.mine), channel_id=1, source_target_pairs={{0,16},{4,20},{8,24},{12,28},{16,0},{20,4},{24,8},{28,12},{32,48},... | collective-permute-start | bytes 393224 | tf_op jit(solution)/shard_map/ppermute | solution.py:302
  48.6 45.8 %collective-permute-start.10 = (f32[256,256]{1,0:T(8,128)S(1)}, f32[256,256]{1,0:T(8,128)S(1)}, u32[]{:S(2)}, u32[]{:S(2)}) collective-permute-start(f32[256,256]{1,0:T(8,128)S(1)} %shard_map.65.mine), channel_id=1, source_target_pairs={{0,16},{4,20},{8,24},{12,28},{16,0},{20,4},{24,8},{28,12},{32,48},... | collective-permute-start | bytes 786440 | tf_op jit(solution)/shard_map/ppermute | solution.py:302
  49.1 46.4 %collective-permute-start.7 = (f32[256,256]{1,0:T(8,128)S(1)}, f32[256,256]{1,0:T(8,128)S(1)}, u32[]{:S(2)}, u32[]{:S(2)}) collective-permute-start(f32[256,256]{1,0:T(8,128)S(1)} %shard_map.61.mine), channel_id=1, source_target_pairs={{0,16},{4,20},{8,24},{12,28},{16,0},{20,4},{24,8},{28,12},{32,48},... | collective-permute-start | bytes 786440 | tf_op jit(solution)/shard_map/ppermute | solution.py:302
  54.5 34.8 %collective-permute-start.18 = (f32[256,128]{1,0:T(8,128)S(1)}, f32[256,128]{1,0:T(8,128)S(1)}, u32[]{:S(2)}, u32[]{:S(2)}) collective-permute-start(f32[256,128]{1,0:T(8,128)S(1)} %shard_map.71.mine), channel_id=1, source_target_pairs={{0,16},{4,20},{8,24},{12,28},{16,0},{20,4},{24,8},{28,12},{32,48},... | collective-permute-start | bytes 393224 | tf_op jit(solution)/shard_map/ppermute | solution.py:302
  55.5 36.5 %collective-permute-start.15 = (f32[256,128]{1,0:T(8,128)S(1)}, f32[256,128]{1,0:T(8,128)S(1)}, u32[]{:S(2)}, u32[]{:S(2)}) collective-permute-start(f32[256,128]{1,0:T(8,128)S(1)} %shard_map.69.mine), channel_id=1, source_target_pairs={{0,16},{4,20},{8,24},{12,28},{16,0},{20,4},{24,8},{28,12},{32,48},... | collective-permute-start | bytes 393224 | tf_op jit(solution)/shard_map/ppermute | solution.py:302
  58.3 35.0 %collective-permute-start.13 = (f32[256,128]{1,0:T(8,128)S(1)}, f32[256,128]{1,0:T(8,128)S(1)}, u32[]{:S(2)}, u32[]{:S(2)}) collective-permute-start(f32[256,128]{1,0:T(8,128)S(1)} %shard_map.68.mine), channel_id=1, source_target_pairs={{0,16},{4,20},{8,24},{12,28},{16,0},{20,4},{24,8},{28,12},{32,48},... | collective-permute-start | bytes 393224 | tf_op jit(solution)/shard_map/ppermute | solution.py:302

commit v3 on v1

--- a/solution.py
+++ b/solution.py
@@ -73,13 +73,19 @@
     return copies
 
 
+def halves_kernel(panel, first, second, sems):
+    cut = first.shape[0]
+    for copy in start_all(((panel.at[:cut], first), (panel.at[cut:], second)), sems):
+        copy.wait()
+
+
 def prepare_kernel(place, panel_t, tree_v, tree_t, trailing, th, tl, *args):
     mixes, (block, tri, vee, tee, sems) = args[:-5], args[-5:]
     ahead = len(mixes) // 2
     pairs = [(panel_t, tri)]
     for level in range(ahead):
         pairs += [(tree_v.at[level], vee.at[level]), (tree_t.at[level], tee.at[level])]
-    copies = start_all(pairs + [(trailing, block)], sems)
+    copies = start_all(pairs + [(trailing.at[:, : block.shape[1]], block)], sems)
     copies[0].wait()
     th[...], tl[...] = split(triangle_factor(tri[...]).T)
     for level in range(ahead):
@@ -105,15 +111,15 @@
     return split(rows), split(rows.T)
 
 
-def early_kernel(place, own, left_a, left_b, right_a, right_b, block, partial, yh, yl, fh, fl):
+def early_kernel(place, own_a, own_b, left_a, left_b, right_a, right_b, block, partial, yh, yl, fh, fl):
     col = place[1]
-    size = own.shape[0]
+    size = own_a.shape[0] + own_b.shape[0]
     count = block.shape[0] // size
     width = partial.shape[1]
     total = None
-    for shift, parts in ((0, (own,)), (count - 1, (left_a, left_b)), (1, (right_a, right_b))):
+    for shift, parts in ((0, (own_a, own_b)), (count - 1, (left_a, left_b)), (1, (right_a, right_b))):
         start = pl.multiple_of(lax.rem(col + shift, count) * size, size)
-        rows = parts[0][...] if len(parts) == 1 else jnp.concatenate([p[...] for p in parts], axis=0)
+        rows = jnp.concatenate([p[...] for p in parts], axis=0)
         here = pl.ds(start, size)
         straight, flipped = both_ways(rows, start)
         yh[here, :], yl[here, :] = straight
@@ -131,7 +137,7 @@
 
 
 def first_kernel(place, partial, opp_a, opp_b, block, th, tl, yh, yl, top, proj, gh, gl, oh, ol, ph, plow):
-    size = 2 * opp_a.shape[0]
+    size = opp_a.shape[0] + opp_b.shape[0]
     width = partial.shape[1]
     start = opposite_rows(place[1], size, block.shape[0] // size)
     rows = jnp.concatenate([opp_a[...], opp_b[...]], axis=0)
@@ -236,13 +242,21 @@
     size, width = panel_y.shape
     rows, columns = trailing.shape
     levels = tree_v.shape[0]
-    half = size // 2
+    cut = size * 9 // 16
     count = lax.axis_size("col")
     place = jnp.stack([lax.axis_index("row"), lax.axis_index("col")]).astype(jnp.int32)
     onward = [(c, (c + 1) % count) for c in range(count)]
     backward = [(c, (c - 1) % count) for c in range(count)]
 
-    own_a, own_b = panel_y[:half], panel_y[half:]
+    own_a, own_b = call(
+        halves_kernel,
+        out_shape=[shaped((cut, width)), shaped((size - cut, width))],
+        in_specs=[HBM],
+        out_specs=[VMEM] * 2,
+        scratch_shapes=[pltpu.SemaphoreType.DMA((2,))],
+        mib=4,
+        cost=(0, 1 << 19),
+    )(fixed(panel_y))
     left_a = lax.ppermute(own_a, "col", onward)
     right_b = lax.ppermute(own_b, "col", backward)
     left_b = lax.ppermute(own_b, "col", onward)
@@ -255,13 +269,12 @@
     tall = shaped((rows, width), BF16)
     wide = shaped((width, rows), BF16)
     cube = 2 * 3 * width**3
-    trailing = fixed(trailing)
     panel_t, tree_v, tree_t = fixed(panel_t), fixed(tree_v), fixed(tree_t)
     units, chunks = layout()
     ahead = levels - 1
     th, tl, *mixes, block = call(
         prepare_kernel,
-        out_shape=[square, square] + [mix] * (2 * ahead) + [shaped((rows, columns))],
+        out_shape=[square, square] + [mix] * (2 * ahead) + [shaped((rows, units[0][1]))],
         in_specs=[SMEM] + [HBM] * 4,
         out_specs=[VMEM] * (3 + 2 * ahead),
         scratch_shapes=[pltpu.VMEM((width, width), F32)]
@@ -269,17 +282,17 @@
         + [pltpu.SemaphoreType.DMA((2 * ahead + 2,))],
         mib=16,
         cost=(5 * cube, 5 << 20),
-    )(place, panel_t, tree_v, tree_t, trailing)
+    )(place, panel_t, tree_v, tree_t, fixed(trailing))
 
     w = units[0][1]
     partial, yh, yl, fh, fl = call(
         early_kernel,
         out_shape=[shaped((width, w)), tall, tall, wide, wide],
-        in_specs=[SMEM] + [VMEM] * 6,
+        in_specs=[SMEM] + [VMEM] * 7,
         out_specs=[VMEM] * 5,
         mib=16,
         cost=(2 * cube, 4 << 20),
-    )(place, panel_y, left_a, left_b, right_a, right_b, block)
+    )(place, own_a, own_b, left_a, left_b, right_a, right_b, block)
 
     top, proj, gh, gl, *opposite = call(
         first_kernel,
@@ -324,7 +337,7 @@
                 out_specs=[VMEM] * 2,
                 mib=16,
                 cost=(5 * cube * w // width, 2 << 20),
-            )(block, fh, fl, gh, gl)
+            )(trailing, fh, fl, gh, gl)
         projs.append(proj)
         tops += combine(0, top, UNITS[u])
 
@@ -357,7 +370,7 @@
                 input_output_aliases={5 + len(group): 0} if out else {},
                 mib=16,
                 cost=(10 * cube, 4 << 20),
-            )(block, yh, yl, th, tl, *[projs[u] for u in group], *out),
+            )(trailing, yh, yl, th, tl, *[projs[u] for u in group], *out),
         )
     out = out[0]
 
@@ -383,6 +396,4 @@
         P(None, "row", None),
         P(None, "row", None),
     )
-    return jax.shard_map(
-        update, mesh=mesh, in_specs=placed, out_specs=P("row", "col"), check_vma=False
-    )
+    return jax.shard_map(update, mesh=mesh, in_specs=placed, out_specs=P("row", "col"), check_vma=False)

time: 94.6 us -> 96.9 us (1.024)
  waiting for transfers between devices: 37.3 us -> 41.6 us
  starting transfers between devices: 29.7 us -> 28.2 us
  local copies, waits for them, and re-layouts: 1.03 us -> 0.01 us
    ppermute x1, waiting for transfers between devices: 0.01 us -> 2.19 us  [update(): right_b = lax.ppermute(own_b, 'col', backward)]
    ppermute x1, waiting for transfers between devices: 0.01 us -> 2.17 us  [update(): opp_a = lax.ppermute(left_a, 'col', onward)]
    ppermute x1, starting transfers between devices: 2.96 us -> 1.55 us  [update(): right_a = lax.ppermute(own_a, 'col', backward)]
    ppermute x1, starting transfers between devices: 1.28 us -> 0.01 us  [update(): opp_a = lax.ppermute(left_a, 'col', onward)]
    ppermute x1, starting transfers between devices: 1.95 us -> 3.01 us  [update(): opp_b = lax.ppermute(right_b, 'col', backward)]
    slice x1 -> x0, local copies, waits for them, and re-layouts: 1.03 us -> none  [update(): own_a, own_b = (panel_y[:half], panel_y[half:])]
    pallas_call x0 -> x1, Pallas kernels: none -> 0.99 us  [update(): call(halves_kernel, out_shape=[shaped((cut, width)), shaped((size - cut,...]
  transfers between devices with their start and end apart: 22 -> 22, of which waited for: 5 -> 6; matrix products, arithmetic and copies ran while one was open for 0% -> 0% of each run, Pallas kernels for 23% -> 22%
where the time goes in v3:
time: 96.9 us; the launch traced here: 96.8 us
  waiting for transfers between devices  41.6 us (43%)
  starting transfers between devices  28.2 us (29%)
  Pallas kernels  26.5 us (27%)
    ppermute x16, waiting for transfers between devices, swap(): return lax.ppermute(values, 'row', route)  37.2 us
    ppermute x16, starting transfers between devices, swap(): return lax.ppermute(values, 'row', route)  19.9 us
    pallas_call x6, Pallas kernels, update(): call(functools.partial(final_kernel, first), out_shape=shaped((rows, colu...  6.32 us
    pallas_call x2, Pallas kernels, update(): call(functools.partial(rest_kernel, first), out_shape=shaped((rows, colum...  3.93 us
    pallas_call x10, Pallas kernels, combine(): call(level_kernel, out_shape=[shaped((width, w)) for w in widths], in_spe...  3.77 us
    pallas_call x3, Pallas kernels, update(): call(functools.partial(next_kernel, slice(first, first + w)), out_shape=[...  3.01 us
    ppermute x1, starting transfers between devices, update(): opp_b = lax.ppermute(right_b, 'col', backward)  3.01 us
    pallas_call x1, Pallas kernels, update(): call(prepare_kernel, out_shape=[square, square] + [mix] * (2 * ahead) + [...  2.79 us
  transfers between devices with their start and end apart: 22, of which 6 were waited for; matrix products, arithmetic and copies ran while one was open for 0% of the time, Pallas kernels for 22%

profile of v3, /device:TPU:8, one launch (start us, length us, event | category | flops | bytes accessed | tf_op | source)
XLA Modules:
  0.0 96.8 jit_solution(13907127372908882226)
XLA Ops:
  0.0 1.0 %shard_map.55 = (f32[144,256]{1,0:T(8,128)S(1)}, f32[112,256]{1,0:T(8,128)S(1)}) custom-call(f32[256,256]{1,0:T(8,128)} %panel.1), custom_call_target="tpu_custom_call" | custom-call | bytes 524288 | tf_op jit(solution)/shard_map/pallas_call | solution.py:251
  1.0 1.6 %collective-permute-start = (f32[144,256]{1,0:T(8,128)S(1)}, f32[144,256]{1,0:T(8,128)S(1)}, u32[]{:S(2)}, u32[]{:S(2)}) collective-permute-start(f32[144,256]{1,0:T(8,128)S(1)} %get-tuple-element.43.own_a), channel_id=1, source_target_pairs={{0,1},{1,2},{2,3},{3,0},{4,5},{5,6},{6,7},{7,4},{8,9},{9,10},{10,1... | collective-permute-start | bytes 442376 | tf_op jit(solution)/shard_map/ppermute | solution.py:260
  2.6 1.7 %collective-permute-start.3 = (f32[112,256]{1,0:T(8,128)S(1)}, f32[112,256]{1,0:T(8,128)S(1)}, u32[]{:S(2)}, u32[]{:S(2)}) collective-permute-start(f32[112,256]{1,0:T(8,128)S(1)} %get-tuple-element.44.own_b), channel_id=1, source_target_pairs={{0,3},{1,0},{2,1},{3,2},{4,7},{5,4},{6,5},{7,6},{8,11},{9,8},{10,9... | collective-permute-start | bytes 344072 | tf_op jit(solution)/shard_map/ppermute | solution.py:261
  4.3 1.5 %collective-permute-start.2 = (f32[144,256]{1,0:T(8,128)S(1)}, f32[144,256]{1,0:T(8,128)S(1)}, u32[]{:S(2)}, u32[]{:S(2)}) collective-permute-start(f32[144,256]{1,0:T(8,128)S(1)} %get-tuple-element.43.own_a), channel_id=1, source_target_pairs={{0,3},{1,0},{2,1},{3,2},{4,7},{5,4},{6,5},{7,6},{8,11},{9,8},{10,9... | collective-permute-start | bytes 442376 | tf_op jit(solution)/shard_map/ppermute | solution.py:263
  6.3 2.2 %collective-permute-done.3.right_b = f32[112,256]{1,0:T(8,128)S(1)} collective-permute-done((f32[112,256]{1,0:T(8,128)S(1)}, f32[112,256]{1,0:T(8,128)S(1)}, u32[]{:S(2)}, u32[]{:S(2)}) %collective-permute-start.3) | collective-permute-done | bytes 114720 | tf_op jit(solution)/shard_map/ppermute | solution.py:261
  8.5 3.0 %collective-permute-start.5 = (f32[112,256]{1,0:T(8,128)S(1)}, f32[112,256]{1,0:T(8,128)S(1)}, u32[]{:S(2)}, u32[]{:S(2)}) collective-permute-start(f32[112,256]{1,0:T(8,128)S(1)} %collective-permute-done.3.right_b), channel_id=1, source_target_pairs={{0,3},{1,0},{2,1},{3,2},{4,7},{5,4},{6,5},{7,6},{8,11},{9,8},{10,9... | collective-permute-start | bytes 344072 | tf_op jit(solution)/shard_map/ppermute | solution.py:265
  11.6 2.8 %shard_map.56 = (bf16[256,256]{1,0:T(8,128)(2,1)S(1)}, bf16[256,256]{1,0:T(8,128)(2,1)S(1)}, bf16[256,512]{1,0:T(8,128)(2,1)S(1)}, bf16[256,512]{1,0:T(8,128)(2,...) custom-call(s32[2]{0:T(128)S(1)} %pad_add_fusion.place, ...), custom_call_target="tpu_custom_call" | custom-call | flops 503316480 | bytes 5242880 | tf_op jit(solution)/shard_map/pallas_call | solution.py:275
  14.4 1.3 %shard_map.57 = (f32[256,256]{1,0:T(8,128)S(1)}, bf16[1024,256]{1,0:T(8,128)(2,1)S(1)}, bf16[1024,256]{1,0:T(8,128)(2,1)S(1)}, bf16[256,1024]{1,0:T(8,128)(2,1)S(1)}, bf16[256,1024]{1,0:T(8,128)(2,1)S(1)}) custom-call(s32[2]{0:T(128)S(1)} %pad_add_fusion.place, f32[144,256]{1,0:T(8,128)S(1)} %get-tuple-element.43.own_a, ...), custom_call_target="tpu_custom_call" | custom-call | flops 201326592 | bytes 4194304 | tf_op jit(solution)/shard_map/pallas_call | solution.py:288
  15.7 2.2 %collective-permute-done.4.opp_a = f32[144,256]{1,0:T(8,128)S(1)} collective-permute-done((f32[144,256]{1,0:T(8,128)S(1)}, f32[144,256]{1,0:T(8,128)S(1)}, u32[]{:S(2)}, u32[]{:S(2)}) %collective-permute-start.4) | collective-permute-done | bytes 147488 | tf_op jit(solution)/shard_map/ppermute | solution.py:264
  17.9 1.4 %shard_map.58 = (f32[256,256]{1,0:T(8,128)S(1)}, f32[256,256]{1,0:T(8,128)S(1)}, bf16[256,256]{1,0:T(8,128)(2,1)S(1)}, bf16[256,256]{1,0:T(8,128)(2,1)S(1)}, bf1...) custom-call(s32[2]{0:T(128)S(1)} %pad_add_fusion.place, ...), custom_call_target="tpu_custom_call" | custom-call | flops 201326592 | bytes 2097152 | tf_op jit(solution)/shard_map/pallas_call | solution.py:297
  20.0 1.0 %shard_map.64 = (f32[256,256]{1,0:T(8,128)S(1)}, f32[256,256]{1,0:T(8,128)S(1)}) custom-call(f32[1024,1024]{1,0:T(8,128)S(1)} %copy-done, bf16[256,1024]{1,0:T(8,128)(2,1)S(1)} %get-tuple-element.57.fh, bf16[256,1024]{1,0:T(8,128)(2,1)S(1)} %get-tuple-element.58.fl, bf16[256,256]{1,0:T(8,128)(2,1)S(1)} %get-tuple-element.59.gh, ...), custom_call_target="tpu_custom_call" | custom-call | flops 503316480 | bytes 2097152 | tf_op jit(solution)/shard_map/pallas_call | solution.py:333
  21.1 1.0 %shard_map.60 = (f32[256,256]{1,0:T(8,128)S(1)}, f32[256,256]{1,0:T(8,128)S(1)}) custom-call(f32[1024,1024]{1,0:T(8,128)S(1)} %copy-done, bf16[256,1024]{1,0:T(8,128)(2,1)S(1)} %get-tuple-element.57.fh, bf16[256,1024]{1,0:T(8,128)(2,1)S(1)} %get-tuple-element.58.fl, bf16[256,256]{1,0:T(8,128)(2,1)S(1)} %get-tuple-element.59.gh, ...), custom_call_target="tpu_custom_call" | custom-call | flops 503316480 | bytes 2097152 | tf_op jit(solution)/shard_map/pallas_call | solution.py:333
  22.8 1.0 %shard_map.67 = (f32[256,256]{1,0:T(8,128)S(1)}, f32[256,256]{1,0:T(8,128)S(1)}) custom-call(f32[1024,1024]{1,0:T(8,128)S(1)} %copy-done, bf16[256,1024]{1,0:T(8,128)(2,1)S(1)} %get-tuple-element.57.fh, bf16[256,1024]{1,0:T(8,128)(2,1)S(1)} %get-tuple-element.58.fl, bf16[256,256]{1,0:T(8,128)(2,1)S(1)} %get-tuple-element.59.gh, ...), custom_call_target="tpu_custom_call" | custom-call | flops 503316480 | bytes 2097152 | tf_op jit(solution)/shard_map/pallas_call | solution.py:333
  24.9 2.0 %collective-permute-start.10 = (f32[256,256]{1,0:T(8,128)S(1)}, f32[256,256]{1,0:T(8,128)S(1)}, u32[]{:S(2)}, u32[]{:S(2)}) collective-permute-start(f32[256,256]{1,0:T(8,128)S(1)} %shard_map.65.mine), channel_id=1, source_target_pairs={{0,8},{4,12},{8,0},{12,4},{16,24},{20,28},{24,16},{28,20},{32,40},... | collective-permute-start | bytes 786440 | tf_op jit(solution)/shard_map/ppermute | solution.py:317
  27.9 2.0 %collective-permute-start.20 = (f32[256,128]{1,0:T(8,128)S(1)}, f32[256,128]{1,0:T(8,128)S(1)}, u32[]{:S(2)}, u32[]{:S(2)}) collective-permute-start(f32[256,128]{1,0:T(8,128)S(1)} %get-tuple-element.75.mine), channel_id=1, source_target_pairs={{0,8},{4,12},{8,0},{12,4},{16,24},{20,28},{24,16},{28,20},{32,40},... | collective-permute-start | bytes 393224 | tf_op jit(solution)/shard_map/ppermute | solution.py:317
  30.4 2.0 %collective-permute-start.15 = (f32[256,128]{1,0:T(8,128)S(1)}, f32[256,128]{1,0:T(8,128)S(1)}, u32[]{:S(2)}, u32[]{:S(2)}) collective-permute-start(f32[256,128]{1,0:T(8,128)S(1)} %get-tuple-element.72.mine), channel_id=1, source_target_pairs={{0,8},{4,12},{8,0},{12,4},{16,24},{20,28},{24,16},{28,20},{32,40},... | collective-permute-start | bytes 393224 | tf_op jit(solution)/shard_map/ppermute | solution.py:317
  32.4 10.2 %collective-permute-done.20.theirs = f32[256,128]{1,0:T(8,128)S(1)} collective-permute-done((f32[256,128]{1,0:T(8,128)S(1)}, f32[256,128]{1,0:T(8,128)S(1)}, u32[]{:S(2)}, u32[]{:S(2)}) %collective-permute-start.20) | collective-permute-done | bytes 131104 | tf_op jit(solution)/shard_map/ppermute | solution.py:317
  42.6 1.9 %collective-permute-start.13 = (f32[256,128]{1,0:T(8,128)S(1)}, f32[256,128]{1,0:T(8,128)S(1)}, u32[]{:S(2)}, u32[]{:S(2)}) collective-permute-start(f32[256,128]{1,0:T(8,128)S(1)} %get-tuple-element.71.mine), channel_id=1, source_target_pairs={{0,8},{4,12},{8,0},{12,4},{16,24},{20,28},{24,16},{28,20},{32,40},... | collective-permute-start | bytes 393224 | tf_op jit(solution)/shard_map/ppermute | solution.py:317
  44.9 3.3 %collective-permute-start.21 = (f32[256,128]{1,0:T(8,128)S(1)}, f32[256,128]{1,0:T(8,128)S(1)}, u32[]{:S(2)}, u32[]{:S(2)}) collective-permute-start(f32[256,128]{1,0:T(8,128)S(1)} %shard_map.73.mine), channel_id=1, source_target_pairs={{0,16},{4,20},{8,24},{12,28},{16,0},{20,4},{24,8},{28,12},{32,48},... | collective-permute-start | bytes 393224 | tf_op jit(solution)/shard_map/ppermute | solution.py:317
  49.1 3.0 %collective-permute-start.8 = (f32[256,256]{1,0:T(8,128)S(1)}, f32[256,256]{1,0:T(8,128)S(1)}, u32[]{:S(2)}, u32[]{:S(2)}) collective-permute-start(f32[256,256]{1,0:T(8,128)S(1)} %shard_map.62.mine), channel_id=1, source_target_pairs={{0,16},{4,20},{8,24},{12,28},{16,0},{20,4},{24,8},{28,12},{32,48},... | collective-permute-start | bytes 786440 | tf_op jit(solution)/shard_map/ppermute | solution.py:317
  52.1 2.0 %shard_map.74.args_2_ = f32[1024,1024]{1,0:T(8,128)} custom-call(f32[1024,1024]{1,0:T(8,128)S(1)} %copy-done, bf16[1024,256]{1,0:T(8,128)(2,1)S(1)} %get-tuple-element.76.yh, bf16[1024,256]{1,0:T(8,128)(2,1)S(1)} %get-tuple-element.77.yl, bf16[256,256]{1,0:T(8,128)(2,1)S(1)} %get-tuple-element.51.th, bf16[256,256]{1,0:T(8,128)(2,1)S(1)} %get-tuple-element.52.tl, ...), custom_call_target="tpu_custom_call" | custom-call | flops 1006632960 | bytes 4194304 | tf_op jit(solution)/shard_map/pallas_call | solution.py:364
  55.5 2.5 %collective-permute-start.16 = (f32[256,128]{1,0:T(8,128)S(1)}, f32[256,128]{1,0:T(8,128)S(1)}, u32[]{:S(2)}, u32[]{:S(2)}) collective-permute-start(f32[256,128]{1,0:T(8,128)S(1)} %shard_map.70.mine), channel_id=1, source_target_pairs={{0,16},{4,20},{8,24},{12,28},{16,0},{20,4},{24,8},{28,12},{32,48},... | collective-permute-start | bytes 393224 | tf_op jit(solution)/shard_map/ppermute | solution.py:317
  58.9 2.3 %shard_map.63 = (bf16[256,512]{1,0:T(8,128)(2,1)S(1)}, bf16[256,512]{1,0:T(8,128)(2,1)S(1)}) custom-call(s32[2]{0:T(128)S(1)} %pad_add_fusion.place, f32[3,256,256]{2,1,0:T(8,128)} %tree_v.3, f32[3,256,256]{2,1,0:T(8,128)} %tree_t.3, f32[256,256]{1,0:T(8,128)S(1)} %get-tuple-element.66.after.args_1_), custom_call_target="tpu_custom_call" | custom-call | flops 201326592 | bytes 1048576 | tf_op jit(solution)/shard_map/pallas_call | solution.py:348
  61.3 2.0 %shard_map.75.whole = f32[1024,1024]{1,0:T(8,128)} custom-call(f32[1024,1024]{1,0:T(8,128)S(1)} %copy-done, bf16[1024,256]{1,0:T(8,128)(2,1)S(1)} %get-tuple-element.76.yh, bf16[1024,256]{1,0:T(8,128)(2,1)S(1)} %get-tuple-element.77.yl, bf16[256,256]{1,0:T(8,128)(2,1)S(1)} %get-tuple-element.51.th, ...), custom_call_target="tpu_custom_call", output_to_operand_aliasing={{}: (7, {})} | custom-call | flops 1006632960 | bytes 4194304 | tf_op jit(solution)/shard_map/pallas_call | solution.py:364
  63.3 1.0 %shard_map.76.whole = f32[1024,1024]{1,0:T(8,128)} custom-call(f32[256,128]{1,0:T(8,128)S(1)} %shard_map.73.mine, f32[256,128]{1,0:T(8,128)S(1)} %collective-permute-done.21.theirs, bf16[256,512]{1,0:T(8,128)(2,1)S(1)} %get-tuple-element.67.high, bf16[256,512]{1,0:T(8,128)(2,1)S(1)} %get-tuple-element.68.low, ...), custom_call_target="tpu_custom_call", output_to_operand_aliasing={{}: (4, {})} | custom-call | flops 100663296 | bytes 1048576 | tf_op jit(solution)/shard_map/pallas_call | solution.py:378
  64.3 25.0 %collective-permute-done.19.theirs = f32[256,128]{1,0:T(8,128)S(1)} collective-permute-done((f32[256,128]{1,0:T(8,128)S(1)}, f32[256,128]{1,0:T(8,128)S(1)}, u32[]{:S(2)}, u32[]{:S(2)}) %collective-permute-start.19) | collective-permute-done | bytes 131104 | tf_op jit(solution)/shard_map/ppermute | solution.py:317
  89.3 1.0 %shard_map.77.whole = f32[1024,1024]{1,0:T(8,128)} custom-call(f32[256,128]{1,0:T(8,128)S(1)} %shard_map.72.mine, f32[256,128]{1,0:T(8,128)S(1)} %collective-permute-done.19.theirs, bf16[256,512]{1,0:T(8,128)(2,1)S(1)} %get-tuple-element.67.high, bf16[256,512]{1,0:T(8,128)(2,1)S(1)} %get-tuple-element.68.low, ...), custom_call_target="tpu_custom_call", output_to_operand_aliasing={{}: (4, {})} | custom-call | flops 100663296 | bytes 1048576 | tf_op jit(solution)/shard_map/pallas_call | solution.py:378
  90.3 1.6 %collective-permute-done.16.theirs = f32[256,128]{1,0:T(8,128)S(1)} collective-permute-done((f32[256,128]{1,0:T(8,128)S(1)}, f32[256,128]{1,0:T(8,128)S(1)}, u32[]{:S(2)}, u32[]{:S(2)}) %collective-permute-start.16) | collective-permute-done | bytes 131104 | tf_op jit(solution)/shard_map/ppermute | solution.py:317
  92.0 1.0 %shard_map.78.whole = f32[1024,1024]{1,0:T(8,128)} custom-call(f32[256,128]{1,0:T(8,128)S(1)} %shard_map.70.mine, f32[256,128]{1,0:T(8,128)S(1)} %collective-permute-done.16.theirs, bf16[256,512]{1,0:T(8,128)(2,1)S(1)} %get-tuple-element.67.high, bf16[256,512]{1,0:T(8,128)(2,1)S(1)} %get-tuple-element.68.low, ...), custom_call_target="tpu_custom_call", output_to_operand_aliasing={{}: (4, {})} | custom-call | flops 100663296 | bytes 1048576 | tf_op jit(solution)/shard_map/pallas_call | solution.py:378
  93.4 1.0 %shard_map.79.whole = f32[1024,1024]{1,0:T(8,128)} custom-call(f32[256,128]{1,0:T(8,128)S(1)} %shard_map.69.mine, f32[256,128]{1,0:T(8,128)S(1)} %collective-permute-done.14.theirs, bf16[256,512]{1,0:T(8,128)(2,1)S(1)} %get-tuple-element.67.high, bf16[256,512]{1,0:T(8,128)(2,1)S(1)} %get-tuple-element.68.low, ...), custom_call_target="tpu_custom_call", output_to_operand_aliasing={{}: (4, {})} | custom-call | flops 100663296 | bytes 1048576 | tf_op jit(solution)/shard_map/pallas_call | solution.py:378
  94.4 1.1 %shard_map.80.whole = f32[1024,1024]{1,0:T(8,128)} custom-call(f32[256,256]{1,0:T(8,128)S(1)} %shard_map.66.mine, f32[256,256]{1,0:T(8,128)S(1)} %collective-permute-done.11.theirs, bf16[256,512]{1,0:T(8,128)(2,1)S(1)} %get-tuple-element.67.high, bf16[256,512]{1,0:T(8,128)(2,1)S(1)} %get-tuple-element.68.low, ...), custom_call_target="tpu_custom_call", output_to_operand_aliasing={{}: (4, {})} | custom-call | flops 201326592 | bytes 1048576 | tf_op jit(solution)/shard_map/pallas_call | solution.py:378
  95.5 1.1 %shard_map.81 = f32[1024,1024]{1,0:T(8,128)} custom-call(f32[256,256]{1,0:T(8,128)S(1)} %shard_map.62.mine, f32[256,256]{1,0:T(8,128)S(1)} %collective-permute-done.8.theirs, bf16[256,512]{1,0:T(8,128)(2,1)S(1)} %get-tuple-element.67.high, bf16[256,512]{1,0:T(8,128)(2,1)S(1)} %get-tuple-element.68.low, ...), custom_call_target="tpu_custom_call", output_to_operand_aliasing={{}: (4, {})} | custom-call | flops 201326592 | bytes 1048576 | tf_op jit(solution)/shard_map/pallas_call | solution.py:378
  (42 shorter events, 8.5 us)
Async XLA Ops:
  1.0 10.5 %collective-permute-start = (f32[144,256]{1,0:T(8,128)S(1)}, f32[144,256]{1,0:T(8,128)S(1)}, u32[]{:S(2)}, u32[]{:S(2)}) collective-permute-start(f32[144,256]{1,0:T(8,128)S(1)} %get-tuple-element.43.own_a), channel_id=1, source_target_pairs={{0,1},{1,2},{2,3},{3,0},{4,5},{5,6},{6,7},{7,4},{8,9},{9,10},{10,1... | collective-permute-start | bytes 442376 | tf_op jit(solution)/shard_map/ppermute | solution.py:260
  2.6 6.0 %collective-permute-start.3 = (f32[112,256]{1,0:T(8,128)S(1)}, f32[112,256]{1,0:T(8,128)S(1)}, u32[]{:S(2)}, u32[]{:S(2)}) collective-permute-start(f32[112,256]{1,0:T(8,128)S(1)} %get-tuple-element.44.own_b), channel_id=1, source_target_pairs={{0,3},{1,0},{2,1},{3,2},{4,7},{5,4},{6,5},{7,6},{8,11},{9,8},{10,9... | collective-permute-start | bytes 344072 | tf_op jit(solution)/shard_map/ppermute | solution.py:261
  4.3 10.1 %collective-permute-start.2 = (f32[144,256]{1,0:T(8,128)S(1)}, f32[144,256]{1,0:T(8,128)S(1)}, u32[]{:S(2)}, u32[]{:S(2)}) collective-permute-start(f32[144,256]{1,0:T(8,128)S(1)} %get-tuple-element.43.own_a), channel_id=1, source_target_pairs={{0,3},{1,0},{2,1},{3,2},{4,7},{5,4},{6,5},{7,6},{8,11},{9,8},{10,9... | collective-permute-start | bytes 442376 | tf_op jit(solution)/shard_map/ppermute | solution.py:263
  5.9 8.6 %collective-permute-start.1 = (f32[112,256]{1,0:T(8,128)S(1)}, f32[112,256]{1,0:T(8,128)S(1)}, u32[]{:S(2)}, u32[]{:S(2)}) collective-permute-start(f32[112,256]{1,0:T(8,128)S(1)} %get-tuple-element.44.own_b), channel_id=1, source_target_pairs={{0,1},{1,2},{2,3},{3,0},{4,5},{5,6},{6,7},{7,4},{8,9},{9,10},{10,1... | collective-permute-start | bytes 344072 | tf_op jit(solution)/shard_map/ppermute | solution.py:262
  8.5 7.2 %collective-permute-start.5 = (f32[112,256]{1,0:T(8,128)S(1)}, f32[112,256]{1,0:T(8,128)S(1)}, u32[]{:S(2)}, u32[]{:S(2)}) collective-permute-start(f32[112,256]{1,0:T(8,128)S(1)} %collective-permute-done.3.right_b), channel_id=1, source_target_pairs={{0,3},{1,0},{2,1},{3,2},{4,7},{5,4},{6,5},{7,6},{8,11},{9,8},{10,9... | collective-permute-start | bytes 344072 | tf_op jit(solution)/shard_map/ppermute | solution.py:265
  11.5 6.4 %collective-permute-start.4 = (f32[144,256]{1,0:T(8,128)S(1)}, f32[144,256]{1,0:T(8,128)S(1)}, u32[]{:S(2)}, u32[]{:S(2)}) collective-permute-start(f32[144,256]{1,0:T(8,128)S(1)} %collective-permute-done.left_a), channel_id=1, source_target_pairs={{0,1},{1,2},{2,3},{3,0},{4,5},{5,6},{6,7},{7,4},{8,9},{9,10},{10,1... | collective-permute-start | bytes 442376 | tf_op jit(solution)/shard_map/ppermute | solution.py:264
  14.4 5.6 %copy-start = (f32[1024,1024]{1,0:T(8,128)S(1)}, f32[1024,1024]{1,0:T(8,128)}, u32[]{:S(2)}) copy-start(f32[1024,1024]{1,0:T(8,128)} %block.9) | copy-start | bytes 12582916
  21.0 3.5 %collective-permute-start.9 = (f32[256,256]{1,0:T(8,128)S(1)}, f32[256,256]{1,0:T(8,128)S(1)}, u32[]{:S(2)}, u32[]{:S(2)}) collective-permute-start(f32[256,256]{1,0:T(8,128)S(1)} %get-tuple-element.69.mine), channel_id=1, source_target_pairs={{0,4},{4,0},{8,12},{12,8},{16,20},{20,16},{24,28},{28,24},{32,36},... | collective-permute-start | bytes 786440 | tf_op jit(solution)/shard_map/ppermute | solution.py:317
  22.1 4.8 %collective-permute-start.6 = (f32[256,256]{1,0:T(8,128)S(1)}, f32[256,256]{1,0:T(8,128)S(1)}, u32[]{:S(2)}, u32[]{:S(2)}) collective-permute-start(f32[256,256]{1,0:T(8,128)S(1)} %get-tuple-element.61.mine), channel_id=1, source_target_pairs={{0,4},{4,0},{8,12},{12,8},{16,20},{20,16},{24,28},{28,24},{32,36},... | collective-permute-start | bytes 786440 | tf_op jit(solution)/shard_map/ppermute | solution.py:317
  22.7 4.8 %collective-permute-start.17 = (f32[256,256]{1,0:T(8,128)S(1)}, f32[256,256]{1,0:T(8,128)S(1)}, u32[]{:S(2)}, u32[]{:S(2)}) collective-permute-start(f32[256,256]{1,0:T(8,128)S(1)} %get-tuple-element.73.mine), channel_id=1, source_target_pairs={{0,4},{4,0},{8,12},{12,8},{16,20},{20,16},{24,28},{28,24},{32,36},... | collective-permute-start | bytes 786440 | tf_op jit(solution)/shard_map/ppermute | solution.py:317
  23.8 6.2 %collective-permute-start.12 = (f32[256,256]{1,0:T(8,128)S(1)}, f32[256,256]{1,0:T(8,128)S(1)}, u32[]{:S(2)}, u32[]{:S(2)}) collective-permute-start(f32[256,256]{1,0:T(8,128)S(1)} %get-tuple-element.70.mine), channel_id=1, source_target_pairs={{0,4},{4,0},{8,12},{12,8},{16,20},{20,16},{24,28},{28,24},{32,36},... | collective-permute-start | bytes 786440 | tf_op jit(solution)/shard_map/ppermute | solution.py:317
  24.9 20.0 %collective-permute-start.10 = (f32[256,256]{1,0:T(8,128)S(1)}, f32[256,256]{1,0:T(8,128)S(1)}, u32[]{:S(2)}, u32[]{:S(2)}) collective-permute-start(f32[256,256]{1,0:T(8,128)S(1)} %shard_map.65.mine), channel_id=1, source_target_pairs={{0,8},{4,12},{8,0},{12,4},{16,24},{20,28},{24,16},{28,20},{32,40},... | collective-permute-start | bytes 786440 | tf_op jit(solution)/shard_map/ppermute | solution.py:317
  27.3 21.3 %collective-permute-start.7 = (f32[256,256]{1,0:T(8,128)S(1)}, f32[256,256]{1,0:T(8,128)S(1)}, u32[]{:S(2)}, u32[]{:S(2)}) collective-permute-start(f32[256,256]{1,0:T(8,128)S(1)} %shard_map.61.mine), channel_id=1, source_target_pairs={{0,8},{4,12},{8,0},{12,4},{16,24},{20,28},{24,16},{28,20},{32,40},... | collective-permute-start | bytes 786440 | tf_op jit(solution)/shard_map/ppermute | solution.py:317
  27.9 14.7 %collective-permute-start.20 = (f32[256,128]{1,0:T(8,128)S(1)}, f32[256,128]{1,0:T(8,128)S(1)}, u32[]{:S(2)}, u32[]{:S(2)}) collective-permute-start(f32[256,128]{1,0:T(8,128)S(1)} %get-tuple-element.75.mine), channel_id=1, source_target_pairs={{0,8},{4,12},{8,0},{12,4},{16,24},{20,28},{24,16},{28,20},{32,40},... | collective-permute-start | bytes 393224 | tf_op jit(solution)/shard_map/ppermute | solution.py:317
  29.9 19.2 %collective-permute-start.18 = (f32[256,128]{1,0:T(8,128)S(1)}, f32[256,128]{1,0:T(8,128)S(1)}, u32[]{:S(2)}, u32[]{:S(2)}) collective-permute-start(f32[256,128]{1,0:T(8,128)S(1)} %get-tuple-element.74.mine), channel_id=1, source_target_pairs={{0,8},{4,12},{8,0},{12,4},{16,24},{20,28},{24,16},{28,20},{32,40},... | collective-permute-start | bytes 393224 | tf_op jit(solution)/shard_map/ppermute | solution.py:317
  30.4 24.1 %collective-permute-start.15 = (f32[256,128]{1,0:T(8,128)S(1)}, f32[256,128]{1,0:T(8,128)S(1)}, u32[]{:S(2)}, u32[]{:S(2)}) collective-permute-start(f32[256,128]{1,0:T(8,128)S(1)} %get-tuple-element.72.mine), channel_id=1, source_target_pairs={{0,8},{4,12},{8,0},{12,4},{16,24},{20,28},{24,16},{28,20},{32,40},... | collective-permute-start | bytes 393224 | tf_op jit(solution)/shard_map/ppermute | solution.py:317
  42.6 12.9 %collective-permute-start.13 = (f32[256,128]{1,0:T(8,128)S(1)}, f32[256,128]{1,0:T(8,128)S(1)}, u32[]{:S(2)}, u32[]{:S(2)}) collective-permute-start(f32[256,128]{1,0:T(8,128)S(1)} %get-tuple-element.71.mine), channel_id=1, source_target_pairs={{0,8},{4,12},{8,0},{12,4},{16,24},{20,28},{24,16},{28,20},{32,40},... | collective-permute-start | bytes 393224 | tf_op jit(solution)/shard_map/ppermute | solution.py:317
  44.9 13.4 %collective-permute-start.21 = (f32[256,128]{1,0:T(8,128)S(1)}, f32[256,128]{1,0:T(8,128)S(1)}, u32[]{:S(2)}, u32[]{:S(2)}) collective-permute-start(f32[256,128]{1,0:T(8,128)S(1)} %shard_map.73.mine), channel_id=1, source_target_pairs={{0,16},{4,20},{8,24},{12,28},{16,0},{20,4},{24,8},{28,12},{32,48},... | collective-permute-start | bytes 393224 | tf_op jit(solution)/shard_map/ppermute | solution.py:317
  48.6 45.8 %collective-permute-start.11 = (f32[256,256]{1,0:T(8,128)S(1)}, f32[256,256]{1,0:T(8,128)S(1)}, u32[]{:S(2)}, u32[]{:S(2)}) collective-permute-start(f32[256,256]{1,0:T(8,128)S(1)} %shard_map.66.mine), channel_id=1, source_target_pairs={{0,16},{4,20},{8,24},{12,28},{16,0},{20,4},{24,8},{28,12},{32,48},... | collective-permute-start | bytes 786440 | tf_op jit(solution)/shard_map/ppermute | solution.py:317
  49.1 46.4 %collective-permute-start.8 = (f32[256,256]{1,0:T(8,128)S(1)}, f32[256,256]{1,0:T(8,128)S(1)}, u32[]{:S(2)}, u32[]{:S(2)}) collective-permute-start(f32[256,256]{1,0:T(8,128)S(1)} %shard_map.62.mine), channel_id=1, source_target_pairs={{0,16},{4,20},{8,24},{12,28},{16,0},{20,4},{24,8},{28,12},{32,48},... | collective-permute-start | bytes 786440 | tf_op jit(solution)/shard_map/ppermute | solution.py:317
  54.5 34.8 %collective-permute-start.19 = (f32[256,128]{1,0:T(8,128)S(1)}, f32[256,128]{1,0:T(8,128)S(1)}, u32[]{:S(2)}, u32[]{:S(2)}) collective-permute-start(f32[256,128]{1,0:T(8,128)S(1)} %shard_map.72.mine), channel_id=1, source_target_pairs={{0,16},{4,20},{8,24},{12,28},{16,0},{20,4},{24,8},{28,12},{32,48},... | collective-permute-start | bytes 393224 | tf_op jit(solution)/shard_map/ppermute | solution.py:317
  55.5 36.5 %collective-permute-start.16 = (f32[256,128]{1,0:T(8,128)S(1)}, f32[256,128]{1,0:T(8,128)S(1)}, u32[]{:S(2)}, u32[]{:S(2)}) collective-permute-start(f32[256,128]{1,0:T(8,128)S(1)} %shard_map.70.mine), channel_id=1, source_target_pairs={{0,16},{4,20},{8,24},{12,28},{16,0},{20,4},{24,8},{28,12},{32,48},... | collective-permute-start | bytes 393224 | tf_op jit(solution)/shard_map/ppermute | solution.py:317
  58.3 35.0 %collective-permute-start.14 = (f32[256,128]{1,0:T(8,128)S(1)}, f32[256,128]{1,0:T(8,128)S(1)}, u32[]{:S(2)}, u32[]{:S(2)}) collective-permute-start(f32[256,128]{1,0:T(8,128)S(1)} %shard_map.69.mine), channel_id=1, source_target_pairs={{0,16},{4,20},{8,24},{12,28},{16,0},{20,4},{24,8},{28,12},{32,48},... | collective-permute-start | bytes 393224 | tf_op jit(solution)/shard_map/ppermute | solution.py:317

commit v4 on v3

--- a/solution.py
+++ b/solution.py
@@ -24,8 +24,9 @@
 
 
 def dot3(left, right):
-    mul = functools.partial(jnp.dot, preferred_element_type=F32)
-    return mul(left[0], right[0]) + (mul(left[0], right[1]) + mul(left[1], right[0]))
+    (lh, ll), (rh, rl) = left, right
+    long = jnp.concatenate([lh, lh, ll], axis=1), jnp.concatenate([rh, rl, rh], axis=0)
+    return jnp.dot(*long, preferred_element_type=F32)
 
 
 def grids(shape):
@@ -79,27 +80,16 @@
         copy.wait()
 
 
-def prepare_kernel(place, panel_t, tree_v, tree_t, trailing, th, tl, *args):
-    mixes, (block, tri, vee, tee, sems) = args[:-5], args[-5:]
-    ahead = len(mixes) // 2
-    pairs = [(panel_t, tri)]
-    for level in range(ahead):
-        pairs += [(tree_v.at[level], vee.at[level]), (tree_t.at[level], tee.at[level])]
-    copies = start_all(pairs + [(trailing.at[:, : block.shape[1]], block)], sems)
+def prepare_kernel(panel_t, trailing, th, tl, block, tri, sems):
+    copies = start_all(((panel_t, tri), (trailing.at[:, : block.shape[1]], block)), sems)
     copies[0].wait()
     th[...], tl[...] = split(triangle_factor(tri[...]).T)
-    for level in range(ahead):
-        copies[2 * level + 1].wait()
-        copies[2 * level + 2].wait()
-        mix_level((place[0] >> level) & 1 == 0, vee[level], tee[level], *mixes[2 * level : 2 * level + 2])
-    copies[-1].wait()
-
-
-def mixes_kernel(level, place, tree_v, tree_t, after, high, low, vee, tee, sems):
+    copies[1].wait()
+
+
+def mixes_kernel(level, place, tree_v, tree_t, after, high, low):
     del after
-    for copy in start_all(((tree_v.at[level], vee), (tree_t.at[level], tee)), sems):
-        copy.wait()
-    mix_level((place[0] >> level) & 1 == 0, vee[...], tee[...], high, low)
+    mix_level((place[0] >> level) & 1 == 0, tree_v[level], tree_t[level], high, low)
 
 
 def opposite_rows(col, size, count):
@@ -269,20 +259,16 @@
     tall = shaped((rows, width), BF16)
     wide = shaped((width, rows), BF16)
     cube = 2 * 3 * width**3
-    panel_t, tree_v, tree_t = fixed(panel_t), fixed(tree_v), fixed(tree_t)
     units, chunks = layout()
-    ahead = levels - 1
-    th, tl, *mixes, block = call(
+    th, tl, block = call(
         prepare_kernel,
-        out_shape=[square, square] + [mix] * (2 * ahead) + [shaped((rows, units[0][1]))],
-        in_specs=[SMEM] + [HBM] * 4,
-        out_specs=[VMEM] * (3 + 2 * ahead),
-        scratch_shapes=[pltpu.VMEM((width, width), F32)]
-        + [pltpu.VMEM((ahead, width, width), F32)] * 2
-        + [pltpu.SemaphoreType.DMA((2 * ahead + 2,))],
-        mib=16,
-        cost=(5 * cube, 5 << 20),
-    )(place, panel_t, tree_v, tree_t, fixed(trailing))
+        out_shape=[square, square, shaped((rows, units[0][1]))],
+        in_specs=[HBM] * 2,
+        out_specs=[VMEM] * 3,
+        scratch_shapes=[pltpu.VMEM((width, width), F32), pltpu.SemaphoreType.DMA((2,))],
+        mib=8,
+        cost=(cube, 1 << 20),
+    )(fixed(panel_t), fixed(trailing))
 
     w = units[0][1]
     partial, yh, yl, fh, fl = call(
@@ -326,6 +312,20 @@
             mib=8,
             cost=(2 * cube * w // width, 1 << 20),
         )(values, swap(level, values), *mixes[2 * level : 2 * level + 2])
+
+    mixes = []
+
+    def mix_matrices(level, after):
+        mixes.extend(
+            call(
+                functools.partial(mixes_kernel, level),
+                out_shape=[mix] * 2,
+                in_specs=[SMEM] + [VMEM] * 2 + [ANY],
+                out_specs=[VMEM] * 2,
+                mib=8,
+                cost=(2 * cube, 1 << 20),
+            )(place, tree_v, tree_t, after)
+        )
 
     tops, projs = [], []
     for u, (first, w) in enumerate(units):
@@ -339,21 +339,15 @@
                 cost=(5 * cube * w // width, 2 << 20),
             )(trailing, fh, fl, gh, gl)
         projs.append(proj)
+        if u < levels - 1:
+            mix_matrices(u, proj)
         tops += combine(0, top, UNITS[u])
 
     for level in range(1, levels - 1):
         tops = [combine(level, top, (top.shape[1],))[0] for top in tops]
 
     level = levels - 1
-    mixes += call(
-        functools.partial(mixes_kernel, level),
-        out_shape=[mix] * 2,
-        in_specs=[SMEM] + [HBM] * 2 + [ANY],
-        out_specs=[VMEM] * 2,
-        scratch_shapes=[pltpu.VMEM((width, width), F32)] * 2 + [pltpu.SemaphoreType.DMA((2,))],
-        mib=8,
-        cost=(2 * cube, 1 << 20),
-    )(place, tree_v, tree_t, projs[-1])
+    mix_matrices(level, projs[-1])
 
     out = ()
     parts = rows // size - 1
@@ -396,4 +390,6 @@
         P(None, "row", None),
         P(None, "row", None),
     )
-    return jax.shard_map(update, mesh=mesh, in_specs=placed, out_specs=P("row", "col"), check_vma=False)
+    return jax.shard_map(
+        update, mesh=mesh, in_specs=placed, out_specs=P("row", "col"), check_vma=False
+    )

time: 96.9 us -> 97.7 us (level)
  waiting for transfers between devices: 41.6 us -> 42.6 us
    ppermute x1, waiting for transfers between devices: 0.01 us -> 3.37 us  [update(): left_b = lax.ppermute(own_b, 'col', onward)]
    ppermute x1, waiting for transfers between devices: 2.19 us -> 0.01 us  [update(): right_b = lax.ppermute(own_b, 'col', backward)]
    ppermute x1, waiting for transfers between devices: 2.17 us -> 0.01 us  [update(): opp_a = lax.ppermute(left_a, 'col', onward)]
    ppermute x1, waiting for transfers between devices: 0.01 us -> 2.01 us  [update(): left_a = lax.ppermute(own_a, 'col', onward)]
    ppermute x1, starting transfers between devices: 3.01 us -> 1.82 us  [update(): opp_b = lax.ppermute(right_b, 'col', backward)]
    ppermute x1, starting transfers between devices: 0.48 us -> 1.49 us  [update(): left_b = lax.ppermute(own_b, 'col', onward)]
    pallas_call x2 -> x4, Pallas kernels: 5.12 us -> 4.72 us  [the longest x3 3.39 us: mix_matrices(): call(functools.partial(mixes_kernel, level), out_shape=[mix] * 2, in_spec...]
  transfers between devices with their start and end apart: 22 -> 22, of which waited for: 6 -> 7; matrix products, arithmetic and copies ran while one was open for 0% -> 0% of each run, Pallas kernels for 22% -> 21%
where the time goes in v4:
time: 97.7 us; the launch traced here: 97.6 us
  waiting for transfers between devices  42.6 us (44%)
  starting transfers between devices  28.3 us (29%)
  Pallas kernels  26 us (27%)
    ppermute x16, waiting for transfers between devices, swap(): return lax.ppermute(values, 'row', route)  37.3 us
    ppermute x16, starting transfers between devices, swap(): return lax.ppermute(values, 'row', route)  19.8 us
    pallas_call x6, Pallas kernels, update(): call(functools.partial(final_kernel, first), out_shape=shaped((rows, colu...  6.3 us
    pallas_call x2, Pallas kernels, update(): call(functools.partial(rest_kernel, first), out_shape=shaped((rows, colum...  3.91 us
    pallas_call x10, Pallas kernels, combine(): call(level_kernel, out_shape=[shaped((width, w)) for w in widths], in_spe...  3.77 us
    pallas_call x3, Pallas kernels, mix_matrices(): call(functools.partial(mixes_kernel, level), out_shape=[mix] * 2, in_spec...  3.39 us
    ppermute x1, waiting for transfers between devices, update(): left_b = lax.ppermute(own_b, 'col', onward)  3.37 us
    pallas_call x3, Pallas kernels, update(): call(functools.partial(next_kernel, slice(first, first + w)), out_shape=[...  3.01 us
  transfers between devices with their start and end apart: 22, of which 7 were waited for; matrix products, arithmetic and copies ran while one was open for 0% of the time, Pallas kernels for 21%

profile of v4, /device:TPU:8, one launch (start us, length us, event | category | flops | bytes accessed | tf_op | source)
XLA Modules:
  0.0 97.6 jit_solution(1142467153545126449)
XLA Ops:
  1.0 1.6 %collective-permute-start = (f32[144,256]{1,0:T(8,128)S(1)}, f32[144,256]{1,0:T(8,128)S(1)}, u32[]{:S(2)}, u32[]{:S(2)}) collective-permute-start(f32[144,256]{1,0:T(8,128)S(1)} %get-tuple-element.43.own_a), channel_id=1, source_target_pairs={{0,1},{1,2},{2,3},{3,0},{4,5},{5,6},{6,7},{7,4},{8,9},{9,10},{10,1... | collective-permute-start | bytes 442376 | tf_op jit(solution)/shard_map/ppermute | solution.py:250
  2.6 1.7 %collective-permute-start.3 = (f32[112,256]{1,0:T(8,128)S(1)}, f32[112,256]{1,0:T(8,128)S(1)}, u32[]{:S(2)}, u32[]{:S(2)}) collective-permute-start(f32[112,256]{1,0:T(8,128)S(1)} %get-tuple-element.44.own_b), channel_id=1, source_target_pairs={{0,3},{1,0},{2,1},{3,2},{4,7},{5,4},{6,5},{7,6},{8,11},{9,8},{10,9... | collective-permute-start | bytes 344072 | tf_op jit(solution)/shard_map/ppermute | solution.py:251
  4.3 1.5 %collective-permute-start.2 = (f32[144,256]{1,0:T(8,128)S(1)}, f32[144,256]{1,0:T(8,128)S(1)}, u32[]{:S(2)}, u32[]{:S(2)}) collective-permute-start(f32[144,256]{1,0:T(8,128)S(1)} %get-tuple-element.43.own_a), channel_id=1, source_target_pairs={{0,3},{1,0},{2,1},{3,2},{4,7},{5,4},{6,5},{7,6},{8,11},{9,8},{10,9... | collective-permute-start | bytes 442376 | tf_op jit(solution)/shard_map/ppermute | solution.py:253
  5.9 2.0 %collective-permute-done.left_a = f32[144,256]{1,0:T(8,128)S(1)} collective-permute-done((f32[144,256]{1,0:T(8,128)S(1)}, f32[144,256]{1,0:T(8,128)S(1)}, u32[]{:S(2)}, u32[]{:S(2)}) %collective-permute-start) | collective-permute-done | bytes 147488 | tf_op jit(solution)/shard_map/ppermute | solution.py:250
  8.2 1.5 %collective-permute-start.1 = (f32[112,256]{1,0:T(8,128)S(1)}, f32[112,256]{1,0:T(8,128)S(1)}, u32[]{:S(2)}, u32[]{:S(2)}) collective-permute-start(f32[112,256]{1,0:T(8,128)S(1)} %get-tuple-element.44.own_b), channel_id=1, source_target_pairs={{0,1},{1,2},{2,3},{3,0},{4,5},{5,6},{6,7},{7,4},{8,9},{9,10},{10,1... | collective-permute-start | bytes 344072 | tf_op jit(solution)/shard_map/ppermute | solution.py:252
  9.6 1.3 %shard_map.56 = (bf16[256,256]{1,0:T(8,128)(2,1)S(1)}, bf16[256,256]{1,0:T(8,128)(2,1)S(1)}, f32[1024,256]{1,0:T(8,128)S(1)}) custom-call(f32[256,256]{1,0:T(8,128)} %panel_t.1, f32[1024,1024]{1,0:T(8,128)} %block.9), custom_call_target="tpu_custom_call" | custom-call | flops 100663296 | bytes 1048576 | tf_op jit(solution)/shard_map/pallas_call | solution.py:263
  11.0 1.8 %collective-permute-start.5 = (f32[112,256]{1,0:T(8,128)S(1)}, f32[112,256]{1,0:T(8,128)S(1)}, u32[]{:S(2)}, u32[]{:S(2)}) collective-permute-start(f32[112,256]{1,0:T(8,128)S(1)} %collective-permute-done.3.right_b), channel_id=1, source_target_pairs={{0,3},{1,0},{2,1},{3,2},{4,7},{5,4},{6,5},{7,6},{8,11},{9,8},{10,9... | collective-permute-start | bytes 344072 | tf_op jit(solution)/shard_map/ppermute | solution.py:255
  12.9 3.4 %collective-permute-done.1.left_b = f32[112,256]{1,0:T(8,128)S(1)} collective-permute-done((f32[112,256]{1,0:T(8,128)S(1)}, f32[112,256]{1,0:T(8,128)S(1)}, u32[]{:S(2)}, u32[]{:S(2)}) %collective-permute-start.1) | collective-permute-done | bytes 114720 | tf_op jit(solution)/shard_map/ppermute | solution.py:252
  16.3 1.2 %shard_map.57 = (f32[256,256]{1,0:T(8,128)S(1)}, bf16[1024,256]{1,0:T(8,128)(2,1)S(1)}, bf16[1024,256]{1,0:T(8,128)(2,1)S(1)}, bf16[256,1024]{1,0:T(8,128)(2,1)S(1)}, bf16[256,1024]{1,0:T(8,128)(2,1)S(1)}) custom-call(s32[2]{0:T(128)S(1)} %pad_add_fusion.place, f32[144,256]{1,0:T(8,128)S(1)} %get-tuple-element.43.own_a, ...), custom_call_target="tpu_custom_call" | custom-call | flops 201326592 | bytes 4194304 | tf_op jit(solution)/shard_map/pallas_call | solution.py:274
  17.6 1.4 %shard_map.58 = (f32[256,256]{1,0:T(8,128)S(1)}, f32[256,256]{1,0:T(8,128)S(1)}, bf16[256,256]{1,0:T(8,128)(2,1)S(1)}, bf16[256,256]{1,0:T(8,128)(2,1)S(1)}, bf1...) custom-call(s32[2]{0:T(128)S(1)} %pad_add_fusion.place, ...), custom_call_target="tpu_custom_call" | custom-call | flops 201326592 | bytes 2097152 | tf_op jit(solution)/shard_map/pallas_call | solution.py:283
  19.7 1.0 %shard_map.67 = (f32[256,256]{1,0:T(8,128)S(1)}, f32[256,256]{1,0:T(8,128)S(1)}) custom-call(f32[1024,1024]{1,0:T(8,128)S(1)} %copy-done, bf16[256,1024]{1,0:T(8,128)(2,1)S(1)} %get-tuple-element.57.fh, bf16[256,1024]{1,0:T(8,128)(2,1)S(1)} %get-tuple-element.58.fl, bf16[256,256]{1,0:T(8,128)(2,1)S(1)} %get-tuple-element.59.gh, ...), custom_call_target="tpu_custom_call" | custom-call | flops 503316480 | bytes 2097152 | tf_op jit(solution)/shard_map/pallas_call | solution.py:333
  24.0 1.1 %shard_map.61 = (bf16[256,512]{1,0:T(8,128)(2,1)S(1)}, bf16[256,512]{1,0:T(8,128)(2,1)S(1)}) custom-call(s32[2]{0:T(128)S(1)} %pad_add_fusion.place, f32[3,256,256]{2,1,0:T(8,128)S(1)} %copy-done.1, f32[3,256,256]{2,1,0:T(8,128)S(1)} %copy-done.2, f32[256,256]{1,0:T(8,128)S(1)} %get-tuple-element.62.after.args_0_), custom_call_target="tpu_custom_call" | custom-call | flops 201326592 | bytes 1048576 | tf_op jit(solution)/shard_map/pallas_call | solution.py:320
  25.5 2.2 %collective-permute-start.10 = (f32[256,256]{1,0:T(8,128)S(1)}, f32[256,256]{1,0:T(8,128)S(1)}, u32[]{:S(2)}, u32[]{:S(2)}) collective-permute-start(f32[256,256]{1,0:T(8,128)S(1)} %shard_map.68.mine), channel_id=1, source_target_pairs={{0,8},{4,12},{8,0},{12,4},{16,24},{20,28},{24,16},{28,20},{32,40},... | collective-permute-start | bytes 786440 | tf_op jit(solution)/shard_map/ppermute | solution.py:303
  28.7 2.0 %collective-permute-start.20 = (f32[256,128]{1,0:T(8,128)S(1)}, f32[256,128]{1,0:T(8,128)S(1)}, u32[]{:S(2)}, u32[]{:S(2)}) collective-permute-start(f32[256,128]{1,0:T(8,128)S(1)} %get-tuple-element.77.mine), channel_id=1, source_target_pairs={{0,8},{4,12},{8,0},{12,4},{16,24},{20,28},{24,16},{28,20},{32,40},... | collective-permute-start | bytes 393224 | tf_op jit(solution)/shard_map/ppermute | solution.py:303
  30.8 1.1 %shard_map.64 = (bf16[256,512]{1,0:T(8,128)(2,1)S(1)}, bf16[256,512]{1,0:T(8,128)(2,1)S(1)}) custom-call(s32[2]{0:T(128)S(1)} %pad_add_fusion.place, f32[3,256,256]{2,1,0:T(8,128)S(1)} %copy-done.1, f32[3,256,256]{2,1,0:T(8,128)S(1)} %copy-done.2, f32[256,256]{1,0:T(8,128)S(1)} %get-tuple-element.65.after.args_1_), custom_call_target="tpu_custom_call" | custom-call | flops 201326592 | bytes 1048576 | tf_op jit(solution)/shard_map/pallas_call | solution.py:320
  32.3 2.2 %collective-permute-start.15 = (f32[256,128]{1,0:T(8,128)S(1)}, f32[256,128]{1,0:T(8,128)S(1)}, u32[]{:S(2)}, u32[]{:S(2)}) collective-permute-start(f32[256,128]{1,0:T(8,128)S(1)} %get-tuple-element.74.mine), channel_id=1, source_target_pairs={{0,8},{4,12},{8,0},{12,4},{16,24},{20,28},{24,16},{28,20},{32,40},... | collective-permute-start | bytes 393224 | tf_op jit(solution)/shard_map/ppermute | solution.py:303
  34.5 8.9 %collective-permute-done.20.theirs = f32[256,128]{1,0:T(8,128)S(1)} collective-permute-done((f32[256,128]{1,0:T(8,128)S(1)}, f32[256,128]{1,0:T(8,128)S(1)}, u32[]{:S(2)}, u32[]{:S(2)}) %collective-permute-start.20) | collective-permute-done | bytes 131104 | tf_op jit(solution)/shard_map/ppermute | solution.py:303
  43.4 1.9 %collective-permute-start.13 = (f32[256,128]{1,0:T(8,128)S(1)}, f32[256,128]{1,0:T(8,128)S(1)}, u32[]{:S(2)}, u32[]{:S(2)}) collective-permute-start(f32[256,128]{1,0:T(8,128)S(1)} %get-tuple-element.73.mine), channel_id=1, source_target_pairs={{0,8},{4,12},{8,0},{12,4},{16,24},{20,28},{24,16},{28,20},{32,40},... | collective-permute-start | bytes 393224 | tf_op jit(solution)/shard_map/ppermute | solution.py:303
  45.6 3.4 %collective-permute-start.21 = (f32[256,128]{1,0:T(8,128)S(1)}, f32[256,128]{1,0:T(8,128)S(1)}, u32[]{:S(2)}, u32[]{:S(2)}) collective-permute-start(f32[256,128]{1,0:T(8,128)S(1)} %shard_map.75.mine), channel_id=1, source_target_pairs={{0,16},{4,20},{8,24},{12,28},{16,0},{20,4},{24,8},{28,12},{32,48},... | collective-permute-start | bytes 393224 | tf_op jit(solution)/shard_map/ppermute | solution.py:303
  49.9 3.0 %collective-permute-start.8 = (f32[256,256]{1,0:T(8,128)S(1)}, f32[256,256]{1,0:T(8,128)S(1)}, u32[]{:S(2)}, u32[]{:S(2)}) collective-permute-start(f32[256,256]{1,0:T(8,128)S(1)} %shard_map.65.mine), channel_id=1, source_target_pairs={{0,16},{4,20},{8,24},{12,28},{16,0},{20,4},{24,8},{28,12},{32,48},... | collective-permute-start | bytes 786440 | tf_op jit(solution)/shard_map/ppermute | solution.py:303
  52.9 2.0 %shard_map.76.args_2_ = f32[1024,1024]{1,0:T(8,128)} custom-call(f32[1024,1024]{1,0:T(8,128)S(1)} %copy-done, bf16[1024,256]{1,0:T(8,128)(2,1)S(1)} %get-tuple-element.78.yh, bf16[1024,256]{1,0:T(8,128)(2,1)S(1)} %get-tuple-element.79.yl, bf16[256,256]{1,0:T(8,128)(2,1)S(1)} %get-tuple-element.51.th, bf16[256,256]{1,0:T(8,128)(2,1)S(1)} %get-tuple-element.52.tl, ...), custom_call_target="tpu_custom_call" | custom-call | flops 1006632960 | bytes 4194304 | tf_op jit(solution)/shard_map/pallas_call | solution.py:358
  56.3 2.5 %collective-permute-start.16 = (f32[256,128]{1,0:T(8,128)S(1)}, f32[256,128]{1,0:T(8,128)S(1)}, u32[]{:S(2)}, u32[]{:S(2)}) collective-permute-start(f32[256,128]{1,0:T(8,128)S(1)} %shard_map.72.mine), channel_id=1, source_target_pairs={{0,16},{4,20},{8,24},{12,28},{16,0},{20,4},{24,8},{28,12},{32,48},... | collective-permute-start | bytes 393224 | tf_op jit(solution)/shard_map/ppermute | solution.py:303
  59.6 1.3 %shard_map.66 = (bf16[256,512]{1,0:T(8,128)(2,1)S(1)}, bf16[256,512]{1,0:T(8,128)(2,1)S(1)}) custom-call(s32[2]{0:T(128)S(1)} %pad_add_fusion.place, f32[3,256,256]{2,1,0:T(8,128)S(1)} %copy-done.1, f32[3,256,256]{2,1,0:T(8,128)S(1)} %copy-done.2, f32[256,256]{1,0:T(8,128)S(1)} %get-tuple-element.68.after.args_1_), custom_call_target="tpu_custom_call" | custom-call | flops 201326592 | bytes 1048576 | tf_op jit(solution)/shard_map/pallas_call | solution.py:320
  60.9 2.0 %shard_map.77.whole = f32[1024,1024]{1,0:T(8,128)} custom-call(f32[1024,1024]{1,0:T(8,128)S(1)} %copy-done, bf16[1024,256]{1,0:T(8,128)(2,1)S(1)} %get-tuple-element.78.yh, bf16[1024,256]{1,0:T(8,128)(2,1)S(1)} %get-tuple-element.79.yl, bf16[256,256]{1,0:T(8,128)(2,1)S(1)} %get-tuple-element.51.th, ...), custom_call_target="tpu_custom_call", output_to_operand_aliasing={{}: (7, {})} | custom-call | flops 1006632960 | bytes 4194304 | tf_op jit(solution)/shard_map/pallas_call | solution.py:358
  62.9 1.0 %shard_map.78.whole = f32[1024,1024]{1,0:T(8,128)} custom-call(f32[256,128]{1,0:T(8,128)S(1)} %shard_map.75.mine, f32[256,128]{1,0:T(8,128)S(1)} %collective-permute-done.21.theirs, bf16[256,512]{1,0:T(8,128)(2,1)S(1)} %get-tuple-element.69.high, bf16[256,512]{1,0:T(8,128)(2,1)S(1)} %get-tuple-element.70.low, ...), custom_call_target="tpu_custom_call", output_to_operand_aliasing={{}: (4, {})} | custom-call | flops 100663296 | bytes 1048576 | tf_op jit(solution)/shard_map/pallas_call | solution.py:372
  63.9 26.3 %collective-permute-done.19.theirs = f32[256,128]{1,0:T(8,128)S(1)} collective-permute-done((f32[256,128]{1,0:T(8,128)S(1)}, f32[256,128]{1,0:T(8,128)S(1)}, u32[]{:S(2)}, u32[]{:S(2)}) %collective-permute-start.19) | collective-permute-done | bytes 131104 | tf_op jit(solution)/shard_map/ppermute | solution.py:303
  90.3 1.0 %shard_map.79.whole = f32[1024,1024]{1,0:T(8,128)} custom-call(f32[256,128]{1,0:T(8,128)S(1)} %shard_map.74.mine, f32[256,128]{1,0:T(8,128)S(1)} %collective-permute-done.19.theirs, bf16[256,512]{1,0:T(8,128)(2,1)S(1)} %get-tuple-element.69.high, bf16[256,512]{1,0:T(8,128)(2,1)S(1)} %get-tuple-element.70.low, ...), custom_call_target="tpu_custom_call", output_to_operand_aliasing={{}: (4, {})} | custom-call | flops 100663296 | bytes 1048576 | tf_op jit(solution)/shard_map/pallas_call | solution.py:372
  91.3 1.4 %collective-permute-done.16.theirs = f32[256,128]{1,0:T(8,128)S(1)} collective-permute-done((f32[256,128]{1,0:T(8,128)S(1)}, f32[256,128]{1,0:T(8,128)S(1)}, u32[]{:S(2)}, u32[]{:S(2)}) %collective-permute-start.16) | collective-permute-done | bytes 131104 | tf_op jit(solution)/shard_map/ppermute | solution.py:303
  92.7 1.0 %shard_map.80.whole = f32[1024,1024]{1,0:T(8,128)} custom-call(f32[256,128]{1,0:T(8,128)S(1)} %shard_map.72.mine, f32[256,128]{1,0:T(8,128)S(1)} %collective-permute-done.16.theirs, bf16[256,512]{1,0:T(8,128)(2,1)S(1)} %get-tuple-element.69.high, bf16[256,512]{1,0:T(8,128)(2,1)S(1)} %get-tuple-element.70.low, ...), custom_call_target="tpu_custom_call", output_to_operand_aliasing={{}: (4, {})} | custom-call | flops 100663296 | bytes 1048576 | tf_op jit(solution)/shard_map/pallas_call | solution.py:372
  94.1 1.0 %shard_map.81.whole = f32[1024,1024]{1,0:T(8,128)} custom-call(f32[256,128]{1,0:T(8,128)S(1)} %shard_map.71.mine, f32[256,128]{1,0:T(8,128)S(1)} %collective-permute-done.14.theirs, bf16[256,512]{1,0:T(8,128)(2,1)S(1)} %get-tuple-element.69.high, bf16[256,512]{1,0:T(8,128)(2,1)S(1)} %get-tuple-element.70.low, ...), custom_call_target="tpu_custom_call", output_to_operand_aliasing={{}: (4, {})} | custom-call | flops 100663296 | bytes 1048576 | tf_op jit(solution)/shard_map/pallas_call | solution.py:372
  95.2 1.1 %shard_map.82.whole = f32[1024,1024]{1,0:T(8,128)} custom-call(f32[256,256]{1,0:T(8,128)S(1)} %shard_map.69.mine, f32[256,256]{1,0:T(8,128)S(1)} %collective-permute-done.11.theirs, bf16[256,512]{1,0:T(8,128)(2,1)S(1)} %get-tuple-element.69.high, bf16[256,512]{1,0:T(8,128)(2,1)S(1)} %get-tuple-element.70.low, ...), custom_call_target="tpu_custom_call", output_to_operand_aliasing={{}: (4, {})} | custom-call | flops 201326592 | bytes 1048576 | tf_op jit(solution)/shard_map/pallas_call | solution.py:372
  96.3 1.1 %shard_map.83 = f32[1024,1024]{1,0:T(8,128)} custom-call(f32[256,256]{1,0:T(8,128)S(1)} %shard_map.65.mine, f32[256,256]{1,0:T(8,128)S(1)} %collective-permute-done.8.theirs, bf16[256,512]{1,0:T(8,128)(2,1)S(1)} %get-tuple-element.69.high, bf16[256,512]{1,0:T(8,128)(2,1)S(1)} %get-tuple-element.70.low, ...), custom_call_target="tpu_custom_call", output_to_operand_aliasing={{}: (4, {})} | custom-call | flops 201326592 | bytes 1048576 | tf_op jit(solution)/shard_map/pallas_call | solution.py:372
  (48 shorter events, 11.2 us)
Async XLA Ops:
  1.0 6.9 %collective-permute-start = (f32[144,256]{1,0:T(8,128)S(1)}, f32[144,256]{1,0:T(8,128)S(1)}, u32[]{:S(2)}, u32[]{:S(2)}) collective-permute-start(f32[144,256]{1,0:T(8,128)S(1)} %get-tuple-element.43.own_a), channel_id=1, source_target_pairs={{0,1},{1,2},{2,3},{3,0},{4,5},{5,6},{6,7},{7,4},{8,9},{9,10},{10,1... | collective-permute-start | bytes 442376 | tf_op jit(solution)/shard_map/ppermute | solution.py:250
  2.6 8.4 %collective-permute-start.3 = (f32[112,256]{1,0:T(8,128)S(1)}, f32[112,256]{1,0:T(8,128)S(1)}, u32[]{:S(2)}, u32[]{:S(2)}) collective-permute-start(f32[112,256]{1,0:T(8,128)S(1)} %get-tuple-element.44.own_b), channel_id=1, source_target_pairs={{0,3},{1,0},{2,1},{3,2},{4,7},{5,4},{6,5},{7,6},{8,11},{9,8},{10,9... | collective-permute-start | bytes 344072 | tf_op jit(solution)/shard_map/ppermute | solution.py:251
  4.3 12.0 %collective-permute-start.2 = (f32[144,256]{1,0:T(8,128)S(1)}, f32[144,256]{1,0:T(8,128)S(1)}, u32[]{:S(2)}, u32[]{:S(2)}) collective-permute-start(f32[144,256]{1,0:T(8,128)S(1)} %get-tuple-element.43.own_a), channel_id=1, source_target_pairs={{0,3},{1,0},{2,1},{3,2},{4,7},{5,4},{6,5},{7,6},{8,11},{9,8},{10,9... | collective-permute-start | bytes 442376 | tf_op jit(solution)/shard_map/ppermute | solution.py:253
  7.9 9.7 %collective-permute-start.4 = (f32[144,256]{1,0:T(8,128)S(1)}, f32[144,256]{1,0:T(8,128)S(1)}, u32[]{:S(2)}, u32[]{:S(2)}) collective-permute-start(f32[144,256]{1,0:T(8,128)S(1)} %collective-permute-done.left_a), channel_id=1, source_target_pairs={{0,1},{1,2},{2,3},{3,0},{4,5},{5,6},{6,7},{7,4},{8,9},{9,10},{10,1... | collective-permute-start | bytes 442376 | tf_op jit(solution)/shard_map/ppermute | solution.py:254
  8.2 8.1 %collective-permute-start.1 = (f32[112,256]{1,0:T(8,128)S(1)}, f32[112,256]{1,0:T(8,128)S(1)}, u32[]{:S(2)}, u32[]{:S(2)}) collective-permute-start(f32[112,256]{1,0:T(8,128)S(1)} %get-tuple-element.44.own_b), channel_id=1, source_target_pairs={{0,1},{1,2},{2,3},{3,0},{4,5},{5,6},{6,7},{7,4},{8,9},{9,10},{10,1... | collective-permute-start | bytes 344072 | tf_op jit(solution)/shard_map/ppermute | solution.py:252
  11.0 8.7 %copy-start = (f32[1024,1024]{1,0:T(8,128)S(1)}, f32[1024,1024]{1,0:T(8,128)}, u32[]{:S(2)}) copy-start(f32[1024,1024]{1,0:T(8,128)} %block.9) | copy-start | bytes 12582916
  11.0 6.5 %collective-permute-start.5 = (f32[112,256]{1,0:T(8,128)S(1)}, f32[112,256]{1,0:T(8,128)S(1)}, u32[]{:S(2)}, u32[]{:S(2)}) collective-permute-start(f32[112,256]{1,0:T(8,128)S(1)} %collective-permute-done.3.right_b), channel_id=1, source_target_pairs={{0,3},{1,0},{2,1},{3,2},{4,7},{5,4},{6,5},{7,6},{8,11},{9,8},{10,9... | collective-permute-start | bytes 344072 | tf_op jit(solution)/shard_map/ppermute | solution.py:255
  20.7 3.3 %copy-start.1 = (f32[3,256,256]{2,1,0:T(8,128)S(1)}, f32[3,256,256]{2,1,0:T(8,128)}, u32[]{:S(2)}) copy-start(f32[3,256,256]{2,1,0:T(8,128)} %tree_v.5) | copy-start | bytes 2359300
  20.7 3.3 %copy-start.2 = (f32[3,256,256]{2,1,0:T(8,128)S(1)}, f32[3,256,256]{2,1,0:T(8,128)}, u32[]{:S(2)}) copy-start(f32[3,256,256]{2,1,0:T(8,128)} %tree_t.5) | copy-start | bytes 2359300
  20.7 4.4 %collective-permute-start.9 = (f32[256,256]{1,0:T(8,128)S(1)}, f32[256,256]{1,0:T(8,128)S(1)}, u32[]{:S(2)}, u32[]{:S(2)}) collective-permute-start(f32[256,256]{1,0:T(8,128)S(1)} %get-tuple-element.71.mine), channel_id=1, source_target_pairs={{0,4},{4,0},{8,12},{12,8},{16,20},{20,16},{24,28},{28,24},{32,36},... | collective-permute-start | bytes 786440 | tf_op jit(solution)/shard_map/ppermute | solution.py:303
  21.8 5.9 %collective-permute-start.6 = (f32[256,256]{1,0:T(8,128)S(1)}, f32[256,256]{1,0:T(8,128)S(1)}, u32[]{:S(2)}, u32[]{:S(2)}) collective-permute-start(f32[256,256]{1,0:T(8,128)S(1)} %get-tuple-element.61.mine), channel_id=1, source_target_pairs={{0,4},{4,0},{8,12},{12,8},{16,20},{20,16},{24,28},{28,24},{32,36},... | collective-permute-start | bytes 786440 | tf_op jit(solution)/shard_map/ppermute | solution.py:303
  22.4 5.9 %collective-permute-start.17 = (f32[256,256]{1,0:T(8,128)S(1)}, f32[256,256]{1,0:T(8,128)S(1)}, u32[]{:S(2)}, u32[]{:S(2)}) collective-permute-start(f32[256,256]{1,0:T(8,128)S(1)} %get-tuple-element.75.mine), channel_id=1, source_target_pairs={{0,4},{4,0},{8,12},{12,8},{16,20},{20,16},{24,28},{28,24},{32,36},... | collective-permute-start | bytes 786440 | tf_op jit(solution)/shard_map/ppermute | solution.py:303
  23.5 8.4 %collective-permute-start.12 = (f32[256,256]{1,0:T(8,128)S(1)}, f32[256,256]{1,0:T(8,128)S(1)}, u32[]{:S(2)}, u32[]{:S(2)}) collective-permute-start(f32[256,256]{1,0:T(8,128)S(1)} %get-tuple-element.72.mine), channel_id=1, source_target_pairs={{0,4},{4,0},{8,12},{12,8},{16,20},{20,16},{24,28},{28,24},{32,36},... | collective-permute-start | bytes 786440 | tf_op jit(solution)/shard_map/ppermute | solution.py:303
  25.5 20.2 %collective-permute-start.10 = (f32[256,256]{1,0:T(8,128)S(1)}, f32[256,256]{1,0:T(8,128)S(1)}, u32[]{:S(2)}, u32[]{:S(2)}) collective-permute-start(f32[256,256]{1,0:T(8,128)S(1)} %shard_map.68.mine), channel_id=1, source_target_pairs={{0,8},{4,12},{8,0},{12,4},{16,24},{20,28},{24,16},{28,20},{32,40},... | collective-permute-start | bytes 786440 | tf_op jit(solution)/shard_map/ppermute | solution.py:303
  28.1 21.3 %collective-permute-start.7 = (f32[256,256]{1,0:T(8,128)S(1)}, f32[256,256]{1,0:T(8,128)S(1)}, u32[]{:S(2)}, u32[]{:S(2)}) collective-permute-start(f32[256,256]{1,0:T(8,128)S(1)} %shard_map.62.mine), channel_id=1, source_target_pairs={{0,8},{4,12},{8,0},{12,4},{16,24},{20,28},{24,16},{28,20},{32,40},... | collective-permute-start | bytes 786440 | tf_op jit(solution)/shard_map/ppermute | solution.py:303
  28.7 14.7 %collective-permute-start.20 = (f32[256,128]{1,0:T(8,128)S(1)}, f32[256,128]{1,0:T(8,128)S(1)}, u32[]{:S(2)}, u32[]{:S(2)}) collective-permute-start(f32[256,128]{1,0:T(8,128)S(1)} %get-tuple-element.77.mine), channel_id=1, source_target_pairs={{0,8},{4,12},{8,0},{12,4},{16,24},{20,28},{24,16},{28,20},{32,40},... | collective-permute-start | bytes 393224 | tf_op jit(solution)/shard_map/ppermute | solution.py:303
  30.7 19.2 %collective-permute-start.18 = (f32[256,128]{1,0:T(8,128)S(1)}, f32[256,128]{1,0:T(8,128)S(1)}, u32[]{:S(2)}, u32[]{:S(2)}) collective-permute-start(f32[256,128]{1,0:T(8,128)S(1)} %get-tuple-element.76.mine), channel_id=1, source_target_pairs={{0,8},{4,12},{8,0},{12,4},{16,24},{20,28},{24,16},{28,20},{32,40},... | collective-permute-start | bytes 393224 | tf_op jit(solution)/shard_map/ppermute | solution.py:303
  32.3 23.0 %collective-permute-start.15 = (f32[256,128]{1,0:T(8,128)S(1)}, f32[256,128]{1,0:T(8,128)S(1)}, u32[]{:S(2)}, u32[]{:S(2)}) collective-permute-start(f32[256,128]{1,0:T(8,128)S(1)} %get-tuple-element.74.mine), channel_id=1, source_target_pairs={{0,8},{4,12},{8,0},{12,4},{16,24},{20,28},{24,16},{28,20},{32,40},... | collective-permute-start | bytes 393224 | tf_op jit(solution)/shard_map/ppermute | solution.py:303
  43.4 12.9 %collective-permute-start.13 = (f32[256,128]{1,0:T(8,128)S(1)}, f32[256,128]{1,0:T(8,128)S(1)}, u32[]{:S(2)}, u32[]{:S(2)}) collective-permute-start(f32[256,128]{1,0:T(8,128)S(1)} %get-tuple-element.73.mine), channel_id=1, source_target_pairs={{0,8},{4,12},{8,0},{12,4},{16,24},{20,28},{24,16},{28,20},{32,40},... | collective-permute-start | bytes 393224 | tf_op jit(solution)/shard_map/ppermute | solution.py:303
  45.6 13.4 %collective-permute-start.21 = (f32[256,128]{1,0:T(8,128)S(1)}, f32[256,128]{1,0:T(8,128)S(1)}, u32[]{:S(2)}, u32[]{:S(2)}) collective-permute-start(f32[256,128]{1,0:T(8,128)S(1)} %shard_map.75.mine), channel_id=1, source_target_pairs={{0,16},{4,20},{8,24},{12,28},{16,0},{20,4},{24,8},{28,12},{32,48},... | collective-permute-start | bytes 393224 | tf_op jit(solution)/shard_map/ppermute | solution.py:303
  49.4 45.8 %collective-permute-start.11 = (f32[256,256]{1,0:T(8,128)S(1)}, f32[256,256]{1,0:T(8,128)S(1)}, u32[]{:S(2)}, u32[]{:S(2)}) collective-permute-start(f32[256,256]{1,0:T(8,128)S(1)} %shard_map.69.mine), channel_id=1, source_target_pairs={{0,16},{4,20},{8,24},{12,28},{16,0},{20,4},{24,8},{28,12},{32,48},... | collective-permute-start | bytes 786440 | tf_op jit(solution)/shard_map/ppermute | solution.py:303
  49.9 46.4 %collective-permute-start.8 = (f32[256,256]{1,0:T(8,128)S(1)}, f32[256,256]{1,0:T(8,128)S(1)}, u32[]{:S(2)}, u32[]{:S(2)}) collective-permute-start(f32[256,256]{1,0:T(8,128)S(1)} %shard_map.65.mine), channel_id=1, source_target_pairs={{0,16},{4,20},{8,24},{12,28},{16,0},{20,4},{24,8},{28,12},{32,48},... | collective-permute-start | bytes 786440 | tf_op jit(solution)/shard_map/ppermute | solution.py:303
  55.2 35.0 %collective-permute-start.19 = (f32[256,128]{1,0:T(8,128)S(1)}, f32[256,128]{1,0:T(8,128)S(1)}, u32[]{:S(2)}, u32[]{:S(2)}) collective-permute-start(f32[256,128]{1,0:T(8,128)S(1)} %shard_map.74.mine), channel_id=1, source_target_pairs={{0,16},{4,20},{8,24},{12,28},{16,0},{20,4},{24,8},{28,12},{32,48},... | collective-permute-start | bytes 393224 | tf_op jit(solution)/shard_map/ppermute | solution.py:303
  56.3 36.5 %collective-permute-start.16 = (f32[256,128]{1,0:T(8,128)S(1)}, f32[256,128]{1,0:T(8,128)S(1)}, u32[]{:S(2)}, u32[]{:S(2)}) collective-permute-start(f32[256,128]{1,0:T(8,128)S(1)} %shard_map.72.mine), channel_id=1, source_target_pairs={{0,16},{4,20},{8,24},{12,28},{16,0},{20,4},{24,8},{28,12},{32,48},... | collective-permute-start | bytes 393224 | tf_op jit(solution)/shard_map/ppermute | solution.py:303
  59.1 35.0 %collective-permute-start.14 = (f32[256,128]{1,0:T(8,128)S(1)}, f32[256,128]{1,0:T(8,128)S(1)}, u32[]{:S(2)}, u32[]{:S(2)}) collective-permute-start(f32[256,128]{1,0:T(8,128)S(1)} %shard_map.71.mine), channel_id=1, source_target_pairs={{0,16},{4,20},{8,24},{12,28},{16,0},{20,4},{24,8},{28,12},{32,48},... | collective-permute-start | bytes 393224 | tf_op jit(solution)/shard_map/ppermute | solution.py:303

commit v5 on v4

--- a/solution.py
+++ b/solution.py
@@ -9,7 +9,7 @@
 from jax.sharding import PartitionSpec as P
 
 
-UNITS = ((128, 128), (128, 128), (256,), (256,))
+UNITS = ((128,), (128, 128), (128, 256), (256,))
 F32 = jnp.float32
 BF16 = jnp.bfloat16
 VMEM = pl.BlockSpec(memory_space=pltpu.VMEM)
@@ -24,9 +24,8 @@
 
 
 def dot3(left, right):
-    (lh, ll), (rh, rl) = left, right
-    long = jnp.concatenate([lh, lh, ll], axis=1), jnp.concatenate([rh, rl, rh], axis=0)
-    return jnp.dot(*long, preferred_element_type=F32)
+    mul = functools.partial(jnp.dot, preferred_element_type=F32)
+    return mul(left[0], right[0]) + (mul(left[0], right[1]) + mul(left[1], right[0]))
 
 
 def grids(shape):
@@ -74,17 +73,15 @@
     return copies
 
 
-def halves_kernel(panel, first, second, sems):
-    cut = first.shape[0]
-    for copy in start_all(((panel.at[:cut], first), (panel.at[cut:], second)), sems):
-        copy.wait()
-
-
-def prepare_kernel(panel_t, trailing, th, tl, block, tri, sems):
-    copies = start_all(((panel_t, tri), (trailing.at[:, : block.shape[1]], block)), sems)
+def prepare_kernel(place, panel_t, tree_v, tree_t, trailing, th, tl, high, low, block, tri, vee, tee, sems):
+    piece = trailing.at[:, : block.shape[1]]
+    copies = start_all(((panel_t, tri), (tree_v.at[0], vee), (tree_t.at[0], tee), (piece, block)), sems)
     copies[0].wait()
     th[...], tl[...] = split(triangle_factor(tri[...]).T)
     copies[1].wait()
+    copies[2].wait()
+    mix_level(place[0] & 1 == 0, vee[...], tee[...], high, low)
+    copies[3].wait()
 
 
 def mixes_kernel(level, place, tree_v, tree_t, after, high, low):
@@ -232,21 +229,13 @@
     size, width = panel_y.shape
     rows, columns = trailing.shape
     levels = tree_v.shape[0]
-    cut = size * 9 // 16
+    cut = size // 2
     count = lax.axis_size("col")
     place = jnp.stack([lax.axis_index("row"), lax.axis_index("col")]).astype(jnp.int32)
     onward = [(c, (c + 1) % count) for c in range(count)]
     backward = [(c, (c - 1) % count) for c in range(count)]
 
-    own_a, own_b = call(
-        halves_kernel,
-        out_shape=[shaped((cut, width)), shaped((size - cut, width))],
-        in_specs=[HBM],
-        out_specs=[VMEM] * 2,
-        scratch_shapes=[pltpu.SemaphoreType.DMA((2,))],
-        mib=4,
-        cost=(0, 1 << 19),
-    )(fixed(panel_y))
+    own_a, own_b = panel_y[:cut], panel_y[cut:]
     left_a = lax.ppermute(own_a, "col", onward)
     right_b = lax.ppermute(own_b, "col", backward)
     left_b = lax.ppermute(own_b, "col", onward)
@@ -260,15 +249,15 @@
     wide = shaped((width, rows), BF16)
     cube = 2 * 3 * width**3
     units, chunks = layout()
-    th, tl, block = call(
+    th, tl, *mixes, block = call(
         prepare_kernel,
-        out_shape=[square, square, shaped((rows, units[0][1]))],
-        in_specs=[HBM] * 2,
-        out_specs=[VMEM] * 3,
-        scratch_shapes=[pltpu.VMEM((width, width), F32), pltpu.SemaphoreType.DMA((2,))],
+        out_shape=[square, square, mix, mix, shaped((rows, units[0][1]))],
+        in_specs=[SMEM] + [HBM] * 4,
+        out_specs=[VMEM] * 5,
+        scratch_shapes=[pltpu.VMEM((width, width), F32)] * 3 + [pltpu.SemaphoreType.DMA((4,))],
         mib=8,
-        cost=(cube, 1 << 20),
-    )(fixed(panel_t), fixed(trailing))
+        cost=(3 * cube, 1 << 20),
+    )(place, fixed(panel_t), fixed(tree_v), fixed(tree_t), fixed(trailing))
 
     w = units[0][1]
     partial, yh, yl, fh, fl = call(
@@ -312,8 +301,6 @@
             mib=8,
             cost=(2 * cube * w // width, 1 << 20),
         )(values, swap(level, values), *mixes[2 * level : 2 * level + 2])
-
-    mixes = []
 
     def mix_matrices(level, after):
         mixes.extend(
@@ -339,7 +326,7 @@
                 cost=(5 * cube * w // width, 2 << 20),
             )(trailing, fh, fl, gh, gl)
         projs.append(proj)
-        if u < levels - 1:
+        if 0 < u < levels - 1:
             mix_matrices(u, proj)
         tops += combine(0, top, UNITS[u])
 
@@ -390,6 +377,4 @@
         P(None, "row", None),
         P(None, "row", None),
     )
-    return jax.shard_map(
-        update, mesh=mesh, in_specs=placed, out_specs=P("row", "col"), check_vma=False
-    )
+    return jax.shard_map(update, mesh=mesh, in_specs=placed, out_specs=P("row", "col"), check_vma=False)

time: 97.7 us -> 93 us (0.952); the launches traced: 97.6 us -> 91.1 us
  waiting for transfers between devices: 42.6 us -> 36.8 us
  starting transfers between devices: 28.3 us -> 27.1 us
  local copies, waits for them, and re-layouts: 0.02 us -> 1 us
    ppermute x1, waiting for transfers between devices: 3.37 us -> 0.01 us  [update(): left_b = lax.ppermute(own_b, 'col', onward)]
    ppermute x16, starting transfers between devices: 19.8 us -> 17.4 us  [swap(): return lax.ppermute(values, 'row', route)]
    ppermute x1, waiting for transfers between devices: 2.01 us -> 0.1 us  [update(): left_a = lax.ppermute(own_a, 'col', onward)]
    ppermute x1, starting transfers between devices: 1.55 us -> 2.96 us  [update(): right_a = lax.ppermute(own_a, 'col', backward)]
    ppermute x1, starting transfers between devices: 1.49 us -> 0.28 us  [update(): left_b = lax.ppermute(own_b, 'col', onward)]
    pallas_call x3 -> x2, Pallas kernels: 3.39 us -> 2.34 us  [mix_matrices(): call(functools.partial(mixes_kernel, level), out_shape=[mix] * 2, in_spec...]
    ppermute x1, starting transfers between devices: 0.28 us -> 1.28 us  [update(): opp_a = lax.ppermute(left_a, 'col', onward)]
    slice x0 -> x1, local copies, waits for them, and re-layouts: none -> 0.99 us  [update(): own_a, own_b = (panel_y[:cut], panel_y[cut:])]
  transfers between devices with their start and end apart: 22 -> 22, of which waited for: 7 -> 7; matrix products, arithmetic and copies ran while one was open for 0% -> 0% of each run, Pallas kernels for 21% -> 23%
where the time goes in v5:
time: 93 us; the launch traced here: 91.1 us
  waiting for transfers between devices  36.8 us (40%)
  starting transfers between devices  27.1 us (29%)
  Pallas kernels  25.6 us (28%)
  local copies, waits for them, and re-layouts  1 us (1%)
    ppermute x16, waiting for transfers between devices, swap(): return lax.ppermute(values, 'row', route)  36.7 us
    ppermute x16, starting transfers between devices, swap(): return lax.ppermute(values, 'row', route)  17.4 us
    pallas_call x6, Pallas kernels, update(): call(functools.partial(final_kernel, first), out_shape=shaped((rows, colu...  6.32 us
    pallas_call x2, Pallas kernels, update(): call(functools.partial(rest_kernel, first), out_shape=shaped((rows, colum...  4.36 us
    pallas_call x10, Pallas kernels, combine(): call(level_kernel, out_shape=[shaped((width, w)) for w in widths], in_spe...  3.92 us
    pallas_call x3, Pallas kernels, update(): call(functools.partial(next_kernel, slice(first, first + w)), out_shape=[...  3.33 us
    ppermute x1, starting transfers between devices, update(): right_a = lax.ppermute(own_a, 'col', backward)  2.96 us
    pallas_call x2, Pallas kernels, mix_matrices(): call(functools.partial(mixes_kernel, level), out_shape=[mix] * 2, in_spec...  2.34 us
  transfers between devices with their start and end apart: 22, of which 7 were waited for; matrix products, arithmetic and copies ran while one was open for 0% of the time, Pallas kernels for 23%

profile of v5, /device:TPU:8, one launch (start us, length us, event | category | flops | bytes accessed | tf_op | source)
XLA Modules:
  0.0 91.1 jit_solution(9440783071299478861)
XLA Ops:
  1.0 1.6 %collective-permute-start = (f32[128,256]{1,0:T(8,128)S(1)}, f32[128,256]{1,0:T(8,128)S(1)}, u32[]{:S(2)}, u32[]{:S(2)}) collective-permute-start(f32[128,256]{1,0:T(8,128)S(1)} %get-tuple-element.78.own_a), channel_id=1, source_target_pairs={{0,1},{1,2},{2,3},{3,0},{4,5},{5,6},{6,7},{7,4},{8,9},{9,10},{10,1... | collective-permute-start | bytes 393224 | tf_op jit(solution)/shard_map/ppermute | solution.py:239
  2.6 1.7 %collective-permute-start.3 = (f32[128,256]{1,0:T(8,128)S(1)}, f32[128,256]{1,0:T(8,128)S(1)}, u32[]{:S(2)}, u32[]{:S(2)}) collective-permute-start(f32[128,256]{1,0:T(8,128)S(1)} %get-tuple-element.77.own_b), channel_id=1, source_target_pairs={{0,3},{1,0},{2,1},{3,2},{4,7},{5,4},{6,5},{7,6},{8,11},{9,8},{10,9... | collective-permute-start | bytes 393224 | tf_op jit(solution)/shard_map/ppermute | solution.py:240
  4.6 3.0 %collective-permute-start.2 = (f32[128,256]{1,0:T(8,128)S(1)}, f32[128,256]{1,0:T(8,128)S(1)}, u32[]{:S(2)}, u32[]{:S(2)}) collective-permute-start(f32[128,256]{1,0:T(8,128)S(1)} %get-tuple-element.78.own_a), channel_id=1, source_target_pairs={{0,3},{1,0},{2,1},{3,2},{4,7},{5,4},{6,5},{7,6},{8,11},{9,8},{10,9... | collective-permute-start | bytes 393224 | tf_op jit(solution)/shard_map/ppermute | solution.py:242
  7.6 1.3 %collective-permute-start.4 = (f32[128,256]{1,0:T(8,128)S(1)}, f32[128,256]{1,0:T(8,128)S(1)}, u32[]{:S(2)}, u32[]{:S(2)}) collective-permute-start(f32[128,256]{1,0:T(8,128)S(1)} %collective-permute-done.left_a), channel_id=1, source_target_pairs={{0,1},{1,2},{2,3},{3,0},{4,5},{5,6},{6,7},{7,4},{8,9},{9,10},{10,1... | collective-permute-start | bytes 393224 | tf_op jit(solution)/shard_map/ppermute | solution.py:243
  8.9 2.0 %collective-permute-start.5 = (f32[128,256]{1,0:T(8,128)S(1)}, f32[128,256]{1,0:T(8,128)S(1)}, u32[]{:S(2)}, u32[]{:S(2)}) collective-permute-start(f32[128,256]{1,0:T(8,128)S(1)} %collective-permute-done.3.right_b), channel_id=1, source_target_pairs={{0,3},{1,0},{2,1},{3,2},{4,7},{5,4},{6,5},{7,6},{8,11},{9,8},{10,9... | collective-permute-start | bytes 393224 | tf_op jit(solution)/shard_map/ppermute | solution.py:244
  11.0 2.2 %shard_map.55 = (bf16[256,256]{1,0:T(8,128)(2,1)S(1)}, bf16[256,256]{1,0:T(8,128)(2,1)S(1)}, bf16[256,512]{1,0:T(8,128)(2,1)S(1)}, bf16[256,512]{1,0:T(8,128)(2,1)S(1)}, f32[1024,128]{1,0:T(8,128)S(1)}) custom-call(s32[2]{0:T(128)S(1)} %pad_add_fusion.place, f32[256,256]{1,0:T(8,128)} %panel_t.1, f32[3,256,256]{2,1,0:T(8,128)} %tree_v.5, ...), custom_call_target="tpu_custom_call" | custom-call | flops 301989888 | bytes 1048576 | tf_op jit(solution)/shard_map/pallas_call | solution.py:252
  13.2 1.2 %shard_map.56 = (f32[256,128]{1,0:T(8,128)S(1)}, bf16[1024,256]{1,0:T(8,128)(2,1)S(1)}, bf16[1024,256]{1,0:T(8,128)(2,1)S(1)}, bf16[256,1024]{1,0:T(8,128)(2,1)S(1)}, bf16[256,1024]{1,0:T(8,128)(2,1)S(1)}) custom-call(s32[2]{0:T(128)S(1)} %pad_add_fusion.place, f32[128,256]{1,0:T(8,128)S(1)} %get-tuple-element.78.own_a, ...), custom_call_target="tpu_custom_call" | custom-call | flops 201326592 | bytes 4194304 | tf_op jit(solution)/shard_map/pallas_call | solution.py:263
  14.4 1.2 %shard_map.57 = (f32[256,128]{1,0:T(8,128)S(1)}, f32[256,128]{1,0:T(8,128)S(1)}, bf16[256,256]{1,0:T(8,128)(2,1)S(1)}, bf16[256,256]{1,0:T(8,128)(2,1)S(1)}, bf1...) custom-call(s32[2]{0:T(128)S(1)} %pad_add_fusion.place, ...), custom_call_target="tpu_custom_call" | custom-call | flops 201326592 | bytes 2097152 | tf_op jit(solution)/shard_map/pallas_call | solution.py:272
  16.4 1.3 %shard_map.65 = (f32[256,384]{1,0:T(8,128)S(1)}, f32[256,384]{1,0:T(8,128)S(1)}) custom-call(f32[1024,1024]{1,0:T(8,128)S(1)} %copy-done, bf16[256,1024]{1,0:T(8,128)(2,1)S(1)} %get-tuple-element.53.fh, bf16[256,1024]{1,0:T(8,128)(2,1)S(1)} %get-tuple-element.54.fl, bf16[256,256]{1,0:T(8,128)(2,1)S(1)} %get-tuple-element.55.gh, ...), custom_call_target="tpu_custom_call" | custom-call | flops 754974720 | bytes 2097152 | tf_op jit(solution)/shard_map/pallas_call | solution.py:320
  19.5 1.0 %shard_map.61 = (f32[256,256]{1,0:T(8,128)S(1)}, f32[256,256]{1,0:T(8,128)S(1)}) custom-call(f32[1024,1024]{1,0:T(8,128)S(1)} %copy-done, bf16[256,1024]{1,0:T(8,128)(2,1)S(1)} %get-tuple-element.53.fh, bf16[256,1024]{1,0:T(8,128)(2,1)S(1)} %get-tuple-element.54.fl, bf16[256,256]{1,0:T(8,128)(2,1)S(1)} %get-tuple-element.55.gh, ...), custom_call_target="tpu_custom_call" | custom-call | flops 503316480 | bytes 2097152 | tf_op jit(solution)/shard_map/pallas_call | solution.py:320
  21.5 2.2 %collective-permute-start.7 = (f32[256,256]{1,0:T(8,128)S(1)}, f32[256,256]{1,0:T(8,128)S(1)}, u32[]{:S(2)}, u32[]{:S(2)}) collective-permute-start(f32[256,256]{1,0:T(8,128)S(1)} %shard_map.60.mine), channel_id=1, source_target_pairs={{0,8},{4,12},{8,0},{12,4},{16,24},{20,28},{24,16},{28,20},{32,40},... | collective-permute-start | bytes 786440 | tf_op jit(solution)/shard_map/ppermute | solution.py:292
  24.8 2.0 %collective-permute-start.20 = (f32[256,128]{1,0:T(8,128)S(1)}, f32[256,128]{1,0:T(8,128)S(1)}, u32[]{:S(2)}, u32[]{:S(2)}) collective-permute-start(f32[256,128]{1,0:T(8,128)S(1)} %shard_map.72.mine), channel_id=1, source_target_pairs={{0,8},{4,12},{8,0},{12,4},{16,24},{20,28},{24,16},{28,20},{32,40},... | collective-permute-start | bytes 393224 | tf_op jit(solution)/shard_map/ppermute | solution.py:292
  27.4 1.1 %shard_map.62 = (bf16[256,512]{1,0:T(8,128)(2,1)S(1)}, bf16[256,512]{1,0:T(8,128)(2,1)S(1)}) custom-call(s32[2]{0:T(128)S(1)} %pad_add_fusion.place, f32[3,256,256]{2,1,0:T(8,128)S(1)} %copy-done.1, f32[3,256,256]{2,1,0:T(8,128)S(1)} %copy-done.2, f32[256,256]{1,0:T(8,128)S(1)} %get-tuple-element.60.after.args_1_), custom_call_target="tpu_custom_call" | custom-call | flops 201326592 | bytes 1048576 | tf_op jit(solution)/shard_map/pallas_call | solution.py:307
  28.5 10.9 %collective-permute-done.20.theirs = f32[256,128]{1,0:T(8,128)S(1)} collective-permute-done((f32[256,128]{1,0:T(8,128)S(1)}, f32[256,128]{1,0:T(8,128)S(1)}, u32[]{:S(2)}, u32[]{:S(2)}) %collective-permute-start.20) | collective-permute-done | bytes 131104 | tf_op jit(solution)/shard_map/ppermute | solution.py:292
  39.7 3.4 %collective-permute-start.21 = (f32[256,128]{1,0:T(8,128)S(1)}, f32[256,128]{1,0:T(8,128)S(1)}, u32[]{:S(2)}, u32[]{:S(2)}) collective-permute-start(f32[256,128]{1,0:T(8,128)S(1)} %shard_map.73.mine), channel_id=1, source_target_pairs={{0,16},{4,20},{8,24},{12,28},{16,0},{20,4},{24,8},{28,12},{32,48},... | collective-permute-start | bytes 393224 | tf_op jit(solution)/shard_map/ppermute | solution.py:292
  43.1 1.9 %collective-permute-start.15 = (f32[256,128]{1,0:T(8,128)S(1)}, f32[256,128]{1,0:T(8,128)S(1)}, u32[]{:S(2)}, u32[]{:S(2)}) collective-permute-start(f32[256,128]{1,0:T(8,128)S(1)} %get-tuple-element.70.mine), channel_id=1, source_target_pairs={{0,8},{4,12},{8,0},{12,4},{16,24},{20,28},{24,16},{28,20},{32,40},... | collective-permute-start | bytes 393224 | tf_op jit(solution)/shard_map/ppermute | solution.py:292
  46.1 2.9 %collective-permute-start.11 = (f32[256,256]{1,0:T(8,128)S(1)}, f32[256,256]{1,0:T(8,128)S(1)}, u32[]{:S(2)}, u32[]{:S(2)}) collective-permute-start(f32[256,256]{1,0:T(8,128)S(1)} %shard_map.67.mine), channel_id=1, source_target_pairs={{0,16},{4,20},{8,24},{12,28},{16,0},{20,4},{24,8},{28,12},{32,48},... | collective-permute-start | bytes 786440 | tf_op jit(solution)/shard_map/ppermute | solution.py:292
  49.0 1.9 %shard_map.74.args_2_ = f32[1024,1024]{1,0:T(8,128)} custom-call(f32[1024,1024]{1,0:T(8,128)S(1)} %copy-done, bf16[1024,256]{1,0:T(8,128)(2,1)S(1)} %get-tuple-element.73.yh, bf16[1024,256]{1,0:T(8,128)(2,1)S(1)} %get-tuple-element.74.yl, bf16[256,256]{1,0:T(8,128)(2,1)S(1)} %get-tuple-element.47.th, bf16[256,256]{1,0:T(8,128)(2,1)S(1)} %get-tuple-element.48.tl, ...), custom_call_target="tpu_custom_call" | custom-call | flops 1006632960 | bytes 4194304 | tf_op jit(solution)/shard_map/pallas_call | solution.py:345
  51.3 2.7 %collective-permute-done.15.theirs = f32[256,128]{1,0:T(8,128)S(1)} collective-permute-done((f32[256,128]{1,0:T(8,128)S(1)}, f32[256,128]{1,0:T(8,128)S(1)}, u32[]{:S(2)}, u32[]{:S(2)}) %collective-permute-start.15) | collective-permute-done | bytes 131104 | tf_op jit(solution)/shard_map/ppermute | solution.py:292
  54.3 1.4 %collective-permute-done.12.theirs = f32[256,128]{1,0:T(8,128)S(1)} collective-permute-done((f32[256,128]{1,0:T(8,128)S(1)}, f32[256,128]{1,0:T(8,128)S(1)}, u32[]{:S(2)}, u32[]{:S(2)}) %collective-permute-start.12) | collective-permute-done | bytes 131104 | tf_op jit(solution)/shard_map/ppermute | solution.py:292
  55.7 1.6 %collective-permute-start.16 = (f32[256,128]{1,0:T(8,128)S(1)}, f32[256,128]{1,0:T(8,128)S(1)}, u32[]{:S(2)}, u32[]{:S(2)}) collective-permute-start(f32[256,128]{1,0:T(8,128)S(1)} %shard_map.70.mine), channel_id=1, source_target_pairs={{0,16},{4,20},{8,24},{12,28},{16,0},{20,4},{24,8},{28,12},{32,48},... | collective-permute-start | bytes 393224 | tf_op jit(solution)/shard_map/ppermute | solution.py:292
  57.7 1.4 %collective-permute-start.13 = (f32[256,128]{1,0:T(8,128)S(1)}, f32[256,128]{1,0:T(8,128)S(1)}, u32[]{:S(2)}, u32[]{:S(2)}) collective-permute-start(f32[256,128]{1,0:T(8,128)S(1)} %shard_map.68.mine), channel_id=1, source_target_pairs={{0,16},{4,20},{8,24},{12,28},{16,0},{20,4},{24,8},{28,12},{32,48},... | collective-permute-start | bytes 393224 | tf_op jit(solution)/shard_map/ppermute | solution.py:292
  59.1 1.3 %shard_map.64 = (bf16[256,512]{1,0:T(8,128)(2,1)S(1)}, bf16[256,512]{1,0:T(8,128)(2,1)S(1)}) custom-call(s32[2]{0:T(128)S(1)} %pad_add_fusion.place, f32[3,256,256]{2,1,0:T(8,128)S(1)} %copy-done.1, f32[3,256,256]{2,1,0:T(8,128)S(1)} %copy-done.2, f32[256,256]{1,0:T(8,128)S(1)} %get-tuple-element.63.after.args_1_), custom_call_target="tpu_custom_call" | custom-call | flops 201326592 | bytes 1048576 | tf_op jit(solution)/shard_map/pallas_call | solution.py:307
  60.4 2.5 %shard_map.75.whole = f32[1024,1024]{1,0:T(8,128)} custom-call(f32[1024,1024]{1,0:T(8,128)S(1)} %copy-done, bf16[1024,256]{1,0:T(8,128)(2,1)S(1)} %get-tuple-element.73.yh, bf16[1024,256]{1,0:T(8,128)(2,1)S(1)} %get-tuple-element.74.yl, bf16[256,256]{1,0:T(8,128)(2,1)S(1)} %get-tuple-element.47.th, ...), custom_call_target="tpu_custom_call", output_to_operand_aliasing={{}: (7, {})} | custom-call | flops 1006632960 | bytes 4194304 | tf_op jit(solution)/shard_map/pallas_call | solution.py:345
  62.8 1.0 %shard_map.76.whole = f32[1024,1024]{1,0:T(8,128)} custom-call(f32[256,128]{1,0:T(8,128)S(1)} %shard_map.73.mine, f32[256,128]{1,0:T(8,128)S(1)} %collective-permute-done.21.theirs, bf16[256,512]{1,0:T(8,128)(2,1)S(1)} %get-tuple-element.64.high, bf16[256,512]{1,0:T(8,128)(2,1)S(1)} %get-tuple-element.65.low, ...), custom_call_target="tpu_custom_call", output_to_operand_aliasing={{}: (4, {})} | custom-call | flops 100663296 | bytes 1048576 | tf_op jit(solution)/shard_map/pallas_call | solution.py:359
  63.9 19.9 %collective-permute-done.18.theirs = f32[256,128]{1,0:T(8,128)S(1)} collective-permute-done((f32[256,128]{1,0:T(8,128)S(1)}, f32[256,128]{1,0:T(8,128)S(1)}, u32[]{:S(2)}, u32[]{:S(2)}) %collective-permute-start.18) | collective-permute-done | bytes 131104 | tf_op jit(solution)/shard_map/ppermute | solution.py:292
  83.8 1.0 %shard_map.77.whole = f32[1024,1024]{1,0:T(8,128)} custom-call(f32[256,128]{1,0:T(8,128)S(1)} %shard_map.71.mine, f32[256,128]{1,0:T(8,128)S(1)} %collective-permute-done.18.theirs, bf16[256,512]{1,0:T(8,128)(2,1)S(1)} %get-tuple-element.64.high, bf16[256,512]{1,0:T(8,128)(2,1)S(1)} %get-tuple-element.65.low, ...), custom_call_target="tpu_custom_call", output_to_operand_aliasing={{}: (4, {})} | custom-call | flops 100663296 | bytes 1048576 | tf_op jit(solution)/shard_map/pallas_call | solution.py:359
  84.8 1.5 %collective-permute-done.16.theirs = f32[256,128]{1,0:T(8,128)S(1)} collective-permute-done((f32[256,128]{1,0:T(8,128)S(1)}, f32[256,128]{1,0:T(8,128)S(1)}, u32[]{:S(2)}, u32[]{:S(2)}) %collective-permute-start.16) | collective-permute-done | bytes 131104 | tf_op jit(solution)/shard_map/ppermute | solution.py:292
  86.3 1.0 %shard_map.78.whole = f32[1024,1024]{1,0:T(8,128)} custom-call(f32[256,128]{1,0:T(8,128)S(1)} %shard_map.70.mine, f32[256,128]{1,0:T(8,128)S(1)} %collective-permute-done.16.theirs, bf16[256,512]{1,0:T(8,128)(2,1)S(1)} %get-tuple-element.64.high, bf16[256,512]{1,0:T(8,128)(2,1)S(1)} %get-tuple-element.65.low, ...), custom_call_target="tpu_custom_call", output_to_operand_aliasing={{}: (4, {})} | custom-call | flops 100663296 | bytes 1048576 | tf_op jit(solution)/shard_map/pallas_call | solution.py:359
  87.7 1.0 %shard_map.79.whole = f32[1024,1024]{1,0:T(8,128)} custom-call(f32[256,128]{1,0:T(8,128)S(1)} %shard_map.68.mine, f32[256,128]{1,0:T(8,128)S(1)} %collective-permute-done.13.theirs, bf16[256,512]{1,0:T(8,128)(2,1)S(1)} %get-tuple-element.64.high, bf16[256,512]{1,0:T(8,128)(2,1)S(1)} %get-tuple-element.65.low, ...), custom_call_target="tpu_custom_call", output_to_operand_aliasing={{}: (4, {})} | custom-call | flops 100663296 | bytes 1048576 | tf_op jit(solution)/shard_map/pallas_call | solution.py:359
  88.7 1.1 %shard_map.80.whole = f32[1024,1024]{1,0:T(8,128)} custom-call(f32[256,256]{1,0:T(8,128)S(1)} %shard_map.67.mine, f32[256,256]{1,0:T(8,128)S(1)} %collective-permute-done.11.theirs, bf16[256,512]{1,0:T(8,128)(2,1)S(1)} %get-tuple-element.64.high, bf16[256,512]{1,0:T(8,128)(2,1)S(1)} %get-tuple-element.65.low, ...), custom_call_target="tpu_custom_call", output_to_operand_aliasing={{}: (4, {})} | custom-call | flops 201326592 | bytes 1048576 | tf_op jit(solution)/shard_map/pallas_call | solution.py:359
  89.9 1.1 %shard_map.81 = f32[1024,1024]{1,0:T(8,128)} custom-call(f32[256,256]{1,0:T(8,128)S(1)} %shard_map.63.mine, f32[256,256]{1,0:T(8,128)S(1)} %collective-permute-done.8.theirs, bf16[256,512]{1,0:T(8,128)(2,1)S(1)} %get-tuple-element.64.high, bf16[256,512]{1,0:T(8,128)(2,1)S(1)} %get-tuple-element.65.low, ...), custom_call_target="tpu_custom_call", output_to_operand_aliasing={{}: (4, {})} | custom-call | flops 201326592 | bytes 1048576 | tf_op jit(solution)/shard_map/pallas_call | solution.py:359
  (47 shorter events, 9.5 us)
Async XLA Ops:
  1.0 6.7 %collective-permute-start = (f32[128,256]{1,0:T(8,128)S(1)}, f32[128,256]{1,0:T(8,128)S(1)}, u32[]{:S(2)}, u32[]{:S(2)}) collective-permute-start(f32[128,256]{1,0:T(8,128)S(1)} %get-tuple-element.78.own_a), channel_id=1, source_target_pairs={{0,1},{1,2},{2,3},{3,0},{4,5},{5,6},{6,7},{7,4},{8,9},{9,10},{10,1... | collective-permute-start | bytes 393224 | tf_op jit(solution)/shard_map/ppermute | solution.py:239
  2.6 6.4 %collective-permute-start.3 = (f32[128,256]{1,0:T(8,128)S(1)}, f32[128,256]{1,0:T(8,128)S(1)}, u32[]{:S(2)}, u32[]{:S(2)}) collective-permute-start(f32[128,256]{1,0:T(8,128)S(1)} %get-tuple-element.77.own_b), channel_id=1, source_target_pairs={{0,3},{1,0},{2,1},{3,2},{4,7},{5,4},{6,5},{7,6},{8,11},{9,8},{10,9... | collective-permute-start | bytes 393224 | tf_op jit(solution)/shard_map/ppermute | solution.py:240
  4.3 8.9 %collective-permute-start.1 = (f32[128,256]{1,0:T(8,128)S(1)}, f32[128,256]{1,0:T(8,128)S(1)}, u32[]{:S(2)}, u32[]{:S(2)}) collective-permute-start(f32[128,256]{1,0:T(8,128)S(1)} %get-tuple-element.77.own_b), channel_id=1, source_target_pairs={{0,1},{1,2},{2,3},{3,0},{4,5},{5,6},{6,7},{7,4},{8,9},{9,10},{10,1... | collective-permute-start | bytes 393224 | tf_op jit(solution)/shard_map/ppermute | solution.py:241
  4.6 8.6 %collective-permute-start.2 = (f32[128,256]{1,0:T(8,128)S(1)}, f32[128,256]{1,0:T(8,128)S(1)}, u32[]{:S(2)}, u32[]{:S(2)}) collective-permute-start(f32[128,256]{1,0:T(8,128)S(1)} %get-tuple-element.78.own_a), channel_id=1, source_target_pairs={{0,3},{1,0},{2,1},{3,2},{4,7},{5,4},{6,5},{7,6},{8,11},{9,8},{10,9... | collective-permute-start | bytes 393224 | tf_op jit(solution)/shard_map/ppermute | solution.py:242
  7.6 6.8 %collective-permute-start.4 = (f32[128,256]{1,0:T(8,128)S(1)}, f32[128,256]{1,0:T(8,128)S(1)}, u32[]{:S(2)}, u32[]{:S(2)}) collective-permute-start(f32[128,256]{1,0:T(8,128)S(1)} %collective-permute-done.left_a), channel_id=1, source_target_pairs={{0,1},{1,2},{2,3},{3,0},{4,5},{5,6},{6,7},{7,4},{8,9},{9,10},{10,1... | collective-permute-start | bytes 393224 | tf_op jit(solution)/shard_map/ppermute | solution.py:243
  8.9 5.5 %collective-permute-start.5 = (f32[128,256]{1,0:T(8,128)S(1)}, f32[128,256]{1,0:T(8,128)S(1)}, u32[]{:S(2)}, u32[]{:S(2)}) collective-permute-start(f32[128,256]{1,0:T(8,128)S(1)} %collective-permute-done.3.right_b), channel_id=1, source_target_pairs={{0,3},{1,0},{2,1},{3,2},{4,7},{5,4},{6,5},{7,6},{8,11},{9,8},{10,9... | collective-permute-start | bytes 393224 | tf_op jit(solution)/shard_map/ppermute | solution.py:244
  13.2 3.2 %copy-start = (f32[1024,1024]{1,0:T(8,128)S(1)}, f32[1024,1024]{1,0:T(8,128)}, u32[]{:S(2)}) copy-start(f32[1024,1024]{1,0:T(8,128)} %block.9) | copy-start | bytes 12582916
  17.8 5.9 %collective-permute-start.9 = (f32[256,384]{1,0:T(8,128)S(1)}, f32[256,384]{1,0:T(8,128)S(1)}, u32[]{:S(2)}, u32[]{:S(2)}) collective-permute-start(f32[256,384]{1,0:T(8,128)S(1)} %get-tuple-element.66.mine), channel_id=1, source_target_pairs={{0,4},{4,0},{8,12},{12,8},{16,20},{20,16},{24,28},{28,24},{32,36},... | collective-permute-start | bytes 1179656 | tf_op jit(solution)/shard_map/ppermute | solution.py:292
  18.9 8.6 %copy-start.1 = (f32[3,256,256]{2,1,0:T(8,128)S(1)}, f32[3,256,256]{2,1,0:T(8,128)}, u32[]{:S(2)}) copy-start(f32[3,256,256]{2,1,0:T(8,128)} %tree_v.5) | copy-start | bytes 2359300
  18.9 8.5 %copy-start.2 = (f32[3,256,256]{2,1,0:T(8,128)S(1)}, f32[3,256,256]{2,1,0:T(8,128)}, u32[]{:S(2)}) copy-start(f32[3,256,256]{2,1,0:T(8,128)} %tree_t.5) | copy-start | bytes 2359300
  18.9 2.2 %collective-permute-start.6 = (f32[256,256]{1,0:T(8,128)S(1)}, f32[256,256]{1,0:T(8,128)S(1)}, u32[]{:S(2)}, u32[]{:S(2)}) collective-permute-start(f32[256,256]{1,0:T(8,128)S(1)} %get-tuple-element.57.mine), channel_id=1, source_target_pairs={{0,4},{4,0},{8,12},{12,8},{16,20},{20,16},{24,28},{28,24},{32,36},... | collective-permute-start | bytes 786440 | tf_op jit(solution)/shard_map/ppermute | solution.py:292
  20.5 6.3 %collective-permute-start.14 = (f32[256,256]{1,0:T(8,128)S(1)}, f32[256,256]{1,0:T(8,128)S(1)}, u32[]{:S(2)}, u32[]{:S(2)}) collective-permute-start(f32[256,256]{1,0:T(8,128)S(1)} %get-tuple-element.69.mine), channel_id=1, source_target_pairs={{0,4},{4,0},{8,12},{12,8},{16,20},{20,16},{24,28},{28,24},{32,36},... | collective-permute-start | bytes 786440 | tf_op jit(solution)/shard_map/ppermute | solution.py:292
  20.6 3.9 %collective-permute-start.19 = (f32[256,128]{1,0:T(8,128)S(1)}, f32[256,128]{1,0:T(8,128)S(1)}, u32[]{:S(2)}, u32[]{:S(2)}) collective-permute-start(f32[256,128]{1,0:T(8,128)S(1)} %get-tuple-element.72.mine), channel_id=1, source_target_pairs={{0,4},{4,0},{8,12},{12,8},{16,20},{20,16},{24,28},{28,24},{32,36},... | collective-permute-start | bytes 393224 | tf_op jit(solution)/shard_map/ppermute | solution.py:292
  21.5 23.5 %collective-permute-start.7 = (f32[256,256]{1,0:T(8,128)S(1)}, f32[256,256]{1,0:T(8,128)S(1)}, u32[]{:S(2)}, u32[]{:S(2)}) collective-permute-start(f32[256,256]{1,0:T(8,128)S(1)} %shard_map.60.mine), channel_id=1, source_target_pairs={{0,8},{4,12},{8,0},{12,4},{16,24},{20,28},{24,16},{28,20},{32,40},... | collective-permute-start | bytes 786440 | tf_op jit(solution)/shard_map/ppermute | solution.py:292
  24.3 21.3 %collective-permute-start.10 = (f32[256,256]{1,0:T(8,128)S(1)}, f32[256,256]{1,0:T(8,128)S(1)}, u32[]{:S(2)}, u32[]{:S(2)}) collective-permute-start(f32[256,256]{1,0:T(8,128)S(1)} %get-tuple-element.67.mine), channel_id=1, source_target_pairs={{0,8},{4,12},{8,0},{12,4},{16,24},{20,28},{24,16},{28,20},{32,40},... | collective-permute-start | bytes 786440 | tf_op jit(solution)/shard_map/ppermute | solution.py:292
  24.8 14.5 %collective-permute-start.20 = (f32[256,128]{1,0:T(8,128)S(1)}, f32[256,128]{1,0:T(8,128)S(1)}, u32[]{:S(2)}, u32[]{:S(2)}) collective-permute-start(f32[256,128]{1,0:T(8,128)S(1)} %shard_map.72.mine), channel_id=1, source_target_pairs={{0,8},{4,12},{8,0},{12,4},{16,24},{20,28},{24,16},{28,20},{32,40},... | collective-permute-start | bytes 393224 | tf_op jit(solution)/shard_map/ppermute | solution.py:292
  27.2 18.9 %collective-permute-start.17 = (f32[256,128]{1,0:T(8,128)S(1)}, f32[256,128]{1,0:T(8,128)S(1)}, u32[]{:S(2)}, u32[]{:S(2)}) collective-permute-start(f32[256,128]{1,0:T(8,128)S(1)} %get-tuple-element.71.mine), channel_id=1, source_target_pairs={{0,8},{4,12},{8,0},{12,4},{16,24},{20,28},{24,16},{28,20},{32,40},... | collective-permute-start | bytes 393224 | tf_op jit(solution)/shard_map/ppermute | solution.py:292
  39.7 18.0 %collective-permute-start.21 = (f32[256,128]{1,0:T(8,128)S(1)}, f32[256,128]{1,0:T(8,128)S(1)}, u32[]{:S(2)}, u32[]{:S(2)}) collective-permute-start(f32[256,128]{1,0:T(8,128)S(1)} %shard_map.73.mine), channel_id=1, source_target_pairs={{0,16},{4,20},{8,24},{12,28},{16,0},{20,4},{24,8},{28,12},{32,48},... | collective-permute-start | bytes 393224 | tf_op jit(solution)/shard_map/ppermute | solution.py:292
  43.1 10.9 %collective-permute-start.15 = (f32[256,128]{1,0:T(8,128)S(1)}, f32[256,128]{1,0:T(8,128)S(1)}, u32[]{:S(2)}, u32[]{:S(2)}) collective-permute-start(f32[256,128]{1,0:T(8,128)S(1)} %get-tuple-element.70.mine), channel_id=1, source_target_pairs={{0,8},{4,12},{8,0},{12,4},{16,24},{20,28},{24,16},{28,20},{32,40},... | collective-permute-start | bytes 393224 | tf_op jit(solution)/shard_map/ppermute | solution.py:292
  45.0 10.7 %collective-permute-start.12 = (f32[256,128]{1,0:T(8,128)S(1)}, f32[256,128]{1,0:T(8,128)S(1)}, u32[]{:S(2)}, u32[]{:S(2)}) collective-permute-start(f32[256,128]{1,0:T(8,128)S(1)} %get-tuple-element.68.mine), channel_id=1, source_target_pairs={{0,8},{4,12},{8,0},{12,4},{16,24},{20,28},{24,16},{28,20},{32,40},... | collective-permute-start | bytes 393224 | tf_op jit(solution)/shard_map/ppermute | solution.py:292
  45.5 44.3 %collective-permute-start.8 = (f32[256,256]{1,0:T(8,128)S(1)}, f32[256,256]{1,0:T(8,128)S(1)}, u32[]{:S(2)}, u32[]{:S(2)}) collective-permute-start(f32[256,256]{1,0:T(8,128)S(1)} %shard_map.63.mine), channel_id=1, source_target_pairs={{0,16},{4,20},{8,24},{12,28},{16,0},{20,4},{24,8},{28,12},{32,48},... | collective-permute-start | bytes 786440 | tf_op jit(solution)/shard_map/ppermute | solution.py:292
  46.1 42.6 %collective-permute-start.11 = (f32[256,256]{1,0:T(8,128)S(1)}, f32[256,256]{1,0:T(8,128)S(1)}, u32[]{:S(2)}, u32[]{:S(2)}) collective-permute-start(f32[256,256]{1,0:T(8,128)S(1)} %shard_map.67.mine), channel_id=1, source_target_pairs={{0,16},{4,20},{8,24},{12,28},{16,0},{20,4},{24,8},{28,12},{32,48},... | collective-permute-start | bytes 786440 | tf_op jit(solution)/shard_map/ppermute | solution.py:292
  53.9 29.8 %collective-permute-start.18 = (f32[256,128]{1,0:T(8,128)S(1)}, f32[256,128]{1,0:T(8,128)S(1)}, u32[]{:S(2)}, u32[]{:S(2)}) collective-permute-start(f32[256,128]{1,0:T(8,128)S(1)} %shard_map.71.mine), channel_id=1, source_target_pairs={{0,16},{4,20},{8,24},{12,28},{16,0},{20,4},{24,8},{28,12},{32,48},... | collective-permute-start | bytes 393224 | tf_op jit(solution)/shard_map/ppermute | solution.py:292
  55.7 30.6 %collective-permute-start.16 = (f32[256,128]{1,0:T(8,128)S(1)}, f32[256,128]{1,0:T(8,128)S(1)}, u32[]{:S(2)}, u32[]{:S(2)}) collective-permute-start(f32[256,128]{1,0:T(8,128)S(1)} %shard_map.70.mine), channel_id=1, source_target_pairs={{0,16},{4,20},{8,24},{12,28},{16,0},{20,4},{24,8},{28,12},{32,48},... | collective-permute-start | bytes 393224 | tf_op jit(solution)/shard_map/ppermute | solution.py:292
  57.7 30.0 %collective-permute-start.13 = (f32[256,128]{1,0:T(8,128)S(1)}, f32[256,128]{1,0:T(8,128)S(1)}, u32[]{:S(2)}, u32[]{:S(2)}) collective-permute-start(f32[256,128]{1,0:T(8,128)S(1)} %shard_map.68.mine), channel_id=1, source_target_pairs={{0,16},{4,20},{8,24},{12,28},{16,0},{20,4},{24,8},{28,12},{32,48},... | collective-permute-start | bytes 393224 | tf_op jit(solution)/shard_map/ppermute | solution.py:292

commit v6 on v5

--- a/solution.py
+++ b/solution.py
@@ -9,7 +9,8 @@
 from jax.sharding import PartitionSpec as P
 
 
-UNITS = ((128,), (128, 128), (128, 256), (256,))
+UNITS = ((128,), (128,), (128, 128), (256,), (128, 128))
+STEPS = ((0, 1), (2,), (3,), (4,))
 F32 = jnp.float32
 BF16 = jnp.bfloat16
 VMEM = pl.BlockSpec(memory_space=pltpu.VMEM)
@@ -73,7 +74,7 @@
     return copies
 
 
-def prepare_kernel(place, panel_t, tree_v, tree_t, trailing, th, tl, high, low, block, tri, vee, tee, sems):
+def prepare(place, panel_t, tree_v, tree_t, trailing, th, tl, high, low, block, tri, vee, tee, sems):
     piece = trailing.at[:, : block.shape[1]]
     copies = start_all(((panel_t, tri), (tree_v.at[0], vee), (tree_t.at[0], tee), (piece, block)), sems)
     copies[0].wait()
@@ -82,6 +83,25 @@
     copies[2].wait()
     mix_level(place[0] & 1 == 0, vee[...], tee[...], high, low)
     copies[3].wait()
+
+
+def odd_core():
+    return lax.rem(lax.axis_index("row"), 2) == 1
+
+
+def ahead_kernel(*args):
+    pl.when(odd_core())(lambda: prepare(*args))
+
+
+def prepare_kernel(*args):
+    olds, inputs, rest = args[:5], args[5:10], args[10:]
+
+    @pl.when(odd_core())
+    def _():
+        for old, out in zip(olds, rest[:5]):
+            out[...] = old[...]
+
+    pl.when(jnp.logical_not(odd_core()))(lambda: prepare(*inputs, *rest))
 
 
 def mixes_kernel(level, place, tree_v, tree_t, after, high, low):
@@ -123,7 +143,8 @@
         first += part.shape[1]
 
 
-def first_kernel(place, partial, opp_a, opp_b, block, th, tl, yh, yl, top, proj, gh, gl, oh, ol, ph, plow):
+def first_kernel(place, partial, opp_a, opp_b, block, th, tl, yh, yl, *outs):
+    tops, (proj, gh, gl, oh, ol, ph, plow) = outs[:-7], outs[-7:]
     size = opp_a.shape[0] + opp_b.shape[0]
     width = partial.shape[1]
     start = opposite_rows(place[1], size, block.shape[0] // size)
@@ -132,7 +153,7 @@
     upper = [jnp.where(start == 0, new, old[:size, :]) for new, old in zip(straight, (yh, yl))]
     gain = split(dot3(upper, (th[...], tl[...])))
     value = partial[...] + dot3(flipped, split(block[pl.ds(start, size), :width]))
-    top[...] = block[:size, :width] - dot3(gain, split(value))
+    store_parts(block[:size, :width] - dot3(gain, split(value)), tops)
     proj[...] = value
     gh[...], gl[...] = gain
     oh[...], ol[...] = straight
@@ -249,17 +270,30 @@
     wide = shaped((width, rows), BF16)
     cube = 2 * 3 * width**3
     units, chunks = layout()
+    steps = [(units[step[0]][0], sum(units[u][1] for u in step)) for step in STEPS]
+    w = steps[0][1]
+    sources = (place, fixed(panel_t), fixed(tree_v), fixed(tree_t), fixed(trailing))
+    ready = [square, square, mix, mix, shaped((rows, w))]
+    local = [pltpu.VMEM((width, width), F32)] * 3 + [pltpu.SemaphoreType.DMA((4,))]
+    olds = call(
+        ahead_kernel,
+        out_shape=ready,
+        in_specs=[SMEM] + [HBM] * 4,
+        out_specs=[VMEM] * 5,
+        scratch_shapes=local,
+        mib=8,
+        cost=(3 * cube, 1 << 20),
+    )(*sources)
     th, tl, *mixes, block = call(
         prepare_kernel,
-        out_shape=[square, square, mix, mix, shaped((rows, units[0][1]))],
-        in_specs=[SMEM] + [HBM] * 4,
+        out_shape=ready,
+        in_specs=[VMEM] * 5 + [SMEM] + [HBM] * 4,
         out_specs=[VMEM] * 5,
-        scratch_shapes=[pltpu.VMEM((width, width), F32)] * 3 + [pltpu.SemaphoreType.DMA((4,))],
+        scratch_shapes=local,
         mib=8,
         cost=(3 * cube, 1 << 20),
-    )(place, fixed(panel_t), fixed(tree_v), fixed(tree_t), fixed(trailing))
-
-    w = units[0][1]
+    )(*olds, *sources)
+
     partial, yh, yl, fh, fl = call(
         early_kernel,
         out_shape=[shaped((width, w)), tall, tall, wide, wide],
@@ -269,14 +303,16 @@
         cost=(2 * cube, 4 << 20),
     )(place, own_a, own_b, left_a, left_b, right_a, right_b, block)
 
-    top, proj, gh, gl, *opposite = call(
+    outs = call(
         first_kernel,
-        out_shape=[shaped((width, w))] * 2 + [square] * 6,
+        out_shape=[shaped((width, units[u][1])) for u in STEPS[0]] + [shaped((width, w))] + [square] * 6,
         in_specs=[SMEM] + [VMEM] * 8,
-        out_specs=[VMEM] * 8,
+        out_specs=[VMEM] * (7 + len(STEPS[0])),
         mib=16,
         cost=(2 * cube, 2 << 20),
     )(place, partial, opp_a, opp_b, block, th, tl, yh, yl)
+    raw, (proj, gh, gl, *opposite) = list(outs[:-7]), outs[-7:]
+    projs = [proj]
 
     yh, yl, fh, fl = call(
         assemble_kernel,
@@ -314,9 +350,8 @@
             )(place, tree_v, tree_t, after)
         )
 
-    tops, projs = [], []
-    for u, (first, w) in enumerate(units):
-        if u:
+    for k, (first, w) in enumerate(steps):
+        if k:
             top, proj = call(
                 functools.partial(next_kernel, slice(first, first + w)),
                 out_shape=[shaped((width, w))] * 2,
@@ -325,22 +360,23 @@
                 mib=16,
                 cost=(5 * cube * w // width, 2 << 20),
             )(trailing, fh, fl, gh, gl)
-        projs.append(proj)
-        if 0 < u < levels - 1:
-            mix_matrices(u, proj)
+            raw.append(top)
+            projs.append(proj)
+    for level in range(1, levels):
+        mix_matrices(level, projs[0] if level < levels - 1 else projs[-1])
+    tops = []
+    for u, top in enumerate(raw):
         tops += combine(0, top, UNITS[u])
 
     for level in range(1, levels - 1):
         tops = [combine(level, top, (top.shape[1],))[0] for top in tops]
 
     level = levels - 1
-    mix_matrices(level, projs[-1])
-
     out = ()
     parts = rows // size - 1
     for group in ((0, 1), (2, 3)):
-        first = units[group[0]][0]
-        w = sum(units[u][1] for u in group)
+        first = steps[group[0]][0]
+        w = sum(steps[k][1] for k in group)
         out = (
             call(
                 functools.partial(rest_kernel, first),
@@ -351,7 +387,7 @@
                 input_output_aliases={5 + len(group): 0} if out else {},
                 mib=16,
                 cost=(10 * cube, 4 << 20),
-            )(trailing, yh, yl, th, tl, *[projs[u] for u in group], *out),
+            )(trailing, yh, yl, th, tl, *[projs[k] for k in group], *out),
         )
     out = out[0]
 

time: 93 us -> 89.4 us (0.961); the launches traced: 91.1 us -> 88.7 us
  waiting for transfers between devices: 36.8 us -> 28.4 us
  starting transfers between devices: 27.1 us -> 31.7 us
  Pallas kernels: 25.6 us -> 27 us
    ppermute x16 -> x19, waiting for transfers between devices: 36.7 us -> 28.3 us  [swap(): return lax.ppermute(values, 'row', route)]
    ppermute x16 -> x19, starting transfers between devices: 17.4 us -> 21.9 us  [swap(): return lax.ppermute(values, 'row', route)]
    pallas_call x6 -> x7, Pallas kernels: 6.32 us -> 7.27 us  [update(): call(functools.partial(final_kernel, first), out_shape=shaped((rows, colu...]
    pallas_call x2 -> x3, Pallas kernels: 3.46 us -> 4.21 us  [the longest x1 2.25 us: update(): call(prepare_kernel, out_shape=ready, in_specs=[VMEM] * 5 + [SMEM] + [HBM...]
    pallas_call x10 -> x12, Pallas kernels: 3.92 us -> 4.43 us  [combine(): call(level_kernel, out_shape=[shaped((width, w)) for w in widths], in_spe...]
  transfers between devices with their start and end apart: 22 -> 25, of which waited for: 7 -> 7; matrix products, arithmetic and copies ran while one was open for 0% -> 0% of each run, Pallas kernels for 23% -> 26%
where the time goes in v6:
time: 89.4 us; the launch traced here: 88.7 us
  starting transfers between devices  31.7 us (35%)
  waiting for transfers between devices  28.4 us (32%)
  Pallas kernels  27 us (30%)
  local copies, waits for them, and re-layouts  1 us (1%)
    ppermute x19, waiting for transfers between devices, swap(): return lax.ppermute(values, 'row', route)  28.3 us
    ppermute x19, starting transfers between devices, swap(): return lax.ppermute(values, 'row', route)  21.9 us
    pallas_call x7, Pallas kernels, update(): call(functools.partial(final_kernel, first), out_shape=shaped((rows, colu...  7.27 us
    pallas_call x12, Pallas kernels, combine(): call(level_kernel, out_shape=[shaped((width, w)) for w in widths], in_spe...  4.43 us
    pallas_call x2, Pallas kernels, update(): call(functools.partial(rest_kernel, first), out_shape=shaped((rows, colum...  3.93 us
    pallas_call x3, Pallas kernels, update(): call(functools.partial(next_kernel, slice(first, first + w)), out_shape=[...  3.02 us
    ppermute x1, starting transfers between devices, update(): right_a = lax.ppermute(own_a, 'col', backward)  2.96 us
    pallas_call x1, Pallas kernels, update(): call(prepare_kernel, out_shape=ready, in_specs=[VMEM] * 5 + [SMEM] + [HBM...  2.25 us
  transfers between devices with their start and end apart: 25, of which 7 were waited for; matrix products, arithmetic and copies ran while one was open for 0% of the time, Pallas kernels for 26%

profile of v6, /device:TPU:8, one launch (start us, length us, event | category | flops | bytes accessed | tf_op | source)
XLA Modules:
  0.0 88.7 jit_solution(18441502664663249859)
XLA Ops:
  1.0 1.6 %collective-permute-start = (f32[128,256]{1,0:T(8,128)S(1)}, f32[128,256]{1,0:T(8,128)S(1)}, u32[]{:S(2)}, u32[]{:S(2)}) collective-permute-start(f32[128,256]{1,0:T(8,128)S(1)} %get-tuple-element.90.own_a), channel_id=1, source_target_pairs={{0,1},{1,2},{2,3},{3,0},{4,5},{5,6},{6,7},{7,4},{8,9},{9,10},{10,1... | collective-permute-start | bytes 393224 | tf_op jit(solution)/shard_map/ppermute | solution.py:260
  2.6 1.7 %collective-permute-start.3 = (f32[128,256]{1,0:T(8,128)S(1)}, f32[128,256]{1,0:T(8,128)S(1)}, u32[]{:S(2)}, u32[]{:S(2)}) collective-permute-start(f32[128,256]{1,0:T(8,128)S(1)} %get-tuple-element.89.own_b), channel_id=1, source_target_pairs={{0,3},{1,0},{2,1},{3,2},{4,7},{5,4},{6,5},{7,6},{8,11},{9,8},{10,9... | collective-permute-start | bytes 393224 | tf_op jit(solution)/shard_map/ppermute | solution.py:261
  4.6 3.0 %collective-permute-start.2 = (f32[128,256]{1,0:T(8,128)S(1)}, f32[128,256]{1,0:T(8,128)S(1)}, u32[]{:S(2)}, u32[]{:S(2)}) collective-permute-start(f32[128,256]{1,0:T(8,128)S(1)} %get-tuple-element.90.own_a), channel_id=1, source_target_pairs={{0,3},{1,0},{2,1},{3,2},{4,7},{5,4},{6,5},{7,6},{8,11},{9,8},{10,9... | collective-permute-start | bytes 393224 | tf_op jit(solution)/shard_map/ppermute | solution.py:263
  7.6 1.3 %collective-permute-start.4 = (f32[128,256]{1,0:T(8,128)S(1)}, f32[128,256]{1,0:T(8,128)S(1)}, u32[]{:S(2)}, u32[]{:S(2)}) collective-permute-start(f32[128,256]{1,0:T(8,128)S(1)} %collective-permute-done.left_a), channel_id=1, source_target_pairs={{0,1},{1,2},{2,3},{3,0},{4,5},{5,6},{6,7},{7,4},{8,9},{9,10},{10,1... | collective-permute-start | bytes 393224 | tf_op jit(solution)/shard_map/ppermute | solution.py:264
  8.9 2.0 %collective-permute-start.5 = (f32[128,256]{1,0:T(8,128)S(1)}, f32[128,256]{1,0:T(8,128)S(1)}, u32[]{:S(2)}, u32[]{:S(2)}) collective-permute-start(f32[128,256]{1,0:T(8,128)S(1)} %collective-permute-done.3.right_b), channel_id=1, source_target_pairs={{0,3},{1,0},{2,1},{3,2},{4,7},{5,4},{6,5},{7,6},{8,11},{9,8},{10,9... | collective-permute-start | bytes 393224 | tf_op jit(solution)/shard_map/ppermute | solution.py:265
  11.6 2.3 %shard_map.56 = (bf16[256,256]{1,0:T(8,128)(2,1)S(1)}, bf16[256,256]{1,0:T(8,128)(2,1)S(1)}, bf16[256,512]{1,0:T(8,128)(2,1)S(1)}, bf16[256,512]{1,0:T(8,128)(2,1)S(1)}, f32[1024,256]{1,0:T(8,128)S(1)}) custom-call(bf16[256,256]{1,0:T(8,128)(2,1)S(1)} %get-tuple-element.47.args_0_, bf16[256,256]{1,0:T(8,128)(2,1)S(1)} %get-tuple-element.48.args_1_, ...), custom_call_target="tpu_custom_call" | custom-call | flops 301989888 | bytes 1048576 | tf_op jit(solution)/shard_map/pallas_call | solution.py:287
  13.8 1.3 %shard_map.57 = (f32[256,256]{1,0:T(8,128)S(1)}, bf16[1024,256]{1,0:T(8,128)(2,1)S(1)}, bf16[1024,256]{1,0:T(8,128)(2,1)S(1)}, bf16[256,1024]{1,0:T(8,128)(2,1)S(1)}, bf16[256,1024]{1,0:T(8,128)(2,1)S(1)}) custom-call(s32[2]{0:T(128)S(1)} %pad_add_fusion.args_0_.args_5_.place, f32[128,256]{1,0:T(8,128)S(1)} %get-tuple-element.90.own_a, ...), custom_call_target="tpu_custom_call" | custom-call | flops 201326592 | bytes 4194304 | tf_op jit(solution)/shard_map/pallas_call | solution.py:297
  15.1 1.4 %shard_map.58 = (f32[256,128]{1,0:T(8,128)S(1)}, f32[256,128]{1,0:T(8,128)S(1)}, f32[256,256]{1,0:T(8,128)S(1)}, bf16[256,256]{1,0:T(8,128)(2,1)S(1)}, bf16[256,...) custom-call(s32[2]{0:T(128)S(1)} %pad_add_fusion.args_0_.args_5_.pla, ...), custom_call_target="tpu_custom_call" | custom-call | flops 201326592 | bytes 2097152 | tf_op jit(solution)/shard_map/pallas_call | solution.py:306
  22.3 2.0 %collective-permute-start.12 = (f32[256,256]{1,0:T(8,128)S(1)}, f32[256,256]{1,0:T(8,128)S(1)}, u32[]{:S(2)}, u32[]{:S(2)}) collective-permute-start(f32[256,256]{1,0:T(8,128)S(1)} %shard_map.67.mine), channel_id=1, source_target_pairs={{0,8},{4,12},{8,0},{12,4},{16,24},{20,28},{24,16},{28,20},{32,40},... | collective-permute-start | bytes 786440 | tf_op jit(solution)/shard_map/ppermute | solution.py:328
  25.2 2.0 %collective-permute-start.20 = (f32[256,128]{1,0:T(8,128)S(1)}, f32[256,128]{1,0:T(8,128)S(1)}, u32[]{:S(2)}, u32[]{:S(2)}) collective-permute-start(f32[256,128]{1,0:T(8,128)S(1)} %shard_map.73.mine), channel_id=1, source_target_pairs={{0,8},{4,12},{8,0},{12,4},{16,24},{20,28},{24,16},{28,20},{32,40},... | collective-permute-start | bytes 393224 | tf_op jit(solution)/shard_map/ppermute | solution.py:328
  27.8 6.5 %collective-permute-done.23.theirs = f32[256,128]{1,0:T(8,128)S(1)} collective-permute-done((f32[256,128]{1,0:T(8,128)S(1)}, f32[256,128]{1,0:T(8,128)S(1)}, u32[]{:S(2)}, u32[]{:S(2)}) %collective-permute-start.23) | collective-permute-done | bytes 131104 | tf_op jit(solution)/shard_map/ppermute | solution.py:328
  34.4 1.9 %collective-permute-start.15 = (f32[256,128]{1,0:T(8,128)S(1)}, f32[256,128]{1,0:T(8,128)S(1)}, u32[]{:S(2)}, u32[]{:S(2)}) collective-permute-start(f32[256,128]{1,0:T(8,128)S(1)} %get-tuple-element.81.mine), channel_id=1, source_target_pairs={{0,8},{4,12},{8,0},{12,4},{16,24},{20,28},{24,16},{28,20},{32,40},... | collective-permute-start | bytes 393224 | tf_op jit(solution)/shard_map/ppermute | solution.py:328
  36.2 1.1 %shard_map.62 = (bf16[256,512]{1,0:T(8,128)(2,1)S(1)}, bf16[256,512]{1,0:T(8,128)(2,1)S(1)}) custom-call(s32[2]{0:T(128)S(1)} %pad_add_fusion.args_0_.args_5_.place, f32[3,256,256]{2,1,0:T(8,128)S(1)} %copy-done.1, f32[3,256,256]{2,1,0:T(8,128)S(1)} %copy-done.2, f32[256,256]{1,0:T(8,128)S(1)} %get-tuple-element.72.after.args_0_), custom_call_target="tpu_custom_call" | custom-call | flops 201326592 | bytes 1048576 | tf_op jit(solution)/shard_map/pallas_call | solution.py:343
  37.3 1.1 %shard_map.64 = (bf16[256,512]{1,0:T(8,128)(2,1)S(1)}, bf16[256,512]{1,0:T(8,128)(2,1)S(1)}) custom-call(s32[2]{0:T(128)S(1)} %pad_add_fusion.args_0_.args_5_.place, f32[3,256,256]{2,1,0:T(8,128)S(1)} %copy-done.1, f32[3,256,256]{2,1,0:T(8,128)S(1)} %copy-done.2, f32[256,256]{1,0:T(8,128)S(1)} %get-tuple-element.75.after.args_1_), custom_call_target="tpu_custom_call" | custom-call | flops 201326592 | bytes 1048576 | tf_op jit(solution)/shard_map/pallas_call | solution.py:343
  38.8 3.6 %collective-permute-start.24 = (f32[256,128]{1,0:T(8,128)S(1)}, f32[256,128]{1,0:T(8,128)S(1)}, u32[]{:S(2)}, u32[]{:S(2)}) collective-permute-start(f32[256,128]{1,0:T(8,128)S(1)} %shard_map.76.mine), channel_id=1, source_target_pairs={{0,16},{4,20},{8,24},{12,28},{16,0},{20,4},{24,8},{28,12},{32,48},... | collective-permute-start | bytes 393224 | tf_op jit(solution)/shard_map/ppermute | solution.py:328
  43.6 1.8 %collective-permute-start.7 = (f32[256,128]{1,0:T(8,128)S(1)}, f32[256,128]{1,0:T(8,128)S(1)}, u32[]{:S(2)}, u32[]{:S(2)}) collective-permute-start(f32[256,128]{1,0:T(8,128)S(1)} %get-tuple-element.71.mine), channel_id=1, source_target_pairs={{0,8},{4,12},{8,0},{12,4},{16,24},{20,28},{24,16},{28,20},{32,40},... | collective-permute-start | bytes 393224 | tf_op jit(solution)/shard_map/ppermute | solution.py:328
  45.9 2.9 %collective-permute-start.13 = (f32[256,256]{1,0:T(8,128)S(1)}, f32[256,256]{1,0:T(8,128)S(1)}, u32[]{:S(2)}, u32[]{:S(2)}) collective-permute-start(f32[256,256]{1,0:T(8,128)S(1)} %shard_map.68.mine), channel_id=1, source_target_pairs={{0,16},{4,20},{8,24},{12,28},{16,0},{20,4},{24,8},{28,12},{32,48},... | collective-permute-start | bytes 786440 | tf_op jit(solution)/shard_map/ppermute | solution.py:328
  48.8 2.0 %shard_map.77.args_2_ = f32[1024,1024]{1,0:T(8,128)} custom-call(f32[1024,1024]{1,0:T(8,128)S(1)} %copy-done, bf16[1024,256]{1,0:T(8,128)(2,1)S(1)} %get-tuple-element.85.yh, bf16[1024,256]{1,0:T(8,128)(2,1)S(1)} %get-tuple-element.86.yl, bf16[256,256]{1,0:T(8,128)(2,1)S(1)} %get-tuple-element.58.th, bf16[256,256]{1,0:T(8,128)(2,1)S(1)} %get-tuple-element.59.tl, ...), custom_call_target="tpu_custom_call" | custom-call | flops 1006632960 | bytes 4194304 | tf_op jit(solution)/shard_map/pallas_call | solution.py:381
  51.5 3.4 %collective-permute-done.9.theirs = f32[256,128]{1,0:T(8,128)S(1)} collective-permute-done((f32[256,128]{1,0:T(8,128)S(1)}, f32[256,128]{1,0:T(8,128)S(1)}, u32[]{:S(2)}, u32[]{:S(2)}) %collective-permute-start.9) | collective-permute-done | bytes 131104 | tf_op jit(solution)/shard_map/ppermute | solution.py:328
  56.3 1.9 %collective-permute-start.16 = (f32[256,128]{1,0:T(8,128)S(1)}, f32[256,128]{1,0:T(8,128)S(1)}, u32[]{:S(2)}, u32[]{:S(2)}) collective-permute-start(f32[256,128]{1,0:T(8,128)S(1)} %shard_map.71.mine), channel_id=1, source_target_pairs={{0,16},{4,20},{8,24},{12,28},{16,0},{20,4},{24,8},{28,12},{32,48},... | collective-permute-start | bytes 393224 | tf_op jit(solution)/shard_map/ppermute | solution.py:328
  58.6 1.1 %collective-permute-start.10 = (f32[256,128]{1,0:T(8,128)S(1)}, f32[256,128]{1,0:T(8,128)S(1)}, u32[]{:S(2)}, u32[]{:S(2)}) collective-permute-start(f32[256,128]{1,0:T(8,128)S(1)} %shard_map.65.mine), channel_id=1, source_target_pairs={{0,16},{4,20},{8,24},{12,28},{16,0},{20,4},{24,8},{28,12},{32,48},... | collective-permute-start | bytes 393224 | tf_op jit(solution)/shard_map/ppermute | solution.py:328
  59.7 1.9 %collective-permute-start.8 = (f32[256,128]{1,0:T(8,128)S(1)}, f32[256,128]{1,0:T(8,128)S(1)}, u32[]{:S(2)}, u32[]{:S(2)}) collective-permute-start(f32[256,128]{1,0:T(8,128)S(1)} %shard_map.63.mine), channel_id=1, source_target_pairs={{0,16},{4,20},{8,24},{12,28},{16,0},{20,4},{24,8},{28,12},{32,48},... | collective-permute-start | bytes 393224 | tf_op jit(solution)/shard_map/ppermute | solution.py:328
  61.6 2.0 %shard_map.78.whole = f32[1024,1024]{1,0:T(8,128)} custom-call(f32[1024,1024]{1,0:T(8,128)S(1)} %copy-done, bf16[1024,256]{1,0:T(8,128)(2,1)S(1)} %get-tuple-element.85.yh, bf16[1024,256]{1,0:T(8,128)(2,1)S(1)} %get-tuple-element.86.yl, bf16[256,256]{1,0:T(8,128)(2,1)S(1)} %get-tuple-element.58.th, ...), custom_call_target="tpu_custom_call", output_to_operand_aliasing={{}: (7, {})} | custom-call | flops 1006632960 | bytes 4194304 | tf_op jit(solution)/shard_map/pallas_call | solution.py:381
  63.6 1.0 %shard_map.79.whole = f32[1024,1024]{1,0:T(8,128)} custom-call(f32[256,128]{1,0:T(8,128)S(1)} %shard_map.76.mine, f32[256,128]{1,0:T(8,128)S(1)} %collective-permute-done.24.theirs, bf16[256,512]{1,0:T(8,128)(2,1)S(1)} %get-tuple-element.76.high, bf16[256,512]{1,0:T(8,128)(2,1)S(1)} %get-tuple-element.77.low, ...), custom_call_target="tpu_custom_call", output_to_operand_aliasing={{}: (4, {})} | custom-call | flops 100663296 | bytes 1048576 | tf_op jit(solution)/shard_map/pallas_call | solution.py:395
  64.6 1.0 %shard_map.80.whole = f32[1024,1024]{1,0:T(8,128)} custom-call(f32[256,128]{1,0:T(8,128)S(1)} %shard_map.74.mine, f32[256,128]{1,0:T(8,128)S(1)} %collective-permute-done.21.theirs, bf16[256,512]{1,0:T(8,128)(2,1)S(1)} %get-tuple-element.76.high, bf16[256,512]{1,0:T(8,128)(2,1)S(1)} %get-tuple-element.77.low, ...), custom_call_target="tpu_custom_call", output_to_operand_aliasing={{}: (4, {})} | custom-call | flops 100663296 | bytes 1048576 | tf_op jit(solution)/shard_map/pallas_call | solution.py:395
  65.7 15.5 %collective-permute-done.18.theirs = f32[256,128]{1,0:T(8,128)S(1)} collective-permute-done((f32[256,128]{1,0:T(8,128)S(1)}, f32[256,128]{1,0:T(8,128)S(1)}, u32[]{:S(2)}, u32[]{:S(2)}) %collective-permute-start.18) | collective-permute-done | bytes 131104 | tf_op jit(solution)/shard_map/ppermute | solution.py:328
  81.2 1.0 %shard_map.81.whole = f32[1024,1024]{1,0:T(8,128)} custom-call(f32[256,128]{1,0:T(8,128)S(1)} %shard_map.72.mine, f32[256,128]{1,0:T(8,128)S(1)} %collective-permute-done.18.theirs, bf16[256,512]{1,0:T(8,128)(2,1)S(1)} %get-tuple-element.76.high, bf16[256,512]{1,0:T(8,128)(2,1)S(1)} %get-tuple-element.77.low, ...), custom_call_target="tpu_custom_call", output_to_operand_aliasing={{}: (4, {})} | custom-call | flops 100663296 | bytes 1048576 | tf_op jit(solution)/shard_map/pallas_call | solution.py:395
  82.2 1.8 %collective-permute-done.16.theirs = f32[256,128]{1,0:T(8,128)S(1)} collective-permute-done((f32[256,128]{1,0:T(8,128)S(1)}, f32[256,128]{1,0:T(8,128)S(1)}, u32[]{:S(2)}, u32[]{:S(2)}) %collective-permute-start.16) | collective-permute-done | bytes 131104 | tf_op jit(solution)/shard_map/ppermute | solution.py:328
  84.0 1.0 %shard_map.82.whole = f32[1024,1024]{1,0:T(8,128)} custom-call(f32[256,128]{1,0:T(8,128)S(1)} %shard_map.71.mine, f32[256,128]{1,0:T(8,128)S(1)} %collective-permute-done.16.theirs, bf16[256,512]{1,0:T(8,128)(2,1)S(1)} %get-tuple-element.76.high, bf16[256,512]{1,0:T(8,128)(2,1)S(1)} %get-tuple-element.77.low, ...), custom_call_target="tpu_custom_call", output_to_operand_aliasing={{}: (4, {})} | custom-call | flops 100663296 | bytes 1048576 | tf_op jit(solution)/shard_map/pallas_call | solution.py:395
  85.1 1.1 %shard_map.83.whole = f32[1024,1024]{1,0:T(8,128)} custom-call(f32[256,256]{1,0:T(8,128)S(1)} %shard_map.68.mine, f32[256,256]{1,0:T(8,128)S(1)} %collective-permute-done.13.theirs, bf16[256,512]{1,0:T(8,128)(2,1)S(1)} %get-tuple-element.76.high, bf16[256,512]{1,0:T(8,128)(2,1)S(1)} %get-tuple-element.77.low, ...), custom_call_target="tpu_custom_call", output_to_operand_aliasing={{}: (4, {})} | custom-call | flops 201326592 | bytes 1048576 | tf_op jit(solution)/shard_map/pallas_call | solution.py:395
  86.2 1.0 %shard_map.84.whole = f32[1024,1024]{1,0:T(8,128)} custom-call(f32[256,128]{1,0:T(8,128)S(1)} %shard_map.65.mine, f32[256,128]{1,0:T(8,128)S(1)} %collective-permute-done.10.theirs, bf16[256,512]{1,0:T(8,128)(2,1)S(1)} %get-tuple-element.76.high, bf16[256,512]{1,0:T(8,128)(2,1)S(1)} %get-tuple-element.77.low, ...), custom_call_target="tpu_custom_call", output_to_operand_aliasing={{}: (4, {})} | custom-call | flops 100663296 | bytes 1048576 | tf_op jit(solution)/shard_map/pallas_call | solution.py:395
  87.5 1.0 %shard_map.85 = f32[1024,1024]{1,0:T(8,128)} custom-call(f32[256,128]{1,0:T(8,128)S(1)} %shard_map.63.mine, f32[256,128]{1,0:T(8,128)S(1)} %collective-permute-done.8.theirs, bf16[256,512]{1,0:T(8,128)(2,1)S(1)} %get-tuple-element.76.high, bf16[256,512]{1,0:T(8,128)(2,1)S(1)} %get-tuple-element.77.low, ...), custom_call_target="tpu_custom_call", output_to_operand_aliasing={{}: (4, {})} | custom-call | flops 100663296 | bytes 1048576 | tf_op jit(solution)/shard_map/pallas_call | solution.py:395
  (57 shorter events, 14.2 us)
Async XLA Ops:
  1.0 6.7 %collective-permute-start = (f32[128,256]{1,0:T(8,128)S(1)}, f32[128,256]{1,0:T(8,128)S(1)}, u32[]{:S(2)}, u32[]{:S(2)}) collective-permute-start(f32[128,256]{1,0:T(8,128)S(1)} %get-tuple-element.90.own_a), channel_id=1, source_target_pairs={{0,1},{1,2},{2,3},{3,0},{4,5},{5,6},{6,7},{7,4},{8,9},{9,10},{10,1... | collective-permute-start | bytes 393224 | tf_op jit(solution)/shard_map/ppermute | solution.py:260
  2.6 6.4 %collective-permute-start.3 = (f32[128,256]{1,0:T(8,128)S(1)}, f32[128,256]{1,0:T(8,128)S(1)}, u32[]{:S(2)}, u32[]{:S(2)}) collective-permute-start(f32[128,256]{1,0:T(8,128)S(1)} %get-tuple-element.89.own_b), channel_id=1, source_target_pairs={{0,3},{1,0},{2,1},{3,2},{4,7},{5,4},{6,5},{7,6},{8,11},{9,8},{10,9... | collective-permute-start | bytes 393224 | tf_op jit(solution)/shard_map/ppermute | solution.py:261
  4.3 9.5 %collective-permute-start.1 = (f32[128,256]{1,0:T(8,128)S(1)}, f32[128,256]{1,0:T(8,128)S(1)}, u32[]{:S(2)}, u32[]{:S(2)}) collective-permute-start(f32[128,256]{1,0:T(8,128)S(1)} %get-tuple-element.89.own_b), channel_id=1, source_target_pairs={{0,1},{1,2},{2,3},{3,0},{4,5},{5,6},{6,7},{7,4},{8,9},{9,10},{10,1... | collective-permute-start | bytes 393224 | tf_op jit(solution)/shard_map/ppermute | solution.py:262
  4.6 9.3 %collective-permute-start.2 = (f32[128,256]{1,0:T(8,128)S(1)}, f32[128,256]{1,0:T(8,128)S(1)}, u32[]{:S(2)}, u32[]{:S(2)}) collective-permute-start(f32[128,256]{1,0:T(8,128)S(1)} %get-tuple-element.90.own_a), channel_id=1, source_target_pairs={{0,3},{1,0},{2,1},{3,2},{4,7},{5,4},{6,5},{7,6},{8,11},{9,8},{10,9... | collective-permute-start | bytes 393224 | tf_op jit(solution)/shard_map/ppermute | solution.py:263
  7.6 7.5 %collective-permute-start.4 = (f32[128,256]{1,0:T(8,128)S(1)}, f32[128,256]{1,0:T(8,128)S(1)}, u32[]{:S(2)}, u32[]{:S(2)}) collective-permute-start(f32[128,256]{1,0:T(8,128)S(1)} %collective-permute-done.left_a), channel_id=1, source_target_pairs={{0,1},{1,2},{2,3},{3,0},{4,5},{5,6},{6,7},{7,4},{8,9},{9,10},{10,1... | collective-permute-start | bytes 393224 | tf_op jit(solution)/shard_map/ppermute | solution.py:264
  8.9 6.2 %collective-permute-start.5 = (f32[128,256]{1,0:T(8,128)S(1)}, f32[128,256]{1,0:T(8,128)S(1)}, u32[]{:S(2)}, u32[]{:S(2)}) collective-permute-start(f32[128,256]{1,0:T(8,128)S(1)} %collective-permute-done.3.right_b), channel_id=1, source_target_pairs={{0,3},{1,0},{2,1},{3,2},{4,7},{5,4},{6,5},{7,6},{8,11},{9,8},{10,9... | collective-permute-start | bytes 393224 | tf_op jit(solution)/shard_map/ppermute | solution.py:265
  13.8 3.4 %copy-start = (f32[1024,1024]{1,0:T(8,128)S(1)}, f32[1024,1024]{1,0:T(8,128)}, u32[]{:S(2)}) copy-start(f32[1024,1024]{1,0:T(8,128)} %block.9) | copy-start | bytes 12582916
  18.3 3.6 %collective-permute-start.11 = (f32[256,256]{1,0:T(8,128)S(1)}, f32[256,256]{1,0:T(8,128)S(1)}, u32[]{:S(2)}, u32[]{:S(2)}) collective-permute-start(f32[256,256]{1,0:T(8,128)S(1)} %get-tuple-element.79.mine), channel_id=1, source_target_pairs={{0,4},{4,0},{8,12},{12,8},{16,20},{20,16},{24,28},{28,24},{32,36},... | collective-permute-start | bytes 786440 | tf_op jit(solution)/shard_map/ppermute | solution.py:328
  19.4 7.8 %collective-permute-start.14 = (f32[256,256]{1,0:T(8,128)S(1)}, f32[256,256]{1,0:T(8,128)S(1)}, u32[]{:S(2)}, u32[]{:S(2)}) collective-permute-start(f32[256,256]{1,0:T(8,128)S(1)} %get-tuple-element.80.mine), channel_id=1, source_target_pairs={{0,4},{4,0},{8,12},{12,8},{16,20},{20,16},{24,28},{28,24},{32,36},... | collective-permute-start | bytes 786440 | tf_op jit(solution)/shard_map/ppermute | solution.py:328
  20.0 16.3 %copy-start.1 = (f32[3,256,256]{2,1,0:T(8,128)S(1)}, f32[3,256,256]{2,1,0:T(8,128)}, u32[]{:S(2)}) copy-start(f32[3,256,256]{2,1,0:T(8,128)} %tree_v.3) | copy-start | bytes 2359300
  20.0 16.3 %copy-start.2 = (f32[3,256,256]{2,1,0:T(8,128)S(1)}, f32[3,256,256]{2,1,0:T(8,128)}, u32[]{:S(2)}) copy-start(f32[3,256,256]{2,1,0:T(8,128)} %tree_t.3) | copy-start | bytes 2359300
  20.0 4.3 %collective-permute-start.22 = (f32[256,128]{1,0:T(8,128)S(1)}, f32[256,128]{1,0:T(8,128)S(1)}, u32[]{:S(2)}, u32[]{:S(2)}) collective-permute-start(f32[256,128]{1,0:T(8,128)S(1)} %get-tuple-element.84.mine), channel_id=1, source_target_pairs={{0,4},{4,0},{8,12},{12,8},{16,20},{20,16},{24,28},{28,24},{32,36},... | collective-permute-start | bytes 393224 | tf_op jit(solution)/shard_map/ppermute | solution.py:328
  21.1 17.7 %collective-permute-start.6 = (f32[256,256]{1,0:T(8,128)S(1)}, f32[256,256]{1,0:T(8,128)S(1)}, u32[]{:S(2)}, u32[]{:S(2)}) collective-permute-start(f32[256,256]{1,0:T(8,128)S(1)} %get-tuple-element.68.mine), channel_id=1, source_target_pairs={{0,4},{4,0},{8,12},{12,8},{16,20},{20,16},{24,28},{28,24},{32,36},... | collective-permute-start | bytes 786440 | tf_op jit(solution)/shard_map/ppermute | solution.py:328
  21.8 3.1 %collective-permute-start.19 = (f32[256,128]{1,0:T(8,128)S(1)}, f32[256,128]{1,0:T(8,128)S(1)}, u32[]{:S(2)}, u32[]{:S(2)}) collective-permute-start(f32[256,128]{1,0:T(8,128)S(1)} %get-tuple-element.83.mine), channel_id=1, source_target_pairs={{0,4},{4,0},{8,12},{12,8},{16,20},{20,16},{24,28},{28,24},{32,36},... | collective-permute-start | bytes 393224 | tf_op jit(solution)/shard_map/ppermute | solution.py:328
  22.3 21.3 %collective-permute-start.12 = (f32[256,256]{1,0:T(8,128)S(1)}, f32[256,256]{1,0:T(8,128)S(1)}, u32[]{:S(2)}, u32[]{:S(2)}) collective-permute-start(f32[256,256]{1,0:T(8,128)S(1)} %shard_map.67.mine), channel_id=1, source_target_pairs={{0,8},{4,12},{8,0},{12,4},{16,24},{20,28},{24,16},{28,20},{32,40},... | collective-permute-start | bytes 786440 | tf_op jit(solution)/shard_map/ppermute | solution.py:328
  24.6 9.7 %collective-permute-start.23 = (f32[256,128]{1,0:T(8,128)S(1)}, f32[256,128]{1,0:T(8,128)S(1)}, u32[]{:S(2)}, u32[]{:S(2)}) collective-permute-start(f32[256,128]{1,0:T(8,128)S(1)} %shard_map.75.mine), channel_id=1, source_target_pairs={{0,8},{4,12},{8,0},{12,4},{16,24},{20,28},{24,16},{28,20},{32,40},... | collective-permute-start | bytes 393224 | tf_op jit(solution)/shard_map/ppermute | solution.py:328
  25.2 17.6 %collective-permute-start.20 = (f32[256,128]{1,0:T(8,128)S(1)}, f32[256,128]{1,0:T(8,128)S(1)}, u32[]{:S(2)}, u32[]{:S(2)}) collective-permute-start(f32[256,128]{1,0:T(8,128)S(1)} %shard_map.73.mine), channel_id=1, source_target_pairs={{0,8},{4,12},{8,0},{12,4},{16,24},{20,28},{24,16},{28,20},{32,40},... | collective-permute-start | bytes 393224 | tf_op jit(solution)/shard_map/ppermute | solution.py:328
  27.6 18.2 %collective-permute-start.17 = (f32[256,128]{1,0:T(8,128)S(1)}, f32[256,128]{1,0:T(8,128)S(1)}, u32[]{:S(2)}, u32[]{:S(2)}) collective-permute-start(f32[256,128]{1,0:T(8,128)S(1)} %get-tuple-element.82.mine), channel_id=1, source_target_pairs={{0,8},{4,12},{8,0},{12,4},{16,24},{20,28},{24,16},{28,20},{32,40},... | collective-permute-start | bytes 393224 | tf_op jit(solution)/shard_map/ppermute | solution.py:328
  34.4 11.5 %collective-permute-start.15 = (f32[256,128]{1,0:T(8,128)S(1)}, f32[256,128]{1,0:T(8,128)S(1)}, u32[]{:S(2)}, u32[]{:S(2)}) collective-permute-start(f32[256,128]{1,0:T(8,128)S(1)} %get-tuple-element.81.mine), channel_id=1, source_target_pairs={{0,8},{4,12},{8,0},{12,4},{16,24},{20,28},{24,16},{28,20},{32,40},... | collective-permute-start | bytes 393224 | tf_op jit(solution)/shard_map/ppermute | solution.py:328
  38.8 19.8 %collective-permute-start.24 = (f32[256,128]{1,0:T(8,128)S(1)}, f32[256,128]{1,0:T(8,128)S(1)}, u32[]{:S(2)}, u32[]{:S(2)}) collective-permute-start(f32[256,128]{1,0:T(8,128)S(1)} %shard_map.76.mine), channel_id=1, source_target_pairs={{0,16},{4,20},{8,24},{12,28},{16,0},{20,4},{24,8},{28,12},{32,48},... | collective-permute-start | bytes 393224 | tf_op jit(solution)/shard_map/ppermute | solution.py:328
  42.8 12.1 %collective-permute-start.9 = (f32[256,128]{1,0:T(8,128)S(1)}, f32[256,128]{1,0:T(8,128)S(1)}, u32[]{:S(2)}, u32[]{:S(2)}) collective-permute-start(f32[256,128]{1,0:T(8,128)S(1)} %get-tuple-element.78.mine), channel_id=1, source_target_pairs={{0,8},{4,12},{8,0},{12,4},{16,24},{20,28},{24,16},{28,20},{32,40},... | collective-permute-start | bytes 393224 | tf_op jit(solution)/shard_map/ppermute | solution.py:328
  43.6 12.8 %collective-permute-start.7 = (f32[256,128]{1,0:T(8,128)S(1)}, f32[256,128]{1,0:T(8,128)S(1)}, u32[]{:S(2)}, u32[]{:S(2)}) collective-permute-start(f32[256,128]{1,0:T(8,128)S(1)} %get-tuple-element.71.mine), channel_id=1, source_target_pairs={{0,8},{4,12},{8,0},{12,4},{16,24},{20,28},{24,16},{28,20},{32,40},... | collective-permute-start | bytes 393224 | tf_op jit(solution)/shard_map/ppermute | solution.py:328
  45.8 14.0 %collective-permute-start.21 = (f32[256,128]{1,0:T(8,128)S(1)}, f32[256,128]{1,0:T(8,128)S(1)}, u32[]{:S(2)}, u32[]{:S(2)}) collective-permute-start(f32[256,128]{1,0:T(8,128)S(1)} %shard_map.74.mine), channel_id=1, source_target_pairs={{0,16},{4,20},{8,24},{12,28},{16,0},{20,4},{24,8},{28,12},{32,48},... | collective-permute-start | bytes 393224 | tf_op jit(solution)/shard_map/ppermute | solution.py:328
  45.9 39.2 %collective-permute-start.13 = (f32[256,256]{1,0:T(8,128)S(1)}, f32[256,256]{1,0:T(8,128)S(1)}, u32[]{:S(2)}, u32[]{:S(2)}) collective-permute-start(f32[256,256]{1,0:T(8,128)S(1)} %shard_map.68.mine), channel_id=1, source_target_pairs={{0,16},{4,20},{8,24},{12,28},{16,0},{20,4},{24,8},{28,12},{32,48},... | collective-permute-start | bytes 786440 | tf_op jit(solution)/shard_map/ppermute | solution.py:328
  54.9 26.4 %collective-permute-start.18 = (f32[256,128]{1,0:T(8,128)S(1)}, f32[256,128]{1,0:T(8,128)S(1)}, u32[]{:S(2)}, u32[]{:S(2)}) collective-permute-start(f32[256,128]{1,0:T(8,128)S(1)} %shard_map.72.mine), channel_id=1, source_target_pairs={{0,16},{4,20},{8,24},{12,28},{16,0},{20,4},{24,8},{28,12},{32,48},... | collective-permute-start | bytes 393224 | tf_op jit(solution)/shard_map/ppermute | solution.py:328
  56.3 27.7 %collective-permute-start.16 = (f32[256,128]{1,0:T(8,128)S(1)}, f32[256,128]{1,0:T(8,128)S(1)}, u32[]{:S(2)}, u32[]{:S(2)}) collective-permute-start(f32[256,128]{1,0:T(8,128)S(1)} %shard_map.71.mine), channel_id=1, source_target_pairs={{0,16},{4,20},{8,24},{12,28},{16,0},{20,4},{24,8},{28,12},{32,48},... | collective-permute-start | bytes 393224 | tf_op jit(solution)/shard_map/ppermute | solution.py:328
  58.6 27.6 %collective-permute-start.10 = (f32[256,128]{1,0:T(8,128)S(1)}, f32[256,128]{1,0:T(8,128)S(1)}, u32[]{:S(2)}, u32[]{:S(2)}) collective-permute-start(f32[256,128]{1,0:T(8,128)S(1)} %shard_map.65.mine), channel_id=1, source_target_pairs={{0,16},{4,20},{8,24},{12,28},{16,0},{20,4},{24,8},{28,12},{32,48},... | collective-permute-start | bytes 393224 | tf_op jit(solution)/shard_map/ppermute | solution.py:328
  59.7 27.8 %collective-permute-start.8 = (f32[256,128]{1,0:T(8,128)S(1)}, f32[256,128]{1,0:T(8,128)S(1)}, u32[]{:S(2)}, u32[]{:S(2)}) collective-permute-start(f32[256,128]{1,0:T(8,128)S(1)} %shard_map.63.mine), channel_id=1, source_target_pairs={{0,16},{4,20},{8,24},{12,28},{16,0},{20,4},{24,8},{28,12},{32,48},... | collective-permute-start | bytes 393224 | tf_op jit(solution)/shard_map/ppermute | solution.py:328

commit v7 on v6

--- a/solution.py
+++ b/solution.py
@@ -9,7 +9,7 @@
 from jax.sharding import PartitionSpec as P
 
 
-UNITS = ((128,), (128,), (128, 128), (256,), (128, 128))
+UNITS = ((128,), (128,), (128, 128), (128, 128), (128, 128))
 STEPS = ((0, 1), (2,), (3,), (4,))
 F32 = jnp.float32
 BF16 = jnp.bfloat16
@@ -74,7 +74,7 @@
     return copies
 
 
-def prepare(place, panel_t, tree_v, tree_t, trailing, th, tl, high, low, block, tri, vee, tee, sems):
+def prepare_kernel(place, panel_t, tree_v, tree_t, trailing, th, tl, high, low, block, tri, vee, tee, sems):
     piece = trailing.at[:, : block.shape[1]]
     copies = start_all(((panel_t, tri), (tree_v.at[0], vee), (tree_t.at[0], tee), (piece, block)), sems)
     copies[0].wait()
@@ -83,25 +83,6 @@
     copies[2].wait()
     mix_level(place[0] & 1 == 0, vee[...], tee[...], high, low)
     copies[3].wait()
-
-
-def odd_core():
-    return lax.rem(lax.axis_index("row"), 2) == 1
-
-
-def ahead_kernel(*args):
-    pl.when(odd_core())(lambda: prepare(*args))
-
-
-def prepare_kernel(*args):
-    olds, inputs, rest = args[:5], args[5:10], args[10:]
-
-    @pl.when(odd_core())
-    def _():
-        for old, out in zip(olds, rest[:5]):
-            out[...] = old[...]
-
-    pl.when(jnp.logical_not(odd_core()))(lambda: prepare(*inputs, *rest))
 
 
 def mixes_kernel(level, place, tree_v, tree_t, after, high, low):
@@ -272,27 +253,15 @@
     units, chunks = layout()
     steps = [(units[step[0]][0], sum(units[u][1] for u in step)) for step in STEPS]
     w = steps[0][1]
-    sources = (place, fixed(panel_t), fixed(tree_v), fixed(tree_t), fixed(trailing))
-    ready = [square, square, mix, mix, shaped((rows, w))]
-    local = [pltpu.VMEM((width, width), F32)] * 3 + [pltpu.SemaphoreType.DMA((4,))]
-    olds = call(
-        ahead_kernel,
-        out_shape=ready,
+    th, tl, *mixes, block = call(
+        prepare_kernel,
+        out_shape=[square, square, mix, mix, shaped((rows, w))],
         in_specs=[SMEM] + [HBM] * 4,
         out_specs=[VMEM] * 5,
-        scratch_shapes=local,
+        scratch_shapes=[pltpu.VMEM((width, width), F32)] * 3 + [pltpu.SemaphoreType.DMA((4,))],
         mib=8,
         cost=(3 * cube, 1 << 20),
-    )(*sources)
-    th, tl, *mixes, block = call(
-        prepare_kernel,
-        out_shape=ready,
-        in_specs=[VMEM] * 5 + [SMEM] + [HBM] * 4,
-        out_specs=[VMEM] * 5,
-        scratch_shapes=local,
-        mib=8,
-        cost=(3 * cube, 1 << 20),
-    )(*olds, *sources)
+    )(place, fixed(panel_t), fixed(tree_v), fixed(tree_t), fixed(trailing))
 
     partial, yh, yl, fh, fl = call(
         early_kernel,

time: 89.4 us -> 88.9 us (level)
  waiting for transfers between devices: 28.4 us -> 23.2 us
  starting transfers between devices: 31.7 us -> 35.3 us
    ppermute x19 -> x21, waiting for transfers between devices: 28.3 us -> 23.1 us  [swap(): return lax.ppermute(values, 'row', route)]
    ppermute x19 -> x21, starting transfers between devices: 21.9 us -> 25.5 us  [swap(): return lax.ppermute(values, 'row', route)]
    pallas_call x7 -> x8, Pallas kernels: 7.27 us -> 8.2 us  [update(): call(functools.partial(final_kernel, first), out_shape=shaped((rows, colu...]
    pallas_call x2 -> x1, Pallas kernels: 2.84 us -> 2.23 us  [update(): call(prepare_kernel, out_shape=[square, square, mix, mix, shaped((rows, w...]
    pallas_call x12 -> x13, Pallas kernels: 4.43 us -> 4.78 us  [combine(): call(level_kernel, out_shape=[shaped((width, w)) for w in widths], in_spe...]
  transfers between devices with their start and end apart: 25 -> 27, of which waited for: 7 -> 11; matrix products, arithmetic and copies ran while one was open for 0% -> 0% of each run, Pallas kernels for 26% -> 27%
where the time goes in v7:
time: 88.9 us; the launch traced here: 87.7 us
  starting transfers between devices  35.3 us (40%)
  Pallas kernels  27.6 us (31%)
  waiting for transfers between devices  23.2 us (26%)
  local copies, waits for them, and re-layouts  1 us (1%)
    ppermute x21, starting transfers between devices, swap(): return lax.ppermute(values, 'row', route)  25.5 us
    ppermute x21, waiting for transfers between devices, swap(): return lax.ppermute(values, 'row', route)  23.1 us
    pallas_call x8, Pallas kernels, update(): call(functools.partial(final_kernel, first), out_shape=shaped((rows, colu...  8.2 us
    pallas_call x13, Pallas kernels, combine(): call(level_kernel, out_shape=[shaped((width, w)) for w in widths], in_spe...  4.78 us
    pallas_call x2, Pallas kernels, update(): call(functools.partial(rest_kernel, first), out_shape=shaped((rows, colum...  3.91 us
    pallas_call x3, Pallas kernels, update(): call(functools.partial(next_kernel, slice(first, first + w)), out_shape=[...  3.01 us
    ppermute x1, starting transfers between devices, update(): right_a = lax.ppermute(own_a, 'col', backward)  2.96 us
    pallas_call x1, Pallas kernels, update(): call(prepare_kernel, out_shape=[square, square, mix, mix, shaped((rows, w...  2.23 us
  transfers between devices with their start and end apart: 27, of which 11 were waited for; matrix products, arithmetic and copies ran while one was open for 0% of the time, Pallas kernels for 27%

profile of v7, /device:TPU:8, one launch (start us, length us, event | category | flops | bytes accessed | tf_op | source)
XLA Modules:
  0.0 87.7 jit_solution(6029408760595894960)
XLA Ops:
  1.0 1.6 %collective-permute-start = (f32[128,256]{1,0:T(8,128)S(1)}, f32[128,256]{1,0:T(8,128)S(1)}, u32[]{:S(2)}, u32[]{:S(2)}) collective-permute-start(f32[128,256]{1,0:T(8,128)S(1)} %get-tuple-element.84.own_a), channel_id=1, source_target_pairs={{0,1},{1,2},{2,3},{3,0},{4,5},{5,6},{6,7},{7,4},{8,9},{9,10},{10,1... | collective-permute-start | bytes 393224 | tf_op jit(solution)/shard_map/ppermute | solution.py:241
  2.6 1.7 %collective-permute-start.3 = (f32[128,256]{1,0:T(8,128)S(1)}, f32[128,256]{1,0:T(8,128)S(1)}, u32[]{:S(2)}, u32[]{:S(2)}) collective-permute-start(f32[128,256]{1,0:T(8,128)S(1)} %get-tuple-element.83.own_b), channel_id=1, source_target_pairs={{0,3},{1,0},{2,1},{3,2},{4,7},{5,4},{6,5},{7,6},{8,11},{9,8},{10,9... | collective-permute-start | bytes 393224 | tf_op jit(solution)/shard_map/ppermute | solution.py:242
  4.6 3.0 %collective-permute-start.2 = (f32[128,256]{1,0:T(8,128)S(1)}, f32[128,256]{1,0:T(8,128)S(1)}, u32[]{:S(2)}, u32[]{:S(2)}) collective-permute-start(f32[128,256]{1,0:T(8,128)S(1)} %get-tuple-element.84.own_a), channel_id=1, source_target_pairs={{0,3},{1,0},{2,1},{3,2},{4,7},{5,4},{6,5},{7,6},{8,11},{9,8},{10,9... | collective-permute-start | bytes 393224 | tf_op jit(solution)/shard_map/ppermute | solution.py:244
  7.6 1.3 %collective-permute-start.4 = (f32[128,256]{1,0:T(8,128)S(1)}, f32[128,256]{1,0:T(8,128)S(1)}, u32[]{:S(2)}, u32[]{:S(2)}) collective-permute-start(f32[128,256]{1,0:T(8,128)S(1)} %collective-permute-done.left_a), channel_id=1, source_target_pairs={{0,1},{1,2},{2,3},{3,0},{4,5},{5,6},{6,7},{7,4},{8,9},{9,10},{10,1... | collective-permute-start | bytes 393224 | tf_op jit(solution)/shard_map/ppermute | solution.py:245
  8.9 2.0 %collective-permute-start.5 = (f32[128,256]{1,0:T(8,128)S(1)}, f32[128,256]{1,0:T(8,128)S(1)}, u32[]{:S(2)}, u32[]{:S(2)}) collective-permute-start(f32[128,256]{1,0:T(8,128)S(1)} %collective-permute-done.3.right_b), channel_id=1, source_target_pairs={{0,3},{1,0},{2,1},{3,2},{4,7},{5,4},{6,5},{7,6},{8,11},{9,8},{10,9... | collective-permute-start | bytes 393224 | tf_op jit(solution)/shard_map/ppermute | solution.py:246
  11.0 2.2 %shard_map.55 = (bf16[256,256]{1,0:T(8,128)(2,1)S(1)}, bf16[256,256]{1,0:T(8,128)(2,1)S(1)}, bf16[256,512]{1,0:T(8,128)(2,1)S(1)}, bf16[256,512]{1,0:T(8,128)(2,1)S(1)}, f32[1024,256]{1,0:T(8,128)S(1)}) custom-call(s32[2]{0:T(128)S(1)} %pad_add_fusion.place, f32[256,256]{1,0:T(8,128)} %panel_t.1, f32[3,256,256]{2,1,0:T(8,128)} %tree_v.5, ...), custom_call_target="tpu_custom_call" | custom-call | flops 301989888 | bytes 1048576 | tf_op jit(solution)/shard_map/pallas_call | solution.py:256
  13.2 1.3 %shard_map.56 = (f32[256,256]{1,0:T(8,128)S(1)}, bf16[1024,256]{1,0:T(8,128)(2,1)S(1)}, bf16[1024,256]{1,0:T(8,128)(2,1)S(1)}, bf16[256,1024]{1,0:T(8,128)(2,1)S(1)}, bf16[256,1024]{1,0:T(8,128)(2,1)S(1)}) custom-call(s32[2]{0:T(128)S(1)} %pad_add_fusion.place, f32[128,256]{1,0:T(8,128)S(1)} %get-tuple-element.84.own_a, ...), custom_call_target="tpu_custom_call" | custom-call | flops 201326592 | bytes 4194304 | tf_op jit(solution)/shard_map/pallas_call | solution.py:266
  14.5 1.4 %shard_map.57 = (f32[256,128]{1,0:T(8,128)S(1)}, f32[256,128]{1,0:T(8,128)S(1)}, f32[256,256]{1,0:T(8,128)S(1)}, bf16[256,256]{1,0:T(8,128)(2,1)S(1)}, bf16[256,...) custom-call(s32[2]{0:T(128)S(1)} %pad_add_fusion.place, ...), custom_call_target="tpu_custom_call" | custom-call | flops 201326592 | bytes 2097152 | tf_op jit(solution)/shard_map/pallas_call | solution.py:275
  21.4 2.2 %collective-permute-start.25 = (f32[256,128]{1,0:T(8,128)S(1)}, f32[256,128]{1,0:T(8,128)S(1)}, u32[]{:S(2)}, u32[]{:S(2)}) collective-permute-start(f32[256,128]{1,0:T(8,128)S(1)} %shard_map.75.mine), channel_id=1, source_target_pairs={{0,8},{4,12},{8,0},{12,4},{16,24},{20,28},{24,16},{28,20},{32,40},... | collective-permute-start | bytes 393224 | tf_op jit(solution)/shard_map/ppermute | solution.py:297
  24.5 2.0 %collective-permute-start.19 = (f32[256,128]{1,0:T(8,128)S(1)}, f32[256,128]{1,0:T(8,128)S(1)}, u32[]{:S(2)}, u32[]{:S(2)}) collective-permute-start(f32[256,128]{1,0:T(8,128)S(1)} %get-tuple-element.76.mine), channel_id=1, source_target_pairs={{0,8},{4,12},{8,0},{12,4},{16,24},{20,28},{24,16},{28,20},{32,40},... | collective-permute-start | bytes 393224 | tf_op jit(solution)/shard_map/ppermute | solution.py:297
  28.0 1.9 %collective-permute-start.14 = (f32[256,128]{1,0:T(8,128)S(1)}, f32[256,128]{1,0:T(8,128)S(1)}, u32[]{:S(2)}, u32[]{:S(2)}) collective-permute-start(f32[256,128]{1,0:T(8,128)S(1)} %get-tuple-element.73.mine), channel_id=1, source_target_pairs={{0,8},{4,12},{8,0},{12,4},{16,24},{20,28},{24,16},{28,20},{32,40},... | collective-permute-start | bytes 393224 | tf_op jit(solution)/shard_map/ppermute | solution.py:297
  30.8 1.9 %collective-permute-start.12 = (f32[256,128]{1,0:T(8,128)S(1)}, f32[256,128]{1,0:T(8,128)S(1)}, u32[]{:S(2)}, u32[]{:S(2)}) collective-permute-start(f32[256,128]{1,0:T(8,128)S(1)} %get-tuple-element.72.mine), channel_id=1, source_target_pairs={{0,8},{4,12},{8,0},{12,4},{16,24},{20,28},{24,16},{28,20},{32,40},... | collective-permute-start | bytes 393224 | tf_op jit(solution)/shard_map/ppermute | solution.py:297
  32.8 1.1 %shard_map.61 = (bf16[256,512]{1,0:T(8,128)(2,1)S(1)}, bf16[256,512]{1,0:T(8,128)(2,1)S(1)}) custom-call(s32[2]{0:T(128)S(1)} %pad_add_fusion.place, f32[3,256,256]{2,1,0:T(8,128)S(1)} %copy-done.1, f32[3,256,256]{2,1,0:T(8,128)S(1)} %copy-done.2, f32[256,256]{1,0:T(8,128)S(1)} %get-tuple-element.64.after.args_0_), custom_call_target="tpu_custom_call" | custom-call | flops 201326592 | bytes 1048576 | tf_op jit(solution)/shard_map/pallas_call | solution.py:312
  33.8 1.1 %shard_map.63 = (bf16[256,512]{1,0:T(8,128)(2,1)S(1)}, bf16[256,512]{1,0:T(8,128)(2,1)S(1)}) custom-call(s32[2]{0:T(128)S(1)} %pad_add_fusion.place, f32[3,256,256]{2,1,0:T(8,128)S(1)} %copy-done.1, f32[3,256,256]{2,1,0:T(8,128)S(1)} %copy-done.2, f32[256,256]{1,0:T(8,128)S(1)} %get-tuple-element.67.after.args_1_), custom_call_target="tpu_custom_call" | custom-call | flops 201326592 | bytes 1048576 | tf_op jit(solution)/shard_map/pallas_call | solution.py:312
  35.7 3.6 %collective-permute-start.26 = (f32[256,128]{1,0:T(8,128)S(1)}, f32[256,128]{1,0:T(8,128)S(1)}, u32[]{:S(2)}, u32[]{:S(2)}) collective-permute-start(f32[256,128]{1,0:T(8,128)S(1)} %shard_map.76.mine), channel_id=1, source_target_pairs={{0,16},{4,20},{8,24},{12,28},{16,0},{20,4},{24,8},{28,12},{32,48},... | collective-permute-start | bytes 393224 | tf_op jit(solution)/shard_map/ppermute | solution.py:297
  40.7 1.7 %collective-permute-start.7 = (f32[256,128]{1,0:T(8,128)S(1)}, f32[256,128]{1,0:T(8,128)S(1)}, u32[]{:S(2)}, u32[]{:S(2)}) collective-permute-start(f32[256,128]{1,0:T(8,128)S(1)} %get-tuple-element.63.mine), channel_id=1, source_target_pairs={{0,8},{4,12},{8,0},{12,4},{16,24},{20,28},{24,16},{28,20},{32,40},... | collective-permute-start | bytes 393224 | tf_op jit(solution)/shard_map/ppermute | solution.py:297
  42.3 4.1 %collective-permute-done.12.theirs = f32[256,128]{1,0:T(8,128)S(1)} collective-permute-done((f32[256,128]{1,0:T(8,128)S(1)}, f32[256,128]{1,0:T(8,128)S(1)}, u32[]{:S(2)}, u32[]{:S(2)}) %collective-permute-start.12) | collective-permute-done | bytes 131104 | tf_op jit(solution)/shard_map/ppermute | solution.py:297
  46.4 4.0 %collective-permute-start.20 = (f32[256,128]{1,0:T(8,128)S(1)}, f32[256,128]{1,0:T(8,128)S(1)}, u32[]{:S(2)}, u32[]{:S(2)}) collective-permute-start(f32[256,128]{1,0:T(8,128)S(1)} %shard_map.72.mine), channel_id=1, source_target_pairs={{0,16},{4,20},{8,24},{12,28},{16,0},{20,4},{24,8},{28,12},{32,48},... | collective-permute-start | bytes 393224 | tf_op jit(solution)/shard_map/ppermute | solution.py:297
  50.4 2.0 %shard_map.77.args_2_ = f32[1024,1024]{1,0:T(8,128)} custom-call(f32[1024,1024]{1,0:T(8,128)S(1)} %copy-done, bf16[1024,256]{1,0:T(8,128)(2,1)S(1)} %get-tuple-element.79.yh, bf16[1024,256]{1,0:T(8,128)(2,1)S(1)} %get-tuple-element.80.yl, bf16[256,256]{1,0:T(8,128)(2,1)S(1)} %get-tuple-element.50.th, bf16[256,256]{1,0:T(8,128)(2,1)S(1)} %get-tuple-element.51.tl, ...), custom_call_target="tpu_custom_call" | custom-call | flops 1006632960 | bytes 4194304 | tf_op jit(solution)/shard_map/pallas_call | solution.py:350
  54.0 1.8 %collective-permute-done.7.theirs = f32[256,128]{1,0:T(8,128)S(1)} collective-permute-done((f32[256,128]{1,0:T(8,128)S(1)}, f32[256,128]{1,0:T(8,128)S(1)}, u32[]{:S(2)}, u32[]{:S(2)}) %collective-permute-start.7) | collective-permute-done | bytes 131104 | tf_op jit(solution)/shard_map/ppermute | solution.py:297
  55.7 1.5 %collective-permute-start.15 = (f32[256,128]{1,0:T(8,128)S(1)}, f32[256,128]{1,0:T(8,128)S(1)}, u32[]{:S(2)}, u32[]{:S(2)}) collective-permute-start(f32[256,128]{1,0:T(8,128)S(1)} %shard_map.68.mine), channel_id=1, source_target_pairs={{0,16},{4,20},{8,24},{12,28},{16,0},{20,4},{24,8},{28,12},{32,48},... | collective-permute-start | bytes 393224 | tf_op jit(solution)/shard_map/ppermute | solution.py:297
  57.6 1.6 %collective-permute-start.13 = (f32[256,128]{1,0:T(8,128)S(1)}, f32[256,128]{1,0:T(8,128)S(1)}, u32[]{:S(2)}, u32[]{:S(2)}) collective-permute-start(f32[256,128]{1,0:T(8,128)S(1)} %shard_map.67.mine), channel_id=1, source_target_pairs={{0,16},{4,20},{8,24},{12,28},{16,0},{20,4},{24,8},{28,12},{32,48},... | collective-permute-start | bytes 393224 | tf_op jit(solution)/shard_map/ppermute | solution.py:297
  59.1 1.5 %collective-permute-start.10 = (f32[256,128]{1,0:T(8,128)S(1)}, f32[256,128]{1,0:T(8,128)S(1)}, u32[]{:S(2)}, u32[]{:S(2)}) collective-permute-start(f32[256,128]{1,0:T(8,128)S(1)} %shard_map.64.mine), channel_id=1, source_target_pairs={{0,16},{4,20},{8,24},{12,28},{16,0},{20,4},{24,8},{28,12},{32,48},... | collective-permute-start | bytes 393224 | tf_op jit(solution)/shard_map/ppermute | solution.py:297
  60.6 1.5 %collective-permute-start.8 = (f32[256,128]{1,0:T(8,128)S(1)}, f32[256,128]{1,0:T(8,128)S(1)}, u32[]{:S(2)}, u32[]{:S(2)}) collective-permute-start(f32[256,128]{1,0:T(8,128)S(1)} %shard_map.62.mine), channel_id=1, source_target_pairs={{0,16},{4,20},{8,24},{12,28},{16,0},{20,4},{24,8},{28,12},{32,48},... | collective-permute-start | bytes 393224 | tf_op jit(solution)/shard_map/ppermute | solution.py:297
  62.0 2.0 %shard_map.78.whole = f32[1024,1024]{1,0:T(8,128)} custom-call(f32[1024,1024]{1,0:T(8,128)S(1)} %copy-done, bf16[1024,256]{1,0:T(8,128)(2,1)S(1)} %get-tuple-element.79.yh, bf16[1024,256]{1,0:T(8,128)(2,1)S(1)} %get-tuple-element.80.yl, bf16[256,256]{1,0:T(8,128)(2,1)S(1)} %get-tuple-element.50.th, ...), custom_call_target="tpu_custom_call", output_to_operand_aliasing={{}: (7, {})} | custom-call | flops 1006632960 | bytes 4194304 | tf_op jit(solution)/shard_map/pallas_call | solution.py:350
  64.0 1.0 %shard_map.79.whole = f32[1024,1024]{1,0:T(8,128)} custom-call(f32[256,128]{1,0:T(8,128)S(1)} %shard_map.76.mine, f32[256,128]{1,0:T(8,128)S(1)} %collective-permute-done.26.theirs, bf16[256,512]{1,0:T(8,128)(2,1)S(1)} %get-tuple-element.68.high, bf16[256,512]{1,0:T(8,128)(2,1)S(1)} %get-tuple-element.69.low, ...), custom_call_target="tpu_custom_call", output_to_operand_aliasing={{}: (4, {})} | custom-call | flops 100663296 | bytes 1048576 | tf_op jit(solution)/shard_map/pallas_call | solution.py:364
  66.1 1.0 %shard_map.81.whole = f32[1024,1024]{1,0:T(8,128)} custom-call(f32[256,128]{1,0:T(8,128)S(1)} %shard_map.72.mine, f32[256,128]{1,0:T(8,128)S(1)} %collective-permute-done.20.theirs, bf16[256,512]{1,0:T(8,128)(2,1)S(1)} %get-tuple-element.68.high, bf16[256,512]{1,0:T(8,128)(2,1)S(1)} %get-tuple-element.69.low, ...), custom_call_target="tpu_custom_call", output_to_operand_aliasing={{}: (4, {})} | custom-call | flops 100663296 | bytes 1048576 | tf_op jit(solution)/shard_map/pallas_call | solution.py:364
  67.1 7.0 %collective-permute-done.18.theirs = f32[256,128]{1,0:T(8,128)S(1)} collective-permute-done((f32[256,128]{1,0:T(8,128)S(1)}, f32[256,128]{1,0:T(8,128)S(1)}, u32[]{:S(2)}, u32[]{:S(2)}) %collective-permute-start.18) | collective-permute-done | bytes 131104 | tf_op jit(solution)/shard_map/ppermute | solution.py:297
  75.1 1.8 %collective-permute-done.15.theirs = f32[256,128]{1,0:T(8,128)S(1)} collective-permute-done((f32[256,128]{1,0:T(8,128)S(1)}, f32[256,128]{1,0:T(8,128)S(1)}, u32[]{:S(2)}, u32[]{:S(2)}) %collective-permute-start.15) | collective-permute-done | bytes 131104 | tf_op jit(solution)/shard_map/ppermute | solution.py:297
  77.9 3.2 %collective-permute-done.13.theirs = f32[256,128]{1,0:T(8,128)S(1)} collective-permute-done((f32[256,128]{1,0:T(8,128)S(1)}, f32[256,128]{1,0:T(8,128)S(1)}, u32[]{:S(2)}, u32[]{:S(2)}) %collective-permute-start.13) | collective-permute-done | bytes 131104 | tf_op jit(solution)/shard_map/ppermute | solution.py:297
  82.1 1.8 %collective-permute-done.10.theirs = f32[256,128]{1,0:T(8,128)S(1)} collective-permute-done((f32[256,128]{1,0:T(8,128)S(1)}, f32[256,128]{1,0:T(8,128)S(1)}, u32[]{:S(2)}, u32[]{:S(2)}) %collective-permute-start.10) | collective-permute-done | bytes 131104 | tf_op jit(solution)/shard_map/ppermute | solution.py:297
  84.9 1.5 %collective-permute-done.8.theirs = f32[256,128]{1,0:T(8,128)S(1)} collective-permute-done((f32[256,128]{1,0:T(8,128)S(1)}, f32[256,128]{1,0:T(8,128)S(1)}, u32[]{:S(2)}, u32[]{:S(2)}) %collective-permute-start.8) | collective-permute-done | bytes 131104 | tf_op jit(solution)/shard_map/ppermute | solution.py:297
  (62 shorter events, 20.4 us)
Async XLA Ops:
  1.0 6.7 %collective-permute-start = (f32[128,256]{1,0:T(8,128)S(1)}, f32[128,256]{1,0:T(8,128)S(1)}, u32[]{:S(2)}, u32[]{:S(2)}) collective-permute-start(f32[128,256]{1,0:T(8,128)S(1)} %get-tuple-element.84.own_a), channel_id=1, source_target_pairs={{0,1},{1,2},{2,3},{3,0},{4,5},{5,6},{6,7},{7,4},{8,9},{9,10},{10,1... | collective-permute-start | bytes 393224 | tf_op jit(solution)/shard_map/ppermute | solution.py:241
  2.6 6.4 %collective-permute-start.3 = (f32[128,256]{1,0:T(8,128)S(1)}, f32[128,256]{1,0:T(8,128)S(1)}, u32[]{:S(2)}, u32[]{:S(2)}) collective-permute-start(f32[128,256]{1,0:T(8,128)S(1)} %get-tuple-element.83.own_b), channel_id=1, source_target_pairs={{0,3},{1,0},{2,1},{3,2},{4,7},{5,4},{6,5},{7,6},{8,11},{9,8},{10,9... | collective-permute-start | bytes 393224 | tf_op jit(solution)/shard_map/ppermute | solution.py:242
  4.3 8.9 %collective-permute-start.1 = (f32[128,256]{1,0:T(8,128)S(1)}, f32[128,256]{1,0:T(8,128)S(1)}, u32[]{:S(2)}, u32[]{:S(2)}) collective-permute-start(f32[128,256]{1,0:T(8,128)S(1)} %get-tuple-element.83.own_b), channel_id=1, source_target_pairs={{0,1},{1,2},{2,3},{3,0},{4,5},{5,6},{6,7},{7,4},{8,9},{9,10},{10,1... | collective-permute-start | bytes 393224 | tf_op jit(solution)/shard_map/ppermute | solution.py:243
  4.6 8.6 %collective-permute-start.2 = (f32[128,256]{1,0:T(8,128)S(1)}, f32[128,256]{1,0:T(8,128)S(1)}, u32[]{:S(2)}, u32[]{:S(2)}) collective-permute-start(f32[128,256]{1,0:T(8,128)S(1)} %get-tuple-element.84.own_a), channel_id=1, source_target_pairs={{0,3},{1,0},{2,1},{3,2},{4,7},{5,4},{6,5},{7,6},{8,11},{9,8},{10,9... | collective-permute-start | bytes 393224 | tf_op jit(solution)/shard_map/ppermute | solution.py:244
  7.6 6.8 %collective-permute-start.4 = (f32[128,256]{1,0:T(8,128)S(1)}, f32[128,256]{1,0:T(8,128)S(1)}, u32[]{:S(2)}, u32[]{:S(2)}) collective-permute-start(f32[128,256]{1,0:T(8,128)S(1)} %collective-permute-done.left_a), channel_id=1, source_target_pairs={{0,1},{1,2},{2,3},{3,0},{4,5},{5,6},{6,7},{7,4},{8,9},{9,10},{10,1... | collective-permute-start | bytes 393224 | tf_op jit(solution)/shard_map/ppermute | solution.py:245
  8.9 5.6 %collective-permute-start.5 = (f32[128,256]{1,0:T(8,128)S(1)}, f32[128,256]{1,0:T(8,128)S(1)}, u32[]{:S(2)}, u32[]{:S(2)}) collective-permute-start(f32[128,256]{1,0:T(8,128)S(1)} %collective-permute-done.3.right_b), channel_id=1, source_target_pairs={{0,3},{1,0},{2,1},{3,2},{4,7},{5,4},{6,5},{7,6},{8,11},{9,8},{10,9... | collective-permute-start | bytes 393224 | tf_op jit(solution)/shard_map/ppermute | solution.py:246
  13.2 3.4 %copy-start = (f32[1024,1024]{1,0:T(8,128)S(1)}, f32[1024,1024]{1,0:T(8,128)}, u32[]{:S(2)}) copy-start(f32[1024,1024]{1,0:T(8,128)} %block.9) | copy-start | bytes 12582916
  17.6 6.5 %collective-permute-start.16 = (f32[256,256]{1,0:T(8,128)S(1)}, f32[256,256]{1,0:T(8,128)S(1)}, u32[]{:S(2)}, u32[]{:S(2)}) collective-permute-start(f32[256,256]{1,0:T(8,128)S(1)} %get-tuple-element.74.mine), channel_id=1, source_target_pairs={{0,4},{4,0},{8,12},{12,8},{16,20},{20,16},{24,28},{28,24},{32,36},... | collective-permute-start | bytes 786440 | tf_op jit(solution)/shard_map/ppermute | solution.py:297
  18.7 7.8 %collective-permute-start.11 = (f32[256,256]{1,0:T(8,128)S(1)}, f32[256,256]{1,0:T(8,128)S(1)}, u32[]{:S(2)}, u32[]{:S(2)}) collective-permute-start(f32[256,256]{1,0:T(8,128)S(1)} %get-tuple-element.71.mine), channel_id=1, source_target_pairs={{0,4},{4,0},{8,12},{12,8},{16,20},{20,16},{24,28},{28,24},{32,36},... | collective-permute-start | bytes 786440 | tf_op jit(solution)/shard_map/ppermute | solution.py:297
  19.3 1.7 %collective-permute-start.24 = (f32[256,128]{1,0:T(8,128)S(1)}, f32[256,128]{1,0:T(8,128)S(1)}, u32[]{:S(2)}, u32[]{:S(2)}) collective-permute-start(f32[256,128]{1,0:T(8,128)S(1)} %get-tuple-element.78.mine), channel_id=1, source_target_pairs={{0,4},{4,0},{8,12},{12,8},{16,20},{20,16},{24,28},{28,24},{32,36},... | collective-permute-start | bytes 393224 | tf_op jit(solution)/shard_map/ppermute | solution.py:297
  19.4 13.4 %copy-start.1 = (f32[3,256,256]{2,1,0:T(8,128)S(1)}, f32[3,256,256]{2,1,0:T(8,128)}, u32[]{:S(2)}) copy-start(f32[3,256,256]{2,1,0:T(8,128)} %tree_v.5) | copy-start | bytes 2359300
  19.4 13.4 %copy-start.2 = (f32[3,256,256]{2,1,0:T(8,128)S(1)}, f32[3,256,256]{2,1,0:T(8,128)}, u32[]{:S(2)}) copy-start(f32[3,256,256]{2,1,0:T(8,128)} %tree_t.5) | copy-start | bytes 2359300
  19.4 4.2 %collective-permute-start.21 = (f32[256,128]{1,0:T(8,128)S(1)}, f32[256,128]{1,0:T(8,128)S(1)}, u32[]{:S(2)}, u32[]{:S(2)}) collective-permute-start(f32[256,128]{1,0:T(8,128)S(1)} %get-tuple-element.77.mine), channel_id=1, source_target_pairs={{0,4},{4,0},{8,12},{12,8},{16,20},{20,16},{24,28},{28,24},{32,36},... | collective-permute-start | bytes 393224 | tf_op jit(solution)/shard_map/ppermute | solution.py:297
  20.8 14.8 %collective-permute-start.6 = (f32[256,256]{1,0:T(8,128)S(1)}, f32[256,256]{1,0:T(8,128)S(1)}, u32[]{:S(2)}, u32[]{:S(2)}) collective-permute-start(f32[256,256]{1,0:T(8,128)S(1)} %get-tuple-element.60.mine), channel_id=1, source_target_pairs={{0,4},{4,0},{8,12},{12,8},{16,20},{20,16},{24,28},{28,24},{32,36},... | collective-permute-start | bytes 786440 | tf_op jit(solution)/shard_map/ppermute | solution.py:297
  21.4 6.6 %collective-permute-start.25 = (f32[256,128]{1,0:T(8,128)S(1)}, f32[256,128]{1,0:T(8,128)S(1)}, u32[]{:S(2)}, u32[]{:S(2)}) collective-permute-start(f32[256,128]{1,0:T(8,128)S(1)} %shard_map.75.mine), channel_id=1, source_target_pairs={{0,8},{4,12},{8,0},{12,4},{16,24},{20,28},{24,16},{28,20},{32,40},... | collective-permute-start | bytes 393224 | tf_op jit(solution)/shard_map/ppermute | solution.py:297
  24.0 6.9 %collective-permute-start.22 = (f32[256,128]{1,0:T(8,128)S(1)}, f32[256,128]{1,0:T(8,128)S(1)}, u32[]{:S(2)}, u32[]{:S(2)}) collective-permute-start(f32[256,128]{1,0:T(8,128)S(1)} %shard_map.73.mine), channel_id=1, source_target_pairs={{0,8},{4,12},{8,0},{12,4},{16,24},{20,28},{24,16},{28,20},{32,40},... | collective-permute-start | bytes 393224 | tf_op jit(solution)/shard_map/ppermute | solution.py:297
  24.5 15.1 %collective-permute-start.19 = (f32[256,128]{1,0:T(8,128)S(1)}, f32[256,128]{1,0:T(8,128)S(1)}, u32[]{:S(2)}, u32[]{:S(2)}) collective-permute-start(f32[256,128]{1,0:T(8,128)S(1)} %get-tuple-element.76.mine), channel_id=1, source_target_pairs={{0,8},{4,12},{8,0},{12,4},{16,24},{20,28},{24,16},{28,20},{32,40},... | collective-permute-start | bytes 393224 | tf_op jit(solution)/shard_map/ppermute | solution.py:297
  26.6 13.9 %collective-permute-start.17 = (f32[256,128]{1,0:T(8,128)S(1)}, f32[256,128]{1,0:T(8,128)S(1)}, u32[]{:S(2)}, u32[]{:S(2)}) collective-permute-start(f32[256,128]{1,0:T(8,128)S(1)} %get-tuple-element.75.mine), channel_id=1, source_target_pairs={{0,8},{4,12},{8,0},{12,4},{16,24},{20,28},{24,16},{28,20},{32,40},... | collective-permute-start | bytes 393224 | tf_op jit(solution)/shard_map/ppermute | solution.py:297
  28.0 12.6 %collective-permute-start.14 = (f32[256,128]{1,0:T(8,128)S(1)}, f32[256,128]{1,0:T(8,128)S(1)}, u32[]{:S(2)}, u32[]{:S(2)}) collective-permute-start(f32[256,128]{1,0:T(8,128)S(1)} %get-tuple-element.73.mine), channel_id=1, source_target_pairs={{0,8},{4,12},{8,0},{12,4},{16,24},{20,28},{24,16},{28,20},{32,40},... | collective-permute-start | bytes 393224 | tf_op jit(solution)/shard_map/ppermute | solution.py:297
  30.8 15.5 %collective-permute-start.12 = (f32[256,128]{1,0:T(8,128)S(1)}, f32[256,128]{1,0:T(8,128)S(1)}, u32[]{:S(2)}, u32[]{:S(2)}) collective-permute-start(f32[256,128]{1,0:T(8,128)S(1)} %get-tuple-element.72.mine), channel_id=1, source_target_pairs={{0,8},{4,12},{8,0},{12,4},{16,24},{20,28},{24,16},{28,20},{32,40},... | collective-permute-start | bytes 393224 | tf_op jit(solution)/shard_map/ppermute | solution.py:297
  35.7 21.9 %collective-permute-start.26 = (f32[256,128]{1,0:T(8,128)S(1)}, f32[256,128]{1,0:T(8,128)S(1)}, u32[]{:S(2)}, u32[]{:S(2)}) collective-permute-start(f32[256,128]{1,0:T(8,128)S(1)} %shard_map.76.mine), channel_id=1, source_target_pairs={{0,16},{4,20},{8,24},{12,28},{16,0},{20,4},{24,8},{28,12},{32,48},... | collective-permute-start | bytes 393224 | tf_op jit(solution)/shard_map/ppermute | solution.py:297
  39.6 13.8 %collective-permute-start.9 = (f32[256,128]{1,0:T(8,128)S(1)}, f32[256,128]{1,0:T(8,128)S(1)}, u32[]{:S(2)}, u32[]{:S(2)}) collective-permute-start(f32[256,128]{1,0:T(8,128)S(1)} %get-tuple-element.70.mine), channel_id=1, source_target_pairs={{0,8},{4,12},{8,0},{12,4},{16,24},{20,28},{24,16},{28,20},{32,40},... | collective-permute-start | bytes 393224 | tf_op jit(solution)/shard_map/ppermute | solution.py:297
  40.4 18.7 %collective-permute-start.23 = (f32[256,128]{1,0:T(8,128)S(1)}, f32[256,128]{1,0:T(8,128)S(1)}, u32[]{:S(2)}, u32[]{:S(2)}) collective-permute-start(f32[256,128]{1,0:T(8,128)S(1)} %shard_map.74.mine), channel_id=1, source_target_pairs={{0,16},{4,20},{8,24},{12,28},{16,0},{20,4},{24,8},{28,12},{32,48},... | collective-permute-start | bytes 393224 | tf_op jit(solution)/shard_map/ppermute | solution.py:297
  40.7 15.0 %collective-permute-start.7 = (f32[256,128]{1,0:T(8,128)S(1)}, f32[256,128]{1,0:T(8,128)S(1)}, u32[]{:S(2)}, u32[]{:S(2)}) collective-permute-start(f32[256,128]{1,0:T(8,128)S(1)} %get-tuple-element.63.mine), channel_id=1, source_target_pairs={{0,8},{4,12},{8,0},{12,4},{16,24},{20,28},{24,16},{28,20},{32,40},... | collective-permute-start | bytes 393224 | tf_op jit(solution)/shard_map/ppermute | solution.py:297
  46.4 14.2 %collective-permute-start.20 = (f32[256,128]{1,0:T(8,128)S(1)}, f32[256,128]{1,0:T(8,128)S(1)}, u32[]{:S(2)}, u32[]{:S(2)}) collective-permute-start(f32[256,128]{1,0:T(8,128)S(1)} %shard_map.72.mine), channel_id=1, source_target_pairs={{0,16},{4,20},{8,24},{12,28},{16,0},{20,4},{24,8},{28,12},{32,48},... | collective-permute-start | bytes 393224 | tf_op jit(solution)/shard_map/ppermute | solution.py:297
  53.5 20.6 %collective-permute-start.18 = (f32[256,128]{1,0:T(8,128)S(1)}, f32[256,128]{1,0:T(8,128)S(1)}, u32[]{:S(2)}, u32[]{:S(2)}) collective-permute-start(f32[256,128]{1,0:T(8,128)S(1)} %shard_map.71.mine), channel_id=1, source_target_pairs={{0,16},{4,20},{8,24},{12,28},{16,0},{20,4},{24,8},{28,12},{32,48},... | collective-permute-start | bytes 393224 | tf_op jit(solution)/shard_map/ppermute | solution.py:297
  55.7 21.2 %collective-permute-start.15 = (f32[256,128]{1,0:T(8,128)S(1)}, f32[256,128]{1,0:T(8,128)S(1)}, u32[]{:S(2)}, u32[]{:S(2)}) collective-permute-start(f32[256,128]{1,0:T(8,128)S(1)} %shard_map.68.mine), channel_id=1, source_target_pairs={{0,16},{4,20},{8,24},{12,28},{16,0},{20,4},{24,8},{28,12},{32,48},... | collective-permute-start | bytes 393224 | tf_op jit(solution)/shard_map/ppermute | solution.py:297
  57.6 23.5 %collective-permute-start.13 = (f32[256,128]{1,0:T(8,128)S(1)}, f32[256,128]{1,0:T(8,128)S(1)}, u32[]{:S(2)}, u32[]{:S(2)}) collective-permute-start(f32[256,128]{1,0:T(8,128)S(1)} %shard_map.67.mine), channel_id=1, source_target_pairs={{0,16},{4,20},{8,24},{12,28},{16,0},{20,4},{24,8},{28,12},{32,48},... | collective-permute-start | bytes 393224 | tf_op jit(solution)/shard_map/ppermute | solution.py:297
  59.1 24.8 %collective-permute-start.10 = (f32[256,128]{1,0:T(8,128)S(1)}, f32[256,128]{1,0:T(8,128)S(1)}, u32[]{:S(2)}, u32[]{:S(2)}) collective-permute-start(f32[256,128]{1,0:T(8,128)S(1)} %shard_map.64.mine), channel_id=1, source_target_pairs={{0,16},{4,20},{8,24},{12,28},{16,0},{20,4},{24,8},{28,12},{32,48},... | collective-permute-start | bytes 393224 | tf_op jit(solution)/shard_map/ppermute | solution.py:297
  60.6 25.9 %collective-permute-start.8 = (f32[256,128]{1,0:T(8,128)S(1)}, f32[256,128]{1,0:T(8,128)S(1)}, u32[]{:S(2)}, u32[]{:S(2)}) collective-permute-start(f32[256,128]{1,0:T(8,128)S(1)} %shard_map.62.mine), channel_id=1, source_target_pairs={{0,16},{4,20},{8,24},{12,28},{16,0},{20,4},{24,8},{28,12},{32,48},... | collective-permute-start | bytes 393224 | tf_op jit(solution)/shard_map/ppermute | solution.py:297

commit v8 on v7

--- a/solution.py
+++ b/solution.py
@@ -11,6 +11,7 @@
 
 UNITS = ((128,), (128,), (128, 128), (128, 128), (128, 128))
 STEPS = ((0, 1), (2,), (3,), (4,))
+ENDS = ((0, 1, 2, 3), (4, 5), (6,), (7,))
 F32 = jnp.float32
 BF16 = jnp.bfloat16
 VMEM = pl.BlockSpec(memory_space=pltpu.VMEM)
@@ -99,7 +100,7 @@
     return split(rows), split(rows.T)
 
 
-def early_kernel(place, own_a, own_b, left_a, left_b, right_a, right_b, block, partial, yh, yl, fh, fl):
+def early_kernel(place, own_a, own_b, left_a, left_b, right_a, right_b, block, th, tl, partial, gh, gl, yh, yl, fh, fl):
     col = place[1]
     size = own_a.shape[0] + own_b.shape[0]
     count = block.shape[0] // size
@@ -116,6 +117,10 @@
         total = term if total is None else total + term
     partial[...] = total
 
+    @pl.when(lax.rem(col + count // 2, count) != 0)
+    def _():
+        gh[...], gl[...] = split(dot3((yh[:size, :], yl[:size, :]), (th[...], tl[...])))
+
 
 def store_parts(value, parts):
     first = 0
@@ -124,19 +129,25 @@
         first += part.shape[1]
 
 
-def first_kernel(place, partial, opp_a, opp_b, block, th, tl, yh, yl, *outs):
+def first_kernel(place, partial, opp_a, opp_b, block, th, tl, old_gh, old_gl, *outs):
     tops, (proj, gh, gl, oh, ol, ph, plow) = outs[:-7], outs[-7:]
     size = opp_a.shape[0] + opp_b.shape[0]
     width = partial.shape[1]
     start = opposite_rows(place[1], size, block.shape[0] // size)
     rows = jnp.concatenate([opp_a[...], opp_b[...]], axis=0)
     straight, flipped = both_ways(rows, start)
-    upper = [jnp.where(start == 0, new, old[:size, :]) for new, old in zip(straight, (yh, yl))]
-    gain = split(dot3(upper, (th[...], tl[...])))
+
+    @pl.when(start == 0)
+    def _():
+        gh[...], gl[...] = split(dot3(straight, (th[...], tl[...])))
+
+    @pl.when(start != 0)
+    def _():
+        gh[...], gl[...] = old_gh[...], old_gl[...]
+
     value = partial[...] + dot3(flipped, split(block[pl.ds(start, size), :width]))
-    store_parts(block[:size, :width] - dot3(gain, split(value)), tops)
+    store_parts(block[:size, :width] - dot3((gh[...], gl[...]), split(value)), tops)
     proj[...] = value
-    gh[...], gl[...] = gain
     oh[...], ol[...] = straight
     ph[...], plow[...] = flipped
 
@@ -190,12 +201,21 @@
     store_parts(mixed(mine, theirs, high, low), parts)
 
 
-def final_kernel(first, mine, theirs, high, low, whole, out, slot, sem):
-    del whole
-    slot[...] = mixed(mine, theirs, high, low)
-    copy = pltpu.make_async_copy(slot, out.at[pl.ds(0, slot.shape[0]), pl.ds(first, slot.shape[1])], sem)
-    copy.start()
-    copy.wait()
+def final_kernel(first, count, high, low, *args):
+    pieces, (out, slots, sems) = args[: 2 * count], args[-3:]
+    half, w = slots.shape[2:]
+    copies = []
+    for k in range(count):
+        mine, theirs = pieces[2 * k : 2 * k + 2]
+        both = split(jnp.concatenate([mine[...], theirs[...]], axis=0))
+        for i in range(2):
+            rows = slice(i * half, (i + 1) * half)
+            slots[k, i] = mine[rows, :] - dot3((high[rows, :], low[rows, :]), both)
+            target = out.at[pl.ds(i * half, half), pl.ds(first + k * w, w)]
+            copies.append(pltpu.make_async_copy(slots.at[k, i], target, sems.at[k, i]))
+            copies[-1].start()
+    for copy in copies:
+        copy.wait()
 
 
 def shaped(shape, dtype=F32):
@@ -263,14 +283,14 @@
         cost=(3 * cube, 1 << 20),
     )(place, fixed(panel_t), fixed(tree_v), fixed(tree_t), fixed(trailing))
 
-    partial, yh, yl, fh, fl = call(
+    partial, gh, gl, yh, yl, fh, fl = call(
         early_kernel,
-        out_shape=[shaped((width, w)), tall, tall, wide, wide],
-        in_specs=[SMEM] + [VMEM] * 7,
-        out_specs=[VMEM] * 5,
+        out_shape=[shaped((width, w)), square, square, tall, tall, wide, wide],
+        in_specs=[SMEM] + [VMEM] * 9,
+        out_specs=[VMEM] * 7,
         mib=16,
         cost=(2 * cube, 4 << 20),
-    )(place, own_a, own_b, left_a, left_b, right_a, right_b, block)
+    )(place, own_a, own_b, left_a, left_b, right_a, right_b, block, th, tl)
 
     outs = call(
         first_kernel,
@@ -279,7 +299,7 @@
         out_specs=[VMEM] * (7 + len(STEPS[0])),
         mib=16,
         cost=(2 * cube, 2 << 20),
-    )(place, partial, opp_a, opp_b, block, th, tl, yh, yl)
+    )(place, partial, opp_a, opp_b, block, th, tl, gh, gl)
     raw, (proj, gh, gl, *opposite) = list(outs[:-7]), outs[-7:]
     projs = [proj]
 
@@ -360,17 +380,22 @@
         )
     out = out[0]
 
-    for k, (first, w) in enumerate(chunks):
+    for group in ENDS:
+        first, w = chunks[group[0]]
+        n = len(group)
+        pieces = []
+        for k in group:
+            pieces += [tops[k], swap(level, tops[k])]
         out = call(
-            functools.partial(final_kernel, first),
+            functools.partial(final_kernel, first, n),
             out_shape=shaped((rows, columns)),
-            in_specs=[VMEM] * 4 + [HBM],
+            in_specs=[VMEM] * (2 + 2 * n) + [HBM],
             out_specs=HBM,
-            scratch_shapes=[pltpu.VMEM((width, w), F32), pltpu.SemaphoreType.DMA],
-            input_output_aliases={4: 0},
+            scratch_shapes=[pltpu.VMEM((n, 2, width // 2, w), F32), pltpu.SemaphoreType.DMA((n, 2))],
+            input_output_aliases={2 + 2 * n: 0},
             mib=8,
-            cost=(2 * cube * w // width, 1 << 20),
-        )(tops[k], swap(level, tops[k]), *mixes[2 * level :], out)
+            cost=(2 * cube * n * w // width, 1 << 20),
+        )(*mixes[2 * level :], *pieces, out)
     return out
 
 

time: 88.9 us -> 88.6 us (level)
  Pallas kernels: 27.6 us -> 24.6 us
  starting transfers between devices: 35.3 us -> 37.9 us
    pallas_call x9 -> x5, Pallas kernels: 9.46 us -> 6.46 us  [the longest x4 4.93 us: update(): call(functools.partial(final_kernel, first, n), out_shape=shaped((rows, c...]
    ppermute x21, starting transfers between devices: 25.5 us -> 28.1 us  [swap(): return lax.ppermute(values, 'row', route)]
  transfers between devices with their start and end apart: 27 -> 27, of which waited for: 11 -> 9; matrix products, arithmetic and copies ran while one was open for 0% -> 0% of each run, Pallas kernels for 27% -> 22%
where the time goes in v8:
time: 88.6 us; the launch traced here: 87.8 us
  starting transfers between devices  37.9 us (43%)
  Pallas kernels  24.6 us (28%)
  waiting for transfers between devices  23.8 us (27%)
  local copies, waits for them, and re-layouts  1 us (1%)
    ppermute x21, starting transfers between devices, swap(): return lax.ppermute(values, 'row', route)  28.1 us
    ppermute x21, waiting for transfers between devices, swap(): return lax.ppermute(values, 'row', route)  23.7 us
    pallas_call x4, Pallas kernels, update(): call(functools.partial(final_kernel, first, n), out_shape=shaped((rows, c...  4.93 us
    pallas_call x13, Pallas kernels, combine(): call(level_kernel, out_shape=[shaped((width, w)) for w in widths], in_spe...  4.77 us
    pallas_call x2, Pallas kernels, update(): call(functools.partial(rest_kernel, first), out_shape=shaped((rows, colum...  3.92 us
    pallas_call x3, Pallas kernels, update(): call(functools.partial(next_kernel, slice(first, first + w)), out_shape=[...  3.01 us
    ppermute x1, starting transfers between devices, update(): right_a = lax.ppermute(own_a, 'col', backward)  2.96 us
    pallas_call x1, Pallas kernels, update(): call(prepare_kernel, out_shape=[square, square, mix, mix, shaped((rows, w...  2.23 us
  transfers between devices with their start and end apart: 27, of which 9 were waited for; matrix products, arithmetic and copies ran while one was open for 0% of the time, Pallas kernels for 22%

profile of v8, /device:TPU:8, one launch (start us, length us, event | category | flops | bytes accessed | tf_op | source)
XLA Modules:
  0.0 87.8 jit_solution(15043230579113331070)
XLA Ops:
  1.0 1.6 %collective-permute-start = (f32[128,256]{1,0:T(8,128)S(1)}, f32[128,256]{1,0:T(8,128)S(1)}, u32[]{:S(2)}, u32[]{:S(2)}) collective-permute-start(f32[128,256]{1,0:T(8,128)S(1)} %get-tuple-element.88.own_a), channel_id=1, source_target_pairs={{0,1},{1,2},{2,3},{3,0},{4,5},{5,6},{6,7},{7,4},{8,9},{9,10},{10,1... | collective-permute-start | bytes 393224 | tf_op jit(solution)/shard_map/ppermute | solution.py:261
  2.6 1.7 %collective-permute-start.3 = (f32[128,256]{1,0:T(8,128)S(1)}, f32[128,256]{1,0:T(8,128)S(1)}, u32[]{:S(2)}, u32[]{:S(2)}) collective-permute-start(f32[128,256]{1,0:T(8,128)S(1)} %get-tuple-element.87.own_b), channel_id=1, source_target_pairs={{0,3},{1,0},{2,1},{3,2},{4,7},{5,4},{6,5},{7,6},{8,11},{9,8},{10,9... | collective-permute-start | bytes 393224 | tf_op jit(solution)/shard_map/ppermute | solution.py:262
  4.6 3.0 %collective-permute-start.2 = (f32[128,256]{1,0:T(8,128)S(1)}, f32[128,256]{1,0:T(8,128)S(1)}, u32[]{:S(2)}, u32[]{:S(2)}) collective-permute-start(f32[128,256]{1,0:T(8,128)S(1)} %get-tuple-element.88.own_a), channel_id=1, source_target_pairs={{0,3},{1,0},{2,1},{3,2},{4,7},{5,4},{6,5},{7,6},{8,11},{9,8},{10,9... | collective-permute-start | bytes 393224 | tf_op jit(solution)/shard_map/ppermute | solution.py:264
  7.6 1.3 %collective-permute-start.4 = (f32[128,256]{1,0:T(8,128)S(1)}, f32[128,256]{1,0:T(8,128)S(1)}, u32[]{:S(2)}, u32[]{:S(2)}) collective-permute-start(f32[128,256]{1,0:T(8,128)S(1)} %collective-permute-done.left_a), channel_id=1, source_target_pairs={{0,1},{1,2},{2,3},{3,0},{4,5},{5,6},{6,7},{7,4},{8,9},{9,10},{10,1... | collective-permute-start | bytes 393224 | tf_op jit(solution)/shard_map/ppermute | solution.py:265
  8.9 2.0 %collective-permute-start.5 = (f32[128,256]{1,0:T(8,128)S(1)}, f32[128,256]{1,0:T(8,128)S(1)}, u32[]{:S(2)}, u32[]{:S(2)}) collective-permute-start(f32[128,256]{1,0:T(8,128)S(1)} %collective-permute-done.3.right_b), channel_id=1, source_target_pairs={{0,3},{1,0},{2,1},{3,2},{4,7},{5,4},{6,5},{7,6},{8,11},{9,8},{10,9... | collective-permute-start | bytes 393224 | tf_op jit(solution)/shard_map/ppermute | solution.py:266
  11.0 2.2 %shard_map.55 = (bf16[256,256]{1,0:T(8,128)(2,1)S(1)}, bf16[256,256]{1,0:T(8,128)(2,1)S(1)}, bf16[256,512]{1,0:T(8,128)(2,1)S(1)}, bf16[256,512]{1,0:T(8,128)(2,1)S(1)}, f32[1024,256]{1,0:T(8,128)S(1)}) custom-call(s32[2]{0:T(128)S(1)} %pad_add_fusion.place, f32[256,256]{1,0:T(8,128)} %panel_t.1, f32[3,256,256]{2,1,0:T(8,128)} %tree_v.5, ...), custom_call_target="tpu_custom_call" | custom-call | flops 301989888 | bytes 1048576 | tf_op jit(solution)/shard_map/pallas_call | solution.py:276
  13.2 1.5 %shard_map.56 = (f32[256,256]{1,0:T(8,128)S(1)}, bf16[256,256]{1,0:T(8,128)(2,1)S(1)}, bf16[256,256]{1,0:T(8,128)(2,1)S(1)}, bf16[1024,256]{1,0:T(8,128)(2,1)S(1...) custom-call(s32[2]{0:T(128)S(1)} %pad_add_fusion.place, ...), custom_call_target="tpu_custom_call" | custom-call | flops 201326592 | bytes 4194304 | tf_op jit(solution)/shard_map/pallas_call | solution.py:286
  14.8 1.4 %shard_map.57 = (f32[256,128]{1,0:T(8,128)S(1)}, f32[256,128]{1,0:T(8,128)S(1)}, f32[256,256]{1,0:T(8,128)S(1)}, bf16[256,256]{1,0:T(8,128)(2,1)S(1)}, bf16[256,...) custom-call(s32[2]{0:T(128)S(1)} %pad_add_fusion.place, ...), custom_call_target="tpu_custom_call" | custom-call | flops 201326592 | bytes 2097152 | tf_op jit(solution)/shard_map/pallas_call | solution.py:295
  21.8 2.0 %collective-permute-start.20 = (f32[256,128]{1,0:T(8,128)S(1)}, f32[256,128]{1,0:T(8,128)S(1)}, u32[]{:S(2)}, u32[]{:S(2)}) collective-permute-start(f32[256,128]{1,0:T(8,128)S(1)} %shard_map.71.mine), channel_id=1, source_target_pairs={{0,8},{4,12},{8,0},{12,4},{16,24},{20,28},{24,16},{28,20},{32,40},... | collective-permute-start | bytes 393224 | tf_op jit(solution)/shard_map/ppermute | solution.py:317
  25.3 1.5 %collective-permute-start.25 = (f32[256,128]{1,0:T(8,128)S(1)}, f32[256,128]{1,0:T(8,128)S(1)}, u32[]{:S(2)}, u32[]{:S(2)}) collective-permute-start(f32[256,128]{1,0:T(8,128)S(1)} %get-tuple-element.82.mine), channel_id=1, source_target_pairs={{0,8},{4,12},{8,0},{12,4},{16,24},{20,28},{24,16},{28,20},{32,40},... | collective-permute-start | bytes 393224 | tf_op jit(solution)/shard_map/ppermute | solution.py:317
  28.3 1.9 %collective-permute-start.14 = (f32[256,128]{1,0:T(8,128)S(1)}, f32[256,128]{1,0:T(8,128)S(1)}, u32[]{:S(2)}, u32[]{:S(2)}) collective-permute-start(f32[256,128]{1,0:T(8,128)S(1)} %get-tuple-element.77.mine), channel_id=1, source_target_pairs={{0,8},{4,12},{8,0},{12,4},{16,24},{20,28},{24,16},{28,20},{32,40},... | collective-permute-start | bytes 393224 | tf_op jit(solution)/shard_map/ppermute | solution.py:317
  30.3 1.1 %shard_map.62 = (bf16[256,512]{1,0:T(8,128)(2,1)S(1)}, bf16[256,512]{1,0:T(8,128)(2,1)S(1)}) custom-call(s32[2]{0:T(128)S(1)} %pad_add_fusion.place, f32[3,256,256]{2,1,0:T(8,128)S(1)} %copy-done.1, f32[3,256,256]{2,1,0:T(8,128)S(1)} %copy-done.2, f32[256,256]{1,0:T(8,128)S(1)} %get-tuple-element.71.after.args_0_), custom_call_target="tpu_custom_call" | custom-call | flops 201326592 | bytes 1048576 | tf_op jit(solution)/shard_map/pallas_call | solution.py:332
  31.4 1.1 %shard_map.60 = (bf16[256,512]{1,0:T(8,128)(2,1)S(1)}, bf16[256,512]{1,0:T(8,128)(2,1)S(1)}) custom-call(s32[2]{0:T(128)S(1)} %pad_add_fusion.place, f32[3,256,256]{2,1,0:T(8,128)S(1)} %copy-done.1, f32[3,256,256]{2,1,0:T(8,128)S(1)} %copy-done.2, f32[256,256]{1,0:T(8,128)S(1)} %get-tuple-element.64.after.args_1_), custom_call_target="tpu_custom_call" | custom-call | flops 201326592 | bytes 1048576 | tf_op jit(solution)/shard_map/pallas_call | solution.py:332
  32.8 2.2 %collective-permute-start.9 = (f32[256,128]{1,0:T(8,128)S(1)}, f32[256,128]{1,0:T(8,128)S(1)}, u32[]{:S(2)}, u32[]{:S(2)}) collective-permute-start(f32[256,128]{1,0:T(8,128)S(1)} %get-tuple-element.74.mine), channel_id=1, source_target_pairs={{0,8},{4,12},{8,0},{12,4},{16,24},{20,28},{24,16},{28,20},{32,40},... | collective-permute-start | bytes 393224 | tf_op jit(solution)/shard_map/ppermute | solution.py:317
  35.8 3.6 %collective-permute-start.21 = (f32[256,128]{1,0:T(8,128)S(1)}, f32[256,128]{1,0:T(8,128)S(1)}, u32[]{:S(2)}, u32[]{:S(2)}) collective-permute-start(f32[256,128]{1,0:T(8,128)S(1)} %shard_map.72.args_2_), channel_id=1, source_target_pairs={{0,16},{4,20},{8,24},{12,28},{16,0},{20,4},{24,8},{28,12},{32,48},... | collective-permute-start | bytes 393224 | tf_op jit(solution)/shard_map/ppermute | solution.py:317
  40.9 2.4 %collective-permute-start.7 = (f32[256,128]{1,0:T(8,128)S(1)}, f32[256,128]{1,0:T(8,128)S(1)}, u32[]{:S(2)}, u32[]{:S(2)}) collective-permute-start(f32[256,128]{1,0:T(8,128)S(1)} %get-tuple-element.70.mine), channel_id=1, source_target_pairs={{0,8},{4,12},{8,0},{12,4},{16,24},{20,28},{24,16},{28,20},{32,40},... | collective-permute-start | bytes 393224 | tf_op jit(solution)/shard_map/ppermute | solution.py:317
  43.3 4.6 %collective-permute-done.12.theirs = f32[256,128]{1,0:T(8,128)S(1)} collective-permute-done((f32[256,128]{1,0:T(8,128)S(1)}, f32[256,128]{1,0:T(8,128)S(1)}, u32[]{:S(2)}, u32[]{:S(2)}) %collective-permute-start.12) | collective-permute-done | bytes 131104 | tf_op jit(solution)/shard_map/ppermute | solution.py:317
  47.9 2.3 %collective-permute-start.26 = (f32[256,128]{1,0:T(8,128)S(1)}, f32[256,128]{1,0:T(8,128)S(1)}, u32[]{:S(2)}, u32[]{:S(2)}) collective-permute-start(f32[256,128]{1,0:T(8,128)S(1)} %shard_map.76.args_6_), channel_id=1, source_target_pairs={{0,16},{4,20},{8,24},{12,28},{16,0},{20,4},{24,8},{28,12},{32,48},... | collective-permute-start | bytes 393224 | tf_op jit(solution)/shard_map/ppermute | solution.py:317
  50.3 2.0 %shard_map.77.args_2_ = f32[1024,1024]{1,0:T(8,128)} custom-call(f32[1024,1024]{1,0:T(8,128)S(1)} %copy-done, bf16[1024,256]{1,0:T(8,128)(2,1)S(1)} %get-tuple-element.83.yh, bf16[1024,256]{1,0:T(8,128)(2,1)S(1)} %get-tuple-element.84.yl, bf16[256,256]{1,0:T(8,128)(2,1)S(1)} %get-tuple-element.47.th, bf16[256,256]{1,0:T(8,128)(2,1)S(1)} %get-tuple-element.48.tl, ...), custom_call_target="tpu_custom_call" | custom-call | flops 1006632960 | bytes 4194304 | tf_op jit(solution)/shard_map/pallas_call | solution.py:370
  52.6 2.3 %collective-permute-start.24 = (f32[256,128]{1,0:T(8,128)S(1)}, f32[256,128]{1,0:T(8,128)S(1)}, u32[]{:S(2)}, u32[]{:S(2)}) collective-permute-start(f32[256,128]{1,0:T(8,128)S(1)} %shard_map.75.args_4_), channel_id=1, source_target_pairs={{0,16},{4,20},{8,24},{12,28},{16,0},{20,4},{24,8},{28,12},{32,48},... | collective-permute-start | bytes 393224 | tf_op jit(solution)/shard_map/ppermute | solution.py:317
  56.0 1.3 %collective-permute-start.15 = (f32[256,128]{1,0:T(8,128)S(1)}, f32[256,128]{1,0:T(8,128)S(1)}, u32[]{:S(2)}, u32[]{:S(2)}) collective-permute-start(f32[256,128]{1,0:T(8,128)S(1)} %shard_map.68.args_2_), channel_id=1, source_target_pairs={{0,16},{4,20},{8,24},{12,28},{16,0},{20,4},{24,8},{28,12},{32,48},... | collective-permute-start | bytes 393224 | tf_op jit(solution)/shard_map/ppermute | solution.py:317
  57.7 1.8 %collective-permute-start.13 = (f32[256,128]{1,0:T(8,128)S(1)}, f32[256,128]{1,0:T(8,128)S(1)}, u32[]{:S(2)}, u32[]{:S(2)}) collective-permute-start(f32[256,128]{1,0:T(8,128)S(1)} %shard_map.67.args_0_), channel_id=1, source_target_pairs={{0,16},{4,20},{8,24},{12,28},{16,0},{20,4},{24,8},{28,12},{32,48},... | collective-permute-start | bytes 393224 | tf_op jit(solution)/shard_map/ppermute | solution.py:317
  59.5 1.2 %collective-permute-start.10 = (f32[256,128]{1,0:T(8,128)S(1)}, f32[256,128]{1,0:T(8,128)S(1)}, u32[]{:S(2)}, u32[]{:S(2)}) collective-permute-start(f32[256,128]{1,0:T(8,128)S(1)} %shard_map.64.args_0_), channel_id=1, source_target_pairs={{0,16},{4,20},{8,24},{12,28},{16,0},{20,4},{24,8},{28,12},{32,48},... | collective-permute-start | bytes 393224 | tf_op jit(solution)/shard_map/ppermute | solution.py:317
  60.7 1.7 %collective-permute-start.8 = (f32[256,128]{1,0:T(8,128)S(1)}, f32[256,128]{1,0:T(8,128)S(1)}, u32[]{:S(2)}, u32[]{:S(2)}) collective-permute-start(f32[256,128]{1,0:T(8,128)S(1)} %shard_map.63.args_0_), channel_id=1, source_target_pairs={{0,16},{4,20},{8,24},{12,28},{16,0},{20,4},{24,8},{28,12},{32,48},... | collective-permute-start | bytes 393224 | tf_op jit(solution)/shard_map/ppermute | solution.py:317
  62.4 2.0 %shard_map.78.args_8_ = f32[1024,1024]{1,0:T(8,128)} custom-call(f32[1024,1024]{1,0:T(8,128)S(1)} %copy-done, bf16[1024,256]{1,0:T(8,128)(2,1)S(1)} %get-tuple-element.83.yh, bf16[1024,256]{1,0:T(8,128)(2,1)S(1)} %get-tuple-element.84.yl, bf16[256,256]{1,0:T(8,128)(2,1)S(1)} %get-tuple-element.47.th, ...), custom_call_target="tpu_custom_call", output_to_operand_aliasing={{}: (7, {})} | custom-call | flops 1006632960 | bytes 4194304 | tf_op jit(solution)/shard_map/pallas_call | solution.py:370
  64.4 9.7 %collective-permute-done.24.args_5_ = f32[256,128]{1,0:T(8,128)S(1)} collective-permute-done((f32[256,128]{1,0:T(8,128)S(1)}, f32[256,128]{1,0:T(8,128)S(1)}, u32[]{:S(2)}, u32[]{:S(2)}) %collective-permute-start.24) | collective-permute-done | bytes 131104 | tf_op jit(solution)/shard_map/ppermute | solution.py:317
  74.1 1.7 %shard_map.79.args_4_ = f32[1024,1024]{1,0:T(8,128)} custom-call(bf16[256,512]{1,0:T(8,128)(2,1)S(1)} %get-tuple-element.65.high, bf16[256,512]{1,0:T(8,128)(2,1)S(1)} %get-tuple-element.66.low, f32[256,128]{1,0:T(8,128)S(1)} %shard_map.70.args_0_, f32[256,128]{1,0:T(8,128)S(1)} %collective-permute-done.18.args_1_, ...), custom_call_target="tpu_custom_call", output_to_operand_aliasing={{}: (10, {})} | custom-call | flops 402653184 | bytes 1048576 | tf_op jit(solution)/shard_map/pallas_call | solution.py:389
  75.8 1.1 %collective-permute-done.15.args_3_ = f32[256,128]{1,0:T(8,128)S(1)} collective-permute-done((f32[256,128]{1,0:T(8,128)S(1)}, f32[256,128]{1,0:T(8,128)S(1)}, u32[]{:S(2)}, u32[]{:S(2)}) %collective-permute-start.15) | collective-permute-done | bytes 131104 | tf_op jit(solution)/shard_map/ppermute | solution.py:317
  76.9 4.2 %collective-permute-done.13.args_1_ = f32[256,128]{1,0:T(8,128)S(1)} collective-permute-done((f32[256,128]{1,0:T(8,128)S(1)}, f32[256,128]{1,0:T(8,128)S(1)}, u32[]{:S(2)}, u32[]{:S(2)}) %collective-permute-start.13) | collective-permute-done | bytes 131104 | tf_op jit(solution)/shard_map/ppermute | solution.py:317
  81.1 1.2 %shard_map.80.args_2_ = f32[1024,1024]{1,0:T(8,128)} custom-call(bf16[256,512]{1,0:T(8,128)(2,1)S(1)} %get-tuple-element.65.high, bf16[256,512]{1,0:T(8,128)(2,1)S(1)} %get-tuple-element.66.low, f32[256,128]{1,0:T(8,128)S(1)} %shard_map.67.args_0_, f32[256,128]{1,0:T(8,128)S(1)} %collective-permute-done.13.args_1_, ...), custom_call_target="tpu_custom_call", output_to_operand_aliasing={{}: (6, {})} | custom-call | flops 201326592 | bytes 1048576 | tf_op jit(solution)/shard_map/pallas_call | solution.py:389
  82.3 1.6 %collective-permute-done.10.args_1_ = f32[256,128]{1,0:T(8,128)S(1)} collective-permute-done((f32[256,128]{1,0:T(8,128)S(1)}, f32[256,128]{1,0:T(8,128)S(1)}, u32[]{:S(2)}, u32[]{:S(2)}) %collective-permute-start.10) | collective-permute-done | bytes 131104 | tf_op jit(solution)/shard_map/ppermute | solution.py:317
  84.9 1.7 %collective-permute-done.8.args_1_ = f32[256,128]{1,0:T(8,128)S(1)} collective-permute-done((f32[256,128]{1,0:T(8,128)S(1)}, f32[256,128]{1,0:T(8,128)S(1)}, u32[]{:S(2)}, u32[]{:S(2)}) %collective-permute-start.8) | collective-permute-done | bytes 131104 | tf_op jit(solution)/shard_map/ppermute | solution.py:317
  (58 shorter events, 16.5 us)
Async XLA Ops:
  1.0 6.7 %collective-permute-start = (f32[128,256]{1,0:T(8,128)S(1)}, f32[128,256]{1,0:T(8,128)S(1)}, u32[]{:S(2)}, u32[]{:S(2)}) collective-permute-start(f32[128,256]{1,0:T(8,128)S(1)} %get-tuple-element.88.own_a), channel_id=1, source_target_pairs={{0,1},{1,2},{2,3},{3,0},{4,5},{5,6},{6,7},{7,4},{8,9},{9,10},{10,1... | collective-permute-start | bytes 393224 | tf_op jit(solution)/shard_map/ppermute | solution.py:261
  2.6 6.4 %collective-permute-start.3 = (f32[128,256]{1,0:T(8,128)S(1)}, f32[128,256]{1,0:T(8,128)S(1)}, u32[]{:S(2)}, u32[]{:S(2)}) collective-permute-start(f32[128,256]{1,0:T(8,128)S(1)} %get-tuple-element.87.own_b), channel_id=1, source_target_pairs={{0,3},{1,0},{2,1},{3,2},{4,7},{5,4},{6,5},{7,6},{8,11},{9,8},{10,9... | collective-permute-start | bytes 393224 | tf_op jit(solution)/shard_map/ppermute | solution.py:262
  4.3 8.9 %collective-permute-start.1 = (f32[128,256]{1,0:T(8,128)S(1)}, f32[128,256]{1,0:T(8,128)S(1)}, u32[]{:S(2)}, u32[]{:S(2)}) collective-permute-start(f32[128,256]{1,0:T(8,128)S(1)} %get-tuple-element.87.own_b), channel_id=1, source_target_pairs={{0,1},{1,2},{2,3},{3,0},{4,5},{5,6},{6,7},{7,4},{8,9},{9,10},{10,1... | collective-permute-start | bytes 393224 | tf_op jit(solution)/shard_map/ppermute | solution.py:263
  4.6 8.6 %collective-permute-start.2 = (f32[128,256]{1,0:T(8,128)S(1)}, f32[128,256]{1,0:T(8,128)S(1)}, u32[]{:S(2)}, u32[]{:S(2)}) collective-permute-start(f32[128,256]{1,0:T(8,128)S(1)} %get-tuple-element.88.own_a), channel_id=1, source_target_pairs={{0,3},{1,0},{2,1},{3,2},{4,7},{5,4},{6,5},{7,6},{8,11},{9,8},{10,9... | collective-permute-start | bytes 393224 | tf_op jit(solution)/shard_map/ppermute | solution.py:264
  7.6 7.1 %collective-permute-start.4 = (f32[128,256]{1,0:T(8,128)S(1)}, f32[128,256]{1,0:T(8,128)S(1)}, u32[]{:S(2)}, u32[]{:S(2)}) collective-permute-start(f32[128,256]{1,0:T(8,128)S(1)} %collective-permute-done.left_a), channel_id=1, source_target_pairs={{0,1},{1,2},{2,3},{3,0},{4,5},{5,6},{6,7},{7,4},{8,9},{9,10},{10,1... | collective-permute-start | bytes 393224 | tf_op jit(solution)/shard_map/ppermute | solution.py:265
  8.9 5.9 %collective-permute-start.5 = (f32[128,256]{1,0:T(8,128)S(1)}, f32[128,256]{1,0:T(8,128)S(1)}, u32[]{:S(2)}, u32[]{:S(2)}) collective-permute-start(f32[128,256]{1,0:T(8,128)S(1)} %collective-permute-done.3.right_b), channel_id=1, source_target_pairs={{0,3},{1,0},{2,1},{3,2},{4,7},{5,4},{6,5},{7,6},{8,11},{9,8},{10,9... | collective-permute-start | bytes 393224 | tf_op jit(solution)/shard_map/ppermute | solution.py:266
  13.2 3.7 %copy-start = (f32[1024,1024]{1,0:T(8,128)S(1)}, f32[1024,1024]{1,0:T(8,128)}, u32[]{:S(2)}) copy-start(f32[1024,1024]{1,0:T(8,128)} %block.9) | copy-start | bytes 12582916
  19.0 5.9 %collective-permute-start.22 = (f32[256,256]{1,0:T(8,128)S(1)}, f32[256,256]{1,0:T(8,128)S(1)}, u32[]{:S(2)}, u32[]{:S(2)}) collective-permute-start(f32[256,256]{1,0:T(8,128)S(1)} %get-tuple-element.80.mine), channel_id=1, source_target_pairs={{0,4},{4,0},{8,12},{12,8},{16,20},{20,16},{24,28},{28,24},{32,36},... | collective-permute-start | bytes 786440 | tf_op jit(solution)/shard_map/ppermute | solution.py:317
  19.1 2.4 %collective-permute-start.19 = (f32[256,128]{1,0:T(8,128)S(1)}, f32[256,128]{1,0:T(8,128)S(1)}, u32[]{:S(2)}, u32[]{:S(2)}) collective-permute-start(f32[256,128]{1,0:T(8,128)S(1)} %get-tuple-element.79.mine), channel_id=1, source_target_pairs={{0,4},{4,0},{8,12},{12,8},{16,20},{20,16},{24,28},{28,24},{32,36},... | collective-permute-start | bytes 393224 | tf_op jit(solution)/shard_map/ppermute | solution.py:317
  19.5 10.7 %copy-start.1 = (f32[3,256,256]{2,1,0:T(8,128)S(1)}, f32[3,256,256]{2,1,0:T(8,128)}, u32[]{:S(2)}) copy-start(f32[3,256,256]{2,1,0:T(8,128)} %tree_v.5) | copy-start | bytes 2359300
  19.6 10.7 %copy-start.2 = (f32[3,256,256]{2,1,0:T(8,128)S(1)}, f32[3,256,256]{2,1,0:T(8,128)}, u32[]{:S(2)}) copy-start(f32[3,256,256]{2,1,0:T(8,128)} %tree_t.5) | copy-start | bytes 2359300
  19.6 7.2 %collective-permute-start.11 = (f32[256,256]{1,0:T(8,128)S(1)}, f32[256,256]{1,0:T(8,128)S(1)}, u32[]{:S(2)}, u32[]{:S(2)}) collective-permute-start(f32[256,256]{1,0:T(8,128)S(1)} %get-tuple-element.75.mine), channel_id=1, source_target_pairs={{0,4},{4,0},{8,12},{12,8},{16,20},{20,16},{24,28},{28,24},{32,36},... | collective-permute-start | bytes 786440 | tf_op jit(solution)/shard_map/ppermute | solution.py:317
  20.7 9.5 %collective-permute-start.6 = (f32[256,256]{1,0:T(8,128)S(1)}, f32[256,256]{1,0:T(8,128)S(1)}, u32[]{:S(2)}, u32[]{:S(2)}) collective-permute-start(f32[256,256]{1,0:T(8,128)S(1)} %get-tuple-element.67.mine), channel_id=1, source_target_pairs={{0,4},{4,0},{8,12},{12,8},{16,20},{20,16},{24,28},{28,24},{32,36},... | collective-permute-start | bytes 786440 | tf_op jit(solution)/shard_map/ppermute | solution.py:317
  21.2 2.7 %collective-permute-start.16 = (f32[256,128]{1,0:T(8,128)S(1)}, f32[256,128]{1,0:T(8,128)S(1)}, u32[]{:S(2)}, u32[]{:S(2)}) collective-permute-start(f32[256,128]{1,0:T(8,128)S(1)} %get-tuple-element.78.mine), channel_id=1, source_target_pairs={{0,4},{4,0},{8,12},{12,8},{16,20},{20,16},{24,28},{28,24},{32,36},... | collective-permute-start | bytes 393224 | tf_op jit(solution)/shard_map/ppermute | solution.py:317
  21.8 6.5 %collective-permute-start.20 = (f32[256,128]{1,0:T(8,128)S(1)}, f32[256,128]{1,0:T(8,128)S(1)}, u32[]{:S(2)}, u32[]{:S(2)}) collective-permute-start(f32[256,128]{1,0:T(8,128)S(1)} %shard_map.71.mine), channel_id=1, source_target_pairs={{0,8},{4,12},{8,0},{12,4},{16,24},{20,28},{24,16},{28,20},{32,40},... | collective-permute-start | bytes 393224 | tf_op jit(solution)/shard_map/ppermute | solution.py:317
  24.2 8.6 %collective-permute-start.17 = (f32[256,128]{1,0:T(8,128)S(1)}, f32[256,128]{1,0:T(8,128)S(1)}, u32[]{:S(2)}, u32[]{:S(2)}) collective-permute-start(f32[256,128]{1,0:T(8,128)S(1)} %shard_map.69.mine), channel_id=1, source_target_pairs={{0,8},{4,12},{8,0},{12,4},{16,24},{20,28},{24,16},{28,20},{32,40},... | collective-permute-start | bytes 393224 | tf_op jit(solution)/shard_map/ppermute | solution.py:317
  25.3 10.5 %collective-permute-start.25 = (f32[256,128]{1,0:T(8,128)S(1)}, f32[256,128]{1,0:T(8,128)S(1)}, u32[]{:S(2)}, u32[]{:S(2)}) collective-permute-start(f32[256,128]{1,0:T(8,128)S(1)} %get-tuple-element.82.mine), channel_id=1, source_target_pairs={{0,8},{4,12},{8,0},{12,4},{16,24},{20,28},{24,16},{28,20},{32,40},... | collective-permute-start | bytes 393224 | tf_op jit(solution)/shard_map/ppermute | solution.py:317
  26.8 13.0 %collective-permute-start.23 = (f32[256,128]{1,0:T(8,128)S(1)}, f32[256,128]{1,0:T(8,128)S(1)}, u32[]{:S(2)}, u32[]{:S(2)}) collective-permute-start(f32[256,128]{1,0:T(8,128)S(1)} %get-tuple-element.81.mine), channel_id=1, source_target_pairs={{0,8},{4,12},{8,0},{12,4},{16,24},{20,28},{24,16},{28,20},{32,40},... | collective-permute-start | bytes 393224 | tf_op jit(solution)/shard_map/ppermute | solution.py:317
  28.3 12.7 %collective-permute-start.14 = (f32[256,128]{1,0:T(8,128)S(1)}, f32[256,128]{1,0:T(8,128)S(1)}, u32[]{:S(2)}, u32[]{:S(2)}) collective-permute-start(f32[256,128]{1,0:T(8,128)S(1)} %get-tuple-element.77.mine), channel_id=1, source_target_pairs={{0,8},{4,12},{8,0},{12,4},{16,24},{20,28},{24,16},{28,20},{32,40},... | collective-permute-start | bytes 393224 | tf_op jit(solution)/shard_map/ppermute | solution.py:317
  30.2 17.7 %collective-permute-start.12 = (f32[256,128]{1,0:T(8,128)S(1)}, f32[256,128]{1,0:T(8,128)S(1)}, u32[]{:S(2)}, u32[]{:S(2)}) collective-permute-start(f32[256,128]{1,0:T(8,128)S(1)} %get-tuple-element.76.mine), channel_id=1, source_target_pairs={{0,8},{4,12},{8,0},{12,4},{16,24},{20,28},{24,16},{28,20},{32,40},... | collective-permute-start | bytes 393224 | tf_op jit(solution)/shard_map/ppermute | solution.py:317
  32.8 19.7 %collective-permute-start.9 = (f32[256,128]{1,0:T(8,128)S(1)}, f32[256,128]{1,0:T(8,128)S(1)}, u32[]{:S(2)}, u32[]{:S(2)}) collective-permute-start(f32[256,128]{1,0:T(8,128)S(1)} %get-tuple-element.74.mine), channel_id=1, source_target_pairs={{0,8},{4,12},{8,0},{12,4},{16,24},{20,28},{24,16},{28,20},{32,40},... | collective-permute-start | bytes 393224 | tf_op jit(solution)/shard_map/ppermute | solution.py:317
  35.8 21.9 %collective-permute-start.21 = (f32[256,128]{1,0:T(8,128)S(1)}, f32[256,128]{1,0:T(8,128)S(1)}, u32[]{:S(2)}, u32[]{:S(2)}) collective-permute-start(f32[256,128]{1,0:T(8,128)S(1)} %shard_map.72.args_2_), channel_id=1, source_target_pairs={{0,16},{4,20},{8,24},{12,28},{16,0},{20,4},{24,8},{28,12},{32,48},... | collective-permute-start | bytes 393224 | tf_op jit(solution)/shard_map/ppermute | solution.py:317
  39.8 19.7 %collective-permute-start.18 = (f32[256,128]{1,0:T(8,128)S(1)}, f32[256,128]{1,0:T(8,128)S(1)}, u32[]{:S(2)}, u32[]{:S(2)}) collective-permute-start(f32[256,128]{1,0:T(8,128)S(1)} %shard_map.70.args_0_), channel_id=1, source_target_pairs={{0,16},{4,20},{8,24},{12,28},{16,0},{20,4},{24,8},{28,12},{32,48},... | collective-permute-start | bytes 393224 | tf_op jit(solution)/shard_map/ppermute | solution.py:317
  40.9 15.1 %collective-permute-start.7 = (f32[256,128]{1,0:T(8,128)S(1)}, f32[256,128]{1,0:T(8,128)S(1)}, u32[]{:S(2)}, u32[]{:S(2)}) collective-permute-start(f32[256,128]{1,0:T(8,128)S(1)} %get-tuple-element.70.mine), channel_id=1, source_target_pairs={{0,8},{4,12},{8,0},{12,4},{16,24},{20,28},{24,16},{28,20},{32,40},... | collective-permute-start | bytes 393224 | tf_op jit(solution)/shard_map/ppermute | solution.py:317
  47.9 12.8 %collective-permute-start.26 = (f32[256,128]{1,0:T(8,128)S(1)}, f32[256,128]{1,0:T(8,128)S(1)}, u32[]{:S(2)}, u32[]{:S(2)}) collective-permute-start(f32[256,128]{1,0:T(8,128)S(1)} %shard_map.76.args_6_), channel_id=1, source_target_pairs={{0,16},{4,20},{8,24},{12,28},{16,0},{20,4},{24,8},{28,12},{32,48},... | collective-permute-start | bytes 393224 | tf_op jit(solution)/shard_map/ppermute | solution.py:317
  52.6 21.5 %collective-permute-start.24 = (f32[256,128]{1,0:T(8,128)S(1)}, f32[256,128]{1,0:T(8,128)S(1)}, u32[]{:S(2)}, u32[]{:S(2)}) collective-permute-start(f32[256,128]{1,0:T(8,128)S(1)} %shard_map.75.args_4_), channel_id=1, source_target_pairs={{0,16},{4,20},{8,24},{12,28},{16,0},{20,4},{24,8},{28,12},{32,48},... | collective-permute-start | bytes 393224 | tf_op jit(solution)/shard_map/ppermute | solution.py:317
  56.0 20.9 %collective-permute-start.15 = (f32[256,128]{1,0:T(8,128)S(1)}, f32[256,128]{1,0:T(8,128)S(1)}, u32[]{:S(2)}, u32[]{:S(2)}) collective-permute-start(f32[256,128]{1,0:T(8,128)S(1)} %shard_map.68.args_2_), channel_id=1, source_target_pairs={{0,16},{4,20},{8,24},{12,28},{16,0},{20,4},{24,8},{28,12},{32,48},... | collective-permute-start | bytes 393224 | tf_op jit(solution)/shard_map/ppermute | solution.py:317
  57.7 23.4 %collective-permute-start.13 = (f32[256,128]{1,0:T(8,128)S(1)}, f32[256,128]{1,0:T(8,128)S(1)}, u32[]{:S(2)}, u32[]{:S(2)}) collective-permute-start(f32[256,128]{1,0:T(8,128)S(1)} %shard_map.67.args_0_), channel_id=1, source_target_pairs={{0,16},{4,20},{8,24},{12,28},{16,0},{20,4},{24,8},{28,12},{32,48},... | collective-permute-start | bytes 393224 | tf_op jit(solution)/shard_map/ppermute | solution.py:317
  59.5 24.4 %collective-permute-start.10 = (f32[256,128]{1,0:T(8,128)S(1)}, f32[256,128]{1,0:T(8,128)S(1)}, u32[]{:S(2)}, u32[]{:S(2)}) collective-permute-start(f32[256,128]{1,0:T(8,128)S(1)} %shard_map.64.args_0_), channel_id=1, source_target_pairs={{0,16},{4,20},{8,24},{12,28},{16,0},{20,4},{24,8},{28,12},{32,48},... | collective-permute-start | bytes 393224 | tf_op jit(solution)/shard_map/ppermute | solution.py:317
  60.7 25.9 %collective-permute-start.8 = (f32[256,128]{1,0:T(8,128)S(1)}, f32[256,128]{1,0:T(8,128)S(1)}, u32[]{:S(2)}, u32[]{:S(2)}) collective-permute-start(f32[256,128]{1,0:T(8,128)S(1)} %shard_map.63.args_0_), channel_id=1, source_target_pairs={{0,16},{4,20},{8,24},{12,28},{16,0},{20,4},{24,8},{28,12},{32,48},... | collective-permute-start | bytes 393224 | tf_op jit(solution)/shard_map/ppermute | solution.py:317

commit v9 on v8

--- a/solution.py
+++ b/solution.py
@@ -100,13 +100,14 @@
     return split(rows), split(rows.T)
 
 
-def early_kernel(place, own_a, own_b, left_a, left_b, right_a, right_b, block, th, tl, partial, gh, gl, yh, yl, fh, fl):
+def early_kernel(place, own_a, own_b, behind_a, behind_b, before_a, before_b, block, partial, yh, yl, fh, fl):
     col = place[1]
     size = own_a.shape[0] + own_b.shape[0]
     count = block.shape[0] // size
     width = partial.shape[1]
     total = None
-    for shift, parts in ((0, (own_a, own_b)), (count - 1, (left_a, left_b)), (1, (right_a, right_b))):
+    behind = jnp.where(place[0] & 1 == 0, count - 1, 1)
+    for shift, parts in ((0, (own_a, own_b)), (behind, (behind_a, behind_b)), (count - behind, (before_a, before_b))):
         start = pl.multiple_of(lax.rem(col + shift, count) * size, size)
         rows = jnp.concatenate([p[...] for p in parts], axis=0)
         here = pl.ds(start, size)
@@ -117,10 +118,6 @@
         total = term if total is None else total + term
     partial[...] = total
 
-    @pl.when(lax.rem(col + count // 2, count) != 0)
-    def _():
-        gh[...], gl[...] = split(dot3((yh[:size, :], yl[:size, :]), (th[...], tl[...])))
-
 
 def store_parts(value, parts):
     first = 0
@@ -129,25 +126,19 @@
         first += part.shape[1]
 
 
-def first_kernel(place, partial, opp_a, opp_b, block, th, tl, old_gh, old_gl, *outs):
+def first_kernel(place, partial, opp_a, opp_b, block, th, tl, yh, yl, *outs):
     tops, (proj, gh, gl, oh, ol, ph, plow) = outs[:-7], outs[-7:]
     size = opp_a.shape[0] + opp_b.shape[0]
     width = partial.shape[1]
     start = opposite_rows(place[1], size, block.shape[0] // size)
     rows = jnp.concatenate([opp_a[...], opp_b[...]], axis=0)
     straight, flipped = both_ways(rows, start)
-
-    @pl.when(start == 0)
-    def _():
-        gh[...], gl[...] = split(dot3(straight, (th[...], tl[...])))
-
-    @pl.when(start != 0)
-    def _():
-        gh[...], gl[...] = old_gh[...], old_gl[...]
-
+    upper = [jnp.where(start == 0, new, old[:size, :]) for new, old in zip(straight, (yh, yl))]
+    gain = split(dot3(upper, (th[...], tl[...])))
     value = partial[...] + dot3(flipped, split(block[pl.ds(start, size), :width]))
-    store_parts(block[:size, :width] - dot3((gh[...], gl[...]), split(value)), tops)
+    store_parts(block[:size, :width] - dot3(gain, split(value)), tops)
     proj[...] = value
+    gh[...], gl[...] = gain
     oh[...], ol[...] = straight
     ph[...], plow[...] = flipped
 
@@ -251,19 +242,24 @@
     size, width = panel_y.shape
     rows, columns = trailing.shape
     levels = tree_v.shape[0]
-    cut = size // 2
     count = lax.axis_size("col")
     place = jnp.stack([lax.axis_index("row"), lax.axis_index("col")]).astype(jnp.int32)
-    onward = [(c, (c + 1) % count) for c in range(count)]
-    backward = [(c, (c - 1) % count) for c in range(count)]
-
-    own_a, own_b = panel_y[:cut], panel_y[cut:]
-    left_a = lax.ppermute(own_a, "col", onward)
-    right_b = lax.ppermute(own_b, "col", backward)
-    left_b = lax.ppermute(own_b, "col", onward)
-    right_a = lax.ppermute(own_a, "col", backward)
-    opp_a = lax.ppermute(left_a, "col", onward)
-    opp_b = lax.ppermute(right_b, "col", backward)
+    own_a, own_b = panel_y[: size // 2], panel_y[size // 2 :]
+
+    def ring(values, step):
+        route = []
+        for r in range(lax.axis_size("row")):
+            for c in range(count):
+                to = (c + (step if r % 2 == 0 else -step)) % count
+                route.append((r * count + c, r * count + to))
+        return lax.ppermute(values, ("row", "col"), route)
+
+    behind_a = ring(own_a, 1)
+    before_b = ring(own_b, -1)
+    behind_b = ring(own_b, 1)
+    before_a = ring(own_a, -1)
+    opp_a = ring(behind_a, 1)
+    opp_b = ring(before_b, -1)
 
     square = shaped((width, width), BF16)
     mix = shaped((width, 2 * width), BF16)
@@ -283,14 +279,14 @@
         cost=(3 * cube, 1 << 20),
     )(place, fixed(panel_t), fixed(tree_v), fixed(tree_t), fixed(trailing))
 
-    partial, gh, gl, yh, yl, fh, fl = call(
+    partial, yh, yl, fh, fl = call(
         early_kernel,
-        out_shape=[shaped((width, w)), square, square, tall, tall, wide, wide],
-        in_specs=[SMEM] + [VMEM] * 9,
-        out_specs=[VMEM] * 7,
+        out_shape=[shaped((width, w)), tall, tall, wide, wide],
+        in_specs=[SMEM] + [VMEM] * 7,
+        out_specs=[VMEM] * 5,
         mib=16,
         cost=(2 * cube, 4 << 20),
-    )(place, own_a, own_b, left_a, left_b, right_a, right_b, block, th, tl)
+    )(place, own_a, own_b, behind_a, behind_b, before_a, before_b, block)
 
     outs = call(
         first_kernel,
@@ -299,7 +295,7 @@
         out_specs=[VMEM] * (7 + len(STEPS[0])),
         mib=16,
         cost=(2 * cube, 2 << 20),
-    )(place, partial, opp_a, opp_b, block, th, tl, gh, gl)
+    )(place, partial, opp_a, opp_b, block, th, tl, yh, yl)
     raw, (proj, gh, gl, *opposite) = list(outs[:-7]), outs[-7:]
     projs = [proj]
 

time: 88.6 us -> 88.7 us (level)
  waiting for transfers between devices: 23.8 us -> 25.1 us
  transfers between devices with their start and end apart: 27 -> 27, of which waited for: 9 -> 10; matrix products, arithmetic and copies ran while one was open for 0% -> 0% of each run, Pallas kernels for 22% -> 22%
where the time goes in v9:
time: 88.7 us; the launch traced here: 88.1 us
  starting transfers between devices  37.1 us (42%)
  waiting for transfers between devices  25.1 us (28%)
  Pallas kernels  24.3 us (27%)
  local copies, waits for them, and re-layouts  1 us (1%)
    ppermute x21, starting transfers between devices, swap(): return lax.ppermute(values, 'row', route)  27.3 us
    ppermute x21, waiting for transfers between devices, swap(): return lax.ppermute(values, 'row', route)  24.5 us
    ppermute x6, starting transfers between devices, ring(): return lax.ppermute(values, ('row', 'col'), route)  9.71 us
    pallas_call x4, Pallas kernels, update(): call(functools.partial(final_kernel, first, n), out_shape=shaped((rows, c...  4.93 us
    pallas_call x13, Pallas kernels, combine(): call(level_kernel, out_shape=[shaped((width, w)) for w in widths], in_spe...  4.78 us
    pallas_call x2, Pallas kernels, update(): call(functools.partial(rest_kernel, first), out_shape=shaped((rows, colum...  3.92 us
    pallas_call x3, Pallas kernels, update(): call(functools.partial(next_kernel, slice(first, first + w)), out_shape=[...  3.02 us
    pallas_call x1, Pallas kernels, update(): call(prepare_kernel, out_shape=[square, square, mix, mix, shaped((rows, w...  2.23 us
  transfers between devices with their start and end apart: 27, of which 10 were waited for; matrix products, arithmetic and copies ran while one was open for 0% of the time, Pallas kernels for 22%

profile of v9, /device:TPU:8, one launch (start us, length us, event | category | flops | bytes accessed | tf_op | source)
XLA Modules:
  0.0 88.1 jit_solution(2136198280050110662)
XLA Ops:
  1.0 1.6 %collective-permute-start = (f32[128,256]{1,0:T(8,128)S(1)}, f32[128,256]{1,0:T(8,128)S(1)}, u32[]{:S(2)}, u32[]{:S(2)}) collective-permute-start(f32[128,256]{1,0:T(8,128)S(1)} %get-tuple-element.84.own_a), channel_id=1, source_target_pairs={{0,1},{1,2},{2,3},{3,0},{4,7},{5,4},{6,5},{7,6},{8,9},{9,10},{10,1... | collective-permute-start | bytes 393224 | tf_op jit(solution)/shard_map/ppermute | solution.py:255
  2.6 1.7 %collective-permute-start.3 = (f32[128,256]{1,0:T(8,128)S(1)}, f32[128,256]{1,0:T(8,128)S(1)}, u32[]{:S(2)}, u32[]{:S(2)}) collective-permute-start(f32[128,256]{1,0:T(8,128)S(1)} %get-tuple-element.83.own_b), channel_id=1, source_target_pairs={{0,3},{1,0},{2,1},{3,2},{4,5},{5,6},{6,7},{7,4},{8,11},{9,8},{10,9... | collective-permute-start | bytes 393224 | tf_op jit(solution)/shard_map/ppermute | solution.py:255
  4.6 3.0 %collective-permute-start.2 = (f32[128,256]{1,0:T(8,128)S(1)}, f32[128,256]{1,0:T(8,128)S(1)}, u32[]{:S(2)}, u32[]{:S(2)}) collective-permute-start(f32[128,256]{1,0:T(8,128)S(1)} %get-tuple-element.84.own_a), channel_id=1, source_target_pairs={{0,3},{1,0},{2,1},{3,2},{4,5},{5,6},{6,7},{7,4},{8,11},{9,8},{10,9... | collective-permute-start | bytes 393224 | tf_op jit(solution)/shard_map/ppermute | solution.py:255
  7.5 1.2 %collective-permute-start.4 = (f32[128,256]{1,0:T(8,128)S(1)}, f32[128,256]{1,0:T(8,128)S(1)}, u32[]{:S(2)}, u32[]{:S(2)}) collective-permute-start(f32[128,256]{1,0:T(8,128)S(1)} %collective-permute-done.behind_a), channel_id=1, source_target_pairs={{0,1},{1,2},{2,3},{3,0},{4,7},{5,4},{6,5},{7,6},{8,9},{9,10},{10,1... | collective-permute-start | bytes 393224 | tf_op jit(solution)/shard_map/ppermute | solution.py:255
  8.9 1.9 %collective-permute-start.5 = (f32[128,256]{1,0:T(8,128)S(1)}, f32[128,256]{1,0:T(8,128)S(1)}, u32[]{:S(2)}, u32[]{:S(2)}) collective-permute-start(f32[128,256]{1,0:T(8,128)S(1)} %collective-permute-done.3.before_b), channel_id=1, source_target_pairs={{0,3},{1,0},{2,1},{3,2},{4,5},{5,6},{6,7},{7,4},{8,11},{9,8},{10,9... | collective-permute-start | bytes 393224 | tf_op jit(solution)/shard_map/ppermute | solution.py:255
  10.9 2.2 %shard_map.55 = (bf16[256,256]{1,0:T(8,128)(2,1)S(1)}, bf16[256,256]{1,0:T(8,128)(2,1)S(1)}, bf16[256,512]{1,0:T(8,128)(2,1)S(1)}, bf16[256,512]{1,0:T(8,128)(2,1)S(1)}, f32[1024,256]{1,0:T(8,128)S(1)}) custom-call(s32[2]{0:T(128)S(1)} %pad_add_fusion.place, f32[256,256]{1,0:T(8,128)} %panel_t.1, f32[3,256,256]{2,1,0:T(8,128)} %tree_v.5, ...), custom_call_target="tpu_custom_call" | custom-call | flops 301989888 | bytes 1048576 | tf_op jit(solution)/shard_map/pallas_call | solution.py:272
  13.2 1.3 %shard_map.56 = (f32[256,256]{1,0:T(8,128)S(1)}, bf16[1024,256]{1,0:T(8,128)(2,1)S(1)}, bf16[1024,256]{1,0:T(8,128)(2,1)S(1)}, bf16[256,1024]{1,0:T(8,128)(2,1)S(1)}, bf16[256,1024]{1,0:T(8,128)(2,1)S(1)}) custom-call(s32[2]{0:T(128)S(1)} %pad_add_fusion.place, f32[128,256]{1,0:T(8,128)S(1)} %get-tuple-element.84.own_a, ...), custom_call_target="tpu_custom_call" | custom-call | flops 201326592 | bytes 4194304 | tf_op jit(solution)/shard_map/pallas_call | solution.py:282
  14.9 1.4 %shard_map.57 = (f32[256,128]{1,0:T(8,128)S(1)}, f32[256,128]{1,0:T(8,128)S(1)}, f32[256,256]{1,0:T(8,128)S(1)}, bf16[256,256]{1,0:T(8,128)(2,1)S(1)}, bf16[256,...) custom-call(s32[2]{0:T(128)S(1)} %pad_add_fusion.place, ...), custom_call_target="tpu_custom_call" | custom-call | flops 201326592 | bytes 2097152 | tf_op jit(solution)/shard_map/pallas_call | solution.py:291
  21.7 2.2 %collective-permute-start.20 = (f32[256,128]{1,0:T(8,128)S(1)}, f32[256,128]{1,0:T(8,128)S(1)}, u32[]{:S(2)}, u32[]{:S(2)}) collective-permute-start(f32[256,128]{1,0:T(8,128)S(1)} %shard_map.71.mine), channel_id=1, source_target_pairs={{0,8},{4,12},{8,0},{12,4},{16,24},{20,28},{24,16},{28,20},{32,40},... | collective-permute-start | bytes 393224 | tf_op jit(solution)/shard_map/ppermute | solution.py:313
  25.4 1.5 %collective-permute-start.25 = (f32[256,128]{1,0:T(8,128)S(1)}, f32[256,128]{1,0:T(8,128)S(1)}, u32[]{:S(2)}, u32[]{:S(2)}) collective-permute-start(f32[256,128]{1,0:T(8,128)S(1)} %get-tuple-element.78.mine), channel_id=1, source_target_pairs={{0,8},{4,12},{8,0},{12,4},{16,24},{20,28},{24,16},{28,20},{32,40},... | collective-permute-start | bytes 393224 | tf_op jit(solution)/shard_map/ppermute | solution.py:313
  28.4 1.9 %collective-permute-start.14 = (f32[256,128]{1,0:T(8,128)S(1)}, f32[256,128]{1,0:T(8,128)S(1)}, u32[]{:S(2)}, u32[]{:S(2)}) collective-permute-start(f32[256,128]{1,0:T(8,128)S(1)} %get-tuple-element.73.mine), channel_id=1, source_target_pairs={{0,8},{4,12},{8,0},{12,4},{16,24},{20,28},{24,16},{28,20},{32,40},... | collective-permute-start | bytes 393224 | tf_op jit(solution)/shard_map/ppermute | solution.py:313
  30.4 1.1 %shard_map.62 = (bf16[256,512]{1,0:T(8,128)(2,1)S(1)}, bf16[256,512]{1,0:T(8,128)(2,1)S(1)}) custom-call(s32[2]{0:T(128)S(1)} %pad_add_fusion.place, f32[3,256,256]{2,1,0:T(8,128)S(1)} %copy-done.1, f32[3,256,256]{2,1,0:T(8,128)S(1)} %copy-done.2, f32[256,256]{1,0:T(8,128)S(1)} %get-tuple-element.67.after.args_0_), custom_call_target="tpu_custom_call" | custom-call | flops 201326592 | bytes 1048576 | tf_op jit(solution)/shard_map/pallas_call | solution.py:328
  31.5 1.1 %shard_map.60 = (bf16[256,512]{1,0:T(8,128)(2,1)S(1)}, bf16[256,512]{1,0:T(8,128)(2,1)S(1)}) custom-call(s32[2]{0:T(128)S(1)} %pad_add_fusion.place, f32[3,256,256]{2,1,0:T(8,128)S(1)} %copy-done.1, f32[3,256,256]{2,1,0:T(8,128)S(1)} %copy-done.2, f32[256,256]{1,0:T(8,128)S(1)} %get-tuple-element.60.after.args_1_), custom_call_target="tpu_custom_call" | custom-call | flops 201326592 | bytes 1048576 | tf_op jit(solution)/shard_map/pallas_call | solution.py:328
  32.9 2.2 %collective-permute-start.9 = (f32[256,128]{1,0:T(8,128)S(1)}, f32[256,128]{1,0:T(8,128)S(1)}, u32[]{:S(2)}, u32[]{:S(2)}) collective-permute-start(f32[256,128]{1,0:T(8,128)S(1)} %get-tuple-element.70.mine), channel_id=1, source_target_pairs={{0,8},{4,12},{8,0},{12,4},{16,24},{20,28},{24,16},{28,20},{32,40},... | collective-permute-start | bytes 393224 | tf_op jit(solution)/shard_map/ppermute | solution.py:313
  35.9 3.6 %collective-permute-start.21 = (f32[256,128]{1,0:T(8,128)S(1)}, f32[256,128]{1,0:T(8,128)S(1)}, u32[]{:S(2)}, u32[]{:S(2)}) collective-permute-start(f32[256,128]{1,0:T(8,128)S(1)} %shard_map.72.args_2_), channel_id=1, source_target_pairs={{0,16},{4,20},{8,24},{12,28},{16,0},{20,4},{24,8},{28,12},{32,48},... | collective-permute-start | bytes 393224 | tf_op jit(solution)/shard_map/ppermute | solution.py:313
  41.0 2.4 %collective-permute-start.7 = (f32[256,128]{1,0:T(8,128)S(1)}, f32[256,128]{1,0:T(8,128)S(1)}, u32[]{:S(2)}, u32[]{:S(2)}) collective-permute-start(f32[256,128]{1,0:T(8,128)S(1)} %get-tuple-element.66.mine), channel_id=1, source_target_pairs={{0,8},{4,12},{8,0},{12,4},{16,24},{20,28},{24,16},{28,20},{32,40},... | collective-permute-start | bytes 393224 | tf_op jit(solution)/shard_map/ppermute | solution.py:313
  43.4 4.6 %collective-permute-done.12.theirs = f32[256,128]{1,0:T(8,128)S(1)} collective-permute-done((f32[256,128]{1,0:T(8,128)S(1)}, f32[256,128]{1,0:T(8,128)S(1)}, u32[]{:S(2)}, u32[]{:S(2)}) %collective-permute-start.12) | collective-permute-done | bytes 131104 | tf_op jit(solution)/shard_map/ppermute | solution.py:313
  48.0 2.5 %collective-permute-start.26 = (f32[256,128]{1,0:T(8,128)S(1)}, f32[256,128]{1,0:T(8,128)S(1)}, u32[]{:S(2)}, u32[]{:S(2)}) collective-permute-start(f32[256,128]{1,0:T(8,128)S(1)} %shard_map.76.args_6_), channel_id=1, source_target_pairs={{0,16},{4,20},{8,24},{12,28},{16,0},{20,4},{24,8},{28,12},{32,48},... | collective-permute-start | bytes 393224 | tf_op jit(solution)/shard_map/ppermute | solution.py:313
  50.5 2.0 %shard_map.77.args_2_ = f32[1024,1024]{1,0:T(8,128)} custom-call(f32[1024,1024]{1,0:T(8,128)S(1)} %copy-done, bf16[1024,256]{1,0:T(8,128)(2,1)S(1)} %get-tuple-element.79.yh, bf16[1024,256]{1,0:T(8,128)(2,1)S(1)} %get-tuple-element.80.yl, bf16[256,256]{1,0:T(8,128)(2,1)S(1)} %get-tuple-element.50.th, bf16[256,256]{1,0:T(8,128)(2,1)S(1)} %get-tuple-element.51.tl, ...), custom_call_target="tpu_custom_call" | custom-call | flops 1006632960 | bytes 4194304 | tf_op jit(solution)/shard_map/pallas_call | solution.py:366
  52.8 2.0 %collective-permute-start.24 = (f32[256,128]{1,0:T(8,128)S(1)}, f32[256,128]{1,0:T(8,128)S(1)}, u32[]{:S(2)}, u32[]{:S(2)}) collective-permute-start(f32[256,128]{1,0:T(8,128)S(1)} %shard_map.75.args_4_), channel_id=1, source_target_pairs={{0,16},{4,20},{8,24},{12,28},{16,0},{20,4},{24,8},{28,12},{32,48},... | collective-permute-start | bytes 393224 | tf_op jit(solution)/shard_map/ppermute | solution.py:313
  55.9 1.6 %collective-permute-start.15 = (f32[256,128]{1,0:T(8,128)S(1)}, f32[256,128]{1,0:T(8,128)S(1)}, u32[]{:S(2)}, u32[]{:S(2)}) collective-permute-start(f32[256,128]{1,0:T(8,128)S(1)} %shard_map.68.args_2_), channel_id=1, source_target_pairs={{0,16},{4,20},{8,24},{12,28},{16,0},{20,4},{24,8},{28,12},{32,48},... | collective-permute-start | bytes 393224 | tf_op jit(solution)/shard_map/ppermute | solution.py:313
  57.9 1.7 %collective-permute-start.13 = (f32[256,128]{1,0:T(8,128)S(1)}, f32[256,128]{1,0:T(8,128)S(1)}, u32[]{:S(2)}, u32[]{:S(2)}) collective-permute-start(f32[256,128]{1,0:T(8,128)S(1)} %shard_map.67.args_0_), channel_id=1, source_target_pairs={{0,16},{4,20},{8,24},{12,28},{16,0},{20,4},{24,8},{28,12},{32,48},... | collective-permute-start | bytes 393224 | tf_op jit(solution)/shard_map/ppermute | solution.py:313
  59.6 1.3 %collective-permute-start.10 = (f32[256,128]{1,0:T(8,128)S(1)}, f32[256,128]{1,0:T(8,128)S(1)}, u32[]{:S(2)}, u32[]{:S(2)}) collective-permute-start(f32[256,128]{1,0:T(8,128)S(1)} %shard_map.64.args_0_), channel_id=1, source_target_pairs={{0,16},{4,20},{8,24},{12,28},{16,0},{20,4},{24,8},{28,12},{32,48},... | collective-permute-start | bytes 393224 | tf_op jit(solution)/shard_map/ppermute | solution.py:313
  60.9 1.6 %collective-permute-start.8 = (f32[256,128]{1,0:T(8,128)S(1)}, f32[256,128]{1,0:T(8,128)S(1)}, u32[]{:S(2)}, u32[]{:S(2)}) collective-permute-start(f32[256,128]{1,0:T(8,128)S(1)} %shard_map.63.args_0_), channel_id=1, source_target_pairs={{0,16},{4,20},{8,24},{12,28},{16,0},{20,4},{24,8},{28,12},{32,48},... | collective-permute-start | bytes 393224 | tf_op jit(solution)/shard_map/ppermute | solution.py:313
  62.5 2.0 %shard_map.78.args_8_ = f32[1024,1024]{1,0:T(8,128)} custom-call(f32[1024,1024]{1,0:T(8,128)S(1)} %copy-done, bf16[1024,256]{1,0:T(8,128)(2,1)S(1)} %get-tuple-element.79.yh, bf16[1024,256]{1,0:T(8,128)(2,1)S(1)} %get-tuple-element.80.yl, bf16[256,256]{1,0:T(8,128)(2,1)S(1)} %get-tuple-element.50.th, ...), custom_call_target="tpu_custom_call", output_to_operand_aliasing={{}: (7, {})} | custom-call | flops 1006632960 | bytes 4194304 | tf_op jit(solution)/shard_map/pallas_call | solution.py:366
  64.5 9.8 %collective-permute-done.24.args_5_ = f32[256,128]{1,0:T(8,128)S(1)} collective-permute-done((f32[256,128]{1,0:T(8,128)S(1)}, f32[256,128]{1,0:T(8,128)S(1)}, u32[]{:S(2)}, u32[]{:S(2)}) %collective-permute-start.24) | collective-permute-done | bytes 131104 | tf_op jit(solution)/shard_map/ppermute | solution.py:313
  74.3 1.7 %shard_map.79.args_4_ = f32[1024,1024]{1,0:T(8,128)} custom-call(bf16[256,512]{1,0:T(8,128)(2,1)S(1)} %get-tuple-element.61.high, bf16[256,512]{1,0:T(8,128)(2,1)S(1)} %get-tuple-element.62.low, f32[256,128]{1,0:T(8,128)S(1)} %shard_map.70.args_0_, f32[256,128]{1,0:T(8,128)S(1)} %collective-permute-done.18.args_1_, ...), custom_call_target="tpu_custom_call", output_to_operand_aliasing={{}: (10, {})} | custom-call | flops 402653184 | bytes 1048576 | tf_op jit(solution)/shard_map/pallas_call | solution.py:385
  76.0 1.1 %collective-permute-done.15.args_3_ = f32[256,128]{1,0:T(8,128)S(1)} collective-permute-done((f32[256,128]{1,0:T(8,128)S(1)}, f32[256,128]{1,0:T(8,128)S(1)}, u32[]{:S(2)}, u32[]{:S(2)}) %collective-permute-start.15) | collective-permute-done | bytes 131104 | tf_op jit(solution)/shard_map/ppermute | solution.py:313
  77.2 4.2 %collective-permute-done.13.args_1_ = f32[256,128]{1,0:T(8,128)S(1)} collective-permute-done((f32[256,128]{1,0:T(8,128)S(1)}, f32[256,128]{1,0:T(8,128)S(1)}, u32[]{:S(2)}, u32[]{:S(2)}) %collective-permute-start.13) | collective-permute-done | bytes 131104 | tf_op jit(solution)/shard_map/ppermute | solution.py:313
  81.4 1.2 %shard_map.80.args_2_ = f32[1024,1024]{1,0:T(8,128)} custom-call(bf16[256,512]{1,0:T(8,128)(2,1)S(1)} %get-tuple-element.61.high, bf16[256,512]{1,0:T(8,128)(2,1)S(1)} %get-tuple-element.62.low, f32[256,128]{1,0:T(8,128)S(1)} %shard_map.67.args_0_, f32[256,128]{1,0:T(8,128)S(1)} %collective-permute-done.13.args_1_, ...), custom_call_target="tpu_custom_call", output_to_operand_aliasing={{}: (6, {})} | custom-call | flops 201326592 | bytes 1048576 | tf_op jit(solution)/shard_map/pallas_call | solution.py:385
  82.6 1.6 %collective-permute-done.10.args_1_ = f32[256,128]{1,0:T(8,128)S(1)} collective-permute-done((f32[256,128]{1,0:T(8,128)S(1)}, f32[256,128]{1,0:T(8,128)S(1)}, u32[]{:S(2)}, u32[]{:S(2)}) %collective-permute-start.10) | collective-permute-done | bytes 131104 | tf_op jit(solution)/shard_map/ppermute | solution.py:313
  85.2 1.7 %collective-permute-done.8.args_1_ = f32[256,128]{1,0:T(8,128)S(1)} collective-permute-done((f32[256,128]{1,0:T(8,128)S(1)}, f32[256,128]{1,0:T(8,128)S(1)}, u32[]{:S(2)}, u32[]{:S(2)}) %collective-permute-start.8) | collective-permute-done | bytes 131104 | tf_op jit(solution)/shard_map/ppermute | solution.py:313
  (58 shorter events, 16.8 us)
Async XLA Ops:
  1.0 6.6 %collective-permute-start = (f32[128,256]{1,0:T(8,128)S(1)}, f32[128,256]{1,0:T(8,128)S(1)}, u32[]{:S(2)}, u32[]{:S(2)}) collective-permute-start(f32[128,256]{1,0:T(8,128)S(1)} %get-tuple-element.84.own_a), channel_id=1, source_target_pairs={{0,1},{1,2},{2,3},{3,0},{4,7},{5,4},{6,5},{7,6},{8,9},{9,10},{10,1... | collective-permute-start | bytes 393224 | tf_op jit(solution)/shard_map/ppermute | solution.py:255
  2.6 6.4 %collective-permute-start.3 = (f32[128,256]{1,0:T(8,128)S(1)}, f32[128,256]{1,0:T(8,128)S(1)}, u32[]{:S(2)}, u32[]{:S(2)}) collective-permute-start(f32[128,256]{1,0:T(8,128)S(1)} %get-tuple-element.83.own_b), channel_id=1, source_target_pairs={{0,3},{1,0},{2,1},{3,2},{4,5},{5,6},{6,7},{7,4},{8,11},{9,8},{10,9... | collective-permute-start | bytes 393224 | tf_op jit(solution)/shard_map/ppermute | solution.py:255
  4.3 8.8 %collective-permute-start.1 = (f32[128,256]{1,0:T(8,128)S(1)}, f32[128,256]{1,0:T(8,128)S(1)}, u32[]{:S(2)}, u32[]{:S(2)}) collective-permute-start(f32[128,256]{1,0:T(8,128)S(1)} %get-tuple-element.83.own_b), channel_id=1, source_target_pairs={{0,1},{1,2},{2,3},{3,0},{4,7},{5,4},{6,5},{7,6},{8,9},{9,10},{10,1... | collective-permute-start | bytes 393224 | tf_op jit(solution)/shard_map/ppermute | solution.py:255
  4.6 8.6 %collective-permute-start.2 = (f32[128,256]{1,0:T(8,128)S(1)}, f32[128,256]{1,0:T(8,128)S(1)}, u32[]{:S(2)}, u32[]{:S(2)}) collective-permute-start(f32[128,256]{1,0:T(8,128)S(1)} %get-tuple-element.84.own_a), channel_id=1, source_target_pairs={{0,3},{1,0},{2,1},{3,2},{4,5},{5,6},{6,7},{7,4},{8,11},{9,8},{10,9... | collective-permute-start | bytes 393224 | tf_op jit(solution)/shard_map/ppermute | solution.py:255
  7.5 7.4 %collective-permute-start.4 = (f32[128,256]{1,0:T(8,128)S(1)}, f32[128,256]{1,0:T(8,128)S(1)}, u32[]{:S(2)}, u32[]{:S(2)}) collective-permute-start(f32[128,256]{1,0:T(8,128)S(1)} %collective-permute-done.behind_a), channel_id=1, source_target_pairs={{0,1},{1,2},{2,3},{3,0},{4,7},{5,4},{6,5},{7,6},{8,9},{9,10},{10,1... | collective-permute-start | bytes 393224 | tf_op jit(solution)/shard_map/ppermute | solution.py:255
  8.9 6.0 %collective-permute-start.5 = (f32[128,256]{1,0:T(8,128)S(1)}, f32[128,256]{1,0:T(8,128)S(1)}, u32[]{:S(2)}, u32[]{:S(2)}) collective-permute-start(f32[128,256]{1,0:T(8,128)S(1)} %collective-permute-done.3.before_b), channel_id=1, source_target_pairs={{0,3},{1,0},{2,1},{3,2},{4,5},{5,6},{6,7},{7,4},{8,11},{9,8},{10,9... | collective-permute-start | bytes 393224 | tf_op jit(solution)/shard_map/ppermute | solution.py:255
  13.1 3.9 %copy-start = (f32[1024,1024]{1,0:T(8,128)S(1)}, f32[1024,1024]{1,0:T(8,128)}, u32[]{:S(2)}) copy-start(f32[1024,1024]{1,0:T(8,128)} %block.9) | copy-start | bytes 12582916
  19.0 5.9 %collective-permute-start.22 = (f32[256,256]{1,0:T(8,128)S(1)}, f32[256,256]{1,0:T(8,128)S(1)}, u32[]{:S(2)}, u32[]{:S(2)}) collective-permute-start(f32[256,256]{1,0:T(8,128)S(1)} %get-tuple-element.76.mine), channel_id=1, source_target_pairs={{0,4},{4,0},{8,12},{12,8},{16,20},{20,16},{24,28},{28,24},{32,36},... | collective-permute-start | bytes 786440 | tf_op jit(solution)/shard_map/ppermute | solution.py:313
  19.2 2.1 %collective-permute-start.19 = (f32[256,128]{1,0:T(8,128)S(1)}, f32[256,128]{1,0:T(8,128)S(1)}, u32[]{:S(2)}, u32[]{:S(2)}) collective-permute-start(f32[256,128]{1,0:T(8,128)S(1)} %get-tuple-element.75.mine), channel_id=1, source_target_pairs={{0,4},{4,0},{8,12},{12,8},{16,20},{20,16},{24,28},{28,24},{32,36},... | collective-permute-start | bytes 393224 | tf_op jit(solution)/shard_map/ppermute | solution.py:313
  19.6 10.8 %copy-start.1 = (f32[3,256,256]{2,1,0:T(8,128)S(1)}, f32[3,256,256]{2,1,0:T(8,128)}, u32[]{:S(2)}) copy-start(f32[3,256,256]{2,1,0:T(8,128)} %tree_v.5) | copy-start | bytes 2359300
  19.6 10.8 %copy-start.2 = (f32[3,256,256]{2,1,0:T(8,128)S(1)}, f32[3,256,256]{2,1,0:T(8,128)}, u32[]{:S(2)}) copy-start(f32[3,256,256]{2,1,0:T(8,128)} %tree_t.5) | copy-start | bytes 2359300
  19.6 7.3 %collective-permute-start.11 = (f32[256,256]{1,0:T(8,128)S(1)}, f32[256,256]{1,0:T(8,128)S(1)}, u32[]{:S(2)}, u32[]{:S(2)}) collective-permute-start(f32[256,256]{1,0:T(8,128)S(1)} %get-tuple-element.71.mine), channel_id=1, source_target_pairs={{0,4},{4,0},{8,12},{12,8},{16,20},{20,16},{24,28},{28,24},{32,36},... | collective-permute-start | bytes 786440 | tf_op jit(solution)/shard_map/ppermute | solution.py:313
  20.8 9.5 %collective-permute-start.6 = (f32[256,256]{1,0:T(8,128)S(1)}, f32[256,256]{1,0:T(8,128)S(1)}, u32[]{:S(2)}, u32[]{:S(2)}) collective-permute-start(f32[256,256]{1,0:T(8,128)S(1)} %get-tuple-element.63.mine), channel_id=1, source_target_pairs={{0,4},{4,0},{8,12},{12,8},{16,20},{20,16},{24,28},{28,24},{32,36},... | collective-permute-start | bytes 786440 | tf_op jit(solution)/shard_map/ppermute | solution.py:313
  21.2 2.7 %collective-permute-start.16 = (f32[256,128]{1,0:T(8,128)S(1)}, f32[256,128]{1,0:T(8,128)S(1)}, u32[]{:S(2)}, u32[]{:S(2)}) collective-permute-start(f32[256,128]{1,0:T(8,128)S(1)} %get-tuple-element.74.mine), channel_id=1, source_target_pairs={{0,4},{4,0},{8,12},{12,8},{16,20},{20,16},{24,28},{28,24},{32,36},... | collective-permute-start | bytes 393224 | tf_op jit(solution)/shard_map/ppermute | solution.py:313
  21.7 6.6 %collective-permute-start.20 = (f32[256,128]{1,0:T(8,128)S(1)}, f32[256,128]{1,0:T(8,128)S(1)}, u32[]{:S(2)}, u32[]{:S(2)}) collective-permute-start(f32[256,128]{1,0:T(8,128)S(1)} %shard_map.71.mine), channel_id=1, source_target_pairs={{0,8},{4,12},{8,0},{12,4},{16,24},{20,28},{24,16},{28,20},{32,40},... | collective-permute-start | bytes 393224 | tf_op jit(solution)/shard_map/ppermute | solution.py:313
  24.3 8.7 %collective-permute-start.17 = (f32[256,128]{1,0:T(8,128)S(1)}, f32[256,128]{1,0:T(8,128)S(1)}, u32[]{:S(2)}, u32[]{:S(2)}) collective-permute-start(f32[256,128]{1,0:T(8,128)S(1)} %shard_map.69.mine), channel_id=1, source_target_pairs={{0,8},{4,12},{8,0},{12,4},{16,24},{20,28},{24,16},{28,20},{32,40},... | collective-permute-start | bytes 393224 | tf_op jit(solution)/shard_map/ppermute | solution.py:313
  25.4 10.6 %collective-permute-start.25 = (f32[256,128]{1,0:T(8,128)S(1)}, f32[256,128]{1,0:T(8,128)S(1)}, u32[]{:S(2)}, u32[]{:S(2)}) collective-permute-start(f32[256,128]{1,0:T(8,128)S(1)} %get-tuple-element.78.mine), channel_id=1, source_target_pairs={{0,8},{4,12},{8,0},{12,4},{16,24},{20,28},{24,16},{28,20},{32,40},... | collective-permute-start | bytes 393224 | tf_op jit(solution)/shard_map/ppermute | solution.py:313
  26.9 13.0 %collective-permute-start.23 = (f32[256,128]{1,0:T(8,128)S(1)}, f32[256,128]{1,0:T(8,128)S(1)}, u32[]{:S(2)}, u32[]{:S(2)}) collective-permute-start(f32[256,128]{1,0:T(8,128)S(1)} %get-tuple-element.77.mine), channel_id=1, source_target_pairs={{0,8},{4,12},{8,0},{12,4},{16,24},{20,28},{24,16},{28,20},{32,40},... | collective-permute-start | bytes 393224 | tf_op jit(solution)/shard_map/ppermute | solution.py:313
  28.4 12.6 %collective-permute-start.14 = (f32[256,128]{1,0:T(8,128)S(1)}, f32[256,128]{1,0:T(8,128)S(1)}, u32[]{:S(2)}, u32[]{:S(2)}) collective-permute-start(f32[256,128]{1,0:T(8,128)S(1)} %get-tuple-element.73.mine), channel_id=1, source_target_pairs={{0,8},{4,12},{8,0},{12,4},{16,24},{20,28},{24,16},{28,20},{32,40},... | collective-permute-start | bytes 393224 | tf_op jit(solution)/shard_map/ppermute | solution.py:313
  30.3 17.7 %collective-permute-start.12 = (f32[256,128]{1,0:T(8,128)S(1)}, f32[256,128]{1,0:T(8,128)S(1)}, u32[]{:S(2)}, u32[]{:S(2)}) collective-permute-start(f32[256,128]{1,0:T(8,128)S(1)} %get-tuple-element.72.mine), channel_id=1, source_target_pairs={{0,8},{4,12},{8,0},{12,4},{16,24},{20,28},{24,16},{28,20},{32,40},... | collective-permute-start | bytes 393224 | tf_op jit(solution)/shard_map/ppermute | solution.py:313
  32.9 19.9 %collective-permute-start.9 = (f32[256,128]{1,0:T(8,128)S(1)}, f32[256,128]{1,0:T(8,128)S(1)}, u32[]{:S(2)}, u32[]{:S(2)}) collective-permute-start(f32[256,128]{1,0:T(8,128)S(1)} %get-tuple-element.70.mine), channel_id=1, source_target_pairs={{0,8},{4,12},{8,0},{12,4},{16,24},{20,28},{24,16},{28,20},{32,40},... | collective-permute-start | bytes 393224 | tf_op jit(solution)/shard_map/ppermute | solution.py:313
  35.9 22.0 %collective-permute-start.21 = (f32[256,128]{1,0:T(8,128)S(1)}, f32[256,128]{1,0:T(8,128)S(1)}, u32[]{:S(2)}, u32[]{:S(2)}) collective-permute-start(f32[256,128]{1,0:T(8,128)S(1)} %shard_map.72.args_2_), channel_id=1, source_target_pairs={{0,16},{4,20},{8,24},{12,28},{16,0},{20,4},{24,8},{28,12},{32,48},... | collective-permute-start | bytes 393224 | tf_op jit(solution)/shard_map/ppermute | solution.py:313
  39.9 19.7 %collective-permute-start.18 = (f32[256,128]{1,0:T(8,128)S(1)}, f32[256,128]{1,0:T(8,128)S(1)}, u32[]{:S(2)}, u32[]{:S(2)}) collective-permute-start(f32[256,128]{1,0:T(8,128)S(1)} %shard_map.70.args_0_), channel_id=1, source_target_pairs={{0,16},{4,20},{8,24},{12,28},{16,0},{20,4},{24,8},{28,12},{32,48},... | collective-permute-start | bytes 393224 | tf_op jit(solution)/shard_map/ppermute | solution.py:313
  41.0 14.9 %collective-permute-start.7 = (f32[256,128]{1,0:T(8,128)S(1)}, f32[256,128]{1,0:T(8,128)S(1)}, u32[]{:S(2)}, u32[]{:S(2)}) collective-permute-start(f32[256,128]{1,0:T(8,128)S(1)} %get-tuple-element.66.mine), channel_id=1, source_target_pairs={{0,8},{4,12},{8,0},{12,4},{16,24},{20,28},{24,16},{28,20},{32,40},... | collective-permute-start | bytes 393224 | tf_op jit(solution)/shard_map/ppermute | solution.py:313
  48.0 12.9 %collective-permute-start.26 = (f32[256,128]{1,0:T(8,128)S(1)}, f32[256,128]{1,0:T(8,128)S(1)}, u32[]{:S(2)}, u32[]{:S(2)}) collective-permute-start(f32[256,128]{1,0:T(8,128)S(1)} %shard_map.76.args_6_), channel_id=1, source_target_pairs={{0,16},{4,20},{8,24},{12,28},{16,0},{20,4},{24,8},{28,12},{32,48},... | collective-permute-start | bytes 393224 | tf_op jit(solution)/shard_map/ppermute | solution.py:313
  52.8 21.5 %collective-permute-start.24 = (f32[256,128]{1,0:T(8,128)S(1)}, f32[256,128]{1,0:T(8,128)S(1)}, u32[]{:S(2)}, u32[]{:S(2)}) collective-permute-start(f32[256,128]{1,0:T(8,128)S(1)} %shard_map.75.args_4_), channel_id=1, source_target_pairs={{0,16},{4,20},{8,24},{12,28},{16,0},{20,4},{24,8},{28,12},{32,48},... | collective-permute-start | bytes 393224 | tf_op jit(solution)/shard_map/ppermute | solution.py:313
  55.9 21.2 %collective-permute-start.15 = (f32[256,128]{1,0:T(8,128)S(1)}, f32[256,128]{1,0:T(8,128)S(1)}, u32[]{:S(2)}, u32[]{:S(2)}) collective-permute-start(f32[256,128]{1,0:T(8,128)S(1)} %shard_map.68.args_2_), channel_id=1, source_target_pairs={{0,16},{4,20},{8,24},{12,28},{16,0},{20,4},{24,8},{28,12},{32,48},... | collective-permute-start | bytes 393224 | tf_op jit(solution)/shard_map/ppermute | solution.py:313
  57.9 23.5 %collective-permute-start.13 = (f32[256,128]{1,0:T(8,128)S(1)}, f32[256,128]{1,0:T(8,128)S(1)}, u32[]{:S(2)}, u32[]{:S(2)}) collective-permute-start(f32[256,128]{1,0:T(8,128)S(1)} %shard_map.67.args_0_), channel_id=1, source_target_pairs={{0,16},{4,20},{8,24},{12,28},{16,0},{20,4},{24,8},{28,12},{32,48},... | collective-permute-start | bytes 393224 | tf_op jit(solution)/shard_map/ppermute | solution.py:313
  59.6 24.6 %collective-permute-start.10 = (f32[256,128]{1,0:T(8,128)S(1)}, f32[256,128]{1,0:T(8,128)S(1)}, u32[]{:S(2)}, u32[]{:S(2)}) collective-permute-start(f32[256,128]{1,0:T(8,128)S(1)} %shard_map.64.args_0_), channel_id=1, source_target_pairs={{0,16},{4,20},{8,24},{12,28},{16,0},{20,4},{24,8},{28,12},{32,48},... | collective-permute-start | bytes 393224 | tf_op jit(solution)/shard_map/ppermute | solution.py:313
  60.9 26.0 %collective-permute-start.8 = (f32[256,128]{1,0:T(8,128)S(1)}, f32[256,128]{1,0:T(8,128)S(1)}, u32[]{:S(2)}, u32[]{:S(2)}) collective-permute-start(f32[256,128]{1,0:T(8,128)S(1)} %shard_map.63.args_0_), channel_id=1, source_target_pairs={{0,16},{4,20},{8,24},{12,28},{16,0},{20,4},{24,8},{28,12},{32,48},... | collective-permute-start | bytes 393224 | tf_op jit(solution)/shard_map/ppermute | solution.py:313

commit v10 on v9

--- a/solution.py
+++ b/solution.py
@@ -100,16 +100,16 @@
     return split(rows), split(rows.T)
 
 
-def early_kernel(place, own_a, own_b, behind_a, behind_b, before_a, before_b, block, partial, yh, yl, fh, fl):
+def early_kernel(place, own, behind, before_a, before_b, block, partial, yh, yl, fh, fl):
     col = place[1]
-    size = own_a.shape[0] + own_b.shape[0]
+    size = own.shape[0]
     count = block.shape[0] // size
     width = partial.shape[1]
     total = None
-    behind = jnp.where(place[0] & 1 == 0, count - 1, 1)
-    for shift, parts in ((0, (own_a, own_b)), (behind, (behind_a, behind_b)), (count - behind, (before_a, before_b))):
+    back = jnp.where(place[0] & 1 == 0, count - 1, 1)
+    for shift, parts in ((0, (own,)), (back, (behind,)), (count - back, (before_a, before_b))):
         start = pl.multiple_of(lax.rem(col + shift, count) * size, size)
-        rows = jnp.concatenate([p[...] for p in parts], axis=0)
+        rows = parts[0][...] if len(parts) == 1 else jnp.concatenate([p[...] for p in parts], axis=0)
         here = pl.ds(start, size)
         straight, flipped = both_ways(rows, start)
         yh[here, :], yl[here, :] = straight
@@ -254,12 +254,11 @@
                 route.append((r * count + c, r * count + to))
         return lax.ppermute(values, ("row", "col"), route)
 
-    behind_a = ring(own_a, 1)
+    behind = ring(panel_y, 1)
     before_b = ring(own_b, -1)
-    behind_b = ring(own_b, 1)
     before_a = ring(own_a, -1)
-    opp_a = ring(behind_a, 1)
     opp_b = ring(before_b, -1)
+    opp_a = ring(behind[: size // 2], 1)
 
     square = shaped((width, width), BF16)
     mix = shaped((width, 2 * width), BF16)
@@ -282,11 +281,11 @@
     partial, yh, yl, fh, fl = call(
         early_kernel,
         out_shape=[shaped((width, w)), tall, tall, wide, wide],
-        in_specs=[SMEM] + [VMEM] * 7,
+        in_specs=[SMEM] + [VMEM] * 5,
         out_specs=[VMEM] * 5,
         mib=16,
         cost=(2 * cube, 4 << 20),
-    )(place, own_a, own_b, behind_a, behind_b, before_a, before_b, block)
+    )(place, panel_y, behind, before_a, before_b, block)
 
     outs = call(
         first_kernel,

time: 88.7 us -> 90.6 us (1.021)
  waiting for transfers between devices: 25.1 us -> 28.4 us
  starting transfers between devices: 37.1 us -> 35.8 us
    ppermute x6 -> x5, waiting for transfers between devices: 0.59 us -> 4.22 us  [ring(): return lax.ppermute(values, ('row', 'col'), route)]
    ppermute x6 -> x5, starting transfers between devices: 9.71 us -> 8.23 us  [ring(): return lax.ppermute(values, ('row', 'col'), route)]
  transfers between devices with their start and end apart: 27 -> 26, of which waited for: 10 -> 10; matrix products, arithmetic and copies ran while one was open for 0% -> 1% of each run, Pallas kernels for 22% -> 21%
where the time goes in v10:
time: 90.6 us; the launch traced here: 90.1 us
  starting transfers between devices  35.8 us (40%)
  waiting for transfers between devices  28.4 us (31%)
  Pallas kernels  24.3 us (27%)
  local copies, waits for them, and re-layouts  1.02 us (1%)
    ppermute x21, starting transfers between devices, swap(): return lax.ppermute(values, 'row', route)  27.6 us
    ppermute x21, waiting for transfers between devices, swap(): return lax.ppermute(values, 'row', route)  24.2 us
    ppermute x5, starting transfers between devices, ring(): return lax.ppermute(values, ('row', 'col'), route)  8.23 us
    pallas_call x4, Pallas kernels, update(): call(functools.partial(final_kernel, first, n), out_shape=shaped((rows, c...  4.93 us
    pallas_call x13, Pallas kernels, combine(): call(level_kernel, out_shape=[shaped((width, w)) for w in widths], in_spe...  4.78 us
    ppermute x5, waiting for transfers between devices, ring(): return lax.ppermute(values, ('row', 'col'), route)  4.22 us
    pallas_call x2, Pallas kernels, update(): call(functools.partial(rest_kernel, first), out_shape=shaped((rows, colum...  3.91 us
    pallas_call x3, Pallas kernels, update(): call(functools.partial(next_kernel, slice(first, first + w)), out_shape=[...  3.01 us
  transfers between devices with their start and end apart: 26, of which 10 were waited for; matrix products, arithmetic and copies ran while one was open for 1% of the time, Pallas kernels for 21%

profile of v10, /device:TPU:8, one launch (start us, length us, event | category | flops | bytes accessed | tf_op | source)
XLA Modules:
  0.0 90.1 jit_solution(11564642301320728599)
XLA Ops:
  0.0 1.5 %collective-permute-start = (f32[256,256]{1,0:T(8,128)}, f32[256,256]{1,0:T(8,128)S(1)}, u32[]{:S(2)}, u32[]{:S(2)}) collective-permute-start(f32[256,256]{1,0:T(8,128)} %own.1), channel_id=1, source_target_pairs={{0,1},{1,2},{2,3},{3,0},{4,7},{5,4},{6,5},{7,6},{8,9},{9,10},{10,1... | collective-permute-start | bytes 786440 | tf_op jit(solution)/shard_map/ppermute | solution.py:255
  2.5 1.8 %collective-permute-start.2 = (f32[128,256]{1,0:T(8,128)S(1)}, f32[128,256]{1,0:T(8,128)S(1)}, u32[]{:S(2)}, u32[]{:S(2)}) collective-permute-start(f32[128,256]{1,0:T(8,128)S(1)} %get-tuple-element.83), channel_id=1, source_target_pairs={{0,3},{1,0},{2,1},{3,2},{4,5},{5,6},{6,7},{7,4},{8,11},{9,8},{10,9... | collective-permute-start | bytes 393224 | tf_op jit(solution)/shard_map/ppermute | solution.py:255
  4.3 1.5 %collective-permute-start.1 = (f32[128,256]{1,0:T(8,128)S(1)}, f32[128,256]{1,0:T(8,128)S(1)}, u32[]{:S(2)}, u32[]{:S(2)}) collective-permute-start(f32[128,256]{1,0:T(8,128)S(1)} %get-tuple-element.84), channel_id=1, source_target_pairs={{0,3},{1,0},{2,1},{3,2},{4,5},{5,6},{6,7},{7,4},{8,11},{9,8},{10,9... | collective-permute-start | bytes 393224 | tf_op jit(solution)/shard_map/ppermute | solution.py:255
  5.9 1.7 %collective-permute-done.2.before_b = f32[128,256]{1,0:T(8,128)S(1)} collective-permute-done((f32[128,256]{1,0:T(8,128)S(1)}, f32[128,256]{1,0:T(8,128)S(1)}, u32[]{:S(2)}, u32[]{:S(2)}) %collective-permute-start.2) | collective-permute-done | bytes 131104 | tf_op jit(solution)/shard_map/ppermute | solution.py:255
  7.5 3.3 %collective-permute-start.4 = (f32[128,256]{1,0:T(8,128)S(1)}, f32[128,256]{1,0:T(8,128)S(1)}, u32[]{:S(2)}, u32[]{:S(2)}) collective-permute-start(f32[128,256]{1,0:T(8,128)S(1)} %collective-permute-done.2.before_b), channel_id=1, source_target_pairs={{0,3},{1,0},{2,1},{3,2},{4,5},{5,6},{6,7},{7,4},{8,11},{9,8},{10,9... | collective-permute-start | bytes 393224 | tf_op jit(solution)/shard_map/ppermute | solution.py:255
  11.0 2.2 %shard_map.55 = (bf16[256,256]{1,0:T(8,128)(2,1)S(1)}, bf16[256,256]{1,0:T(8,128)(2,1)S(1)}, bf16[256,512]{1,0:T(8,128)(2,1)S(1)}, bf16[256,512]{1,0:T(8,128)(2,1)S(1)}, f32[1024,256]{1,0:T(8,128)S(1)}) custom-call(s32[2]{0:T(128)S(1)} %pad_add_fusion.place, f32[256,256]{1,0:T(8,128)} %panel_t.1, f32[3,256,256]{2,1,0:T(8,128)} %tree_v.5, ...), custom_call_target="tpu_custom_call" | custom-call | flops 301989888 | bytes 1048576 | tf_op jit(solution)/shard_map/pallas_call | solution.py:271
  13.3 1.3 %shard_map.56 = (f32[256,256]{1,0:T(8,128)S(1)}, bf16[1024,256]{1,0:T(8,128)(2,1)S(1)}, bf16[1024,256]{1,0:T(8,128)(2,1)S(1)}, bf16[256,1024]{1,0:T(8,128)(2,1)S(1)}, bf16[256,1024]{1,0:T(8,128)(2,1)S(1)}) custom-call(s32[2]{0:T(128)S(1)} %pad_add_fusion.place, f32[256,256]{1,0:T(8,128)S(1)} %copy-done.3, f32[256,256]{1,0:T(8,128)S(1)} %collective-permute-done.behind, ...), custom_call_target="tpu_custom_call" | custom-call | flops 201326592 | bytes 4194304 | tf_op jit(solution)/shard_map/pallas_call | solution.py:281
  14.6 2.5 %collective-permute-done.3.opp_a = f32[128,256]{1,0:T(8,128)S(1)} collective-permute-done((f32[128,256]{1,0:T(8,128)S(1)}, f32[128,256]{1,0:T(8,128)S(1)}, u32[]{:S(2)}, u32[]{:S(2)}) %collective-permute-start.3) | collective-permute-done | bytes 131104 | tf_op jit(solution)/shard_map/ppermute | solution.py:255
  17.1 1.3 %shard_map.57 = (f32[256,128]{1,0:T(8,128)S(1)}, f32[256,128]{1,0:T(8,128)S(1)}, f32[256,256]{1,0:T(8,128)S(1)}, bf16[256,256]{1,0:T(8,128)(2,1)S(1)}, bf16[256,...) custom-call(s32[2]{0:T(128)S(1)} %pad_add_fusion.place, ...), custom_call_target="tpu_custom_call" | custom-call | flops 201326592 | bytes 2097152 | tf_op jit(solution)/shard_map/pallas_call | solution.py:290
  23.9 2.0 %collective-permute-start.19 = (f32[256,128]{1,0:T(8,128)S(1)}, f32[256,128]{1,0:T(8,128)S(1)}, u32[]{:S(2)}, u32[]{:S(2)}) collective-permute-start(f32[256,128]{1,0:T(8,128)S(1)} %shard_map.71.mine), channel_id=1, source_target_pairs={{0,8},{4,12},{8,0},{12,4},{16,24},{20,28},{24,16},{28,20},{32,40},... | collective-permute-start | bytes 393224 | tf_op jit(solution)/shard_map/ppermute | solution.py:312
  27.7 1.3 %collective-permute-start.24 = (f32[256,128]{1,0:T(8,128)S(1)}, f32[256,128]{1,0:T(8,128)S(1)}, u32[]{:S(2)}, u32[]{:S(2)}) collective-permute-start(f32[256,128]{1,0:T(8,128)S(1)} %get-tuple-element.78.mine), channel_id=1, source_target_pairs={{0,8},{4,12},{8,0},{12,4},{16,24},{20,28},{24,16},{28,20},{32,40},... | collective-permute-start | bytes 393224 | tf_op jit(solution)/shard_map/ppermute | solution.py:312
  30.3 1.9 %collective-permute-start.13 = (f32[256,128]{1,0:T(8,128)S(1)}, f32[256,128]{1,0:T(8,128)S(1)}, u32[]{:S(2)}, u32[]{:S(2)}) collective-permute-start(f32[256,128]{1,0:T(8,128)S(1)} %get-tuple-element.73.mine), channel_id=1, source_target_pairs={{0,8},{4,12},{8,0},{12,4},{16,24},{20,28},{24,16},{28,20},{32,40},... | collective-permute-start | bytes 393224 | tf_op jit(solution)/shard_map/ppermute | solution.py:312
  33.4 1.1 %shard_map.60 = (bf16[256,512]{1,0:T(8,128)(2,1)S(1)}, bf16[256,512]{1,0:T(8,128)(2,1)S(1)}) custom-call(s32[2]{0:T(128)S(1)} %pad_add_fusion.place, f32[3,256,256]{2,1,0:T(8,128)S(1)} %copy-done.1, f32[3,256,256]{2,1,0:T(8,128)S(1)} %copy-done.2, f32[256,256]{1,0:T(8,128)S(1)} %get-tuple-element.60.after.args_1_), custom_call_target="tpu_custom_call" | custom-call | flops 201326592 | bytes 1048576 | tf_op jit(solution)/shard_map/pallas_call | solution.py:327
  34.9 2.2 %collective-permute-start.8 = (f32[256,128]{1,0:T(8,128)S(1)}, f32[256,128]{1,0:T(8,128)S(1)}, u32[]{:S(2)}, u32[]{:S(2)}) collective-permute-start(f32[256,128]{1,0:T(8,128)S(1)} %get-tuple-element.70.mine), channel_id=1, source_target_pairs={{0,8},{4,12},{8,0},{12,4},{16,24},{20,28},{24,16},{28,20},{32,40},... | collective-permute-start | bytes 393224 | tf_op jit(solution)/shard_map/ppermute | solution.py:312
  37.9 3.6 %collective-permute-start.20 = (f32[256,128]{1,0:T(8,128)S(1)}, f32[256,128]{1,0:T(8,128)S(1)}, u32[]{:S(2)}, u32[]{:S(2)}) collective-permute-start(f32[256,128]{1,0:T(8,128)S(1)} %shard_map.72.args_2_), channel_id=1, source_target_pairs={{0,16},{4,20},{8,24},{12,28},{16,0},{20,4},{24,8},{28,12},{32,48},... | collective-permute-start | bytes 393224 | tf_op jit(solution)/shard_map/ppermute | solution.py:312
  43.0 2.4 %collective-permute-start.6 = (f32[256,128]{1,0:T(8,128)S(1)}, f32[256,128]{1,0:T(8,128)S(1)}, u32[]{:S(2)}, u32[]{:S(2)}) collective-permute-start(f32[256,128]{1,0:T(8,128)S(1)} %get-tuple-element.66.mine), channel_id=1, source_target_pairs={{0,8},{4,12},{8,0},{12,4},{16,24},{20,28},{24,16},{28,20},{32,40},... | collective-permute-start | bytes 393224 | tf_op jit(solution)/shard_map/ppermute | solution.py:312
  45.4 4.6 %collective-permute-done.11.theirs = f32[256,128]{1,0:T(8,128)S(1)} collective-permute-done((f32[256,128]{1,0:T(8,128)S(1)}, f32[256,128]{1,0:T(8,128)S(1)}, u32[]{:S(2)}, u32[]{:S(2)}) %collective-permute-start.11) | collective-permute-done | bytes 131104 | tf_op jit(solution)/shard_map/ppermute | solution.py:312
  50.0 2.5 %collective-permute-start.25 = (f32[256,128]{1,0:T(8,128)S(1)}, f32[256,128]{1,0:T(8,128)S(1)}, u32[]{:S(2)}, u32[]{:S(2)}) collective-permute-start(f32[256,128]{1,0:T(8,128)S(1)} %shard_map.76.args_6_), channel_id=1, source_target_pairs={{0,16},{4,20},{8,24},{12,28},{16,0},{20,4},{24,8},{28,12},{32,48},... | collective-permute-start | bytes 393224 | tf_op jit(solution)/shard_map/ppermute | solution.py:312
  52.5 2.0 %shard_map.77.args_2_ = f32[1024,1024]{1,0:T(8,128)} custom-call(f32[1024,1024]{1,0:T(8,128)S(1)} %copy-done, bf16[1024,256]{1,0:T(8,128)(2,1)S(1)} %get-tuple-element.79.yh, bf16[1024,256]{1,0:T(8,128)(2,1)S(1)} %get-tuple-element.80.yl, bf16[256,256]{1,0:T(8,128)(2,1)S(1)} %get-tuple-element.50.th, bf16[256,256]{1,0:T(8,128)(2,1)S(1)} %get-tuple-element.51.tl, ...), custom_call_target="tpu_custom_call" | custom-call | flops 1006632960 | bytes 4194304 | tf_op jit(solution)/shard_map/pallas_call | solution.py:365
  54.8 1.9 %collective-permute-start.23 = (f32[256,128]{1,0:T(8,128)S(1)}, f32[256,128]{1,0:T(8,128)S(1)}, u32[]{:S(2)}, u32[]{:S(2)}) collective-permute-start(f32[256,128]{1,0:T(8,128)S(1)} %shard_map.75.args_4_), channel_id=1, source_target_pairs={{0,16},{4,20},{8,24},{12,28},{16,0},{20,4},{24,8},{28,12},{32,48},... | collective-permute-start | bytes 393224 | tf_op jit(solution)/shard_map/ppermute | solution.py:312
  57.9 1.6 %collective-permute-start.14 = (f32[256,128]{1,0:T(8,128)S(1)}, f32[256,128]{1,0:T(8,128)S(1)}, u32[]{:S(2)}, u32[]{:S(2)}) collective-permute-start(f32[256,128]{1,0:T(8,128)S(1)} %shard_map.68.args_2_), channel_id=1, source_target_pairs={{0,16},{4,20},{8,24},{12,28},{16,0},{20,4},{24,8},{28,12},{32,48},... | collective-permute-start | bytes 393224 | tf_op jit(solution)/shard_map/ppermute | solution.py:312
  59.9 1.7 %collective-permute-start.12 = (f32[256,128]{1,0:T(8,128)S(1)}, f32[256,128]{1,0:T(8,128)S(1)}, u32[]{:S(2)}, u32[]{:S(2)}) collective-permute-start(f32[256,128]{1,0:T(8,128)S(1)} %shard_map.67.args_0_), channel_id=1, source_target_pairs={{0,16},{4,20},{8,24},{12,28},{16,0},{20,4},{24,8},{28,12},{32,48},... | collective-permute-start | bytes 393224 | tf_op jit(solution)/shard_map/ppermute | solution.py:312
  61.6 1.5 %collective-permute-start.9 = (f32[256,128]{1,0:T(8,128)S(1)}, f32[256,128]{1,0:T(8,128)S(1)}, u32[]{:S(2)}, u32[]{:S(2)}) collective-permute-start(f32[256,128]{1,0:T(8,128)S(1)} %shard_map.64.args_0_), channel_id=1, source_target_pairs={{0,16},{4,20},{8,24},{12,28},{16,0},{20,4},{24,8},{28,12},{32,48},... | collective-permute-start | bytes 393224 | tf_op jit(solution)/shard_map/ppermute | solution.py:312
  63.1 1.4 %collective-permute-start.7 = (f32[256,128]{1,0:T(8,128)S(1)}, f32[256,128]{1,0:T(8,128)S(1)}, u32[]{:S(2)}, u32[]{:S(2)}) collective-permute-start(f32[256,128]{1,0:T(8,128)S(1)} %shard_map.63.args_0_), channel_id=1, source_target_pairs={{0,16},{4,20},{8,24},{12,28},{16,0},{20,4},{24,8},{28,12},{32,48},... | collective-permute-start | bytes 393224 | tf_op jit(solution)/shard_map/ppermute | solution.py:312
  64.5 2.0 %shard_map.78.args_8_ = f32[1024,1024]{1,0:T(8,128)} custom-call(f32[1024,1024]{1,0:T(8,128)S(1)} %copy-done, bf16[1024,256]{1,0:T(8,128)(2,1)S(1)} %get-tuple-element.79.yh, bf16[1024,256]{1,0:T(8,128)(2,1)S(1)} %get-tuple-element.80.yl, bf16[256,256]{1,0:T(8,128)(2,1)S(1)} %get-tuple-element.50.th, ...), custom_call_target="tpu_custom_call", output_to_operand_aliasing={{}: (7, {})} | custom-call | flops 1006632960 | bytes 4194304 | tf_op jit(solution)/shard_map/pallas_call | solution.py:365
  66.5 9.9 %collective-permute-done.23.args_5_ = f32[256,128]{1,0:T(8,128)S(1)} collective-permute-done((f32[256,128]{1,0:T(8,128)S(1)}, f32[256,128]{1,0:T(8,128)S(1)}, u32[]{:S(2)}, u32[]{:S(2)}) %collective-permute-start.23) | collective-permute-done | bytes 131104 | tf_op jit(solution)/shard_map/ppermute | solution.py:312
  76.3 1.7 %shard_map.79.args_4_ = f32[1024,1024]{1,0:T(8,128)} custom-call(bf16[256,512]{1,0:T(8,128)(2,1)S(1)} %get-tuple-element.61.high, bf16[256,512]{1,0:T(8,128)(2,1)S(1)} %get-tuple-element.62.low, f32[256,128]{1,0:T(8,128)S(1)} %shard_map.70.args_0_, f32[256,128]{1,0:T(8,128)S(1)} %collective-permute-done.17.args_1_, ...), custom_call_target="tpu_custom_call", output_to_operand_aliasing={{}: (10, {})} | custom-call | flops 402653184 | bytes 1048576 | tf_op jit(solution)/shard_map/pallas_call | solution.py:384
  78.0 1.1 %collective-permute-done.14.args_3_ = f32[256,128]{1,0:T(8,128)S(1)} collective-permute-done((f32[256,128]{1,0:T(8,128)S(1)}, f32[256,128]{1,0:T(8,128)S(1)}, u32[]{:S(2)}, u32[]{:S(2)}) %collective-permute-start.14) | collective-permute-done | bytes 131104 | tf_op jit(solution)/shard_map/ppermute | solution.py:312
  79.2 4.2 %collective-permute-done.12.args_1_ = f32[256,128]{1,0:T(8,128)S(1)} collective-permute-done((f32[256,128]{1,0:T(8,128)S(1)}, f32[256,128]{1,0:T(8,128)S(1)}, u32[]{:S(2)}, u32[]{:S(2)}) %collective-permute-start.12) | collective-permute-done | bytes 131104 | tf_op jit(solution)/shard_map/ppermute | solution.py:312
  83.4 1.2 %shard_map.80.args_2_ = f32[1024,1024]{1,0:T(8,128)} custom-call(bf16[256,512]{1,0:T(8,128)(2,1)S(1)} %get-tuple-element.61.high, bf16[256,512]{1,0:T(8,128)(2,1)S(1)} %get-tuple-element.62.low, f32[256,128]{1,0:T(8,128)S(1)} %shard_map.67.args_0_, f32[256,128]{1,0:T(8,128)S(1)} %collective-permute-done.12.args_1_, ...), custom_call_target="tpu_custom_call", output_to_operand_aliasing={{}: (6, {})} | custom-call | flops 201326592 | bytes 1048576 | tf_op jit(solution)/shard_map/pallas_call | solution.py:384
  84.6 1.6 %collective-permute-done.9.args_1_ = f32[256,128]{1,0:T(8,128)S(1)} collective-permute-done((f32[256,128]{1,0:T(8,128)S(1)}, f32[256,128]{1,0:T(8,128)S(1)}, u32[]{:S(2)}, u32[]{:S(2)}) %collective-permute-start.9) | collective-permute-done | bytes 131104 | tf_op jit(solution)/shard_map/ppermute | solution.py:312
  87.2 1.7 %collective-permute-done.7.args_1_ = f32[256,128]{1,0:T(8,128)S(1)} collective-permute-done((f32[256,128]{1,0:T(8,128)S(1)}, f32[256,128]{1,0:T(8,128)S(1)}, u32[]{:S(2)}, u32[]{:S(2)}) %collective-permute-start.7) | collective-permute-done | bytes 131104 | tf_op jit(solution)/shard_map/ppermute | solution.py:312
  (59 shorter events, 17.2 us)
Async XLA Ops:
  0.0 13.3 %copy-start.3 = (f32[256,256]{1,0:T(8,128)S(1)}, f32[256,256]{1,0:T(8,128)}, u32[]{:S(2)}) copy-start(f32[256,256]{1,0:T(8,128)} %own.1) | copy-start | bytes 786436
  0.0 10.8 %collective-permute-start = (f32[256,256]{1,0:T(8,128)}, f32[256,256]{1,0:T(8,128)S(1)}, u32[]{:S(2)}, u32[]{:S(2)}) collective-permute-start(f32[256,256]{1,0:T(8,128)} %own.1), channel_id=1, source_target_pairs={{0,1},{1,2},{2,3},{3,0},{4,7},{5,4},{6,5},{7,6},{8,9},{9,10},{10,1... | collective-permute-start | bytes 786440 | tf_op jit(solution)/shard_map/ppermute | solution.py:255
  2.5 5.0 %collective-permute-start.2 = (f32[128,256]{1,0:T(8,128)S(1)}, f32[128,256]{1,0:T(8,128)S(1)}, u32[]{:S(2)}, u32[]{:S(2)}) collective-permute-start(f32[128,256]{1,0:T(8,128)S(1)} %get-tuple-element.83), channel_id=1, source_target_pairs={{0,3},{1,0},{2,1},{3,2},{4,5},{5,6},{6,7},{7,4},{8,11},{9,8},{10,9... | collective-permute-start | bytes 393224 | tf_op jit(solution)/shard_map/ppermute | solution.py:255
  4.3 8.9 %collective-permute-start.1 = (f32[128,256]{1,0:T(8,128)S(1)}, f32[128,256]{1,0:T(8,128)S(1)}, u32[]{:S(2)}, u32[]{:S(2)}) collective-permute-start(f32[128,256]{1,0:T(8,128)S(1)} %get-tuple-element.84), channel_id=1, source_target_pairs={{0,3},{1,0},{2,1},{3,2},{4,5},{5,6},{6,7},{7,4},{8,11},{9,8},{10,9... | collective-permute-start | bytes 393224 | tf_op jit(solution)/shard_map/ppermute | solution.py:255
  7.5 7.0 %collective-permute-start.4 = (f32[128,256]{1,0:T(8,128)S(1)}, f32[128,256]{1,0:T(8,128)S(1)}, u32[]{:S(2)}, u32[]{:S(2)}) collective-permute-start(f32[128,256]{1,0:T(8,128)S(1)} %collective-permute-done.2.before_b), channel_id=1, source_target_pairs={{0,3},{1,0},{2,1},{3,2},{4,5},{5,6},{6,7},{7,4},{8,11},{9,8},{10,9... | collective-permute-start | bytes 393224 | tf_op jit(solution)/shard_map/ppermute | solution.py:255
  10.8 6.3 %collective-permute-start.3 = (f32[128,256]{1,0:T(8,128)S(1)}, f32[128,256]{1,0:T(8,128)S(1)}, u32[]{:S(2)}, u32[]{:S(2)}) collective-permute-start(f32[128,256]{1,0:T(8,128)S(1)} %slice.12), channel_id=1, source_target_pairs={{0,1},{1,2},{2,3},{3,0},{4,7},{5,4},{6,5},{7,6},{8,9},{9,10},{10,1... | collective-permute-start | bytes 393224 | tf_op jit(solution)/shard_map/ppermute | solution.py:255
  13.2 5.9 %copy-start = (f32[1024,1024]{1,0:T(8,128)S(1)}, f32[1024,1024]{1,0:T(8,128)}, u32[]{:S(2)}) copy-start(f32[1024,1024]{1,0:T(8,128)} %block.9) | copy-start | bytes 12582916
  21.2 6.1 %collective-permute-start.21 = (f32[256,256]{1,0:T(8,128)S(1)}, f32[256,256]{1,0:T(8,128)S(1)}, u32[]{:S(2)}, u32[]{:S(2)}) collective-permute-start(f32[256,256]{1,0:T(8,128)S(1)} %get-tuple-element.76.mine), channel_id=1, source_target_pairs={{0,4},{4,0},{8,12},{12,8},{16,20},{20,16},{24,28},{28,24},{32,36},... | collective-permute-start | bytes 786440 | tf_op jit(solution)/shard_map/ppermute | solution.py:312
  21.3 2.2 %collective-permute-start.18 = (f32[256,128]{1,0:T(8,128)S(1)}, f32[256,128]{1,0:T(8,128)S(1)}, u32[]{:S(2)}, u32[]{:S(2)}) collective-permute-start(f32[256,128]{1,0:T(8,128)S(1)} %get-tuple-element.75.mine), channel_id=1, source_target_pairs={{0,4},{4,0},{8,12},{12,8},{16,20},{20,16},{24,28},{28,24},{32,36},... | collective-permute-start | bytes 393224 | tf_op jit(solution)/shard_map/ppermute | solution.py:312
  21.8 10.6 %copy-start.1 = (f32[3,256,256]{2,1,0:T(8,128)S(1)}, f32[3,256,256]{2,1,0:T(8,128)}, u32[]{:S(2)}) copy-start(f32[3,256,256]{2,1,0:T(8,128)} %tree_v.5) | copy-start | bytes 2359300
  21.8 10.6 %copy-start.2 = (f32[3,256,256]{2,1,0:T(8,128)S(1)}, f32[3,256,256]{2,1,0:T(8,128)}, u32[]{:S(2)}) copy-start(f32[3,256,256]{2,1,0:T(8,128)} %tree_t.5) | copy-start | bytes 2359300
  21.8 7.2 %collective-permute-start.10 = (f32[256,256]{1,0:T(8,128)S(1)}, f32[256,256]{1,0:T(8,128)S(1)}, u32[]{:S(2)}, u32[]{:S(2)}) collective-permute-start(f32[256,256]{1,0:T(8,128)S(1)} %get-tuple-element.71.mine), channel_id=1, source_target_pairs={{0,4},{4,0},{8,12},{12,8},{16,20},{20,16},{24,28},{28,24},{32,36},... | collective-permute-start | bytes 786440 | tf_op jit(solution)/shard_map/ppermute | solution.py:312
  22.9 9.4 %collective-permute-start.5 = (f32[256,256]{1,0:T(8,128)S(1)}, f32[256,256]{1,0:T(8,128)S(1)}, u32[]{:S(2)}, u32[]{:S(2)}) collective-permute-start(f32[256,256]{1,0:T(8,128)S(1)} %get-tuple-element.63.mine), channel_id=1, source_target_pairs={{0,4},{4,0},{8,12},{12,8},{16,20},{20,16},{24,28},{28,24},{32,36},... | collective-permute-start | bytes 786440 | tf_op jit(solution)/shard_map/ppermute | solution.py:312
  23.4 2.5 %collective-permute-start.15 = (f32[256,128]{1,0:T(8,128)S(1)}, f32[256,128]{1,0:T(8,128)S(1)}, u32[]{:S(2)}, u32[]{:S(2)}) collective-permute-start(f32[256,128]{1,0:T(8,128)S(1)} %get-tuple-element.74.mine), channel_id=1, source_target_pairs={{0,4},{4,0},{8,12},{12,8},{16,20},{20,16},{24,28},{28,24},{32,36},... | collective-permute-start | bytes 393224 | tf_op jit(solution)/shard_map/ppermute | solution.py:312
  23.9 6.5 %collective-permute-start.19 = (f32[256,128]{1,0:T(8,128)S(1)}, f32[256,128]{1,0:T(8,128)S(1)}, u32[]{:S(2)}, u32[]{:S(2)}) collective-permute-start(f32[256,128]{1,0:T(8,128)S(1)} %shard_map.71.mine), channel_id=1, source_target_pairs={{0,8},{4,12},{8,0},{12,4},{16,24},{20,28},{24,16},{28,20},{32,40},... | collective-permute-start | bytes 393224 | tf_op jit(solution)/shard_map/ppermute | solution.py:312
  26.3 8.6 %collective-permute-start.16 = (f32[256,128]{1,0:T(8,128)S(1)}, f32[256,128]{1,0:T(8,128)S(1)}, u32[]{:S(2)}, u32[]{:S(2)}) collective-permute-start(f32[256,128]{1,0:T(8,128)S(1)} %shard_map.69.mine), channel_id=1, source_target_pairs={{0,8},{4,12},{8,0},{12,4},{16,24},{20,28},{24,16},{28,20},{32,40},... | collective-permute-start | bytes 393224 | tf_op jit(solution)/shard_map/ppermute | solution.py:312
  27.7 10.2 %collective-permute-start.24 = (f32[256,128]{1,0:T(8,128)S(1)}, f32[256,128]{1,0:T(8,128)S(1)}, u32[]{:S(2)}, u32[]{:S(2)}) collective-permute-start(f32[256,128]{1,0:T(8,128)S(1)} %get-tuple-element.78.mine), channel_id=1, source_target_pairs={{0,8},{4,12},{8,0},{12,4},{16,24},{20,28},{24,16},{28,20},{32,40},... | collective-permute-start | bytes 393224 | tf_op jit(solution)/shard_map/ppermute | solution.py:312
  29.1 12.8 %collective-permute-start.22 = (f32[256,128]{1,0:T(8,128)S(1)}, f32[256,128]{1,0:T(8,128)S(1)}, u32[]{:S(2)}, u32[]{:S(2)}) collective-permute-start(f32[256,128]{1,0:T(8,128)S(1)} %get-tuple-element.77.mine), channel_id=1, source_target_pairs={{0,8},{4,12},{8,0},{12,4},{16,24},{20,28},{24,16},{28,20},{32,40},... | collective-permute-start | bytes 393224 | tf_op jit(solution)/shard_map/ppermute | solution.py:312
  30.3 12.6 %collective-permute-start.13 = (f32[256,128]{1,0:T(8,128)S(1)}, f32[256,128]{1,0:T(8,128)S(1)}, u32[]{:S(2)}, u32[]{:S(2)}) collective-permute-start(f32[256,128]{1,0:T(8,128)S(1)} %get-tuple-element.73.mine), channel_id=1, source_target_pairs={{0,8},{4,12},{8,0},{12,4},{16,24},{20,28},{24,16},{28,20},{32,40},... | collective-permute-start | bytes 393224 | tf_op jit(solution)/shard_map/ppermute | solution.py:312
  32.3 17.7 %collective-permute-start.11 = (f32[256,128]{1,0:T(8,128)S(1)}, f32[256,128]{1,0:T(8,128)S(1)}, u32[]{:S(2)}, u32[]{:S(2)}) collective-permute-start(f32[256,128]{1,0:T(8,128)S(1)} %get-tuple-element.72.mine), channel_id=1, source_target_pairs={{0,8},{4,12},{8,0},{12,4},{16,24},{20,28},{24,16},{28,20},{32,40},... | collective-permute-start | bytes 393224 | tf_op jit(solution)/shard_map/ppermute | solution.py:312
  34.9 19.9 %collective-permute-start.8 = (f32[256,128]{1,0:T(8,128)S(1)}, f32[256,128]{1,0:T(8,128)S(1)}, u32[]{:S(2)}, u32[]{:S(2)}) collective-permute-start(f32[256,128]{1,0:T(8,128)S(1)} %get-tuple-element.70.mine), channel_id=1, source_target_pairs={{0,8},{4,12},{8,0},{12,4},{16,24},{20,28},{24,16},{28,20},{32,40},... | collective-permute-start | bytes 393224 | tf_op jit(solution)/shard_map/ppermute | solution.py:312
  37.9 22.0 %collective-permute-start.20 = (f32[256,128]{1,0:T(8,128)S(1)}, f32[256,128]{1,0:T(8,128)S(1)}, u32[]{:S(2)}, u32[]{:S(2)}) collective-permute-start(f32[256,128]{1,0:T(8,128)S(1)} %shard_map.72.args_2_), channel_id=1, source_target_pairs={{0,16},{4,20},{8,24},{12,28},{16,0},{20,4},{24,8},{28,12},{32,48},... | collective-permute-start | bytes 393224 | tf_op jit(solution)/shard_map/ppermute | solution.py:312
  41.9 19.7 %collective-permute-start.17 = (f32[256,128]{1,0:T(8,128)S(1)}, f32[256,128]{1,0:T(8,128)S(1)}, u32[]{:S(2)}, u32[]{:S(2)}) collective-permute-start(f32[256,128]{1,0:T(8,128)S(1)} %shard_map.70.args_0_), channel_id=1, source_target_pairs={{0,16},{4,20},{8,24},{12,28},{16,0},{20,4},{24,8},{28,12},{32,48},... | collective-permute-start | bytes 393224 | tf_op jit(solution)/shard_map/ppermute | solution.py:312
  43.0 14.9 %collective-permute-start.6 = (f32[256,128]{1,0:T(8,128)S(1)}, f32[256,128]{1,0:T(8,128)S(1)}, u32[]{:S(2)}, u32[]{:S(2)}) collective-permute-start(f32[256,128]{1,0:T(8,128)S(1)} %get-tuple-element.66.mine), channel_id=1, source_target_pairs={{0,8},{4,12},{8,0},{12,4},{16,24},{20,28},{24,16},{28,20},{32,40},... | collective-permute-start | bytes 393224 | tf_op jit(solution)/shard_map/ppermute | solution.py:312
  50.0 13.1 %collective-permute-start.25 = (f32[256,128]{1,0:T(8,128)S(1)}, f32[256,128]{1,0:T(8,128)S(1)}, u32[]{:S(2)}, u32[]{:S(2)}) collective-permute-start(f32[256,128]{1,0:T(8,128)S(1)} %shard_map.76.args_6_), channel_id=1, source_target_pairs={{0,16},{4,20},{8,24},{12,28},{16,0},{20,4},{24,8},{28,12},{32,48},... | collective-permute-start | bytes 393224 | tf_op jit(solution)/shard_map/ppermute | solution.py:312
  54.8 21.5 %collective-permute-start.23 = (f32[256,128]{1,0:T(8,128)S(1)}, f32[256,128]{1,0:T(8,128)S(1)}, u32[]{:S(2)}, u32[]{:S(2)}) collective-permute-start(f32[256,128]{1,0:T(8,128)S(1)} %shard_map.75.args_4_), channel_id=1, source_target_pairs={{0,16},{4,20},{8,24},{12,28},{16,0},{20,4},{24,8},{28,12},{32,48},... | collective-permute-start | bytes 393224 | tf_op jit(solution)/shard_map/ppermute | solution.py:312
  57.9 21.3 %collective-permute-start.14 = (f32[256,128]{1,0:T(8,128)S(1)}, f32[256,128]{1,0:T(8,128)S(1)}, u32[]{:S(2)}, u32[]{:S(2)}) collective-permute-start(f32[256,128]{1,0:T(8,128)S(1)} %shard_map.68.args_2_), channel_id=1, source_target_pairs={{0,16},{4,20},{8,24},{12,28},{16,0},{20,4},{24,8},{28,12},{32,48},... | collective-permute-start | bytes 393224 | tf_op jit(solution)/shard_map/ppermute | solution.py:312
  59.9 23.5 %collective-permute-start.12 = (f32[256,128]{1,0:T(8,128)S(1)}, f32[256,128]{1,0:T(8,128)S(1)}, u32[]{:S(2)}, u32[]{:S(2)}) collective-permute-start(f32[256,128]{1,0:T(8,128)S(1)} %shard_map.67.args_0_), channel_id=1, source_target_pairs={{0,16},{4,20},{8,24},{12,28},{16,0},{20,4},{24,8},{28,12},{32,48},... | collective-permute-start | bytes 393224 | tf_op jit(solution)/shard_map/ppermute | solution.py:312
  61.6 24.6 %collective-permute-start.9 = (f32[256,128]{1,0:T(8,128)S(1)}, f32[256,128]{1,0:T(8,128)S(1)}, u32[]{:S(2)}, u32[]{:S(2)}) collective-permute-start(f32[256,128]{1,0:T(8,128)S(1)} %shard_map.64.args_0_), channel_id=1, source_target_pairs={{0,16},{4,20},{8,24},{12,28},{16,0},{20,4},{24,8},{28,12},{32,48},... | collective-permute-start | bytes 393224 | tf_op jit(solution)/shard_map/ppermute | solution.py:312
  63.1 25.8 %collective-permute-start.7 = (f32[256,128]{1,0:T(8,128)S(1)}, f32[256,128]{1,0:T(8,128)S(1)}, u32[]{:S(2)}, u32[]{:S(2)}) collective-permute-start(f32[256,128]{1,0:T(8,128)S(1)} %shard_map.63.args_0_), channel_id=1, source_target_pairs={{0,16},{4,20},{8,24},{12,28},{16,0},{20,4},{24,8},{28,12},{32,48},... | collective-permute-start | bytes 393224 | tf_op jit(solution)/shard_map/ppermute | solution.py:312

commit v11 on v9

--- a/solution.py
+++ b/solution.py
@@ -188,6 +188,11 @@
     return mine[...] - (one + two)
 
 
+def base_kernel(mine, high, low, base):
+    width = mine.shape[0]
+    base[...] = mine[...] - dot3((high[:, :width], low[:, :width]), split(mine[...]))
+
+
 def level_kernel(mine, theirs, high, low, *parts):
     store_parts(mixed(mine, theirs, high, low), parts)
 
@@ -198,10 +203,12 @@
     copies = []
     for k in range(count):
         mine, theirs = pieces[2 * k : 2 * k + 2]
-        both = split(jnp.concatenate([mine[...], theirs[...]], axis=0))
+        used = [theirs[...]] if count == 1 else [mine[...], theirs[...]]
+        both = split(jnp.concatenate(used, axis=0))
+        first_column = high.shape[1] - both[0].shape[0]
         for i in range(2):
             rows = slice(i * half, (i + 1) * half)
-            slots[k, i] = mine[rows, :] - dot3((high[rows, :], low[rows, :]), both)
+            slots[k, i] = mine[rows, :] - dot3((high[rows, first_column:], low[rows, first_column:]), both)
             target = out.at[pl.ds(i * half, half), pl.ds(first + k * w, w)]
             copies.append(pltpu.make_async_copy(slots.at[k, i], target, sems.at[k, i]))
             copies[-1].start()
@@ -311,6 +318,16 @@
     def swap(level, values):
         route = [(r, r ^ (1 << level)) for r in range(lax.axis_size("row"))]
         return lax.ppermute(values, "row", route)
+
+    def base_of(level, values):
+        return call(
+            base_kernel,
+            out_shape=shaped(values.shape),
+            in_specs=[VMEM] * 3,
+            out_specs=VMEM,
+            mib=8,
+            cost=(cube * values.shape[1] // width, 1 << 19),
+        )(values, *mixes[2 * level : 2 * level + 2])
 
     def combine(level, values, widths):
         w = values.shape[1]
@@ -381,7 +398,7 @@
         n = len(group)
         pieces = []
         for k in group:
-            pieces += [tops[k], swap(level, tops[k])]
+            pieces += [base_of(level, tops[k]) if n == 1 else tops[k], swap(level, tops[k])]
         out = call(
             functools.partial(final_kernel, first, n),
             out_shape=shaped((rows, columns)),

time: 88.7 us -> 88.7 us (level)
  transfers between devices with their start and end apart: 27 -> 27, of which waited for: 10 -> 12; matrix products, arithmetic and copies ran while one was open for 0% -> 0% of each run, Pallas kernels for 22% -> 24%
where the time goes in v11:
time: 88.7 us; the launch traced here: 87.8 us
  starting transfers between devices  37.4 us (42%)
  Pallas kernels  24.6 us (28%)
  waiting for transfers between devices  24.3 us (27%)
  local copies, waits for them, and re-layouts  1 us (1%)
    ppermute x21, starting transfers between devices, swap(): return lax.ppermute(values, 'row', route)  27.6 us
    ppermute x21, waiting for transfers between devices, swap(): return lax.ppermute(values, 'row', route)  23.7 us
    ppermute x6, starting transfers between devices, ring(): return lax.ppermute(values, ('row', 'col'), route)  9.71 us
    pallas_call x13, Pallas kernels, combine(): call(level_kernel, out_shape=[shaped((width, w)) for w in widths], in_spe...  4.77 us
    pallas_call x4, Pallas kernels, update(): call(functools.partial(final_kernel, first, n), out_shape=shaped((rows, c...  4.76 us
    pallas_call x2, Pallas kernels, update(): call(functools.partial(rest_kernel, first), out_shape=shaped((rows, colum...  3.91 us
    pallas_call x3, Pallas kernels, update(): call(functools.partial(next_kernel, slice(first, first + w)), out_shape=[...  3.02 us
    pallas_call x1, Pallas kernels, update(): call(prepare_kernel, out_shape=[square, square, mix, mix, shaped((rows, w...  2.23 us
  transfers between devices with their start and end apart: 27, of which 12 were waited for; matrix products, arithmetic and copies ran while one was open for 0% of the time, Pallas kernels for 24%

profile of v11, /device:TPU:8, one launch (start us, length us, event | category | flops | bytes accessed | tf_op | source)
XLA Modules:
  0.0 87.8 jit_solution(3529350035643002097)
XLA Ops:
  1.0 1.6 %collective-permute-start = (f32[128,256]{1,0:T(8,128)S(1)}, f32[128,256]{1,0:T(8,128)S(1)}, u32[]{:S(2)}, u32[]{:S(2)}) collective-permute-start(f32[128,256]{1,0:T(8,128)S(1)} %get-tuple-element.84.own_a), channel_id=1, source_target_pairs={{0,1},{1,2},{2,3},{3,0},{4,7},{5,4},{6,5},{7,6},{8,9},{9,10},{10,1... | collective-permute-start | bytes 393224 | tf_op jit(solution)/shard_map/ppermute | solution.py:262
  2.6 1.7 %collective-permute-start.3 = (f32[128,256]{1,0:T(8,128)S(1)}, f32[128,256]{1,0:T(8,128)S(1)}, u32[]{:S(2)}, u32[]{:S(2)}) collective-permute-start(f32[128,256]{1,0:T(8,128)S(1)} %get-tuple-element.83.own_b), channel_id=1, source_target_pairs={{0,3},{1,0},{2,1},{3,2},{4,5},{5,6},{6,7},{7,4},{8,11},{9,8},{10,9... | collective-permute-start | bytes 393224 | tf_op jit(solution)/shard_map/ppermute | solution.py:262
  4.6 3.0 %collective-permute-start.2 = (f32[128,256]{1,0:T(8,128)S(1)}, f32[128,256]{1,0:T(8,128)S(1)}, u32[]{:S(2)}, u32[]{:S(2)}) collective-permute-start(f32[128,256]{1,0:T(8,128)S(1)} %get-tuple-element.84.own_a), channel_id=1, source_target_pairs={{0,3},{1,0},{2,1},{3,2},{4,5},{5,6},{6,7},{7,4},{8,11},{9,8},{10,9... | collective-permute-start | bytes 393224 | tf_op jit(solution)/shard_map/ppermute | solution.py:262
  7.5 1.2 %collective-permute-start.4 = (f32[128,256]{1,0:T(8,128)S(1)}, f32[128,256]{1,0:T(8,128)S(1)}, u32[]{:S(2)}, u32[]{:S(2)}) collective-permute-start(f32[128,256]{1,0:T(8,128)S(1)} %collective-permute-done.behind_a), channel_id=1, source_target_pairs={{0,1},{1,2},{2,3},{3,0},{4,7},{5,4},{6,5},{7,6},{8,9},{9,10},{10,1... | collective-permute-start | bytes 393224 | tf_op jit(solution)/shard_map/ppermute | solution.py:262
  8.9 1.9 %collective-permute-start.5 = (f32[128,256]{1,0:T(8,128)S(1)}, f32[128,256]{1,0:T(8,128)S(1)}, u32[]{:S(2)}, u32[]{:S(2)}) collective-permute-start(f32[128,256]{1,0:T(8,128)S(1)} %collective-permute-done.3.before_b), channel_id=1, source_target_pairs={{0,3},{1,0},{2,1},{3,2},{4,5},{5,6},{6,7},{7,4},{8,11},{9,8},{10,9... | collective-permute-start | bytes 393224 | tf_op jit(solution)/shard_map/ppermute | solution.py:262
  10.9 2.2 %shard_map.55 = (bf16[256,256]{1,0:T(8,128)(2,1)S(1)}, bf16[256,256]{1,0:T(8,128)(2,1)S(1)}, bf16[256,512]{1,0:T(8,128)(2,1)S(1)}, bf16[256,512]{1,0:T(8,128)(2,1)S(1)}, f32[1024,256]{1,0:T(8,128)S(1)}) custom-call(s32[2]{0:T(128)S(1)} %pad_add_fusion.place, f32[256,256]{1,0:T(8,128)} %panel_t.1, f32[3,256,256]{2,1,0:T(8,128)} %tree_v.5, ...), custom_call_target="tpu_custom_call" | custom-call | flops 301989888 | bytes 1048576 | tf_op jit(solution)/shard_map/pallas_call | solution.py:279
  13.2 1.3 %shard_map.56 = (f32[256,256]{1,0:T(8,128)S(1)}, bf16[1024,256]{1,0:T(8,128)(2,1)S(1)}, bf16[1024,256]{1,0:T(8,128)(2,1)S(1)}, bf16[256,1024]{1,0:T(8,128)(2,1)S(1)}, bf16[256,1024]{1,0:T(8,128)(2,1)S(1)}) custom-call(s32[2]{0:T(128)S(1)} %pad_add_fusion.place, f32[128,256]{1,0:T(8,128)S(1)} %get-tuple-element.84.own_a, ...), custom_call_target="tpu_custom_call" | custom-call | flops 201326592 | bytes 4194304 | tf_op jit(solution)/shard_map/pallas_call | solution.py:289
  14.9 1.4 %shard_map.57 = (f32[256,128]{1,0:T(8,128)S(1)}, f32[256,128]{1,0:T(8,128)S(1)}, f32[256,256]{1,0:T(8,128)S(1)}, bf16[256,256]{1,0:T(8,128)(2,1)S(1)}, bf16[256,...) custom-call(s32[2]{0:T(128)S(1)} %pad_add_fusion.place, ...), custom_call_target="tpu_custom_call" | custom-call | flops 201326592 | bytes 2097152 | tf_op jit(solution)/shard_map/pallas_call | solution.py:298
  21.8 2.2 %collective-permute-start.20 = (f32[256,128]{1,0:T(8,128)S(1)}, f32[256,128]{1,0:T(8,128)S(1)}, u32[]{:S(2)}, u32[]{:S(2)}) collective-permute-start(f32[256,128]{1,0:T(8,128)S(1)} %shard_map.73.mine), channel_id=1, source_target_pairs={{0,8},{4,12},{8,0},{12,4},{16,24},{20,28},{24,16},{28,20},{32,40},... | collective-permute-start | bytes 393224 | tf_op jit(solution)/shard_map/ppermute | solution.py:320
  25.0 2.0 %collective-permute-start.25 = (f32[256,128]{1,0:T(8,128)S(1)}, f32[256,128]{1,0:T(8,128)S(1)}, u32[]{:S(2)}, u32[]{:S(2)}) collective-permute-start(f32[256,128]{1,0:T(8,128)S(1)} %get-tuple-element.78.mine), channel_id=1, source_target_pairs={{0,8},{4,12},{8,0},{12,4},{16,24},{20,28},{24,16},{28,20},{32,40},... | collective-permute-start | bytes 393224 | tf_op jit(solution)/shard_map/ppermute | solution.py:320
  28.5 1.9 %collective-permute-start.14 = (f32[256,128]{1,0:T(8,128)S(1)}, f32[256,128]{1,0:T(8,128)S(1)}, u32[]{:S(2)}, u32[]{:S(2)}) collective-permute-start(f32[256,128]{1,0:T(8,128)S(1)} %get-tuple-element.73.mine), channel_id=1, source_target_pairs={{0,8},{4,12},{8,0},{12,4},{16,24},{20,28},{24,16},{28,20},{32,40},... | collective-permute-start | bytes 393224 | tf_op jit(solution)/shard_map/ppermute | solution.py:320
  31.3 1.9 %collective-permute-start.12 = (f32[256,128]{1,0:T(8,128)S(1)}, f32[256,128]{1,0:T(8,128)S(1)}, u32[]{:S(2)}, u32[]{:S(2)}) collective-permute-start(f32[256,128]{1,0:T(8,128)S(1)} %get-tuple-element.72.mine), channel_id=1, source_target_pairs={{0,8},{4,12},{8,0},{12,4},{16,24},{20,28},{24,16},{28,20},{32,40},... | collective-permute-start | bytes 393224 | tf_op jit(solution)/shard_map/ppermute | solution.py:320
  35.0 3.4 %collective-permute-start.21 = (f32[256,128]{1,0:T(8,128)S(1)}, f32[256,128]{1,0:T(8,128)S(1)}, u32[]{:S(2)}, u32[]{:S(2)}) collective-permute-start(f32[256,128]{1,0:T(8,128)S(1)} %shard_map.74.args_2_), channel_id=1, source_target_pairs={{0,16},{4,20},{8,24},{12,28},{16,0},{20,4},{24,8},{28,12},{32,48},... | collective-permute-start | bytes 393224 | tf_op jit(solution)/shard_map/ppermute | solution.py:320
  39.6 1.3 %collective-permute-start.18 = (f32[256,128]{1,0:T(8,128)S(1)}, f32[256,128]{1,0:T(8,128)S(1)}, u32[]{:S(2)}, u32[]{:S(2)}) collective-permute-start(f32[256,128]{1,0:T(8,128)S(1)} %shard_map.72.args_0_), channel_id=1, source_target_pairs={{0,16},{4,20},{8,24},{12,28},{16,0},{20,4},{24,8},{28,12},{32,48},... | collective-permute-start | bytes 393224 | tf_op jit(solution)/shard_map/ppermute | solution.py:320
  40.8 3.1 %collective-permute-done.14.theirs = f32[256,128]{1,0:T(8,128)S(1)} collective-permute-done((f32[256,128]{1,0:T(8,128)S(1)}, f32[256,128]{1,0:T(8,128)S(1)}, u32[]{:S(2)}, u32[]{:S(2)}) %collective-permute-start.14) | collective-permute-done | bytes 131104 | tf_op jit(solution)/shard_map/ppermute | solution.py:320
  43.9 2.4 %collective-permute-start.7 = (f32[256,128]{1,0:T(8,128)S(1)}, f32[256,128]{1,0:T(8,128)S(1)}, u32[]{:S(2)}, u32[]{:S(2)}) collective-permute-start(f32[256,128]{1,0:T(8,128)S(1)} %get-tuple-element.66.mine), channel_id=1, source_target_pairs={{0,8},{4,12},{8,0},{12,4},{16,24},{20,28},{24,16},{28,20},{32,40},... | collective-permute-start | bytes 393224 | tf_op jit(solution)/shard_map/ppermute | solution.py:320
  46.3 1.4 %collective-permute-done.12.theirs = f32[256,128]{1,0:T(8,128)S(1)} collective-permute-done((f32[256,128]{1,0:T(8,128)S(1)}, f32[256,128]{1,0:T(8,128)S(1)}, u32[]{:S(2)}, u32[]{:S(2)}) %collective-permute-start.12) | collective-permute-done | bytes 131104 | tf_op jit(solution)/shard_map/ppermute | solution.py:320
  47.6 2.8 %collective-permute-start.26 = (f32[256,128]{1,0:T(8,128)S(1)}, f32[256,128]{1,0:T(8,128)S(1)}, u32[]{:S(2)}, u32[]{:S(2)}) collective-permute-start(f32[256,128]{1,0:T(8,128)S(1)} %shard_map.78.args_6_), channel_id=1, source_target_pairs={{0,16},{4,20},{8,24},{12,28},{16,0},{20,4},{24,8},{28,12},{32,48},... | collective-permute-start | bytes 393224 | tf_op jit(solution)/shard_map/ppermute | solution.py:320
  50.4 2.0 %shard_map.79.args_2_ = f32[1024,1024]{1,0:T(8,128)} custom-call(f32[1024,1024]{1,0:T(8,128)S(1)} %copy-done, bf16[1024,256]{1,0:T(8,128)(2,1)S(1)} %get-tuple-element.79.yh, bf16[1024,256]{1,0:T(8,128)(2,1)S(1)} %get-tuple-element.80.yl, bf16[256,256]{1,0:T(8,128)(2,1)S(1)} %get-tuple-element.50.th, bf16[256,256]{1,0:T(8,128)(2,1)S(1)} %get-tuple-element.51.tl, ...), custom_call_target="tpu_custom_call" | custom-call | flops 1006632960 | bytes 4194304 | tf_op jit(solution)/shard_map/pallas_call | solution.py:383
  53.5 1.5 %collective-permute-start.24 = (f32[256,128]{1,0:T(8,128)S(1)}, f32[256,128]{1,0:T(8,128)S(1)}, u32[]{:S(2)}, u32[]{:S(2)}) collective-permute-start(f32[256,128]{1,0:T(8,128)S(1)} %shard_map.77.args_4_), channel_id=1, source_target_pairs={{0,16},{4,20},{8,24},{12,28},{16,0},{20,4},{24,8},{28,12},{32,48},... | collective-permute-start | bytes 393224 | tf_op jit(solution)/shard_map/ppermute | solution.py:320
  56.3 1.3 %collective-permute-start.15 = (f32[256,128]{1,0:T(8,128)S(1)}, f32[256,128]{1,0:T(8,128)S(1)}, u32[]{:S(2)}, u32[]{:S(2)}) collective-permute-start(f32[256,128]{1,0:T(8,128)S(1)} %shard_map.70.args_2_), channel_id=1, source_target_pairs={{0,16},{4,20},{8,24},{12,28},{16,0},{20,4},{24,8},{28,12},{32,48},... | collective-permute-start | bytes 393224 | tf_op jit(solution)/shard_map/ppermute | solution.py:320
  58.0 1.9 %collective-permute-start.13 = (f32[256,128]{1,0:T(8,128)S(1)}, f32[256,128]{1,0:T(8,128)S(1)}, u32[]{:S(2)}, u32[]{:S(2)}) collective-permute-start(f32[256,128]{1,0:T(8,128)S(1)} %shard_map.69.args_0_), channel_id=1, source_target_pairs={{0,16},{4,20},{8,24},{12,28},{16,0},{20,4},{24,8},{28,12},{32,48},... | collective-permute-start | bytes 393224 | tf_op jit(solution)/shard_map/ppermute | solution.py:320
  59.9 1.3 %collective-permute-start.10 = (f32[256,128]{1,0:T(8,128)S(1)}, f32[256,128]{1,0:T(8,128)S(1)}, u32[]{:S(2)}, u32[]{:S(2)}) collective-permute-start(f32[256,128]{1,0:T(8,128)S(1)} %shard_map.65.mine), channel_id=1, source_target_pairs={{0,16},{4,20},{8,24},{12,28},{16,0},{20,4},{24,8},{28,12},{32,48},... | collective-permute-start | bytes 393224 | tf_op jit(solution)/shard_map/ppermute | solution.py:320
  61.2 1.6 %collective-permute-start.8 = (f32[256,128]{1,0:T(8,128)S(1)}, f32[256,128]{1,0:T(8,128)S(1)}, u32[]{:S(2)}, u32[]{:S(2)}) collective-permute-start(f32[256,128]{1,0:T(8,128)S(1)} %shard_map.63.mine), channel_id=1, source_target_pairs={{0,16},{4,20},{8,24},{12,28},{16,0},{20,4},{24,8},{28,12},{32,48},... | collective-permute-start | bytes 393224 | tf_op jit(solution)/shard_map/ppermute | solution.py:320
  62.9 2.0 %shard_map.80.args_8_ = f32[1024,1024]{1,0:T(8,128)} custom-call(f32[1024,1024]{1,0:T(8,128)S(1)} %copy-done, bf16[1024,256]{1,0:T(8,128)(2,1)S(1)} %get-tuple-element.79.yh, bf16[1024,256]{1,0:T(8,128)(2,1)S(1)} %get-tuple-element.80.yl, bf16[256,256]{1,0:T(8,128)(2,1)S(1)} %get-tuple-element.50.th, ...), custom_call_target="tpu_custom_call", output_to_operand_aliasing={{}: (7, {})} | custom-call | flops 1006632960 | bytes 4194304 | tf_op jit(solution)/shard_map/pallas_call | solution.py:383
  66.4 8.1 %collective-permute-done.24.args_5_ = f32[256,128]{1,0:T(8,128)S(1)} collective-permute-done((f32[256,128]{1,0:T(8,128)S(1)}, f32[256,128]{1,0:T(8,128)S(1)}, u32[]{:S(2)}, u32[]{:S(2)}) %collective-permute-start.24) | collective-permute-done | bytes 131104 | tf_op jit(solution)/shard_map/ppermute | solution.py:320
  74.5 1.7 %shard_map.81.args_4_ = f32[1024,1024]{1,0:T(8,128)} custom-call(bf16[256,512]{1,0:T(8,128)(2,1)S(1)} %get-tuple-element.61.high, bf16[256,512]{1,0:T(8,128)(2,1)S(1)} %get-tuple-element.62.low, f32[256,128]{1,0:T(8,128)S(1)} %shard_map.72.args_0_, f32[256,128]{1,0:T(8,128)S(1)} %collective-permute-done.18.args_1_, ...), custom_call_target="tpu_custom_call", output_to_operand_aliasing={{}: (10, {})} | custom-call | flops 402653184 | bytes 1048576 | tf_op jit(solution)/shard_map/pallas_call | solution.py:402
  76.2 1.1 %collective-permute-done.15.args_3_ = f32[256,128]{1,0:T(8,128)S(1)} collective-permute-done((f32[256,128]{1,0:T(8,128)S(1)}, f32[256,128]{1,0:T(8,128)S(1)}, u32[]{:S(2)}, u32[]{:S(2)}) %collective-permute-start.15) | collective-permute-done | bytes 131104 | tf_op jit(solution)/shard_map/ppermute | solution.py:320
  77.3 4.2 %collective-permute-done.13.args_1_ = f32[256,128]{1,0:T(8,128)S(1)} collective-permute-done((f32[256,128]{1,0:T(8,128)S(1)}, f32[256,128]{1,0:T(8,128)S(1)}, u32[]{:S(2)}, u32[]{:S(2)}) %collective-permute-start.13) | collective-permute-done | bytes 131104 | tf_op jit(solution)/shard_map/ppermute | solution.py:320
  81.5 1.2 %shard_map.82.args_2_ = f32[1024,1024]{1,0:T(8,128)} custom-call(bf16[256,512]{1,0:T(8,128)(2,1)S(1)} %get-tuple-element.61.high, bf16[256,512]{1,0:T(8,128)(2,1)S(1)} %get-tuple-element.62.low, f32[256,128]{1,0:T(8,128)S(1)} %shard_map.69.args_0_, f32[256,128]{1,0:T(8,128)S(1)} %collective-permute-done.13.args_1_, ...), custom_call_target="tpu_custom_call", output_to_operand_aliasing={{}: (6, {})} | custom-call | flops 201326592 | bytes 1048576 | tf_op jit(solution)/shard_map/pallas_call | solution.py:402
  82.7 1.6 %collective-permute-done.10.args_1_ = f32[256,128]{1,0:T(8,128)S(1)} collective-permute-done((f32[256,128]{1,0:T(8,128)S(1)}, f32[256,128]{1,0:T(8,128)S(1)}, u32[]{:S(2)}, u32[]{:S(2)}) %collective-permute-start.10) | collective-permute-done | bytes 131104 | tf_op jit(solution)/shard_map/ppermute | solution.py:320
  85.2 1.5 %collective-permute-done.8.args_1_ = f32[256,128]{1,0:T(8,128)S(1)} collective-permute-done((f32[256,128]{1,0:T(8,128)S(1)}, f32[256,128]{1,0:T(8,128)S(1)}, u32[]{:S(2)}, u32[]{:S(2)}) %collective-permute-start.8) | collective-permute-done | bytes 131104 | tf_op jit(solution)/shard_map/ppermute | solution.py:320
  (60 shorter events, 19.8 us)
Async XLA Ops:
  1.0 6.6 %collective-permute-start = (f32[128,256]{1,0:T(8,128)S(1)}, f32[128,256]{1,0:T(8,128)S(1)}, u32[]{:S(2)}, u32[]{:S(2)}) collective-permute-start(f32[128,256]{1,0:T(8,128)S(1)} %get-tuple-element.84.own_a), channel_id=1, source_target_pairs={{0,1},{1,2},{2,3},{3,0},{4,7},{5,4},{6,5},{7,6},{8,9},{9,10},{10,1... | collective-permute-start | bytes 393224 | tf_op jit(solution)/shard_map/ppermute | solution.py:262
  2.6 6.4 %collective-permute-start.3 = (f32[128,256]{1,0:T(8,128)S(1)}, f32[128,256]{1,0:T(8,128)S(1)}, u32[]{:S(2)}, u32[]{:S(2)}) collective-permute-start(f32[128,256]{1,0:T(8,128)S(1)} %get-tuple-element.83.own_b), channel_id=1, source_target_pairs={{0,3},{1,0},{2,1},{3,2},{4,5},{5,6},{6,7},{7,4},{8,11},{9,8},{10,9... | collective-permute-start | bytes 393224 | tf_op jit(solution)/shard_map/ppermute | solution.py:262
  4.3 8.8 %collective-permute-start.1 = (f32[128,256]{1,0:T(8,128)S(1)}, f32[128,256]{1,0:T(8,128)S(1)}, u32[]{:S(2)}, u32[]{:S(2)}) collective-permute-start(f32[128,256]{1,0:T(8,128)S(1)} %get-tuple-element.83.own_b), channel_id=1, source_target_pairs={{0,1},{1,2},{2,3},{3,0},{4,7},{5,4},{6,5},{7,6},{8,9},{9,10},{10,1... | collective-permute-start | bytes 393224 | tf_op jit(solution)/shard_map/ppermute | solution.py:262
  4.6 8.6 %collective-permute-start.2 = (f32[128,256]{1,0:T(8,128)S(1)}, f32[128,256]{1,0:T(8,128)S(1)}, u32[]{:S(2)}, u32[]{:S(2)}) collective-permute-start(f32[128,256]{1,0:T(8,128)S(1)} %get-tuple-element.84.own_a), channel_id=1, source_target_pairs={{0,3},{1,0},{2,1},{3,2},{4,5},{5,6},{6,7},{7,4},{8,11},{9,8},{10,9... | collective-permute-start | bytes 393224 | tf_op jit(solution)/shard_map/ppermute | solution.py:262
  7.5 7.4 %collective-permute-start.4 = (f32[128,256]{1,0:T(8,128)S(1)}, f32[128,256]{1,0:T(8,128)S(1)}, u32[]{:S(2)}, u32[]{:S(2)}) collective-permute-start(f32[128,256]{1,0:T(8,128)S(1)} %collective-permute-done.behind_a), channel_id=1, source_target_pairs={{0,1},{1,2},{2,3},{3,0},{4,7},{5,4},{6,5},{7,6},{8,9},{9,10},{10,1... | collective-permute-start | bytes 393224 | tf_op jit(solution)/shard_map/ppermute | solution.py:262
  8.9 6.0 %collective-permute-start.5 = (f32[128,256]{1,0:T(8,128)S(1)}, f32[128,256]{1,0:T(8,128)S(1)}, u32[]{:S(2)}, u32[]{:S(2)}) collective-permute-start(f32[128,256]{1,0:T(8,128)S(1)} %collective-permute-done.3.before_b), channel_id=1, source_target_pairs={{0,3},{1,0},{2,1},{3,2},{4,5},{5,6},{6,7},{7,4},{8,11},{9,8},{10,9... | collective-permute-start | bytes 393224 | tf_op jit(solution)/shard_map/ppermute | solution.py:262
  13.1 3.9 %copy-start = (f32[1024,1024]{1,0:T(8,128)S(1)}, f32[1024,1024]{1,0:T(8,128)}, u32[]{:S(2)}) copy-start(f32[1024,1024]{1,0:T(8,128)} %block.9) | copy-start | bytes 12582916
  18.0 6.5 %collective-permute-start.22 = (f32[256,256]{1,0:T(8,128)S(1)}, f32[256,256]{1,0:T(8,128)S(1)}, u32[]{:S(2)}, u32[]{:S(2)}) collective-permute-start(f32[256,256]{1,0:T(8,128)S(1)} %get-tuple-element.76.mine), channel_id=1, source_target_pairs={{0,4},{4,0},{8,12},{12,8},{16,20},{20,16},{24,28},{28,24},{32,36},... | collective-permute-start | bytes 786440 | tf_op jit(solution)/shard_map/ppermute | solution.py:320
  19.2 7.7 %collective-permute-start.11 = (f32[256,256]{1,0:T(8,128)S(1)}, f32[256,256]{1,0:T(8,128)S(1)}, u32[]{:S(2)}, u32[]{:S(2)}) collective-permute-start(f32[256,256]{1,0:T(8,128)S(1)} %get-tuple-element.71.mine), channel_id=1, source_target_pairs={{0,4},{4,0},{8,12},{12,8},{16,20},{20,16},{24,28},{28,24},{32,36},... | collective-permute-start | bytes 786440 | tf_op jit(solution)/shard_map/ppermute | solution.py:320
  19.7 1.7 %collective-permute-start.19 = (f32[256,128]{1,0:T(8,128)S(1)}, f32[256,128]{1,0:T(8,128)S(1)}, u32[]{:S(2)}, u32[]{:S(2)}) collective-permute-start(f32[256,128]{1,0:T(8,128)S(1)} %get-tuple-element.75.mine), channel_id=1, source_target_pairs={{0,4},{4,0},{8,12},{12,8},{16,20},{20,16},{24,28},{28,24},{32,36},... | collective-permute-start | bytes 393224 | tf_op jit(solution)/shard_map/ppermute | solution.py:320
  19.8 13.3 %copy-start.1 = (f32[3,256,256]{2,1,0:T(8,128)S(1)}, f32[3,256,256]{2,1,0:T(8,128)}, u32[]{:S(2)}) copy-start(f32[3,256,256]{2,1,0:T(8,128)} %tree_v.5) | copy-start | bytes 2359300
  19.8 13.3 %copy-start.2 = (f32[3,256,256]{2,1,0:T(8,128)S(1)}, f32[3,256,256]{2,1,0:T(8,128)}, u32[]{:S(2)}) copy-start(f32[3,256,256]{2,1,0:T(8,128)} %tree_t.5) | copy-start | bytes 2359300
  19.8 4.2 %collective-permute-start.16 = (f32[256,128]{1,0:T(8,128)S(1)}, f32[256,128]{1,0:T(8,128)S(1)}, u32[]{:S(2)}, u32[]{:S(2)}) collective-permute-start(f32[256,128]{1,0:T(8,128)S(1)} %get-tuple-element.74.mine), channel_id=1, source_target_pairs={{0,4},{4,0},{8,12},{12,8},{16,20},{20,16},{24,28},{28,24},{32,36},... | collective-permute-start | bytes 393224 | tf_op jit(solution)/shard_map/ppermute | solution.py:320
  21.2 13.7 %collective-permute-start.6 = (f32[256,256]{1,0:T(8,128)S(1)}, f32[256,256]{1,0:T(8,128)S(1)}, u32[]{:S(2)}, u32[]{:S(2)}) collective-permute-start(f32[256,256]{1,0:T(8,128)S(1)} %get-tuple-element.63.mine), channel_id=1, source_target_pairs={{0,4},{4,0},{8,12},{12,8},{16,20},{20,16},{24,28},{28,24},{32,36},... | collective-permute-start | bytes 786440 | tf_op jit(solution)/shard_map/ppermute | solution.py:320
  21.8 6.6 %collective-permute-start.20 = (f32[256,128]{1,0:T(8,128)S(1)}, f32[256,128]{1,0:T(8,128)S(1)}, u32[]{:S(2)}, u32[]{:S(2)}) collective-permute-start(f32[256,128]{1,0:T(8,128)S(1)} %shard_map.73.mine), channel_id=1, source_target_pairs={{0,8},{4,12},{8,0},{12,4},{16,24},{20,28},{24,16},{28,20},{32,40},... | collective-permute-start | bytes 393224 | tf_op jit(solution)/shard_map/ppermute | solution.py:320
  24.4 6.9 %collective-permute-start.17 = (f32[256,128]{1,0:T(8,128)S(1)}, f32[256,128]{1,0:T(8,128)S(1)}, u32[]{:S(2)}, u32[]{:S(2)}) collective-permute-start(f32[256,128]{1,0:T(8,128)S(1)} %shard_map.71.mine), channel_id=1, source_target_pairs={{0,8},{4,12},{8,0},{12,4},{16,24},{20,28},{24,16},{28,20},{32,40},... | collective-permute-start | bytes 393224 | tf_op jit(solution)/shard_map/ppermute | solution.py:320
  25.0 13.8 %collective-permute-start.25 = (f32[256,128]{1,0:T(8,128)S(1)}, f32[256,128]{1,0:T(8,128)S(1)}, u32[]{:S(2)}, u32[]{:S(2)}) collective-permute-start(f32[256,128]{1,0:T(8,128)S(1)} %get-tuple-element.78.mine), channel_id=1, source_target_pairs={{0,8},{4,12},{8,0},{12,4},{16,24},{20,28},{24,16},{28,20},{32,40},... | collective-permute-start | bytes 393224 | tf_op jit(solution)/shard_map/ppermute | solution.py:320
  27.0 12.6 %collective-permute-start.23 = (f32[256,128]{1,0:T(8,128)S(1)}, f32[256,128]{1,0:T(8,128)S(1)}, u32[]{:S(2)}, u32[]{:S(2)}) collective-permute-start(f32[256,128]{1,0:T(8,128)S(1)} %get-tuple-element.77.mine), channel_id=1, source_target_pairs={{0,8},{4,12},{8,0},{12,4},{16,24},{20,28},{24,16},{28,20},{32,40},... | collective-permute-start | bytes 393224 | tf_op jit(solution)/shard_map/ppermute | solution.py:320
  28.5 15.4 %collective-permute-start.14 = (f32[256,128]{1,0:T(8,128)S(1)}, f32[256,128]{1,0:T(8,128)S(1)}, u32[]{:S(2)}, u32[]{:S(2)}) collective-permute-start(f32[256,128]{1,0:T(8,128)S(1)} %get-tuple-element.73.mine), channel_id=1, source_target_pairs={{0,8},{4,12},{8,0},{12,4},{16,24},{20,28},{24,16},{28,20},{32,40},... | collective-permute-start | bytes 393224 | tf_op jit(solution)/shard_map/ppermute | solution.py:320
  31.3 16.4 %collective-permute-start.12 = (f32[256,128]{1,0:T(8,128)S(1)}, f32[256,128]{1,0:T(8,128)S(1)}, u32[]{:S(2)}, u32[]{:S(2)}) collective-permute-start(f32[256,128]{1,0:T(8,128)S(1)} %get-tuple-element.72.mine), channel_id=1, source_target_pairs={{0,8},{4,12},{8,0},{12,4},{16,24},{20,28},{24,16},{28,20},{32,40},... | collective-permute-start | bytes 393224 | tf_op jit(solution)/shard_map/ppermute | solution.py:320
  35.0 23.0 %collective-permute-start.21 = (f32[256,128]{1,0:T(8,128)S(1)}, f32[256,128]{1,0:T(8,128)S(1)}, u32[]{:S(2)}, u32[]{:S(2)}) collective-permute-start(f32[256,128]{1,0:T(8,128)S(1)} %shard_map.74.args_2_), channel_id=1, source_target_pairs={{0,16},{4,20},{8,24},{12,28},{16,0},{20,4},{24,8},{28,12},{32,48},... | collective-permute-start | bytes 393224 | tf_op jit(solution)/shard_map/ppermute | solution.py:320
  38.8 14.7 %collective-permute-start.9 = (f32[256,128]{1,0:T(8,128)S(1)}, f32[256,128]{1,0:T(8,128)S(1)}, u32[]{:S(2)}, u32[]{:S(2)}) collective-permute-start(f32[256,128]{1,0:T(8,128)S(1)} %get-tuple-element.70.mine), channel_id=1, source_target_pairs={{0,8},{4,12},{8,0},{12,4},{16,24},{20,28},{24,16},{28,20},{32,40},... | collective-permute-start | bytes 393224 | tf_op jit(solution)/shard_map/ppermute | solution.py:320
  39.6 20.4 %collective-permute-start.18 = (f32[256,128]{1,0:T(8,128)S(1)}, f32[256,128]{1,0:T(8,128)S(1)}, u32[]{:S(2)}, u32[]{:S(2)}) collective-permute-start(f32[256,128]{1,0:T(8,128)S(1)} %shard_map.72.args_0_), channel_id=1, source_target_pairs={{0,16},{4,20},{8,24},{12,28},{16,0},{20,4},{24,8},{28,12},{32,48},... | collective-permute-start | bytes 393224 | tf_op jit(solution)/shard_map/ppermute | solution.py:320
  43.9 12.4 %collective-permute-start.7 = (f32[256,128]{1,0:T(8,128)S(1)}, f32[256,128]{1,0:T(8,128)S(1)}, u32[]{:S(2)}, u32[]{:S(2)}) collective-permute-start(f32[256,128]{1,0:T(8,128)S(1)} %get-tuple-element.66.mine), channel_id=1, source_target_pairs={{0,8},{4,12},{8,0},{12,4},{16,24},{20,28},{24,16},{28,20},{32,40},... | collective-permute-start | bytes 393224 | tf_op jit(solution)/shard_map/ppermute | solution.py:320
  47.6 13.6 %collective-permute-start.26 = (f32[256,128]{1,0:T(8,128)S(1)}, f32[256,128]{1,0:T(8,128)S(1)}, u32[]{:S(2)}, u32[]{:S(2)}) collective-permute-start(f32[256,128]{1,0:T(8,128)S(1)} %shard_map.78.args_6_), channel_id=1, source_target_pairs={{0,16},{4,20},{8,24},{12,28},{16,0},{20,4},{24,8},{28,12},{32,48},... | collective-permute-start | bytes 393224 | tf_op jit(solution)/shard_map/ppermute | solution.py:320
  53.5 21.0 %collective-permute-start.24 = (f32[256,128]{1,0:T(8,128)S(1)}, f32[256,128]{1,0:T(8,128)S(1)}, u32[]{:S(2)}, u32[]{:S(2)}) collective-permute-start(f32[256,128]{1,0:T(8,128)S(1)} %shard_map.77.args_4_), channel_id=1, source_target_pairs={{0,16},{4,20},{8,24},{12,28},{16,0},{20,4},{24,8},{28,12},{32,48},... | collective-permute-start | bytes 393224 | tf_op jit(solution)/shard_map/ppermute | solution.py:320
  56.3 21.0 %collective-permute-start.15 = (f32[256,128]{1,0:T(8,128)S(1)}, f32[256,128]{1,0:T(8,128)S(1)}, u32[]{:S(2)}, u32[]{:S(2)}) collective-permute-start(f32[256,128]{1,0:T(8,128)S(1)} %shard_map.70.args_2_), channel_id=1, source_target_pairs={{0,16},{4,20},{8,24},{12,28},{16,0},{20,4},{24,8},{28,12},{32,48},... | collective-permute-start | bytes 393224 | tf_op jit(solution)/shard_map/ppermute | solution.py:320
  58.0 23.5 %collective-permute-start.13 = (f32[256,128]{1,0:T(8,128)S(1)}, f32[256,128]{1,0:T(8,128)S(1)}, u32[]{:S(2)}, u32[]{:S(2)}) collective-permute-start(f32[256,128]{1,0:T(8,128)S(1)} %shard_map.69.args_0_), channel_id=1, source_target_pairs={{0,16},{4,20},{8,24},{12,28},{16,0},{20,4},{24,8},{28,12},{32,48},... | collective-permute-start | bytes 393224 | tf_op jit(solution)/shard_map/ppermute | solution.py:320
  59.9 24.4 %collective-permute-start.10 = (f32[256,128]{1,0:T(8,128)S(1)}, f32[256,128]{1,0:T(8,128)S(1)}, u32[]{:S(2)}, u32[]{:S(2)}) collective-permute-start(f32[256,128]{1,0:T(8,128)S(1)} %shard_map.65.mine), channel_id=1, source_target_pairs={{0,16},{4,20},{8,24},{12,28},{16,0},{20,4},{24,8},{28,12},{32,48},... | collective-permute-start | bytes 393224 | tf_op jit(solution)/shard_map/ppermute | solution.py:320
  61.2 25.5 %collective-permute-start.8 = (f32[256,128]{1,0:T(8,128)S(1)}, f32[256,128]{1,0:T(8,128)S(1)}, u32[]{:S(2)}, u32[]{:S(2)}) collective-permute-start(f32[256,128]{1,0:T(8,128)S(1)} %shard_map.63.mine), channel_id=1, source_target_pairs={{0,16},{4,20},{8,24},{12,28},{16,0},{20,4},{24,8},{28,12},{32,48},... | collective-permute-start | bytes 393224 | tf_op jit(solution)/shard_map/ppermute | solution.py:320
